TPU v7x, 512 devices: a whole 4x4x16 slice. The times are simulated.
512 devices in a mesh: rows: 16 (over x, z_hi, core), batch: 32 (over z_lo, y).
Axes of the slice: x: 4, y: 4, z: 16 (z_hi: 2, z_lo: 8; z = z_hi * 8 + z_lo), core: 2. Of those that a mesh axis runs over, the one named last changes fastest.
Arguments:
- features: bfloat16 [384, 32, 32, 512], P('batch', 'rows'), may hold values from -12 to 12
- norm_gain: float32 [512], replicated, may hold values from 0.25 to 1.75
- norm_bias: float32 [512], replicated, may hold values from -2.5 to 2.5
- conv_weight: bfloat16 [4, 4608], replicated, may hold values from -0.09375 to 0.09375
- embed_weight: float32 [16, 1024], replicated, may hold values from -1.5 to 1.5
- embed_bias: float32 [1024], replicated, may hold values from -2.5 to 2.5
- proj_in: bfloat16 [1024, 2048], P('rows'), may hold values from -0.1875 to 0.1875
- proj_in_bias: float32 [2048], replicated, may hold values from -2.5 to 2.5
- proj_out: bfloat16 [2048, 768], P('rows'), may hold values from -0.125 to 0.125
- proj_out_bias: float32 [768], replicated, may hold values from -2.5 to 2.5
- targets: bfloat16 [384, 16, 16, 768], P('batch', 'rows'), may hold values from -6 to 6
Outputs:
- grad_features: bfloat16 [384, 32, 32, 512], P('batch', 'rows')
- grad_conv: float32 [4, 4608], replicated
- grad_gain: float32 [512], replicated
- grad_bias: float32 [512], replicated
- grad_embed: float32 [16, 1024], replicated
All inputs are finite; a program needn't handle non-finite values.
Results may differ from a plain program's by a relative error of at most 0.012.
Values may be sent and summed in bfloat16 or wider, within the bound.
No kernel may reach another device: no remote copies, remote signals or barrier semaphores. Data moves between devices by JAX's collectives and lax.ppermute only.
A program may use at most 128 MiB of HBM per device.

v0:
```python
import jax
import jax.numpy as jnp
from jax import lax
from jax.sharding import PartitionSpec as P

GROUPS = 32
LATENT = 4
PATCH = 2
ALIGN = 768


EPS_NORM = 1e-06
EPS_UNIT = 1e-06


def from_everyone(value, axis):
    length = lax.axis_size(axis)
    return lax.all_to_all(
        jnp.broadcast_to(value[None], (length, *value.shape)), axis, 0, 0, tiled=True
    )


def taken_together(value, axis):
    return from_everyone(value, axis).sum(axis=0)


def packed_total(arrays, axis):
    ends = [0]
    for a in arrays:
        ends.append(ends[-1] + a.size)
    so_far = taken_together(jnp.concatenate([a.ravel() for a in arrays]), axis)
    return tuple((so_far[b:e].reshape(a.shape) for a, b, e in zip(arrays, ends, ends[1:])))


def padded(block, sides, width):
    for axis, dim in sides:
        count = lax.axis_size(axis)
        forward = [(i, i + 1) for i in range(count - 1)]
        backward = [(target, source) for source, target in forward]
        low = lax.ppermute(
            lax.slice_in_dim(block, block.shape[dim] - width, None, axis=dim), axis, forward
        )
        high = lax.ppermute(lax.slice_in_dim(block, 0, width, axis=dim), axis, backward)
        block = jnp.concatenate([low, block, high], axis=dim)
    return block


def laid_out(blocks, dim):
    dims = list(blocks.shape[1:])
    dims[dim] *= blocks.shape[0]
    return jnp.moveaxis(blocks, 0, dim).reshape(dims)


def gather_packed(arrays, axis, dims):
    ravelled = jnp.concatenate([a.reshape(-1) for a in arrays])
    lines, at, finished = (lax.all_gather(ravelled, axis), 0, [])
    for a, dim in zip(arrays, dims):
        blocks = lines[:, at : at + a.size].reshape(-1, *a.shape)
        finished.append(laid_out(blocks, dim))
        at += a.size
    return tuple(finished)


def in_one(arrays, axis):
    ends = [0]
    for a in arrays:
        ends.append(ends[-1] + a.size)
    so_far = lax.psum(jnp.concatenate([a.ravel() for a in arrays]), axis)
    return tuple((so_far[b:e].reshape(a.shape) for a, b, e in zip(arrays, ends, ends[1:])))


def swish_slope(values):
    sig = jax.nn.sigmoid(values)
    return sig * (1.0 + values * (1.0 - sig))


def shards(
    features,
    norm_gain,
    norm_bias,
    conv_weight,
    embed_weight,
    embed_bias,
    proj_in,
    proj_in_bias,
    proj_out,
    proj_out_bias,
    targets,
):
    images, height, across, channels = features.shape
    per_group = channels // GROUPS
    members = lax.axis_size("rows") * height * across * per_group
    cell_count = images * height * across
    values = features.astype(jnp.float32)
    grouped = values.reshape(images, height * across, GROUPS, per_group)
    totals, squares = packed_total(
        (jnp.sum(grouped, axis=(1, 3)), jnp.sum(grouped * grouped, axis=(1, 3))), "rows"
    )
    group_mean = totals / members
    variance = squares / members - group_mean * group_mean
    centred = grouped - group_mean[:, None, :, None]
    inverse = lax.rsqrt(variance + EPS_NORM)[:, None, :, None]
    normed = (centred * inverse).reshape(images, height, across, channels)
    shifted = normed * norm_gain + norm_bias
    active = (shifted * jax.nn.sigmoid(shifted)).astype(jnp.bfloat16)
    active_flat = active.reshape(cell_count, channels)
    kernel_stack = (
        conv_weight.reshape(LATENT, 9, channels).transpose(2, 1, 0).reshape(channels, 9 * LATENT)
    )
    tap_terms = jnp.dot(active_flat, kernel_stack, preferred_element_type=jnp.float32)
    tap_terms = tap_terms.reshape(images, height, across, 9, LATENT)
    tap_pad = jnp.pad(tap_terms, ((0, 0), (2, 2), (1, 1), (0, 0), (0, 0)))
    extended = jnp.zeros((images, height + 2, across, LATENT), jnp.float32)
    for position in range(9):
        row_off, col_off = (position // 3, position % 3)
        extended = (
            extended
            + tap_pad[:, row_off : row_off + height + 2, col_off : col_off + across, position, :]
        )
    edges = jnp.concatenate([extended[:, 0:1], extended[:, height + 1 : height + 2]], axis=1)
    arrived = padded(edges, (("rows", 1),), 1)
    latent = extended[:, 1 : height + 1]
    latent = latent.at[:, 0].add(arrived[:, 0])
    latent = latent.at[:, height - 1].add(arrived[:, 3])
    tok_rows = height // PATCH
    tok_cols = across // PATCH
    tok_count = images * tok_rows * tok_cols
    patches = (
        latent.reshape(images, tok_rows, PATCH, tok_cols, PATCH, LATENT)
        .transpose(0, 1, 3, 2, 4, 5)
        .reshape(tok_count, PATCH * PATCH * LATENT)
    )
    embedded = (
        jnp.dot(patches, embed_weight, precision=lax.Precision.HIGHEST) + embed_bias
    ).astype(jnp.bfloat16)
    full_in, full_out = gather_packed((proj_in, proj_out), "rows", (0, 0))
    hidden_pre = jnp.dot(embedded, full_in, preferred_element_type=jnp.float32) + proj_in_bias
    hidden_act = (hidden_pre * jax.nn.sigmoid(hidden_pre)).astype(jnp.bfloat16)
    projected = jnp.dot(hidden_act, full_out, preferred_element_type=jnp.float32) + proj_out_bias
    target = targets.reshape(tok_count, ALIGN).astype(jnp.float32)
    unit_target = target * lax.rsqrt(jnp.sum(target * target, axis=1, keepdims=True) + EPS_UNIT)
    inv_len = lax.rsqrt(jnp.sum(projected * projected, axis=1, keepdims=True) + EPS_UNIT)
    unit_proj = projected * inv_len
    cosine = jnp.sum(unit_proj * unit_target, axis=1, keepdims=True)
    grad_out = (-inv_len * (unit_target - cosine * unit_proj)).astype(jnp.bfloat16)
    back_hidden = lax.dot_general(
        grad_out, full_out, (((1,), (1,)), ((), ())), preferred_element_type=jnp.float32
    )
    grad_hidden = (back_hidden * swish_slope(hidden_pre)).astype(jnp.bfloat16)
    grad_embedded = lax.dot_general(
        grad_hidden, full_in, (((1,), (1,)), ((), ())), preferred_element_type=jnp.float32
    )
    embed_part = lax.dot_general(
        patches, grad_embedded, (((0,), (0,)), ((), ())), precision=lax.Precision.HIGHEST
    )
    grad_patch = lax.dot_general(
        grad_embedded, embed_weight, (((1,), (1,)), ((), ())), precision=lax.Precision.HIGHEST
    )
    grad_latent = (
        grad_patch.reshape(images, tok_rows, tok_cols, PATCH, PATCH, LATENT)
        .transpose(0, 1, 3, 2, 4, 5)
        .reshape(images, height, across, LATENT)
        .astype(jnp.bfloat16)
    )
    grad_pad = padded(grad_latent, (("rows", 1),), 1)
    grad_pad = jnp.pad(grad_pad, ((0, 0), (0, 0), (1, 1), (0, 0)))
    shifted_grads = []
    for position in range(9):
        row_off, col_off = (position // 3, position % 3)
        shifted_grads.append(
            grad_pad[:, 2 - row_off : 2 - row_off + height, 2 - col_off : 2 - col_off + across, :]
        )
    grad_taps = jnp.concatenate(shifted_grads, axis=3).reshape(cell_count, 9 * LATENT)
    conv_stack = lax.dot_general(
        active_flat, grad_taps, (((0,), (0,)), ((), ())), preferred_element_type=jnp.float32
    )
    conv_part = (
        conv_stack.reshape(channels, 9, LATENT).transpose(2, 1, 0).reshape(LATENT, 9 * channels)
    )
    grad_active = lax.dot_general(
        grad_taps, kernel_stack, (((1,), (1,)), ((), ())), preferred_element_type=jnp.float32
    )
    flat_shift = shifted.reshape(cell_count, channels)
    flat_normed = normed.reshape(cell_count, channels)
    grad_shift = grad_active * swish_slope(flat_shift)
    gain_part = jnp.sum(grad_shift * flat_normed, axis=0)
    bias_part = jnp.sum(grad_shift, axis=0)
    grad_norm = (grad_shift * norm_gain).reshape(images, height * across, GROUPS, per_group)
    normed_groups = flat_normed.reshape(images, height * across, GROUPS, per_group)
    first, second = packed_total(
        (jnp.sum(grad_norm, axis=(1, 3)), jnp.sum(grad_norm * normed_groups, axis=(1, 3))), "rows"
    )
    grad_values = inverse * (
        grad_norm
        - (first / members)[:, None, :, None]
        - normed_groups * (second / members)[:, None, :, None]
    )
    grad_features = grad_values.reshape(images, height, across, channels).astype(jnp.bfloat16)
    grad_conv, grad_gain, grad_bias, grad_embed = in_one(
        (conv_part, gain_part, bias_part, embed_part), ("rows", "batch")
    )
    return (grad_features, grad_conv, grad_gain, grad_bias, grad_embed)


def solution(mesh):
    in_specs = (
        P("batch", "rows", None, None),
        P(),
        P(),
        P(),
        P(),
        P(),
        P("rows", None),
        P(),
        P("rows", None),
        P(),
        P("batch", "rows", None, None),
    )
    out_specs = (P("batch", "rows", None, None), P(), P(), P(), P())
    return jax.shard_map(shards, mesh=mesh, in_specs=in_specs, out_specs=out_specs, check_vma=False)
```

profile of v0, /device:TPU:1, one launch (start us, length us, event | category | flops | bytes accessed | tf_op | source)
XLA Modules:
  0.0 700.5 jit_solution(5764900346737735182)
XLA Ops:
  11.9 19.1 %all-to-all-start = ((f32[16,1,768]{2,1,0:T(1,128)}), f32[16,1,768]{2,1,0:T(1,128)S(1)}, u32[]{:S(2)}, u32[]{:S(2)}) async-start(f32[16,1,768]{2,1,0:T(1,128)} %broadcast_in_dim.4), calls=%async_computation | async-start | bytes 98304 | tf_op jit(solution)/shard_map/all_to_all | solution.py:18
  31.4 14.1 %all-to-all-done = f32[16,1,768]{2,1,0:T(1,128)S(1)} async-done(((f32[16,1,768]{2,1,0:T(1,128)}), f32[16,1,768]{2,1,0:T(1,128)S(1)}, u32[]{:S(2)}, u32[]{:S(2)}) %all-to-all-start) | async-done | bytes 49184 | tf_op jit(solution)/shard_map/all_to_all | solution.py:18
  50.3 2.6 collective-permute-start
  53.8 6.4 copy.181
  60.1 7.7 %reshape.319 = f32[12,64,32,16]{1,0,3,2:T(8,128)} reshape(f32[12,2,32,512]{2,1,0,3:T(2,128)} %copy.181) | data formatting | bytes 3145728 | tf_op jit(solution)/shard_map/reshape | solution.py:95
  68.0 2.1 collective-permute-start.1
  70.1 2.4 sub.64
  72.6 3.3 sub.71
  77.6 2.4 mul.171
  80.1 3.5 mul.179
  87.2 95.1 %all-gather.3.cloned.1.call-done = bf16[3670016]{0:T(1024)(128)(2,1)} async-done(((bf16[229376]{0:T(1024)(128)(2,1)}), bf16[3670016]{0:T(1024)(128)(2,1)}) %all-gather.3.cloned.1.call-update) | async-done | bytes 7340048 | tf_op jit(solution)/shard_map/all_gather | solution.py:56
  182.4 7.0 %reshape.315 = bf16[16,229376]{1,0:T(8,128)(2,1)} reshape(bf16[3670016]{0:T(1024)(128)(2,1)} %all-gather.3.cloned.1.call-done) | data formatting | bytes 14680064 | tf_op jit(solution)/shard_map/all_gather | solution.py:56
  189.4 4.5 slice.241
  193.9 5.0 reshape_reshape.10
  198.8 2.6 reshape_reshape.11
  201.4 3.4 convolution_add_fusion
  206.9 6.5 fusion.11
  217.6 2.6 collective-permute-start.3
  220.8 10.8 %collective-permute-done.3 = bf16[12,1,32,4]{0,2,3,1:T(8,128)(2,1)S(1)} collective-permute-done((bf16[12,1,32,4]{0,2,3,1:T(8,128)(2,1)S(1)}, bf16[12,1,32,4]{0,2,3,1:T(8,128)(2,1)S(1)}, u32[]{:S(2)}, u32[]{:S(2)}) %collective-permute-start.3) | collective-permute-done | bytes 3104 | tf_op jit(solution)/shard_map/ppermute | solution.py:43
  232.9 3.3 fusion.3
  238.6 3.9 reshape.302
  242.6 4.7 fusion.45
  248.3 15.3 %all-to-all-start.1 = ((f32[16,1,768]{2,1,0:T(1,128)}), f32[16,1,768]{2,1,0:T(1,128)S(1)}, u32[]{:S(2)}, u32[]{:S(2)}) async-start(f32[16,1,768]{2,1,0:T(1,128)} %broadcast_in_dim.5), calls=%async_computation.1 | async-start | bytes 98304 | tf_op jit(solution)/shard_map/all_to_all | solution.py:18
  263.6 423.6 %all-reduce.4.cloned.1.call-done = f32[35840]{0:T(1024)} async-done(((f32[35840]{0:T(1024)}), f32[35840]{0:T(1024)}) %all-reduce.4.cloned.1.call-update) | async-done | bytes 143376 | tf_op jit(solution)/shard_map/psum | solution.py:68
  (135 shorter events, 33.8 us)
Async XLA Ops:
  7.2 78.5 %copy-start = (f32[16,1024]{1,0:T(8,128)S(1)}, f32[16,1024]{1,0:T(8,128)}, u32[]{:S(2)}) copy-start(f32[16,1024]{1,0:T(8,128)} %param.19) | copy-start | bytes 196612
  7.2 3.1 copy-start.1
  7.2 175.2 %all-gather.3.cloned.1.call-start = ((), (), s32[]{:S(2)}) async-start(), calls=%async_computation.3 | async-start | bytes 7798784 | tf_op jit(solution)/shard_map/all_gather | solution.py:56
  9.4 21.6 %copy-start.9 = (bf16[12,1,16,768]{3,2,1,0:T(8,128)(2,1)S(1)}, bf16[12,1,16,768]{3,2,1,0:T(8,128)(2,1)}, u32[]{:S(2)}) copy-start(bf16[12,1,16,768]{3,2,1,0:T(8,128)(2,1)} %param.25) | copy-start | bytes 884740
  10.2 21.0 %copy-start.11 = (bf16[4,4608]{1,0:T(4,128)(2,1)S(1)}, bf16[4,4608]{1,0:T(4,128)(2,1)}, u32[]{:S(2)}) copy-start(bf16[4,4608]{1,0:T(4,128)(2,1)} %param.18) | copy-start | bytes 110596
  10.6 35.7 %copy-start.14 = (f32[512]{0:T(512)S(1)}, f32[512]{0:T(512)}, u32[]{:S(2)}) copy-start(f32[512]{0:T(512)} %param.17) | copy-start | bytes 6148
  10.6 35.7 %copy-start.15 = (f32[512]{0:T(512)S(1)}, f32[512]{0:T(512)}, u32[]{:S(2)}) copy-start(f32[512]{0:T(512)} %param.16) | copy-start | bytes 6148
  11.9 33.6 %all-to-all-start = ((f32[16,1,768]{2,1,0:T(1,128)}), f32[16,1,768]{2,1,0:T(1,128)S(1)}, u32[]{:S(2)}, u32[]{:S(2)}) async-start(f32[16,1,768]{2,1,0:T(1,128)} %broadcast_in_dim.4), calls=%async_computation | async-start | bytes 98304 | tf_op jit(solution)/shard_map/all_to_all | solution.py:18
  31.0 656.3 %all-reduce.4.cloned.1.call-start = ((), (), s32[]{:S(2)}) async-start(), calls=%async_computation.2 | async-start | bytes 286720 | tf_op jit(solution)/shard_map/psum | solution.py:68
  50.3 34.9 %collective-permute-start = (f32[12,1,32,4]{2,3,1,0:T(4,128)S(1)}, f32[12,1,32,4]{2,3,1,0:T(4,128)S(1)}, u32[]{:S(2)}, u32[]{:S(2)}) collective-permute-start(f32[12,1,32,4]{2,3,1,0:T(4,128)S(1)} %get-tuple-element.41), channel_id=1, source_target_pairs={{0,32},{32,64},{64,96},{96,128},{128,160},{160,192},{192,224},{224... | collective-permute-start | bytes 18440 | tf_op jit(solution)/shard_map/ppermute | solution.py:40
  68.0 17.2 %collective-permute-start.1 = (f32[12,1,32,4]{2,3,1,0:T(4,128)S(1)}, f32[12,1,32,4]{2,3,1,0:T(4,128)S(1)}, u32[]{:S(2)}, u32[]{:S(2)}) collective-permute-start(f32[12,1,32,4]{2,3,1,0:T(4,128)S(1)} %get-tuple-element.40), channel_id=1, source_target_pairs={{32,0},{64,32},{96,64},{128,96},{160,128},{192,160},{224,192},{256... | collective-permute-start | bytes 18440 | tf_op jit(solution)/shard_map/ppermute | solution.py:43
  83.5 2.1 copy-start.13
  193.9 5.0 slice-start
  198.8 2.6 copy-start.12
  201.4 3.5 copy-start.3
  201.4 3.5 copy-start.16
  204.9 1.2 copy-start.8
  204.9 1.5 copy-start.7
  213.4 6.8 copy-start.6
  215.7 5.1 collective-permute-start.2
  217.6 13.9 %collective-permute-start.3 = (bf16[12,1,32,4]{0,2,3,1:T(8,128)(2,1)S(1)}, bf16[12,1,32,4]{0,2,3,1:T(8,128)(2,1)S(1)}, u32[]{:S(2)}, u32[]{:S(2)}) collective-permute-start(bf16[12,1,32,4]{0,2,3,1:T(8,128)(2,1)S(1)} %get-tuple-element.43), channel_id=1, source_target_pairs={{32,0},{64,32},{96,64},{128,96},{160,128},{192,160},{224,192},{256... | collective-permute-start | bytes 9224 | tf_op jit(solution)/shard_map/ppermute | solution.py:43
  220.7 11.9 %copy-start.5 = (bf16[12,2,32,512]{3,2,1,0:T(8,128)(2,1)S(1)}, bf16[12,2,32,512]{3,2,1,0:T(8,128)(2,1)}, u32[]{:S(2)}) copy-start(bf16[12,2,32,512]{3,2,1,0:T(8,128)(2,1)} %copy-done.4) | copy-start | bytes 2359300
  231.8 1.1 copy-start.2
  248.3 443.4 %all-to-all-start.1 = ((f32[16,1,768]{2,1,0:T(1,128)}), f32[16,1,768]{2,1,0:T(1,128)S(1)}, u32[]{:S(2)}, u32[]{:S(2)}) async-start(f32[16,1,768]{2,1,0:T(1,128)} %broadcast_in_dim.5), calls=%async_computation.1 | async-start | bytes 98304 | tf_op jit(solution)/shard_map/all_to_all | solution.py:18
  (2 other events, 1.7 us)
Sparse Core Ops, SparseCore 0:
  11.9 170.4 all-gather.2
  237.1 450.1 all-reduce.3
where the time goes:
time: 701 us
  waiting for transfers between devices  544 us (78%)
  local copies, waits for them, and re-layouts  67.2 us (10%)
  starting transfers between devices  43.7 us (6%)
  matrix products  19.4 us (3%)
  between operations  14.6 us (2%)
  other arithmetic  12 us (2%)
    psum x1, waiting for transfers between devices, in_one(): so_far = lax.psum(jnp.concatenate([a.ravel() for a in arrays]), axis)  424 us
    all_gather x1, waiting for transfers between devices, gather_packed(): lines, at, finished = (lax.all_gather(ravelled, axis), 0, [])  95.1 us
    all_to_all x2, starting transfers between devices, from_everyone(): lax.all_to_all(jnp.broadcast_to(value[None], (length, *value.shape)), axi...  34.4 us
    all_to_all x2, waiting for transfers between devices, from_everyone(): lax.all_to_all(jnp.broadcast_to(value[None], (length, *value.shape)), axi...  14.1 us
    reshape x2, local copies, waits for them, and re-layouts, shards(): grouped = values.reshape(images, height * across, GROUPS, per_group)  14.1 us
  transfers between devices with their start and end apart: 8, of which 4 were waited for; matrix products, arithmetic and copies ran while one was open for 8% of the time, Pallas kernels for 0%

commit v1 on v0

v1 whole, which is shorter than its diff:
```python
import jax
import jax.numpy as jnp
from jax import lax
from jax.experimental import pallas as pl
from jax.experimental.pallas import tpu as pltpu
from jax.sharding import PartitionSpec as P

GROUPS = 32
LATENT = 4
PATCH = 2
EPS_NORM = 1e-06
EPS_UNIT = 1e-06

XS, ZHI, CORES, ZLO, YS = 4, 2, 2, 8, 4

HIGH = lax.Precision.HIGHEST
F32 = jnp.float32
BF16 = jnp.bfloat16
TAPS = 9
SUB = 8
LANES = 128
STAT_ROWS = 16
CHUNK = 32
AT_EMBED, AT_GAIN, AT_STAT = 9, 17, 18
PARAM_ROWS = 24


def params(limit_mb=48):
    return pltpu.CompilerParams(vmem_limit_bytes=limit_mb << 20)


def vmem():
    return pl.BlockSpec(memory_space=pltpu.VMEM)


def sigmoid(v):
    return 0.5 + 0.5 * jnp.tanh(0.5 * v)


def nt(a, b, precision=None):
    return lax.dot_general(
        a, b, (((1,), (1,)), ((), ())), preferred_element_type=F32, precision=precision
    )


def nn(a, b, precision=None):
    return lax.dot_general(
        a, b, (((1,), (0,)), ((), ())), preferred_element_type=F32, precision=precision
    )


def iota(shape, dim):
    return lax.broadcasted_iota(jnp.int32, shape, dim)


def to_groups(channels, per_group, offset):
    shape = (channels, LANES)
    return (iota(shape, 0) // per_group + offset == iota(shape, 1)).astype(F32)


def from_groups(channels, per_group, offset):
    shape = (LANES, channels)
    return (iota(shape, 1) // per_group + offset == iota(shape, 0)).astype(F32)


def stats_kernel(f_ref, out_ref, sums, squares):
    images, _, channels = f_ref.shape
    sums[...] = jnp.zeros_like(sums)
    squares[...] = jnp.zeros_like(squares)
    for i in range(images):
        v = f_ref[i].astype(F32)
        sums[i : i + 1, :] = jnp.sum(v, axis=0, keepdims=True)
        squares[i : i + 1, :] = jnp.sum(v * v, axis=0, keepdims=True)
    per_group = channels // GROUPS
    total = nn(sums[...], to_groups(channels, per_group, 0), HIGH) + nn(
        squares[...], to_groups(channels, per_group, GROUPS), HIGH
    )
    for r in range(out_ref.shape[0]):
        out_ref[r] = total


def group_stats(features, peers):
    channels = features.shape[-1]
    return pl.pallas_call(
        stats_kernel,
        out_shape=jax.ShapeDtypeStruct((peers, STAT_ROWS, LANES), F32),
        in_specs=[vmem()],
        out_specs=vmem(),
        scratch_shapes=[pltpu.VMEM((STAT_ROWS, channels), F32)] * 2,
        compiler_params=params(),
        name="stats",
    )(features)


def lane_masks(shape, across):
    lane = iota(shape, 1)
    return lane % across, (lane // across) % 2


def roll(v, shift):
    return pltpu.roll(v, shift % v.shape[1], 1)


def conv_kernel(
    across, members, st_ref, f_ref, gain_ref, bias_ref, k_ref,
    lat_ref, up_ref, down_ref, mean_ref, inv_ref, act,
):
    images, cells, channels = f_ref.shape
    per_group = channels // GROUPS
    total = jnp.sum(st_ref[...], axis=0)
    mean = nn(total, from_groups(channels, per_group, 0), HIGH) * (1.0 / members)
    square = nn(total, from_groups(channels, per_group, GROUPS), HIGH) * (1.0 / members)
    inv = lax.rsqrt(jnp.maximum(square - mean * mean, 0.0) + EPS_NORM)
    mean_ref[...] = mean
    inv_ref[...] = inv
    gain, bias = gain_ref[...], bias_ref[...]
    for i in range(images):
        v = f_ref[i].astype(F32)
        shifted = (v - mean[i : i + 1]) * inv[i : i + 1] * gain + bias
        act[i * cells : (i + 1) * cells, :] = (shifted * sigmoid(shifted)).astype(BF16)
    taps = nt(k_ref[...], act[...])
    shape = (SUB, images * cells)
    col, row = lane_masks(shape, across)

    def tap(position):
        return taps[position * SUB : (position + 1) * SUB]

    def line(dy):
        low = jnp.where(col > 0, roll(tap(3 * dy), 1), 0.0)
        high = jnp.where(col < across - 1, roll(tap(3 * dy + 2), -1), 0.0)
        return tap(3 * dy + 1) + low + high

    first, middle, last = line(0), line(1), line(2)
    last_up, first_down = roll(last, -across), roll(first, across)
    lat_ref[...] = middle + jnp.where(row == 0, last_up, first_down)
    up_ref[...] = jnp.where(row == 1, roll(last, across), 0.0)
    down_ref[...] = jnp.where(row == 0, roll(first, -across), 0.0)


def conv_forward(stats, features, gain, bias, kernel_rows, across, members):
    images, cells, channels = features.shape
    line = jax.ShapeDtypeStruct((SUB, images * cells), F32)
    stat = jax.ShapeDtypeStruct((STAT_ROWS, channels), F32)
    return pl.pallas_call(
        lambda *refs: conv_kernel(across, members, *refs),
        out_shape=(line, line, line, stat, stat),
        in_specs=[vmem()] * 5,
        out_specs=(vmem(),) * 5,
        scratch_shapes=[pltpu.VMEM((images * cells, channels), BF16)],
        compiler_params=params(),
        name="conv",
    )(stats, features, gain, bias, kernel_rows)


def mlp_kernel(
    across, width, hidden, align, at_ref, lat_ref, below_ref, above_ref, target_ref,
    ew_ref, eb_ref, pib_ref, pob_ref,
    h0, p0, m0, l0, t0, h1, p1, m1, l1, t1,
    embed_ref, gl_ref, w_in, w_out, pre, emb, acc, grad_emb, sems,
):
    x, core = at_ref[0], at_ref[1]
    depth = width // (XS * ZHI * CORES)
    slab = hidden // (XS * ZHI * CORES)
    copies = []

    def place(piece, at, source_x, zhi, of_core):
        shard = lax.rem(source_x, XS) * (ZHI * CORES) + zhi * CORES + of_core
        lines = pl.ds(at, depth)

        def put(columns, into):
            copy = pltpu.make_async_copy(piece.at[lines, columns], into, sems.at[len(copies)])
            copy.start()
            copies.append(copy)

        put(pl.ds(0, hidden), w_in.at[pl.ds(pl.multiple_of(shard * depth, depth), depth), :])
        for part in range(slab // depth):
            begin = pl.multiple_of(shard * slab + part * depth, depth)
            put(pl.ds(hidden + part * align, align), w_out.at[pl.ds(begin, depth), :])

    for of_core, (own, plus, minus, low, high) in (
        (core, (h0, p0, m0, l0, t0)),
        (1 - core, (h1, p1, m1, l1, t1)),
    ):
        for piece, step in ((own, 0), (plus, 1), (minus, XS - 1)):
            for zhi in range(ZHI):
                place(piece, zhi * depth, x + step, zhi, of_core)
        place(low, 0, x + 2, 0, of_core)
        place(high, 0, x + 2, 1, of_core)

    lat = lat_ref[...] + below_ref[...] + above_ref[...]
    top = lat.astype(BF16)
    rest = lat - top.astype(F32)
    mid = rest.astype(BF16)
    low_part = (rest - mid.astype(F32)).astype(BF16)
    split = jnp.concatenate(
        [top.astype(F32), mid.astype(F32), low_part.astype(F32)], axis=0
    ).astype(BF16)
    cells = lat.shape[1]
    tokens = target_ref.shape[0]
    room = 256
    cols = across // PATCH

    def selection(u, v):
        shape = (cells, room)
        token = iota(shape, 1)
        lane = (token // cols) * (PATCH * across) + u * across + (token % cols) * PATCH + v
        return jnp.where((lane == iota(shape, 0)) & (token < tokens), 1.0, 0.0).astype(BF16)

    picks = [selection(u, v) for u in range(PATCH) for v in range(PATCH)]
    lines = []
    for pick in picks:
        got = nn(split, pick)
        lines.append(got[0:SUB] + got[SUB : 2 * SUB] + got[2 * SUB :])
    patches_t = jnp.concatenate(lines, axis=0)
    patches = patches_t.T
    emb[...] = (nn(patches, ew_ref[...], HIGH) + eb_ref[...])[:tokens].astype(BF16)

    for copy in copies:
        copy.wait()

    step = 512
    acc[...] = jnp.zeros_like(acc)

    @pl.loop(0, hidden // step)
    def _(tile):
        at = pl.ds(pl.multiple_of(tile * step, step), step)
        h = nn(emb[...], w_in[:, at]) + pib_ref[:, at]
        pre[:, at] = h
        acc[...] += nn((h * sigmoid(h)).astype(BF16), w_out[at, :])

    projected = acc[...] + pob_ref[...]
    target = target_ref[...].astype(F32)
    unit_target = target * lax.rsqrt(jnp.sum(target * target, axis=1, keepdims=True) + EPS_UNIT)
    inv_len = lax.rsqrt(jnp.sum(projected * projected, axis=1, keepdims=True) + EPS_UNIT)
    unit_proj = projected * inv_len
    cosine = jnp.sum(unit_proj * unit_target, axis=1, keepdims=True)
    grad_out = (-inv_len * (unit_target - cosine * unit_proj)).astype(BF16)
    grad_emb[...] = jnp.zeros_like(grad_emb)

    @pl.loop(0, hidden // step)
    def _(tile):
        at = pl.ds(pl.multiple_of(tile * step, step), step)
        back = nt(grad_out, w_out[at, :])
        h = pre[:, at]
        sig = sigmoid(h)
        grad_hidden = (back * (sig * (1.0 + h * (1.0 - sig)))).astype(BF16)
        grad_emb[0:tokens, :] += nt(grad_hidden, w_in[:, at])

    grad = grad_emb[...]
    embed_ref[...] = nn(patches_t, grad, HIGH)
    grad_patch = nt(ew_ref[...], grad, HIGH)
    total = jnp.zeros((SUB, cells), F32)
    for position, pick in enumerate(picks):
        part = grad_patch[position * SUB : (position + 1) * SUB].astype(BF16)
        total = total + nt(part, pick)
    gl_ref[...] = total


def projector(at, lat, below, above, target, ew, eb, pib, pob, pieces, across):
    rows, width = ew.shape
    hidden, align = pib.shape[1], pob.shape[1]
    tokens = target.shape[0]
    flops = 2 * tokens * (2 * width * hidden + 2 * hidden * align)
    return pl.pallas_call(
        lambda *refs: mlp_kernel(across, width, hidden, align, *refs),
        out_shape=(
            jax.ShapeDtypeStruct((rows, width), F32),
            jax.ShapeDtypeStruct(lat.shape, F32),
        ),
        in_specs=[pl.BlockSpec(memory_space=pltpu.SMEM)]
        + [vmem()] * 8
        + [pl.BlockSpec(memory_space=pl.ANY)] * len(pieces),
        out_specs=(vmem(), vmem()),
        scratch_shapes=[
            pltpu.VMEM((width, hidden), BF16),
            pltpu.VMEM((hidden, align), BF16),
            pltpu.VMEM((tokens, hidden), F32),
            pltpu.VMEM((tokens, width), BF16),
            pltpu.VMEM((tokens, align), F32),
            pltpu.VMEM((256, width), F32),
            pltpu.SemaphoreType.DMA((48,)),
        ],
        compiler_params=params(),
        cost_estimate=pl.CostEstimate(
            flops=flops, bytes_accessed=8 << 20, transcendentals=2 * tokens * hidden
        ),
        name="projector",
    )(at, lat, below, above, target, ew, eb, pib, pob, *pieces)


def back_kernel(
    across, gl_ref, before_ref, after_ref, f_ref, mean_ref, inv_ref, gain_ref, bias_ref,
    k_ref, embed_ref, send_ref, gs_ref, act, grads_t, by_bias, by_gain,
):
    images, cells, channels = f_ref.shape
    per_group = channels // GROUPS
    gl, before, after = gl_ref[...], before_ref[...], after_ref[...]
    col, row = lane_masks(gl.shape, across)
    lines = (
        jnp.where(row == 0, roll(gl, -across), roll(after, across)),
        gl,
        jnp.where(row == 0, roll(before, -across), roll(gl, across)),
    )
    parts = []
    for g in lines:
        parts.append(jnp.where(col < across - 1, roll(g, -1), 0.0))
        parts.append(g)
        parts.append(jnp.where(col > 0, roll(g, 1), 0.0))
    parts.append(jnp.zeros((LANES - TAPS * SUB, gl.shape[1]), F32))
    grads = jnp.concatenate(parts, axis=0)
    grads_t[...] = grads.T.astype(BF16)
    gain, bias = gain_ref[...], bias_ref[...]
    by_bias[...] = jnp.zeros_like(by_bias)
    by_gain[...] = jnp.zeros_like(by_gain)
    for i in range(images):
        at = slice(i * cells, (i + 1) * cells)
        v = f_ref[i].astype(F32)
        normed = (v - mean_ref[i : i + 1, :]) * inv_ref[i : i + 1, :]
        shifted = normed * gain + bias
        sig = sigmoid(shifted)
        act[at, :] = (shifted * sig).astype(BF16)
        grad_active = nn(grads_t[at, :], k_ref[...])
        gs = grad_active * (sig * (1.0 + shifted * (1.0 - sig)))
        gs_ref[i] = gs
        by_bias[i : i + 1, :] = jnp.sum(gs, axis=0, keepdims=True)
        by_gain[i : i + 1, :] = jnp.sum(gs * normed, axis=0, keepdims=True)
    conv = nn(grads.astype(BF16), act[...])
    stat = nn(by_bias[...] * gain, to_groups(channels, per_group, 0), HIGH) + nn(
        by_gain[...] * gain, to_groups(channels, per_group, GROUPS), HIGH
    )
    bias_part = jnp.sum(by_bias[...], axis=0, keepdims=True)
    gain_part = jnp.sum(by_gain[...], axis=0, keepdims=True)
    blocks = channels // LANES
    for r in range(send_ref.shape[0]):
        block, latent = r // LATENT, r % LATENT
        lanes = slice(block * LANES, (block + 1) * LANES)
        for position in range(TAPS):
            line = position * SUB + latent
            send_ref[r, position : position + 1, :] = conv[line : line + 1, lanes]
        lanes = slice((r // 2) * LANES, (r // 2 + 1) * LANES)
        for half in range(2):
            line = (r % 2) * 2 * SUB + half * SUB
            send_ref[r, AT_EMBED + half * LATENT : AT_EMBED + (half + 1) * LATENT, :] = embed_ref[
                line : line + LATENT, lanes
            ]
        one = gain_part if r < blocks else bias_part
        lanes = slice((r % blocks) * LANES, (r % blocks + 1) * LANES)
        send_ref[r, AT_GAIN : AT_GAIN + 1, :] = one[:, lanes]
        send_ref[r, AT_STAT : AT_STAT + images, :] = stat[0:images]
        send_ref[r, AT_STAT + images : CHUNK, :] = jnp.zeros(
            (CHUNK - AT_STAT - images, LANES), F32
        )


def conv_backward(gl, before, after, features, mean, inv, gain, bias, kernel_rows, embed, across, peers):
    images, cells, channels = features.shape
    return pl.pallas_call(
        lambda *refs: back_kernel(across, *refs),
        out_shape=(
            jax.ShapeDtypeStruct((peers, CHUNK, LANES), F32),
            jax.ShapeDtypeStruct((images, cells, channels), F32),
        ),
        in_specs=[vmem()] * 10,
        out_specs=(vmem(), vmem()),
        scratch_shapes=[
            pltpu.VMEM((images * cells, channels), BF16),
            pltpu.VMEM((images * cells, LANES), BF16),
            pltpu.VMEM((STAT_ROWS, channels), F32),
            pltpu.VMEM((STAT_ROWS, channels), F32),
        ],
        compiler_params=params(),
        name="back",
    )(gl, before, after, features, mean, inv, gain, bias, kernel_rows, embed)


def last_kernel(members, got_ref, f_ref, mean_ref, inv_ref, gain_ref, gs_ref, out_ref):
    images, _, channels = f_ref.shape
    per_group = channels // GROUPS
    total = jnp.sum(got_ref[:, STAT_ROWS:CHUNK, :], axis=0)
    first = nn(total, from_groups(channels, per_group, 0), HIGH) * (1.0 / members)
    second = nn(total, from_groups(channels, per_group, GROUPS), HIGH) * (1.0 / members)
    gain = gain_ref[...]
    skip = AT_STAT - STAT_ROWS
    for i in range(images):
        v = f_ref[i].astype(F32)
        inv = inv_ref[i : i + 1, :]
        normed = (v - mean_ref[i : i + 1, :]) * inv
        j = i + skip
        out = inv * (gs_ref[i] * gain - first[j : j + 1] - normed * second[j : j + 1])
        out_ref[i] = out.astype(BF16)


def feature_grad(got, features, mean, inv, gain, grad_shift, members):
    return pl.pallas_call(
        lambda *refs: last_kernel(members, *refs),
        out_shape=jax.ShapeDtypeStruct(features.shape, BF16),
        in_specs=[vmem()] * 6,
        out_specs=vmem(),
        compiler_params=params(),
        cost_estimate=pl.CostEstimate(
            flops=10 * features.size, bytes_accessed=8 * features.size, transcendentals=0
        ),
        name="last",
    )(got, features, mean, inv, gain, grad_shift)


def unpack_kernel(got_ref, conv_ref, gain_ref, bias_ref, embed_ref):
    channels = gain_ref.shape[1]
    blocks = channels // LANES
    for r in range(got_ref.shape[0]):
        block, latent = r // LATENT, r % LATENT
        for position in range(TAPS):
            at = position * channels + block * LANES
            conv_ref[latent : latent + 1, at : at + LANES] = got_ref[r, position : position + 1, :]
        lanes = slice((r // 2) * LANES, (r // 2 + 1) * LANES)
        line = (r % 2) * SUB
        embed_ref[line : line + SUB, lanes] = got_ref[r, AT_EMBED : AT_EMBED + SUB, :]
        lanes = slice((r % blocks) * LANES, (r % blocks + 1) * LANES)
        if r < blocks:
            gain_ref[:, lanes] = got_ref[r, AT_GAIN : AT_GAIN + 1, :]
        elif r < 2 * blocks:
            bias_ref[:, lanes] = got_ref[r, AT_GAIN : AT_GAIN + 1, :]


def unpack(got, channels, width):
    return pl.pallas_call(
        unpack_kernel,
        out_shape=(
            jax.ShapeDtypeStruct((LATENT, TAPS * channels), F32),
            jax.ShapeDtypeStruct((1, channels), F32),
            jax.ShapeDtypeStruct((1, channels), F32),
            jax.ShapeDtypeStruct((PATCH * PATCH * LATENT, width), F32),
        ),
        in_specs=[vmem()],
        out_specs=(vmem(),) * 4,
        compiler_params=params(),
        name="unpack",
    )(got)


def from_everyone(value, axis):
    length = lax.axis_size(axis)
    return lax.all_to_all(
        jnp.broadcast_to(value[None], (length, *value.shape)), axis, 0, 0, tiled=True
    )


def moved(value, where):
    pairs = []
    for x in range(XS):
        for zhi in range(ZHI):
            for core in range(CORES):
                for zlo in range(ZLO):
                    for y in range(YS):
                        a, b, c, d, e = where(x, zhi, core, zlo, y)
                        source = ((x * ZHI + zhi) * CORES + core) * (ZLO * YS) + zlo * YS + y
                        goal = ((a * ZHI + b) * CORES + c) * (ZLO * YS) + d * YS + e
                        pairs.append((source, goal))
    return lax.ppermute(value, ("rows", "batch"), pairs)


def gathered(shard):
    depth = shard.shape[0]
    rows, batch = lax.axis_index("rows"), lax.axis_index("batch")
    zhi, y = (rows // CORES) % ZHI, batch % YS
    part = depth // YS
    mine = lax.dynamic_slice_in_dim(shard, y * part, part, axis=0)
    cross = moved(mine, lambda x, h, c, d, y: (x, 1 - h, c, ZLO - 1 - d, y))
    other = moved(cross, lambda x, h, c, d, y: (x, h, c, d, y ^ 1))
    even = y % 2 == 0
    pair = jnp.concatenate(
        [jnp.where(even, cross, other), jnp.where(even, other, cross)], axis=0
    )
    far = moved(pair, lambda x, h, c, d, y: (x, h, c, d, YS - 1 - y))
    low = y < 2
    across = jnp.concatenate([jnp.where(low, pair, far), jnp.where(low, far, pair)], axis=0)
    first = zhi == 0
    both = jnp.concatenate(
        [jnp.where(first, shard, across), jnp.where(first, across, shard)], axis=0
    )
    plus = moved(both, lambda x, h, c, d, y: ((x + XS - 1) % XS, h, c, d, y))
    minus = moved(both, lambda x, h, c, d, y: ((x + 1) % XS, h, c, d, y))
    low_half = moved(plus[:depth], lambda x, h, c, d, y: ((x + XS - 1) % XS, h, c, d, y))
    high_half = moved(minus[depth:], lambda x, h, c, d, y: ((x + 1) % XS, h, c, d, y))
    held = [both, plus, minus, low_half, high_half]
    swapped = [moved(v, lambda x, h, c, d, y: (x, h, 1 - c, d, y)) for v in held]
    return held + swapped


def neighbours(up, down):
    count = lax.axis_size("rows")
    forward = [(i, i + 1) for i in range(count - 1)]
    backward = [(b, a) for a, b in forward]
    return lax.ppermute(up, "rows", backward), lax.ppermute(down, "rows", forward)


def shards(
    features,
    norm_gain,
    norm_bias,
    conv_weight,
    embed_weight,
    embed_bias,
    proj_in,
    proj_in_bias,
    proj_out,
    proj_out_bias,
    targets,
):
    images, height, across, channels = features.shape
    width, align = embed_weight.shape[1], proj_out.shape[1]
    peers = lax.axis_size("rows")
    members = peers * height * across * (channels // GROUPS)
    flat = features.reshape(images, height * across, channels)
    gain, bias = norm_gain.reshape(1, channels), norm_bias.reshape(1, channels)
    depth = proj_in.shape[0]
    shard = jnp.concatenate(
        [proj_in] + [proj_out[at : at + depth] for at in range(0, proj_out.shape[0], depth)], axis=1
    )
    pieces = gathered(shard)
    taps = conv_weight.reshape(LATENT, TAPS, channels).transpose(1, 0, 2)
    taps = jnp.pad(taps, ((0, 0), (0, SUB - LATENT), (0, 0))).reshape(TAPS * SUB, channels)
    taps_full = jnp.pad(taps, ((0, LANES - TAPS * SUB), (0, 0)))
    spread = jnp.pad(
        embed_weight.reshape(PATCH * PATCH, LATENT, width), ((0, 0), (0, SUB - LATENT), (0, 0))
    ).reshape(PATCH * PATCH * SUB, width)

    stats = lax.all_to_all(group_stats(flat, peers), "rows", 0, 0, tiled=True)
    lat, up, down, mean, inv = conv_forward(stats, flat, gain, bias, taps, across, members)
    above, below = neighbours(up, down)
    rows = lax.axis_index("rows")
    at = jnp.stack([rows // (ZHI * CORES), rows % CORES]).astype(jnp.int32)
    target = targets.reshape(-1, align)
    embed_part, grad_lat = projector(
        at, lat, below, above, target, spread, embed_bias.reshape(1, -1),
        proj_in_bias.reshape(1, -1), proj_out_bias.reshape(1, -1), pieces, across,
    )
    after, before = neighbours(grad_lat, grad_lat)
    send, grad_shift = conv_backward(
        grad_lat, before, after, flat, mean, inv, gain, bias, taps_full, embed_part, across, peers
    )
    got = lax.all_to_all(send, "rows", 0, 0, tiled=True)
    chunk = jnp.sum(got[:, :PARAM_ROWS], axis=0)
    grad_features = feature_grad(got, flat, mean, inv, gain, grad_shift, members)
    chunk = jnp.sum(from_everyone(chunk, "batch"), axis=0)
    everything = from_everyone(chunk, "rows")
    grad_conv, grad_gain, grad_bias, grad_embed = unpack(everything, channels, width)
    return (
        grad_features.reshape(features.shape),
        grad_conv,
        grad_gain.reshape(channels),
        grad_bias.reshape(channels),
        grad_embed,
    )


def solution(mesh):
    in_specs = (
        P("batch", "rows", None, None),
        P(),
        P(),
        P(),
        P(),
        P(),
        P("rows", None),
        P(),
        P("rows", None),
        P(),
        P("batch", "rows", None, None),
    )
    out_specs = (P("batch", "rows", None, None), P(), P(), P(), P())
    return jax.shard_map(shards, mesh=mesh, in_specs=in_specs, out_specs=out_specs, check_vma=False)
```

time: 701 us -> 247 us (0.35)
  the two profiles are of different devices: /device:TPU:1 before, /device:TPU:32 now
where the time goes in v1:
time: 247 us; the launch traced here: 246 us
  blocking collectives  77.1 us (31%)
  starting transfers between devices  75.4 us (31%)
  waiting for transfers between devices  66.7 us (27%)
  Pallas kernels  20.3 us (8%)
  local copies, waits for them, and re-layouts  3.91 us (2%)
    ppermute x12, starting transfers between devices, moved(): return lax.ppermute(value, ('rows', 'batch'), pairs)  53 us
    all_to_all x1, blocking collectives, shards(): got = lax.all_to_all(send, 'rows', 0, 0, tiled=True)  44.3 us
    all_to_all x1, blocking collectives, from_everyone(): lax.all_to_all(jnp.broadcast_to(value[None], (length, *value.shape)), axi...  32.8 us
    ppermute x12, waiting for transfers between devices, moved(): return lax.ppermute(value, ('rows', 'batch'), pairs)  25.1 us
    all_to_all x1, waiting for transfers between devices, from_everyone(): lax.all_to_all(jnp.broadcast_to(value[None], (length, *value.shape)), axi...  20.8 us
    all_to_all x1, waiting for transfers between devices, shards(): stats = lax.all_to_all(group_stats(flat, peers), 'rows', 0, 0, tiled=True)  19.1 us
    pallas_call x1, Pallas kernels, projector(): pl.pallas_call(lambda *refs: mlp_kernel(across, width, hidden, align, *re...  13.6 us
    all_to_all x1, starting transfers between devices, shards(): stats = lax.all_to_all(group_stats(flat, peers), 'rows', 0, 0, tiled=True)  12.2 us
  transfers between devices with their start and end apart: 18, of which 9 were waited for; matrix products, arithmetic and copies ran while one was open for 1% of the time, Pallas kernels for 2%

profile of v1, /device:TPU:32, one launch (start us, length us, event | category | flops | bytes accessed | tf_op | source)
XLA Modules:
  0.0 246.1 jit_solution(7106605715162011936)
XLA Ops:
  2.7 11.4 %collective-permute-start.2 = (bf16[16,3584]{1,0:T(8,128)(2,1)S(1)}, bf16[16,3584]{1,0:T(8,128)(2,1)S(1)}, u32[]{:S(2)}, u32[]{:S(2)}) collective-permute-start(bf16[16,3584]{1,0:T(8,128)(2,1)S(1)} %constant_dynamic-slice_fusion), channel_id=1, source_target_pairs={{0,92},{1,93},{2,94},{3,95},{4,88},{5,89},{6,90},{7,91},{8,84},{9,... | collective-permute-start | bytes 344072 | tf_op jit(solution)/shard_map/ppermute | solution.py:459
  14.1 8.1 %collective-permute-done.2 = bf16[16,3584]{1,0:T(8,128)(2,1)S(1)} collective-permute-done((bf16[16,3584]{1,0:T(8,128)(2,1)S(1)}, bf16[16,3584]{1,0:T(8,128)(2,1)S(1)}, u32[]{:S(2)}, u32[]{:S(2)}) %collective-permute-start.2) | collective-permute-done | bytes 114720 | tf_op jit(solution)/shard_map/ppermute | solution.py:459
  22.2 3.5 %collective-permute-start.3 = (bf16[16,3584]{1,0:T(8,128)(2,1)S(1)}, bf16[16,3584]{1,0:T(8,128)(2,1)S(1)}, u32[]{:S(2)}, u32[]{:S(2)}) collective-permute-start(bf16[16,3584]{1,0:T(8,128)(2,1)S(1)} %collective-permute-done.2), channel_id=1, source_target_pairs={{0,1},{1,0},{2,3},{3,2},{4,5},{5,4},{6,7},{7,6},{8,9},{9,8},{10,11... | collective-permute-start | bytes 344072 | tf_op jit(solution)/shard_map/ppermute | solution.py:459
  25.7 3.2 %collective-permute-done.3 = bf16[16,3584]{1,0:T(8,128)(2,1)S(1)} collective-permute-done((bf16[16,3584]{1,0:T(8,128)(2,1)S(1)}, bf16[16,3584]{1,0:T(8,128)(2,1)S(1)}, u32[]{:S(2)}, u32[]{:S(2)}) %collective-permute-start.3) | collective-permute-done | bytes 114720 | tf_op jit(solution)/shard_map/ppermute | solution.py:459
  29.0 4.9 %collective-permute-start.4 = (bf16[32,3584]{1,0:T(8,128)(2,1)S(1)}, bf16[32,3584]{1,0:T(8,128)(2,1)S(1)}, u32[]{:S(2)}, u32[]{:S(2)}) collective-permute-start(bf16[32,3584]{1,0:T(8,128)(2,1)S(1)} %pad_maximum_fusion.3), channel_id=1, source_target_pairs={{0,3},{1,2},{2,1},{3,0},{4,7},{5,6},{6,5},{7,4},{8,11},{9,10},{10,... | collective-permute-start | bytes 688136 | tf_op jit(solution)/shard_map/ppermute | solution.py:459
  33.9 4.2 %collective-permute-done.4 = bf16[32,3584]{1,0:T(8,128)(2,1)S(1)} collective-permute-done((bf16[32,3584]{1,0:T(8,128)(2,1)S(1)}, bf16[32,3584]{1,0:T(8,128)(2,1)S(1)}, u32[]{:S(2)}, u32[]{:S(2)}) %collective-permute-start.4) | collective-permute-done | bytes 229408 | tf_op jit(solution)/shard_map/ppermute | solution.py:459
  38.5 4.7 %collective-permute-start.5 = (bf16[128,3584]{1,0:T(8,128)(2,1)S(1)}, bf16[128,3584]{1,0:T(8,128)(2,1)S(1)}, u32[]{:S(2)}, u32[]{:S(2)}) collective-permute-start(bf16[128,3584]{1,0:T(8,128)(2,1)S(1)} %pad_maximum_fusion.refs_9_), channel_id=1, source_target_pairs={{0,384},{1,385},{2,386},{3,387},{4,388},{5,389},{6,390},{7,391},{8... | collective-permute-start | bytes 2752520 | tf_op jit(solution)/shard_map/ppermute | solution.py:459
  43.1 1.9 collective-permute-start.6
  46.3 12.2 %all-to-all-start = ((f32[16,16,128]{2,1,0:T(8,128)}), f32[16,16,128]{2,1,0:T(8,128)S(1)}, u32[]{:S(2)}, u32[]{:S(2)}) async-start(f32[16,16,128]{2,1,0:T(8,128)} %stats.1), calls=%async_computation | async-start | bytes 262144 | tf_op jit(solution)/shard_map/all_to_all | solution.py:528
  58.7 19.1 %all-to-all-done.refs_0_ = f32[16,16,128]{2,1,0:T(8,128)S(1)} async-done(((f32[16,16,128]{2,1,0:T(8,128)}), f32[16,16,128]{2,1,0:T(8,128)S(1)}, u32[]{:S(2)}, u32[]{:S(2)}) %all-to-all-start) | async-done | bytes 131104 | tf_op jit(solution)/shard_map/all_to_all | solution.py:528
  79.0 2.0 collective-permute-start
  82.3 3.0 %collective-permute-start.9 = (bf16[128,3584]{1,0:T(8,128)(2,1)S(1)}, bf16[128,3584]{1,0:T(8,128)(2,1)}, u32[]{:S(2)}, u32[]{:S(2)}) collective-permute-start(bf16[128,3584]{1,0:T(8,128)(2,1)S(1)} %pad_maximum_fusion.refs_9_), channel_id=1, source_target_pairs={{0,32},{1,33},{2,34},{3,35},{4,36},{5,37},{6,38},{7,39},{8,40},{9,... | collective-permute-start | bytes 2752520 | tf_op jit(solution)/shard_map/ppermute | solution.py:459
  85.4 13.6 %collective-permute-start.7 = (bf16[64,3584]{1,0:T(8,128)(2,1)S(1)}, bf16[64,3584]{1,0:T(8,128)(2,1)S(1)}, u32[]{:S(2)}, u32[]{:S(2)}) collective-permute-start(bf16[64,3584]{1,0:T(8,128)(2,1)S(1)} %slice.20), channel_id=1, source_target_pairs={{0,384},{1,385},{2,386},{3,387},{4,388},{5,389},{6,390},{7,391},{8... | collective-permute-start | bytes 1376264 | tf_op jit(solution)/shard_map/ppermute | solution.py:459
  101.9 2.1 collective-permute-start.10
  104.1 2.2 collective-permute-start.11
  106.3 3.1 %collective-permute-done.7.refs_12_ = bf16[64,3584]{1,0:T(8,128)(2,1)S(1)} collective-permute-done((bf16[64,3584]{1,0:T(8,128)(2,1)S(1)}, bf16[64,3584]{1,0:T(8,128)(2,1)S(1)}, u32[]{:S(2)}, u32[]{:S(2)}) %collective-permute-start.7) | collective-permute-done | bytes 458784 | tf_op jit(solution)/shard_map/ppermute | solution.py:459
  111.3 4.6 %collective-permute-done.8.refs_13_ = bf16[64,3584]{1,0:T(8,128)(2,1)} collective-permute-done((bf16[64,3584]{1,0:T(8,128)(2,1)S(1)}, bf16[64,3584]{1,0:T(8,128)(2,1)}, u32[]{:S(2)}, u32[]{:S(2)}) %collective-permute-start.8) | collective-permute-done | bytes 458784 | tf_op jit(solution)/shard_map/ppermute | solution.py:459
  120.9 13.6 %projector.1 = (f32[32,1024]{1,0:T(8,128)S(1)}, f32[8,768]{1,0:T(8,128)S(1)}) custom-call(s32[2]{0:T(128)S(1)} %pad_add_fusion.refs_0_, f32[8,768]{1,0:T(8,128)S(1)} %get-tuple-element.18.refs_1_, f32[8,768]{1,0:T(8,128)S(1)} %collective-permute-done.refs_2_, f32[8,768]{1,0:T(8,128)S(1)} %collective-permute-done.1.refs_3_, bf16[192,768]{1,0:T(8,128)(2,1)S(1)} %bitcast.25, ...), custom_call_target="tpu_custom_call" | custom-call | flops 2818572288 | bytes 8388608 | tf_op jit(solution)/shard_map/projector/pallas_call | solution.py:264
  134.5 2.0 collective-permute-start.14
  139.6 2.0 back.1
  141.6 44.3 %all_to_all.20.refs_0_ = f32[16,32,128]{2,1,0:T(8,128)S(1)} all-to-all(f32[16,32,128]{2,1,0:T(8,128)S(1)} %get-tuple-element.25), channel_id=1, replica_groups=mesh['rows'=16,'batch'=32] {'rows'}, dimensions={0} | all-to-all | bytes 524288 | tf_op jit(solution)/shard_map/all_to_all | solution.py:542
  186.0 32.8 %all_to_all.21 = f32[32,24,128]{2,1,0:T(8,128)S(1)} all-to-all(f32[32,24,128]{2,1,0:T(8,128)S(1)} %broadcast_in_dim.4), channel_id=1, replica_groups=mesh['rows'=16,'batch'=32] {'batch'}, dimensions={0} | all-to-all | bytes 786432 | tf_op jit(solution)/shard_map/all_to_all | solution.py:443
  219.5 3.5 %all-to-all-start.3 = ((f32[16,24,128]{2,1,0:T(8,128)}), f32[16,24,128]{2,1,0:T(8,128)S(1)}, u32[]{:S(2)}, u32[]{:S(2)}) async-start(f32[16,24,128]{2,1,0:T(8,128)} %broadcast_in_dim.5), calls=%async_computation.3 | async-start | bytes 393216 | tf_op jit(solution)/shard_map/all_to_all | solution.py:443
  224.6 20.8 %all-to-all-done.3.got_ref = f32[16,24,128]{2,1,0:T(8,128)S(1)} async-done(((f32[16,24,128]{2,1,0:T(8,128)}), f32[16,24,128]{2,1,0:T(8,128)S(1)}, u32[]{:S(2)}, u32[]{:S(2)}) %all-to-all-start.3) | async-done | bytes 196640 | tf_op jit(solution)/shard_map/all_to_all | solution.py:443
  (62 shorter events, 22.1 us)
Async XLA Ops:
  2.7 19.5 %collective-permute-start.2 = (bf16[16,3584]{1,0:T(8,128)(2,1)S(1)}, bf16[16,3584]{1,0:T(8,128)(2,1)S(1)}, u32[]{:S(2)}, u32[]{:S(2)}) collective-permute-start(bf16[16,3584]{1,0:T(8,128)(2,1)S(1)} %constant_dynamic-slice_fusion), channel_id=1, source_target_pairs={{0,92},{1,93},{2,94},{3,95},{4,88},{5,89},{6,90},{7,91},{8,84},{9,... | collective-permute-start | bytes 344072 | tf_op jit(solution)/shard_map/ppermute | solution.py:459
  22.2 6.7 %collective-permute-start.3 = (bf16[16,3584]{1,0:T(8,128)(2,1)S(1)}, bf16[16,3584]{1,0:T(8,128)(2,1)S(1)}, u32[]{:S(2)}, u32[]{:S(2)}) collective-permute-start(bf16[16,3584]{1,0:T(8,128)(2,1)S(1)} %collective-permute-done.2), channel_id=1, source_target_pairs={{0,1},{1,0},{2,3},{3,2},{4,5},{5,4},{6,7},{7,6},{8,9},{9,8},{10,11... | collective-permute-start | bytes 344072 | tf_op jit(solution)/shard_map/ppermute | solution.py:459
  29.0 9.1 %collective-permute-start.4 = (bf16[32,3584]{1,0:T(8,128)(2,1)S(1)}, bf16[32,3584]{1,0:T(8,128)(2,1)S(1)}, u32[]{:S(2)}, u32[]{:S(2)}) collective-permute-start(bf16[32,3584]{1,0:T(8,128)(2,1)S(1)} %pad_maximum_fusion.3), channel_id=1, source_target_pairs={{0,3},{1,2},{2,1},{3,0},{4,7},{5,6},{6,5},{7,4},{8,11},{9,10},{10,... | collective-permute-start | bytes 688136 | tf_op jit(solution)/shard_map/ppermute | solution.py:459
  38.4 39.5 %copy-start.1 = (f32[512]{0:T(512)S(1)}, f32[512]{0:T(512)}, u32[]{:S(2)}) copy-start(f32[512]{0:T(512)} %param.12) | copy-start | bytes 6148
  38.4 39.5 %copy-start.2 = (f32[512]{0:T(512)S(1)}, f32[512]{0:T(512)}, u32[]{:S(2)}) copy-start(f32[512]{0:T(512)} %param.13) | copy-start | bytes 6148
  38.5 46.9 %collective-permute-start.5 = (bf16[128,3584]{1,0:T(8,128)(2,1)S(1)}, bf16[128,3584]{1,0:T(8,128)(2,1)S(1)}, u32[]{:S(2)}, u32[]{:S(2)}) collective-permute-start(bf16[128,3584]{1,0:T(8,128)(2,1)S(1)} %pad_maximum_fusion.refs_9_), channel_id=1, source_target_pairs={{0,384},{1,385},{2,386},{3,387},{4,388},{5,389},{6,390},{7,391},{8... | collective-permute-start | bytes 2752520 | tf_op jit(solution)/shard_map/ppermute | solution.py:459
  43.1 55.8 %collective-permute-start.6 = (bf16[128,3584]{1,0:T(8,128)(2,1)S(1)}, bf16[128,3584]{1,0:T(8,128)(2,1)}, u32[]{:S(2)}, u32[]{:S(2)}) collective-permute-start(bf16[128,3584]{1,0:T(8,128)(2,1)S(1)} %pad_maximum_fusion.refs_9_), channel_id=1, source_target_pairs={{0,128},{1,129},{2,130},{3,131},{4,132},{5,133},{6,134},{7,135},{8... | collective-permute-start | bytes 2752520 | tf_op jit(solution)/shard_map/ppermute | solution.py:459
  46.3 31.5 %all-to-all-start = ((f32[16,16,128]{2,1,0:T(8,128)}), f32[16,16,128]{2,1,0:T(8,128)S(1)}, u32[]{:S(2)}, u32[]{:S(2)}) async-start(f32[16,16,128]{2,1,0:T(8,128)} %stats.1), calls=%async_computation | async-start | bytes 262144 | tf_op jit(solution)/shard_map/all_to_all | solution.py:528
  58.6 59.2 %copy-start.7 = (f32[16,1024]{1,0:T(8,128)S(1)}, f32[16,1024]{1,0:T(8,128)}, u32[]{:S(2)}) copy-start(f32[16,1024]{1,0:T(8,128)} %param.15) | copy-start | bytes 196612
  58.7 59.2 %copy-start.9 = (f32[768]{0:T(1024)S(1)}, f32[768]{0:T(1024)}, u32[]{:S(2)}) copy-start(f32[768]{0:T(1024)} %param.20) | copy-start | bytes 9220
  77.8 42.1 %copy-start.4 = (f32[2048]{0:T(1024)S(1)}, f32[2048]{0:T(1024)}, u32[]{:S(2)}) copy-start(f32[2048]{0:T(1024)} %param.18) | copy-start | bytes 24580
  77.8 42.1 %copy-start.5 = (f32[1024]{0:T(1024)S(1)}, f32[1024]{0:T(1024)}, u32[]{:S(2)}) copy-start(f32[1024]{0:T(1024)} %param.16) | copy-start | bytes 12292
  79.0 22.9 %collective-permute-start = (f32[8,768]{1,0:T(8,128)S(1)}, f32[8,768]{1,0:T(8,128)S(1)}, u32[]{:S(2)}, u32[]{:S(2)}) collective-permute-start(f32[8,768]{1,0:T(8,128)S(1)} %get-tuple-element.19), channel_id=1, source_target_pairs={{0,32},{32,64},{64,96},{96,128},{128,160},{160,192},{192,224},{224... | collective-permute-start | bytes 73736 | tf_op jit(solution)/shard_map/ppermute | solution.py:494
  81.0 23.1 %collective-permute-start.1 = (f32[8,768]{1,0:T(8,128)S(1)}, f32[8,768]{1,0:T(8,128)S(1)}, u32[]{:S(2)}, u32[]{:S(2)}) collective-permute-start(f32[8,768]{1,0:T(8,128)S(1)} %get-tuple-element.20), channel_id=1, source_target_pairs={{32,0},{64,32},{96,64},{128,96},{160,128},{192,160},{224,192},{256... | collective-permute-start | bytes 73736 | tf_op jit(solution)/shard_map/ppermute | solution.py:494
  82.3 35.7 %collective-permute-start.9 = (bf16[128,3584]{1,0:T(8,128)(2,1)S(1)}, bf16[128,3584]{1,0:T(8,128)(2,1)}, u32[]{:S(2)}, u32[]{:S(2)}) collective-permute-start(bf16[128,3584]{1,0:T(8,128)(2,1)S(1)} %pad_maximum_fusion.refs_9_), channel_id=1, source_target_pairs={{0,32},{1,33},{2,34},{3,35},{4,36},{5,37},{6,38},{7,39},{8,40},{9,... | collective-permute-start | bytes 2752520 | tf_op jit(solution)/shard_map/ppermute | solution.py:459
  85.4 24.0 %collective-permute-start.7 = (bf16[64,3584]{1,0:T(8,128)(2,1)S(1)}, bf16[64,3584]{1,0:T(8,128)(2,1)S(1)}, u32[]{:S(2)}, u32[]{:S(2)}) collective-permute-start(bf16[64,3584]{1,0:T(8,128)(2,1)S(1)} %slice.20), channel_id=1, source_target_pairs={{0,384},{1,385},{2,386},{3,387},{4,388},{5,389},{6,390},{7,391},{8... | collective-permute-start | bytes 1376264 | tf_op jit(solution)/shard_map/ppermute | solution.py:459
  100.0 15.9 %collective-permute-start.8 = (bf16[64,3584]{1,0:T(8,128)(2,1)S(1)}, bf16[64,3584]{1,0:T(8,128)(2,1)}, u32[]{:S(2)}, u32[]{:S(2)}) collective-permute-start(bf16[64,3584]{1,0:T(8,128)(2,1)S(1)} %slice.21), channel_id=1, source_target_pairs={{0,128},{1,129},{2,130},{3,131},{4,132},{5,133},{6,134},{7,135},{8... | collective-permute-start | bytes 1376264 | tf_op jit(solution)/shard_map/ppermute | solution.py:459
  101.9 18.0 %collective-permute-start.10 = (bf16[128,3584]{1,0:T(8,128)(2,1)S(1)}, bf16[128,3584]{1,0:T(8,128)(2,1)}, u32[]{:S(2)}, u32[]{:S(2)}) collective-permute-start(bf16[128,3584]{1,0:T(8,128)(2,1)S(1)} %collective-permute-done.5.refs_10_), channel_id=1, source_target_pairs={{0,32},{1,33},{2,34},{3,35},{4,36},{5,37},{6,38},{7,39},{8,40},{9,... | collective-permute-start | bytes 2752520 | tf_op jit(solution)/shard_map/ppermute | solution.py:459
  104.1 15.8 %collective-permute-start.11 = (bf16[128,3584]{1,0:T(8,128)(2,1)}, bf16[128,3584]{1,0:T(8,128)(2,1)}, u32[]{:S(2)}, u32[]{:S(2)}) collective-permute-start(bf16[128,3584]{1,0:T(8,128)(2,1)} %collective-permute-done.6.refs_11_), channel_id=1, source_target_pairs={{0,32},{1,33},{2,34},{3,35},{4,36},{5,37},{6,38},{7,39},{8,40},{9,... | collective-permute-start | bytes 2752520 | tf_op jit(solution)/shard_map/ppermute | solution.py:459
  109.3 8.6 %collective-permute-start.12 = (bf16[64,3584]{1,0:T(8,128)(2,1)S(1)}, bf16[64,3584]{1,0:T(8,128)(2,1)}, u32[]{:S(2)}, u32[]{:S(2)}) collective-permute-start(bf16[64,3584]{1,0:T(8,128)(2,1)S(1)} %collective-permute-done.7.refs_12_), channel_id=1, source_target_pairs={{0,32},{1,33},{2,34},{3,35},{4,36},{5,37},{6,38},{7,39},{8,40},{9,... | collective-permute-start | bytes 1376264 | tf_op jit(solution)/shard_map/ppermute | solution.py:459
  115.8 4.0 %collective-permute-start.13 = (bf16[64,3584]{1,0:T(8,128)(2,1)}, bf16[64,3584]{1,0:T(8,128)(2,1)}, u32[]{:S(2)}, u32[]{:S(2)}) collective-permute-start(bf16[64,3584]{1,0:T(8,128)(2,1)} %collective-permute-done.8.refs_13_), channel_id=1, source_target_pairs={{0,32},{1,33},{2,34},{3,35},{4,36},{5,37},{6,38},{7,39},{8,40},{9,... | collective-permute-start | bytes 1376264 | tf_op jit(solution)/shard_map/ppermute | solution.py:459
  134.5 3.4 %collective-permute-start.14 = (f32[8,768]{1,0:T(8,128)S(1)}, f32[8,768]{1,0:T(8,128)S(1)}, u32[]{:S(2)}, u32[]{:S(2)}) collective-permute-start(f32[8,768]{1,0:T(8,128)S(1)} %get-tuple-element.21.refs_0_), channel_id=1, source_target_pairs={{0,32},{32,64},{64,96},{96,128},{128,160},{160,192},{192,224},{224... | collective-permute-start | bytes 73736 | tf_op jit(solution)/shard_map/ppermute | solution.py:494
  136.5 3.1 %collective-permute-start.15 = (f32[8,768]{1,0:T(8,128)S(1)}, f32[8,768]{1,0:T(8,128)S(1)}, u32[]{:S(2)}, u32[]{:S(2)}) collective-permute-start(f32[8,768]{1,0:T(8,128)S(1)} %get-tuple-element.21.refs_0_), channel_id=1, source_target_pairs={{32,0},{64,32},{96,64},{128,96},{160,128},{192,160},{224,192},{256... | collective-permute-start | bytes 73736 | tf_op jit(solution)/shard_map/ppermute | solution.py:494
  219.5 25.9 %all-to-all-start.3 = ((f32[16,24,128]{2,1,0:T(8,128)}), f32[16,24,128]{2,1,0:T(8,128)S(1)}, u32[]{:S(2)}, u32[]{:S(2)}) async-start(f32[16,24,128]{2,1,0:T(8,128)} %broadcast_in_dim.5), calls=%async_computation.3 | async-start | bytes 393216 | tf_op jit(solution)/shard_map/all_to_all | solution.py:443
  (4 other events, 64.6 us)

commit v2 on v1

--- a/solution.py
+++ b/solution.py
@@ -20,9 +20,7 @@
 SUB = 8
 LANES = 128
 STAT_ROWS = 16
-CHUNK = 32
-AT_EMBED, AT_GAIN, AT_STAT = 9, 17, 18
-PARAM_ROWS = 24
+CHUNKS, CHUNK_ROWS, ALL_ROWS = 32, 16, 32
 
 
 def params(limit_mb=48):
@@ -61,6 +59,20 @@
 def from_groups(channels, per_group, offset):
     shape = (LANES, channels)
     return (iota(shape, 1) // per_group + offset == iota(shape, 0)).astype(F32)
+
+
+def pack_stats(total):
+    lane = iota((SUB, LANES), 1)
+    return jnp.where(lane < LANES // 2, total[:SUB], pltpu.roll(total[SUB:], LANES // 2, 1))
+
+
+def unpack_stats(packed):
+    return jnp.concatenate([packed, pltpu.roll(packed, LANES // 2, 1)], axis=0)
+
+
+def halves(packed):
+    top = packed.astype(BF16).astype(F32)
+    return jnp.concatenate([top, packed - top], axis=0).astype(BF16)
 
 
 def stats_kernel(f_ref, out_ref, sums, squares):
@@ -75,15 +87,16 @@
     total = nn(sums[...], to_groups(channels, per_group, 0), HIGH) + nn(
         squares[...], to_groups(channels, per_group, GROUPS), HIGH
     )
+    packed = pack_stats(total)
     for r in range(out_ref.shape[0]):
-        out_ref[r] = total
+        out_ref[r] = packed
 
 
 def group_stats(features, peers):
     channels = features.shape[-1]
     return pl.pallas_call(
         stats_kernel,
-        out_shape=jax.ShapeDtypeStruct((peers, STAT_ROWS, LANES), F32),
+        out_shape=jax.ShapeDtypeStruct((peers, SUB, LANES), F32),
         in_specs=[vmem()],
         out_specs=vmem(),
         scratch_shapes=[pltpu.VMEM((STAT_ROWS, channels), F32)] * 2,
@@ -107,7 +120,7 @@
 ):
     images, cells, channels = f_ref.shape
     per_group = channels // GROUPS
-    total = jnp.sum(st_ref[...], axis=0)
+    total = unpack_stats(jnp.sum(st_ref[...], axis=0))
     mean = nn(total, from_groups(channels, per_group, 0), HIGH) * (1.0 / members)
     square = nn(total, from_groups(channels, per_group, GROUPS), HIGH) * (1.0 / members)
     inv = lax.rsqrt(jnp.maximum(square - mean * mean, 0.0) + EPS_NORM)
@@ -155,37 +168,33 @@
 def mlp_kernel(
     across, width, hidden, align, at_ref, lat_ref, below_ref, above_ref, target_ref,
     ew_ref, eb_ref, pib_ref, pob_ref,
-    h0, p0, m0, l0, t0, h1, p1, m1, l1, t1,
+    own, cross, own_other, cross_other,
     embed_ref, gl_ref, w_in, w_out, pre, emb, acc, grad_emb, sems,
 ):
-    x, core = at_ref[0], at_ref[1]
+    zhi, core = at_ref[0], at_ref[1]
     depth = width // (XS * ZHI * CORES)
     slab = hidden // (XS * ZHI * CORES)
     copies = []
 
-    def place(piece, at, source_x, zhi, of_core):
-        shard = lax.rem(source_x, XS) * (ZHI * CORES) + zhi * CORES + of_core
-        lines = pl.ds(at, depth)
-
-        def put(columns, into):
-            copy = pltpu.make_async_copy(piece.at[lines, columns], into, sems.at[len(copies)])
-            copy.start()
-            copies.append(copy)
-
-        put(pl.ds(0, hidden), w_in.at[pl.ds(pl.multiple_of(shard * depth, depth), depth), :])
-        for part in range(slab // depth):
-            begin = pl.multiple_of(shard * slab + part * depth, depth)
-            put(pl.ds(hidden + part * align, align), w_out.at[pl.ds(begin, depth), :])
-
-    for of_core, (own, plus, minus, low, high) in (
-        (core, (h0, p0, m0, l0, t0)),
-        (1 - core, (h1, p1, m1, l1, t1)),
+    for piece, of_zhi, of_core in (
+        (own, zhi, core),
+        (own_other, zhi, 1 - core),
+        (cross, 1 - zhi, core),
+        (cross_other, 1 - zhi, 1 - core),
     ):
-        for piece, step in ((own, 0), (plus, 1), (minus, XS - 1)):
-            for zhi in range(ZHI):
-                place(piece, zhi * depth, x + step, zhi, of_core)
-        place(low, 0, x + 2, 0, of_core)
-        place(high, 0, x + 2, 1, of_core)
+        for x in range(XS):
+            shard = x * (ZHI * CORES) + of_zhi * CORES + of_core
+            lines = pl.ds(x * depth, depth)
+
+            def put(columns, into):
+                copy = pltpu.make_async_copy(piece.at[lines, columns], into, sems.at[len(copies)])
+                copy.start()
+                copies.append(copy)
+
+            put(pl.ds(0, hidden), w_in.at[pl.ds(pl.multiple_of(shard * depth, depth), depth), :])
+            for part in range(slab // depth):
+                begin = pl.multiple_of(shard * slab + part * depth, depth)
+                put(pl.ds(hidden + part * align, align), w_out.at[pl.ds(begin, depth), :])
 
     lat = lat_ref[...] + below_ref[...] + above_ref[...]
     top = lat.astype(BF16)
@@ -290,7 +299,7 @@
 
 def back_kernel(
     across, gl_ref, before_ref, after_ref, f_ref, mean_ref, inv_ref, gain_ref, bias_ref,
-    k_ref, embed_ref, send_ref, gs_ref, act, grads_t, by_bias, by_gain,
+    k_ref, embed_ref, send_ref, gs_ref, act, grads_t, by_bias, by_gain, pack,
 ):
     images, cells, channels = f_ref.shape
     per_group = channels // GROUPS
@@ -330,43 +339,48 @@
     )
     bias_part = jnp.sum(by_bias[...], axis=0, keepdims=True)
     gain_part = jnp.sum(by_gain[...], axis=0, keepdims=True)
+    packed = halves(pack_stats(stat))
+    for r in range(CHUNKS):
+        send_ref[r, CHUNK_ROWS:ALL_ROWS, :] = packed
     blocks = channels // LANES
-    for r in range(send_ref.shape[0]):
+    half = CHUNKS // 2
+    pack[...] = jnp.zeros_like(pack)
+    for r in range(half):
         block, latent = r // LATENT, r % LATENT
         lanes = slice(block * LANES, (block + 1) * LANES)
         for position in range(TAPS):
             line = position * SUB + latent
-            send_ref[r, position : position + 1, :] = conv[line : line + 1, lanes]
+            pack[r, position : position + 1, :] = conv[line : line + 1, lanes]
         lanes = slice((r // 2) * LANES, (r // 2 + 1) * LANES)
-        for half in range(2):
-            line = (r % 2) * 2 * SUB + half * SUB
-            send_ref[r, AT_EMBED + half * LATENT : AT_EMBED + (half + 1) * LATENT, :] = embed_ref[
+        for part in range(2):
+            line = (r % 2) * 2 * SUB + part * SUB
+            pack[half + r, part * LATENT : (part + 1) * LATENT, :] = embed_ref[
                 line : line + LATENT, lanes
             ]
-        one = gain_part if r < blocks else bias_part
-        lanes = slice((r % blocks) * LANES, (r % blocks + 1) * LANES)
-        send_ref[r, AT_GAIN : AT_GAIN + 1, :] = one[:, lanes]
-        send_ref[r, AT_STAT : AT_STAT + images, :] = stat[0:images]
-        send_ref[r, AT_STAT + images : CHUNK, :] = jnp.zeros(
-            (CHUNK - AT_STAT - images, LANES), F32
-        )
-
-
-def conv_backward(gl, before, after, features, mean, inv, gain, bias, kernel_rows, embed, across, peers):
+        if r < 2 * blocks:
+            one = gain_part if r < blocks else bias_part
+            lanes = slice((r % blocks) * LANES, (r % blocks + 1) * LANES)
+            pack[half + r, SUB : SUB + 1, :] = one[:, lanes]
+    for r in range(CHUNKS):
+        send_ref[r, 0:CHUNK_ROWS, :] = pack[r].astype(BF16)
+
+
+def conv_backward(gl, before, after, features, mean, inv, gain, bias, kernel_rows, embed, across):
     images, cells, channels = features.shape
     return pl.pallas_call(
         lambda *refs: back_kernel(across, *refs),
         out_shape=(
-            jax.ShapeDtypeStruct((peers, CHUNK, LANES), F32),
+            jax.ShapeDtypeStruct((CHUNKS, ALL_ROWS, LANES), BF16),
             jax.ShapeDtypeStruct((images, cells, channels), F32),
         ),
         in_specs=[vmem()] * 10,
-        out_specs=(vmem(), vmem()),
+        out_specs=(vmem(),) * 2,
         scratch_shapes=[
             pltpu.VMEM((images * cells, channels), BF16),
             pltpu.VMEM((images * cells, LANES), BF16),
             pltpu.VMEM((STAT_ROWS, channels), F32),
             pltpu.VMEM((STAT_ROWS, channels), F32),
+            pltpu.VMEM((CHUNKS, CHUNK_ROWS, LANES), F32),
         ],
         compiler_params=params(),
         name="back",
@@ -376,17 +390,15 @@
 def last_kernel(members, got_ref, f_ref, mean_ref, inv_ref, gain_ref, gs_ref, out_ref):
     images, _, channels = f_ref.shape
     per_group = channels // GROUPS
-    total = jnp.sum(got_ref[:, STAT_ROWS:CHUNK, :], axis=0)
+    total = unpack_stats(got_ref[...])
     first = nn(total, from_groups(channels, per_group, 0), HIGH) * (1.0 / members)
     second = nn(total, from_groups(channels, per_group, GROUPS), HIGH) * (1.0 / members)
     gain = gain_ref[...]
-    skip = AT_STAT - STAT_ROWS
     for i in range(images):
         v = f_ref[i].astype(F32)
         inv = inv_ref[i : i + 1, :]
         normed = (v - mean_ref[i : i + 1, :]) * inv
-        j = i + skip
-        out = inv * (gs_ref[i] * gain - first[j : j + 1] - normed * second[j : j + 1])
+        out = inv * (gs_ref[i] * gain - first[i : i + 1] - normed * second[i : i + 1])
         out_ref[i] = out.astype(BF16)
 
 
@@ -404,22 +416,75 @@
     )(got, features, mean, inv, gain, grad_shift)
 
 
-def unpack_kernel(got_ref, conv_ref, gain_ref, bias_ref, embed_ref):
+def plane_kernel(at_ref, got_ref, out_ref):
+    chunk = jnp.zeros((CHUNK_ROWS, LANES), F32)
+    stat = jnp.zeros((SUB, LANES), F32)
+    for r in range(CHUNKS):
+        chunk = chunk + got_ref[r, 0:CHUNK_ROWS, :].astype(F32)
+        pair = got_ref[r, CHUNK_ROWS:ALL_ROWS, :].astype(F32)
+        stat = stat + jnp.where(at_ref[2] == (r // CORES) % YS, pair[:SUB] + pair[SUB:], 0.0)
+    chunk, stat = chunk.astype(BF16), halves(stat)
+    for r in range(out_ref.shape[0]):
+        out_ref[r, 0:CHUNK_ROWS, :] = chunk
+        out_ref[r, CHUNK_ROWS:ALL_ROWS, :] = stat
+
+
+def plane_total(at, got):
+    return pl.pallas_call(
+        plane_kernel,
+        out_shape=jax.ShapeDtypeStruct((ZHI * ZLO, ALL_ROWS, LANES), BF16),
+        in_specs=[pl.BlockSpec(memory_space=pltpu.SMEM), vmem()],
+        out_specs=vmem(),
+        compiler_params=params(),
+        name="plane",
+    )(at, got)
+
+
+def column_kernel(at_ref, got_ref, out_ref, stat_ref):
+    chunk = jnp.zeros((CHUNK_ROWS, LANES), F32)
+    stat = jnp.zeros((SUB, LANES), F32)
+    for r in range(ZHI * ZLO):
+        chunk = chunk + got_ref[r, 0:CHUNK_ROWS, :].astype(F32)
+        pair = got_ref[r, CHUNK_ROWS:ALL_ROWS, :].astype(F32)
+        stat = stat + jnp.where(at_ref[3] == r % ZLO, pair[:SUB] + pair[SUB:], 0.0)
+    chunk = chunk.astype(BF16)
+    for r in range(out_ref.shape[0]):
+        out_ref[r] = chunk
+    stat_ref[...] = stat
+
+
+def column_total(at, got):
+    return pl.pallas_call(
+        column_kernel,
+        out_shape=(
+            jax.ShapeDtypeStruct((CHUNKS, CHUNK_ROWS, LANES), BF16),
+            jax.ShapeDtypeStruct((SUB, LANES), F32),
+        ),
+        in_specs=[pl.BlockSpec(memory_space=pltpu.SMEM), vmem()],
+        out_specs=(vmem(), vmem()),
+        compiler_params=params(),
+        name="column",
+    )(at, got)
+
+
+def unpack_kernel(got_ref, conv_ref, gain_ref, bias_ref, embed_ref, wide):
     channels = gain_ref.shape[1]
     blocks = channels // LANES
-    for r in range(got_ref.shape[0]):
+    half = CHUNKS // 2
+    wide[...] = got_ref[...].astype(F32)
+    for r in range(half):
         block, latent = r // LATENT, r % LATENT
         for position in range(TAPS):
             at = position * channels + block * LANES
-            conv_ref[latent : latent + 1, at : at + LANES] = got_ref[r, position : position + 1, :]
+            conv_ref[latent : latent + 1, at : at + LANES] = wide[r, position : position + 1, :]
         lanes = slice((r // 2) * LANES, (r // 2 + 1) * LANES)
         line = (r % 2) * SUB
-        embed_ref[line : line + SUB, lanes] = got_ref[r, AT_EMBED : AT_EMBED + SUB, :]
+        embed_ref[line : line + SUB, lanes] = wide[half + r, 0:SUB, :]
         lanes = slice((r % blocks) * LANES, (r % blocks + 1) * LANES)
         if r < blocks:
-            gain_ref[:, lanes] = got_ref[r, AT_GAIN : AT_GAIN + 1, :]
+            gain_ref[:, lanes] = wide[half + r, SUB : SUB + 1, :]
         elif r < 2 * blocks:
-            bias_ref[:, lanes] = got_ref[r, AT_GAIN : AT_GAIN + 1, :]
+            bias_ref[:, lanes] = wide[half + r, SUB : SUB + 1, :]
 
 
 def unpack(got, channels, width):
@@ -433,16 +498,38 @@
         ),
         in_specs=[vmem()],
         out_specs=(vmem(),) * 4,
+        scratch_shapes=[pltpu.VMEM(got.shape, F32)],
         compiler_params=params(),
         name="unpack",
     )(got)
 
 
-def from_everyone(value, axis):
-    length = lax.axis_size(axis)
-    return lax.all_to_all(
-        jnp.broadcast_to(value[None], (length, *value.shape)), axis, 0, 0, tiled=True
-    )
+def device(x, zhi, core, zlo, y):
+    return ((x * ZHI + zhi) * CORES + core) * (ZLO * YS) + zlo * YS + y
+
+
+BOTH = ("rows", "batch")
+PLANE = [
+    [device(x, h, c, d, y) for x in range(XS) for y in range(YS) for c in range(CORES)]
+    for h in range(ZHI)
+    for d in range(ZLO)
+]
+SHEET = [
+    [device(x, h, c, d, y) for x in range(XS) for y in range(YS)]
+    for h in range(ZHI)
+    for d in range(ZLO)
+    for c in range(CORES)
+]
+COLUMN = [
+    [device(x, h, c, d, y) for h in range(ZHI) for d in range(ZLO)]
+    for x in range(XS)
+    for y in range(YS)
+    for c in range(CORES)
+]
+
+
+def exchanged(value, groups):
+    return lax.all_to_all(value, BOTH, 0, 0, axis_index_groups=groups, tiled=True)
 
 
 def moved(value, where):
@@ -453,38 +540,23 @@
                 for zlo in range(ZLO):
                     for y in range(YS):
                         a, b, c, d, e = where(x, zhi, core, zlo, y)
-                        source = ((x * ZHI + zhi) * CORES + core) * (ZLO * YS) + zlo * YS + y
-                        goal = ((a * ZHI + b) * CORES + c) * (ZLO * YS) + d * YS + e
-                        pairs.append((source, goal))
+                        pairs.append((device(x, zhi, core, zlo, y), device(a, b, c, d, e)))
     return lax.ppermute(value, ("rows", "batch"), pairs)
 
 
-def gathered(shard):
-    depth = shard.shape[0]
-    rows, batch = lax.axis_index("rows"), lax.axis_index("batch")
-    zhi, y = (rows // CORES) % ZHI, batch % YS
-    part = depth // YS
+def crossed(shard):
+    y = lax.axis_index("batch") % YS
+    part = shard.shape[0] // YS
     mine = lax.dynamic_slice_in_dim(shard, y * part, part, axis=0)
-    cross = moved(mine, lambda x, h, c, d, y: (x, 1 - h, c, ZLO - 1 - d, y))
-    other = moved(cross, lambda x, h, c, d, y: (x, h, c, d, y ^ 1))
-    even = y % 2 == 0
-    pair = jnp.concatenate(
-        [jnp.where(even, cross, other), jnp.where(even, other, cross)], axis=0
-    )
-    far = moved(pair, lambda x, h, c, d, y: (x, h, c, d, YS - 1 - y))
-    low = y < 2
-    across = jnp.concatenate([jnp.where(low, pair, far), jnp.where(low, far, pair)], axis=0)
-    first = zhi == 0
-    both = jnp.concatenate(
-        [jnp.where(first, shard, across), jnp.where(first, across, shard)], axis=0
-    )
-    plus = moved(both, lambda x, h, c, d, y: ((x + XS - 1) % XS, h, c, d, y))
-    minus = moved(both, lambda x, h, c, d, y: ((x + 1) % XS, h, c, d, y))
-    low_half = moved(plus[:depth], lambda x, h, c, d, y: ((x + XS - 1) % XS, h, c, d, y))
-    high_half = moved(minus[depth:], lambda x, h, c, d, y: ((x + 1) % XS, h, c, d, y))
-    held = [both, plus, minus, low_half, high_half]
-    swapped = [moved(v, lambda x, h, c, d, y: (x, h, 1 - c, d, y)) for v in held]
-    return held + swapped
+    return mine, moved(mine, lambda x, h, c, d, y: (x, 1 - h, c, ZLO - 1 - d, y))
+
+
+def sheet(part):
+    return lax.all_gather(part, BOTH, axis_index_groups=SHEET, tiled=True)
+
+
+def swapped(value):
+    return moved(value, lambda x, h, c, d, y: (x, h, 1 - c, d, y))
 
 
 def neighbours(up, down):
@@ -517,7 +589,8 @@
     shard = jnp.concatenate(
         [proj_in] + [proj_out[at : at + depth] for at in range(0, proj_out.shape[0], depth)], axis=1
     )
-    pieces = gathered(shard)
+    mine, far = crossed(shard)
+    own = sheet(mine)
     taps = conv_weight.reshape(LATENT, TAPS, channels).transpose(1, 0, 2)
     taps = jnp.pad(taps, ((0, 0), (0, SUB - LATENT), (0, 0))).reshape(TAPS * SUB, channels)
     taps_full = jnp.pad(taps, ((0, LANES - TAPS * SUB), (0, 0)))
@@ -525,11 +598,17 @@
         embed_weight.reshape(PATCH * PATCH, LATENT, width), ((0, 0), (0, SUB - LATENT), (0, 0))
     ).reshape(PATCH * PATCH * SUB, width)
 
-    stats = lax.all_to_all(group_stats(flat, peers), "rows", 0, 0, tiled=True)
+    sums = group_stats(flat, peers)
+    far, _ = lax.optimization_barrier((far, sums))
+    cross = sheet(far)
+    stats = lax.all_to_all(sums, "rows", 0, 0, tiled=True)
     lat, up, down, mean, inv = conv_forward(stats, flat, gain, bias, taps, across, members)
     above, below = neighbours(up, down)
-    rows = lax.axis_index("rows")
-    at = jnp.stack([rows // (ZHI * CORES), rows % CORES]).astype(jnp.int32)
+    own, cross, lat = lax.optimization_barrier((own, cross, lat))
+    pieces = [own, cross, swapped(own), swapped(cross)]
+    rows, batch = lax.axis_index("rows"), lax.axis_index("batch")
+    at = jnp.stack([(rows // CORES) % ZHI, rows % CORES, batch % YS, batch // YS])
+    at = at.astype(jnp.int32)
     target = targets.reshape(-1, align)
     embed_part, grad_lat = projector(
         at, lat, below, above, target, spread, embed_bias.reshape(1, -1),
@@ -537,13 +616,13 @@
     )
     after, before = neighbours(grad_lat, grad_lat)
     send, grad_shift = conv_backward(
-        grad_lat, before, after, flat, mean, inv, gain, bias, taps_full, embed_part, across, peers
-    )
-    got = lax.all_to_all(send, "rows", 0, 0, tiled=True)
-    chunk = jnp.sum(got[:, :PARAM_ROWS], axis=0)
+        grad_lat, before, after, flat, mean, inv, gain, bias, taps_full, embed_part, across
+    )
+    plane = exchanged(send, PLANE)
+    column = exchanged(plane_total(at, plane), COLUMN)
+    chunks, got = column_total(at, column)
+    everything = exchanged(chunks, PLANE)
     grad_features = feature_grad(got, flat, mean, inv, gain, grad_shift, members)
-    chunk = jnp.sum(from_everyone(chunk, "batch"), axis=0)
-    everything = from_everyone(chunk, "rows")
     grad_conv, grad_gain, grad_bias, grad_embed = unpack(everything, channels, width)
     return (
         grad_features.reshape(features.shape),

time: 247 us -> 259 us (1.049)
  the two profiles are of different devices: /device:TPU:32 before, /device:TPU:1 now
where the time goes in v2:
time: 259 us; the launch traced here: 258 us
  waiting for transfers between devices  128 us (49%)
  starting transfers between devices  55.1 us (21%)
  blocking collectives  30.2 us (12%)
  Pallas kernels  22.1 us (9%)
  between operations  14.4 us (6%)
  local copies, waits for them, and re-layouts  6.7 us (3%)
    all_gather x2, waiting for transfers between devices, sheet(): return lax.all_gather(part, BOTH, axis_index_groups=SHEET, tiled=True)  76.8 us
    all_to_all x2, blocking collectives, exchanged(): lax.all_to_all(value, BOTH, 0, 0, axis_index_groups=groups, tiled=True)  30.2 us
    ppermute x2, waiting for transfers between devices, neighbours(): lax.ppermute(up, 'rows', backward)  23.3 us
    ppermute x3, starting transfers between devices, moved(): return lax.ppermute(value, ('rows', 'batch'), pairs)  17.6 us
    ppermute x2, starting transfers between devices, neighbours(): lax.ppermute(down, 'rows', forward)  14.9 us
    all_to_all x1, waiting for transfers between devices, shards(): stats = lax.all_to_all(sums, 'rows', 0, 0, tiled=True)  13.7 us
    pallas_call x1, Pallas kernels, projector(): pl.pallas_call(lambda *refs: mlp_kernel(across, width, hidden, align, *re...  13.4 us
    all_to_all x1, starting transfers between devices, shards(): stats = lax.all_to_all(sums, 'rows', 0, 0, tiled=True)  11.9 us
  transfers between devices with their start and end apart: 11, of which 7 were waited for; matrix products, arithmetic and copies ran while one was open for 0% of the time, Pallas kernels for 2%

profile of v2, /device:TPU:1, one launch (start us, length us, event | category | flops | bytes accessed | tf_op | source)
XLA Modules:
  0.0 258.3 jit_solution(8570546196070618410)
XLA Ops:
  8.3 1.5 fusion.1
  9.9 12.0 %collective-permute-start = (bf16[16,3584]{1,0:T(8,128)(2,1)}, bf16[16,3584]{1,0:T(8,128)(2,1)S(1)}, u32[]{:S(2)}, u32[]{:S(2)}) collective-permute-start(bf16[16,3584]{1,0:T(8,128)(2,1)} %fusion.1), channel_id=1, source_target_pairs={{0,92},{1,93},{2,94},{3,95},{4,88},{5,89},{6,90},{7,91},{8,84},{9,... | collective-permute-start | bytes 344072 | tf_op jit(solution)/shard_map/ppermute | solution.py:544
  24.3 8.3 %collective-permute-done = bf16[16,3584]{1,0:T(8,128)(2,1)S(1)} collective-permute-done((bf16[16,3584]{1,0:T(8,128)(2,1)}, bf16[16,3584]{1,0:T(8,128)(2,1)S(1)}, u32[]{:S(2)}, u32[]{:S(2)}) %collective-permute-start) | collective-permute-done | bytes 114720 | tf_op jit(solution)/shard_map/ppermute | solution.py:544
  33.3 11.9 %all-to-all-start = ((f32[16,8,128]{2,1,0:T(8,128)}), f32[16,8,128]{2,1,0:T(8,128)S(1)}, u32[]{:S(2)}, u32[]{:S(2)}) async-start(f32[16,8,128]{2,1,0:T(8,128)} %stats.1), calls=%async_computation | async-start | bytes 131072 | tf_op jit(solution)/shard_map/all_to_all | solution.py:604
  46.1 13.7 %all-to-all-done.refs_0_ = f32[16,8,128]{2,1,0:T(8,128)S(1)} async-done(((f32[16,8,128]{2,1,0:T(8,128)}), f32[16,8,128]{2,1,0:T(8,128)S(1)}, u32[]{:S(2)}, u32[]{:S(2)}) %all-to-all-start) | async-done | bytes 65568 | tf_op jit(solution)/shard_map/all_to_all | solution.py:604
  61.0 14.6 %all-gather.3.cloned.1.call-done.refs_9_ = bf16[256,3584]{1,0:T(8,128)(2,1)} async-done(((bf16[16,3584]{1,0:T(8,128)(2,1)}), bf16[256,3584]{1,0:T(8,128)(2,1)}) %all-gather.3.cloned.1.call-update) | async-done | bytes 1835024 | tf_op jit(solution)/shard_map/all_gather | solution.py:555
  75.5 62.2 %all-gather.5.cloned.1.call-done.refs_10_ = bf16[256,3584]{1,0:T(8,128)(2,1)} async-done(((bf16[16,3584]{1,0:T(8,128)(2,1)}), bf16[256,3584]{1,0:T(8,128)(2,1)}) %all-gather.5.cloned.1.call-update) | async-done | bytes 1835024 | tf_op jit(solution)/shard_map/all_gather | solution.py:555
  137.8 3.7 %collective-permute-start.3 = (bf16[256,3584]{1,0:T(8,128)(2,1)}, bf16[256,3584]{1,0:T(8,128)(2,1)S(1)}, u32[]{:S(2)}, u32[]{:S(2)}) collective-permute-start(bf16[256,3584]{1,0:T(8,128)(2,1)} %all-gather.3.cloned.1.call-done.refs_9_), channel_id=1, source_target_pairs={{0,32},{1,33},{2,34},{3,35},{4,36},{5,37},{6,38},{7,39},{8,40},{9,... | collective-permute-start | bytes 5505032 | tf_op jit(solution)/shard_map/ppermute | solution.py:544
  141.5 1.9 collective-permute-start.4
  143.5 12.9 %collective-permute-start.1 = (f32[8,768]{1,0:T(8,128)S(1)}, f32[8,768]{1,0:T(8,128)S(1)}, u32[]{:S(2)}, u32[]{:S(2)}) collective-permute-start(f32[8,768]{1,0:T(8,128)S(1)} %get-tuple-element.27), channel_id=1, source_target_pairs={{0,32},{32,64},{64,96},{96,128},{128,160},{160,192},{192,224},{224... | collective-permute-start | bytes 73736 | tf_op jit(solution)/shard_map/ppermute | solution.py:566
  156.4 1.9 collective-permute-start.2
  158.5 11.8 %collective-permute-done.2.refs_3_ = f32[8,768]{1,0:T(8,128)S(1)} collective-permute-done((f32[8,768]{1,0:T(8,128)S(1)}, f32[8,768]{1,0:T(8,128)S(1)}, u32[]{:S(2)}, u32[]{:S(2)}) %collective-permute-start.2) | collective-permute-done | bytes 24608 | tf_op jit(solution)/shard_map/ppermute | solution.py:566
  170.4 1.5 copy-done.4
  171.8 1.5 copy-done.5
  173.3 13.4 %projector.1 = (f32[32,1024]{1,0:T(8,128)S(1)}, f32[8,768]{1,0:T(8,128)S(1)}) custom-call(s32[4]{0:T(128)S(1)} %pad_add_fusion.refs_0_.at_ref, f32[8,768]{1,0:T(8,128)S(1)} %get-tuple-element.26.refs_1_, f32[8,768]{1,0:T(8,128)S(1)} %collective-permute-done.1.refs_2_, f32[8,768]{1,0:T(8,128)S(1)} %collective-permute-done.2.refs_3_, ...), custom_call_target="tpu_custom_call" | custom-call | flops 2818572288 | bytes 8388608 | tf_op jit(solution)/shard_map/projector/pallas_call | solution.py:273
  186.8 1.9 collective-permute-start.5
  188.7 2.4 collective-permute-start.6
  191.2 11.4 %collective-permute-done.6.refs_2_ = f32[8,768]{1,0:T(8,128)S(1)} collective-permute-done((f32[8,768]{1,0:T(8,128)S(1)}, f32[8,768]{1,0:T(8,128)S(1)}, u32[]{:S(2)}, u32[]{:S(2)}) %collective-permute-start.6) | collective-permute-done | bytes 24608 | tf_op jit(solution)/shard_map/ppermute | solution.py:566
  202.6 2.0 back.1
  204.6 13.9 %all_to_all.20.got_ref = bf16[32,32,128]{2,1,0:T(8,128)(2,1)S(1)} all-to-all(bf16[32,32,128]{2,1,0:T(8,128)(2,1)S(1)} %get-tuple-element.35), channel_id=1, replica_groups={{0,32,1,33,2,34,3,35,128,160,129,161,130,162,131,163,256,288,257,289,25..., dimensions={0} | all-to-all | bytes 524288 | tf_op jit(solution)/shard_map/all_to_all | solution.py:532
  219.1 16.3 %all_to_all.21.got_ref = bf16[16,32,128]{2,1,0:T(8,128)(2,1)S(1)} all-to-all(bf16[16,32,128]{2,1,0:T(8,128)(2,1)S(1)} %plane.1), channel_id=1, replica_groups={{0,4,8,12,16,20,24,28,64,68,72,76,80,84,88,92},{32,36,40,44,48,52,56,60..., dimensions={0} | all-to-all | bytes 262144 | tf_op jit(solution)/shard_map/all_to_all | solution.py:532
  236.6 6.4 %all-to-all-start.3 = ((bf16[32,16,128]{2,1,0:T(8,128)(2,1)}), bf16[32,16,128]{2,1,0:T(8,128)(2,1)S(1)}, u32[]{:S(2)}, u32[]{:S(2)}) async-start(bf16[32,16,128]{2,1,0:T(8,128)(2,1)} %get-tuple-element.38), calls=%async_computation.3 | async-start | bytes 262144 | tf_op jit(solution)/shard_map/all_to_all | solution.py:532
  243.0 1.6 last.1
  244.6 6.1 %all-to-all-done.3.got_ref = bf16[32,16,128]{2,1,0:T(8,128)(2,1)S(1)} async-done(((bf16[32,16,128]{2,1,0:T(8,128)(2,1)}), bf16[32,16,128]{2,1,0:T(8,128)(2,1)S(1)}, u32[]{:S(2)}, u32[]{:S(2)}) %all-to-all-start.3) | async-done | bytes 131104 | tf_op jit(solution)/shard_map/all_to_all | solution.py:532
  (44 shorter events, 8.9 us)
Async XLA Ops:
  7.2 52.6 %copy-start.1 = (bf16[12,2,32,512]{3,2,1,0:T(8,128)(2,1)S(1)}, bf16[12,2,32,512]{3,2,1,0:T(8,128)(2,1)}, u32[]{:S(2)}) copy-start(bf16[12,2,32,512]{3,2,1,0:T(8,128)(2,1)} %param.11) | copy-start | bytes 2359300
  7.2 52.6 %copy-start.2 = (f32[512]{0:T(512)S(1)}, f32[512]{0:T(512)}, u32[]{:S(2)}) copy-start(f32[512]{0:T(512)} %param.12) | copy-start | bytes 6148
  7.2 52.6 %copy-start.3 = (f32[512]{0:T(512)S(1)}, f32[512]{0:T(512)}, u32[]{:S(2)}) copy-start(f32[512]{0:T(512)} %param.13) | copy-start | bytes 6148
  7.2 68.3 %all-gather.3.cloned.1.call-start = ((), (), s32[]{:S(2)}) async-start(), calls=%async_computation.4 | async-start | bytes 1949696 | tf_op jit(solution)/shard_map/all_gather | solution.py:555
  8.3 150.2 %copy-start.11 = (f32[768]{0:T(1024)S(1)}, f32[768]{0:T(1024)}, u32[]{:S(2)}) copy-start(f32[768]{0:T(1024)} %param.20) | copy-start | bytes 9220
  8.3 162.0 %copy-start.6 = (bf16[12,1,16,768]{3,2,1,0:T(8,128)(2,1)S(1)}, bf16[12,1,16,768]{3,2,1,0:T(8,128)(2,1)}, u32[]{:S(2)}) copy-start(bf16[12,1,16,768]{3,2,1,0:T(8,128)(2,1)} %param.21) | copy-start | bytes 884740
  8.3 162.0 %copy-start.7 = (f32[2048]{0:T(1024)S(1)}, f32[2048]{0:T(1024)}, u32[]{:S(2)}) copy-start(f32[2048]{0:T(1024)} %param.18) | copy-start | bytes 24580
  8.3 162.0 %copy-start.8 = (f32[1024]{0:T(1024)S(1)}, f32[1024]{0:T(1024)}, u32[]{:S(2)}) copy-start(f32[1024]{0:T(1024)} %param.16) | copy-start | bytes 12292
  9.9 127.9 %all-gather.5.cloned.1.call-start = ((), (), s32[]{:S(2)}) async-start(), calls=%async_computation.5 | async-start | bytes 1949696 | tf_op jit(solution)/shard_map/all_gather | solution.py:555
  9.9 22.7 %collective-permute-start = (bf16[16,3584]{1,0:T(8,128)(2,1)}, bf16[16,3584]{1,0:T(8,128)(2,1)S(1)}, u32[]{:S(2)}, u32[]{:S(2)}) collective-permute-start(bf16[16,3584]{1,0:T(8,128)(2,1)} %fusion.1), channel_id=1, source_target_pairs={{0,92},{1,93},{2,94},{3,95},{4,88},{5,89},{6,90},{7,91},{8,84},{9,... | collective-permute-start | bytes 344072 | tf_op jit(solution)/shard_map/ppermute | solution.py:544
  21.9 1.1 copy-start
  23.0 120.4 %copy-start.10 = (f32[16,1024]{1,0:T(8,128)S(1)}, f32[16,1024]{1,0:T(8,128)}, u32[]{:S(2)}) copy-start(f32[16,1024]{1,0:T(8,128)} %param.15) | copy-start | bytes 196612
  32.7 0.6 copy-start.9
  33.3 26.5 %all-to-all-start = ((f32[16,8,128]{2,1,0:T(8,128)}), f32[16,8,128]{2,1,0:T(8,128)S(1)}, u32[]{:S(2)}, u32[]{:S(2)}) async-start(f32[16,8,128]{2,1,0:T(8,128)} %stats.1), calls=%async_computation | async-start | bytes 131072 | tf_op jit(solution)/shard_map/all_to_all | solution.py:604
  137.8 32.6 %collective-permute-start.3 = (bf16[256,3584]{1,0:T(8,128)(2,1)}, bf16[256,3584]{1,0:T(8,128)(2,1)S(1)}, u32[]{:S(2)}, u32[]{:S(2)}) collective-permute-start(bf16[256,3584]{1,0:T(8,128)(2,1)} %all-gather.3.cloned.1.call-done.refs_9_), channel_id=1, source_target_pairs={{0,32},{1,33},{2,34},{3,35},{4,36},{5,37},{6,38},{7,39},{8,40},{9,... | collective-permute-start | bytes 5505032 | tf_op jit(solution)/shard_map/ppermute | solution.py:544
  141.5 28.8 %collective-permute-start.4 = (bf16[256,3584]{1,0:T(8,128)(2,1)}, bf16[256,3584]{1,0:T(8,128)(2,1)}, u32[]{:S(2)}, u32[]{:S(2)}) collective-permute-start(bf16[256,3584]{1,0:T(8,128)(2,1)} %all-gather.5.cloned.1.call-done.refs_10_), channel_id=1, source_target_pairs={{0,32},{1,33},{2,34},{3,35},{4,36},{5,37},{6,38},{7,39},{8,40},{9,... | collective-permute-start | bytes 5505032 | tf_op jit(solution)/shard_map/ppermute | solution.py:544
  143.5 14.9 %collective-permute-start.1 = (f32[8,768]{1,0:T(8,128)S(1)}, f32[8,768]{1,0:T(8,128)S(1)}, u32[]{:S(2)}, u32[]{:S(2)}) collective-permute-start(f32[8,768]{1,0:T(8,128)S(1)} %get-tuple-element.27), channel_id=1, source_target_pairs={{0,32},{32,64},{64,96},{96,128},{128,160},{160,192},{192,224},{224... | collective-permute-start | bytes 73736 | tf_op jit(solution)/shard_map/ppermute | solution.py:566
  156.4 13.9 %collective-permute-start.2 = (f32[8,768]{1,0:T(8,128)S(1)}, f32[8,768]{1,0:T(8,128)S(1)}, u32[]{:S(2)}, u32[]{:S(2)}) collective-permute-start(f32[8,768]{1,0:T(8,128)S(1)} %get-tuple-element.28), channel_id=1, source_target_pairs={{32,0},{64,32},{96,64},{128,96},{160,128},{192,160},{224,192},{256... | collective-permute-start | bytes 73736 | tf_op jit(solution)/shard_map/ppermute | solution.py:566
  170.3 1.5 copy-start.4
  171.8 1.5 copy-start.5
  186.8 4.4 %collective-permute-start.5 = (f32[8,768]{1,0:T(8,128)S(1)}, f32[8,768]{1,0:T(8,128)S(1)}, u32[]{:S(2)}, u32[]{:S(2)}) collective-permute-start(f32[8,768]{1,0:T(8,128)S(1)} %get-tuple-element.31.refs_0_), channel_id=1, source_target_pairs={{0,32},{32,64},{64,96},{96,128},{128,160},{160,192},{192,224},{224... | collective-permute-start | bytes 73736 | tf_op jit(solution)/shard_map/ppermute | solution.py:566
  188.7 13.9 %collective-permute-start.6 = (f32[8,768]{1,0:T(8,128)S(1)}, f32[8,768]{1,0:T(8,128)S(1)}, u32[]{:S(2)}, u32[]{:S(2)}) collective-permute-start(f32[8,768]{1,0:T(8,128)S(1)} %get-tuple-element.31.refs_0_), channel_id=1, source_target_pairs={{32,0},{64,32},{96,64},{128,96},{160,128},{192,160},{224,192},{256... | collective-permute-start | bytes 73736 | tf_op jit(solution)/shard_map/ppermute | solution.py:566
  236.6 14.1 %all-to-all-start.3 = ((bf16[32,16,128]{2,1,0:T(8,128)(2,1)}), bf16[32,16,128]{2,1,0:T(8,128)(2,1)S(1)}, u32[]{:S(2)}, u32[]{:S(2)}) async-start(bf16[32,16,128]{2,1,0:T(8,128)(2,1)} %get-tuple-element.38), calls=%async_computation.3 | async-start | bytes 262144 | tf_op jit(solution)/shard_map/all_to_all | solution.py:532
Sparse Core Ops, SparseCore 0:
  11.7 63.8 all-gather.2
  78.6 59.1 all-gather.4

commit v3 on v2

--- a/solution.py
+++ b/solution.py
@@ -21,6 +21,8 @@
 LANES = 128
 STAT_ROWS = 16
 CHUNKS, CHUNK_ROWS, ALL_ROWS = 32, 16, 32
+CONV_COST = 20_000_000_000
+PART = 16
 
 
 def params(limit_mb=48):
@@ -68,6 +70,11 @@
 
 def unpack_stats(packed):
     return jnp.concatenate([packed, pltpu.roll(packed, LANES // 2, 1)], axis=0)
+
+
+def parts(v):
+    top = v.astype(BF16)
+    return top, (v - top.astype(F32)).astype(BF16)
 
 
 def halves(packed):
@@ -161,6 +168,9 @@
         out_specs=(vmem(),) * 5,
         scratch_shapes=[pltpu.VMEM((images * cells, channels), BF16)],
         compiler_params=params(),
+        cost_estimate=pl.CostEstimate(
+            flops=CONV_COST, bytes_accessed=features.size * 2, transcendentals=features.size
+        ),
         name="conv",
     )(stats, features, gain, bias, kernel_rows)
 
@@ -168,33 +178,43 @@
 def mlp_kernel(
     across, width, hidden, align, at_ref, lat_ref, below_ref, above_ref, target_ref,
     ew_ref, eb_ref, pib_ref, pob_ref,
-    own, cross, own_other, cross_other,
+    own_near, own_far, cross_near, cross_far, own_near_other, own_far_other,
+    cross_near_other, cross_far_other,
     embed_ref, gl_ref, w_in, w_out, pre, emb, acc, grad_emb, sems,
 ):
-    zhi, core = at_ref[0], at_ref[1]
+    zhi, core, x = at_ref[0], at_ref[1], at_ref[4]
     depth = width // (XS * ZHI * CORES)
     slab = hidden // (XS * ZHI * CORES)
+    rows = ew_ref.shape[0]
     copies = []
-
-    for piece, of_zhi, of_core in (
-        (own, zhi, core),
-        (own_other, zhi, 1 - core),
-        (cross, 1 - zhi, core),
-        (cross_other, 1 - zhi, 1 - core),
+    own, own_other = (own_near, own_far), (own_near_other, own_far_other)
+    cross, cross_other = (cross_near, cross_far), (cross_near_other, cross_far_other)
+
+    def place(piece, at, source_x, of_zhi, of_core, half=0, count=1):
+        shard = lax.rem(source_x, XS) * (ZHI * CORES) + of_zhi * CORES + of_core
+        size = depth // count
+        lines = pl.ds(at, size)
+
+        def put(columns, into):
+            copy = pltpu.make_async_copy(piece.at[lines, columns], into, sems.at[len(copies)])
+            copy.start()
+            copies.append(copy)
+
+        begin = pl.multiple_of(shard * depth + half * size, size)
+        put(pl.ds(0, hidden), w_in.at[pl.ds(begin, size), :])
+        for part in range(slab // depth):
+            begin = pl.multiple_of(shard * slab + part * depth + half * size, size)
+            put(pl.ds(hidden + part * align, align), w_out.at[pl.ds(begin, size), :])
+
+    for of_zhi, by_core in (
+        (zhi, ((core, own), (1 - core, own_other))),
+        (1 - zhi, ((core, cross), (1 - core, cross_other))),
     ):
-        for x in range(XS):
-            shard = x * (ZHI * CORES) + of_zhi * CORES + of_core
-            lines = pl.ds(x * depth, depth)
-
-            def put(columns, into):
-                copy = pltpu.make_async_copy(piece.at[lines, columns], into, sems.at[len(copies)])
-                copy.start()
-                copies.append(copy)
-
-            put(pl.ds(0, hidden), w_in.at[pl.ds(pl.multiple_of(shard * depth, depth), depth), :])
-            for part in range(slab // depth):
-                begin = pl.multiple_of(shard * slab + part * depth, depth)
-                put(pl.ds(hidden + part * align, align), w_out.at[pl.ds(begin, depth), :])
+        for of_core, (near, opposite) in by_core:
+            for k, step in enumerate((0, 1, XS - 1)):
+                place(near, k * depth, x + step, of_zhi, of_core)
+            for half in range(2):
+                place(opposite, half * depth // 2, x + 2, of_zhi, of_core, half, 2)
 
     lat = lat_ref[...] + below_ref[...] + above_ref[...]
     top = lat.astype(BF16)
@@ -222,7 +242,10 @@
         lines.append(got[0:SUB] + got[SUB : 2 * SUB] + got[2 * SUB :])
     patches_t = jnp.concatenate(lines, axis=0)
     patches = patches_t.T
-    emb[...] = (nn(patches, ew_ref[...], HIGH) + eb_ref[...])[:tokens].astype(BF16)
+    ew_top, ew_low = parts(ew_ref[...])
+    p_top, p_low = parts(patches[:tokens])
+    embedded = nn(p_top, ew_top) + nn(p_low, ew_top) + nn(p_top, ew_low)
+    emb[...] = (embedded + eb_ref[...]).astype(BF16)
 
     for copy in copies:
         copy.wait()
@@ -256,8 +279,12 @@
         grad_emb[0:tokens, :] += nt(grad_hidden, w_in[:, at])
 
     grad = grad_emb[...]
-    embed_ref[...] = nn(patches_t, grad, HIGH)
-    grad_patch = nt(ew_ref[...], grad, HIGH)
+    g_top, g_low = parts(grad)
+    t_top, t_low = parts(patches_t)
+    both = nn(jnp.concatenate([t_top, t_low], axis=0), g_top)
+    embed_ref[...] = both[:rows] + both[rows:] + nn(t_top, g_low)
+    both = nt(jnp.concatenate([ew_top, ew_low], axis=0), g_top)
+    grad_patch = both[:rows] + both[rows:] + nt(ew_top, g_low)
     total = jnp.zeros((SUB, cells), F32)
     for position, pick in enumerate(picks):
         part = grad_patch[position * SUB : (position + 1) * SUB].astype(BF16)
@@ -278,7 +305,7 @@
         ),
         in_specs=[pl.BlockSpec(memory_space=pltpu.SMEM)]
         + [vmem()] * 8
-        + [pl.BlockSpec(memory_space=pl.ANY)] * len(pieces),
+        + [pl.BlockSpec(memory_space=pltpu.HBM)] * len(pieces),
         out_specs=(vmem(), vmem()),
         scratch_shapes=[
             pltpu.VMEM((width, hidden), BF16),
@@ -287,7 +314,7 @@
             pltpu.VMEM((tokens, width), BF16),
             pltpu.VMEM((tokens, align), F32),
             pltpu.VMEM((256, width), F32),
-            pltpu.SemaphoreType.DMA((48,)),
+            pltpu.SemaphoreType.DMA((60,)),
         ],
         compiler_params=params(),
         cost_estimate=pl.CostEstimate(
@@ -514,12 +541,6 @@
     for h in range(ZHI)
     for d in range(ZLO)
 ]
-SHEET = [
-    [device(x, h, c, d, y) for x in range(XS) for y in range(YS)]
-    for h in range(ZHI)
-    for d in range(ZLO)
-    for c in range(CORES)
-]
 COLUMN = [
     [device(x, h, c, d, y) for h in range(ZHI) for d in range(ZLO)]
     for x in range(XS)
@@ -546,13 +567,34 @@
 
 def crossed(shard):
     y = lax.axis_index("batch") % YS
-    part = shard.shape[0] // YS
-    mine = lax.dynamic_slice_in_dim(shard, y * part, part, axis=0)
-    return mine, moved(mine, lambda x, h, c, d, y: (x, 1 - h, c, ZLO - 1 - d, y))
-
-
-def sheet(part):
-    return lax.all_gather(part, BOTH, axis_index_groups=SHEET, tiled=True)
+    mine = lax.dynamic_slice_in_dim(shard, y * PART, PART, axis=0)
+    return moved(mine, lambda x, h, c, d, y: (x, 1 - h, c, ZLO - 1 - d, y))
+
+
+def along_y(part):
+    y = lax.axis_index("batch") % YS
+    other = moved(part, lambda x, h, c, d, y: (x, h, c, d, y ^ 1))
+    even = y % 2 == 0
+    pair = jnp.concatenate([jnp.where(even, part, other), jnp.where(even, other, part)], axis=0)
+    far = moved(pair, lambda x, h, c, d, y: (x, h, c, d, YS - 1 - y))
+    low = y < 2
+    return jnp.concatenate([jnp.where(low, pair, far), jnp.where(low, far, pair)], axis=0)
+
+
+def from_next(value):
+    return moved(value, lambda x, h, c, d, y: ((x + XS - 1) % XS, h, c, d, y))
+
+
+def from_last(value):
+    return moved(value, lambda x, h, c, d, y: ((x + 1) % XS, h, c, d, y))
+
+
+def along_x(shard):
+    half = shard.shape[0] // 2
+    plus, minus = from_next(shard), from_last(shard)
+    near = jnp.concatenate([shard, plus, minus], axis=0)
+    opposite = jnp.concatenate([from_next(plus[:half]), from_last(minus[half:])], axis=0)
+    return near, opposite
 
 
 def swapped(value):
@@ -589,8 +631,8 @@
     shard = jnp.concatenate(
         [proj_in] + [proj_out[at : at + depth] for at in range(0, proj_out.shape[0], depth)], axis=1
     )
-    mine, far = crossed(shard)
-    own = sheet(mine)
+    far = crossed(shard)
+    own_near, own_far = along_x(shard)
     taps = conv_weight.reshape(LATENT, TAPS, channels).transpose(1, 0, 2)
     taps = jnp.pad(taps, ((0, 0), (0, SUB - LATENT), (0, 0))).reshape(TAPS * SUB, channels)
     taps_full = jnp.pad(taps, ((0, LANES - TAPS * SUB), (0, 0)))
@@ -599,15 +641,16 @@
     ).reshape(PATCH * PATCH * SUB, width)
 
     sums = group_stats(flat, peers)
-    far, _ = lax.optimization_barrier((far, sums))
-    cross = sheet(far)
     stats = lax.all_to_all(sums, "rows", 0, 0, tiled=True)
+    cross = along_y(far)
+    cross_near, cross_far = along_x(cross)
     lat, up, down, mean, inv = conv_forward(stats, flat, gain, bias, taps, across, members)
     above, below = neighbours(up, down)
-    own, cross, lat = lax.optimization_barrier((own, cross, lat))
-    pieces = [own, cross, swapped(own), swapped(cross)]
+    own_near, own_far, above, below = lax.optimization_barrier((own_near, own_far, above, below))
+    pieces = [own_near, own_far, cross_near, cross_far]
+    pieces = pieces + [swapped(v) for v in pieces]
     rows, batch = lax.axis_index("rows"), lax.axis_index("batch")
-    at = jnp.stack([(rows // CORES) % ZHI, rows % CORES, batch % YS, batch // YS])
+    at = jnp.stack([(rows // CORES) % ZHI, rows % CORES, batch % YS, batch // YS, rows // (ZHI * CORES)])
     at = at.astype(jnp.int32)
     target = targets.reshape(-1, align)
     embed_part, grad_lat = projector(

time: 259 us -> 205 us (0.79)
  waiting for transfers between devices: 128 us -> 45.4 us
  starting transfers between devices: 55.1 us -> 87.3 us
  between operations: 14.4 us -> 1.31 us
  blocking collectives: 30.2 us -> 36.6 us
  local copies, waits for them, and re-layouts: 6.7 us -> 10.3 us
    all_gather x2 -> x0, waiting for transfers between devices: 76.8 us -> none  [sheet(): return lax.all_gather(part, BOTH, axis_index_groups=SHEET, tiled=True)]
    ppermute x3 -> x15, starting transfers between devices: 17.6 us -> 52.4 us  [moved(): return lax.ppermute(value, ('rows', 'batch'), pairs)]
    ppermute x3 -> x15, waiting for transfers between devices: 8.31 us -> 24.7 us  [moved(): return lax.ppermute(value, ('rows', 'batch'), pairs)]
    ppermute x2, waiting for transfers between devices: 23.3 us -> 11.4 us  [neighbours(): lax.ppermute(up, 'rows', backward)]
    all_to_all x1, waiting for transfers between devices: 13.7 us -> 3.22 us  [shards(): stats = lax.all_to_all(sums, 'rows', 0, 0, tiled=True)]
    all_to_all x2, blocking collectives: 30.2 us -> 36.6 us  [exchanged(): lax.all_to_all(value, BOTH, 0, 0, axis_index_groups=groups, tiled=True)]
    unnamed x25 -> x48, local copies, waits for them, and re-layouts: 4.83 us -> 5.97 us
  transfers between devices with their start and end apart: 11 -> 21, of which waited for: 7 -> 7; matrix products, arithmetic and copies ran while one was open for 0% -> 3% of each run, Pallas kernels for 2% -> 2%
where the time goes in v3:
time: 205 us; the launch traced here: 204 us
  starting transfers between devices  87.3 us (43%)
  waiting for transfers between devices  45.4 us (22%)
  blocking collectives  36.6 us (18%)
  Pallas kernels  20.5 us (10%)
  local copies, waits for them, and re-layouts  10.3 us (5%)
  other arithmetic  2.14 us (1%)
    ppermute x15, starting transfers between devices, moved(): return lax.ppermute(value, ('rows', 'batch'), pairs)  52.4 us
    all_to_all x2, blocking collectives, exchanged(): lax.all_to_all(value, BOTH, 0, 0, axis_index_groups=groups, tiled=True)  36.6 us
    ppermute x15, waiting for transfers between devices, moved(): return lax.ppermute(value, ('rows', 'batch'), pairs)  24.7 us
    ppermute x2, starting transfers between devices, neighbours(): lax.ppermute(down, 'rows', forward)  14 us
    pallas_call x1, Pallas kernels, projector(): pl.pallas_call(lambda *refs: mlp_kernel(across, width, hidden, align, *re...  11.8 us
    ppermute x2, waiting for transfers between devices, neighbours(): lax.ppermute(up, 'rows', backward)  11.4 us
    all_to_all x1, starting transfers between devices, shards(): stats = lax.all_to_all(sums, 'rows', 0, 0, tiled=True)  9.61 us
    all_to_all x1, starting transfers between devices, exchanged(): lax.all_to_all(value, BOTH, 0, 0, axis_index_groups=groups, tiled=True)  6.36 us
  transfers between devices with their start and end apart: 21, of which 7 were waited for; matrix products, arithmetic and copies ran while one was open for 3% of the time, Pallas kernels for 2%

profile of v3, /device:TPU:1, one launch (start us, length us, event | category | flops | bytes accessed | tf_op | source)
XLA Modules:
  0.0 203.5 jit_solution(6042451137166611115)
XLA Ops:
  2.7 12.0 %collective-permute-start.6 = (bf16[16,3584]{1,0:T(8,128)(2,1)S(1)}, bf16[16,3584]{1,0:T(8,128)(2,1)S(1)}, u32[]{:S(2)}, u32[]{:S(2)}) collective-permute-start(bf16[16,3584]{1,0:T(8,128)(2,1)S(1)} %constant_dynamic-slice_fusion), channel_id=1, source_target_pairs={{0,92},{1,93},{2,94},{3,95},{4,88},{5,89},{6,90},{7,91},{8,84},{9,... | collective-permute-start | bytes 344072 | tf_op jit(solution)/shard_map/ppermute | solution.py:565
  14.7 4.4 %collective-permute-start = (bf16[64,3584]{1,0:T(8,128)(2,1)S(1)}, bf16[64,3584]{1,0:T(8,128)(2,1)S(1)}, u32[]{:S(2)}, u32[]{:S(2)}) collective-permute-start(bf16[64,3584]{1,0:T(8,128)(2,1)S(1)} %pad_maximum_fusion.2), channel_id=1, source_target_pairs={{0,384},{1,385},{2,386},{3,387},{4,388},{5,389},{6,390},{7,391},{8... | collective-permute-start | bytes 1376264 | tf_op jit(solution)/shard_map/ppermute | solution.py:565
  22.3 9.6 %all-to-all-start = ((f32[16,8,128]{2,1,0:T(8,128)}), f32[16,8,128]{2,1,0:T(8,128)S(1)}, u32[]{:S(2)}, u32[]{:S(2)}) async-start(f32[16,8,128]{2,1,0:T(8,128)} %stats.1), calls=%async_computation | async-start | bytes 131072 | tf_op jit(solution)/shard_map/all_to_all | solution.py:644
  32.0 3.2 %collective-permute-start.7 = (bf16[16,3584]{1,0:T(8,128)(2,1)S(1)}, bf16[16,3584]{1,0:T(8,128)(2,1)S(1)}, u32[]{:S(2)}, u32[]{:S(2)}) collective-permute-start(bf16[16,3584]{1,0:T(8,128)(2,1)S(1)} %collective-permute-done.6), channel_id=1, source_target_pairs={{0,1},{1,0},{2,3},{3,2},{4,5},{5,4},{6,7},{7,6},{8,9},{9,8},{10,11... | collective-permute-start | bytes 344072 | tf_op jit(solution)/shard_map/ppermute | solution.py:565
  35.3 3.2 %collective-permute-done.7 = bf16[16,3584]{1,0:T(8,128)(2,1)S(1)} collective-permute-done((bf16[16,3584]{1,0:T(8,128)(2,1)S(1)}, bf16[16,3584]{1,0:T(8,128)(2,1)S(1)}, u32[]{:S(2)}, u32[]{:S(2)}) %collective-permute-start.7) | collective-permute-done | bytes 114720 | tf_op jit(solution)/shard_map/ppermute | solution.py:565
  38.6 4.6 %collective-permute-start.8 = (bf16[32,3584]{1,0:T(8,128)(2,1)S(1)}, bf16[32,3584]{1,0:T(8,128)(2,1)S(1)}, u32[]{:S(2)}, u32[]{:S(2)}) collective-permute-start(bf16[32,3584]{1,0:T(8,128)(2,1)S(1)} %pad_maximum_fusion.5), channel_id=1, source_target_pairs={{0,3},{1,2},{2,1},{3,0},{4,7},{5,6},{6,5},{7,4},{8,11},{9,10},{10,... | collective-permute-start | bytes 688136 | tf_op jit(solution)/shard_map/ppermute | solution.py:565
  43.3 3.2 %all-to-all-done.refs_0_ = f32[16,8,128]{2,1,0:T(8,128)S(1)} async-done(((f32[16,8,128]{2,1,0:T(8,128)}), f32[16,8,128]{2,1,0:T(8,128)S(1)}, u32[]{:S(2)}, u32[]{:S(2)}) %all-to-all-start) | async-done | bytes 65568 | tf_op jit(solution)/shard_map/all_to_all | solution.py:644
  48.3 2.5 %collective-permute-start.4 = (f32[8,768]{1,0:T(8,128)S(1)}, f32[8,768]{1,0:T(8,128)S(1)}, u32[]{:S(2)}, u32[]{:S(2)}) collective-permute-start(f32[8,768]{1,0:T(8,128)S(1)} %get-tuple-element.25), channel_id=1, source_target_pairs={{32,0},{64,32},{96,64},{128,96},{160,128},{192,160},{224,192},{256... | collective-permute-start | bytes 73736 | tf_op jit(solution)/shard_map/ppermute | solution.py:608
  50.7 11.9 %collective-permute-start.5 = (f32[8,768]{1,0:T(8,128)S(1)}, f32[8,768]{1,0:T(8,128)S(1)}, u32[]{:S(2)}, u32[]{:S(2)}) collective-permute-start(f32[8,768]{1,0:T(8,128)S(1)} %get-tuple-element.26), channel_id=1, source_target_pairs={{0,32},{32,64},{64,96},{96,128},{128,160},{160,192},{192,224},{224... | collective-permute-start | bytes 73736 | tf_op jit(solution)/shard_map/ppermute | solution.py:608
  62.8 2.8 %collective-permute-start.9 = (bf16[64,3584]{1,0:T(8,128)(2,1)S(1)}, bf16[64,3584]{1,0:T(8,128)(2,1)S(1)}, u32[]{:S(2)}, u32[]{:S(2)}) collective-permute-start(bf16[64,3584]{1,0:T(8,128)(2,1)S(1)} %pad_maximum_fusion.4), channel_id=1, source_target_pairs={{0,384},{1,385},{2,386},{3,387},{4,388},{5,389},{6,390},{7,391},{8... | collective-permute-start | bytes 1376264 | tf_op jit(solution)/shard_map/ppermute | solution.py:565
  68.0 3.0 %collective-permute-start.3 = (bf16[32,3584]{1,0:T(8,128)(2,1)S(1)}, bf16[32,3584]{1,0:T(8,128)(2,1)S(1)}, u32[]{:S(2)}, u32[]{:S(2)}) collective-permute-start(bf16[32,3584]{1,0:T(8,128)(2,1)S(1)} %slice.25), channel_id=1, source_target_pairs={{0,128},{1,129},{2,130},{3,131},{4,132},{5,133},{6,134},{7,135},{8... | collective-permute-start | bytes 688136 | tf_op jit(solution)/shard_map/ppermute | solution.py:565
  71.1 8.5 %collective-permute-done.2 = bf16[32,3584]{1,0:T(8,128)(2,1)S(1)} collective-permute-done((bf16[32,3584]{1,0:T(8,128)(2,1)S(1)}, bf16[32,3584]{1,0:T(8,128)(2,1)S(1)}, u32[]{:S(2)}, u32[]{:S(2)}) %collective-permute-start.2) | collective-permute-done | bytes 229408 | tf_op jit(solution)/shard_map/ppermute | solution.py:565
  84.7 4.6 %collective-permute-start.11 = (bf16[32,3584]{1,0:T(8,128)(2,1)S(1)}, bf16[32,3584]{1,0:T(8,128)(2,1)S(1)}, u32[]{:S(2)}, u32[]{:S(2)}) collective-permute-start(bf16[32,3584]{1,0:T(8,128)(2,1)S(1)} %slice.26), channel_id=1, source_target_pairs={{0,384},{1,385},{2,386},{3,387},{4,388},{5,389},{6,390},{7,391},{8... | collective-permute-start | bytes 688136 | tf_op jit(solution)/shard_map/ppermute | solution.py:565
  89.4 5.6 %collective-permute-done.10 = bf16[64,3584]{1,0:T(8,128)(2,1)S(1)} collective-permute-done((bf16[64,3584]{1,0:T(8,128)(2,1)S(1)}, bf16[64,3584]{1,0:T(8,128)(2,1)S(1)}, u32[]{:S(2)}, u32[]{:S(2)}) %collective-permute-start.10) | collective-permute-done | bytes 458784 | tf_op jit(solution)/shard_map/ppermute | solution.py:565
  95.2 2.3 %collective-permute-start.15 = (bf16[192,3584]{1,0:T(8,128)(2,1)S(1)}, bf16[192,3584]{1,0:T(8,128)(2,1)}, u32[]{:S(2)}, u32[]{:S(2)}) collective-permute-start(bf16[192,3584]{1,0:T(8,128)(2,1)S(1)} %pad_maximum_fusion.1.refs_11_), channel_id=1, source_target_pairs={{0,32},{1,33},{2,34},{3,35},{4,36},{5,37},{6,38},{7,39},{8,40},{9,... | collective-permute-start | bytes 4128776 | tf_op jit(solution)/shard_map/ppermute | solution.py:565
  102.2 7.2 %collective-permute-done.12 = bf16[32,3584]{1,0:T(8,128)(2,1)S(1)} collective-permute-done((bf16[32,3584]{1,0:T(8,128)(2,1)S(1)}, bf16[32,3584]{1,0:T(8,128)(2,1)S(1)}, u32[]{:S(2)}, u32[]{:S(2)}) %collective-permute-start.12) | collective-permute-done | bytes 229408 | tf_op jit(solution)/shard_map/ppermute | solution.py:565
  110.1 3.1 %collective-permute-start.16 = (bf16[64,3584]{1,0:T(8,128)(2,1)}, bf16[64,3584]{1,0:T(8,128)(2,1)}, u32[]{:S(2)}, u32[]{:S(2)}) collective-permute-start(bf16[64,3584]{1,0:T(8,128)(2,1)} %constant_dynamic-update-slice_fusion.refs_12_), channel_id=1, source_target_pairs={{0,32},{1,33},{2,34},{3,35},{4,36},{5,37},{6,38},{7,39},{8,40},{9,... | collective-permute-start | bytes 1376264 | tf_op jit(solution)/shard_map/ppermute | solution.py:565
  120.4 11.8 %projector.1 = (f32[32,1024]{1,0:T(8,128)S(1)}, f32[8,768]{1,0:T(8,128)S(1)}) custom-call(s32[5]{0:T(128)S(1)} %stack.23.refs_0_.at_ref, f32[8,768]{1,0:T(8,128)S(1)} %copy-done.19, f32[8,768]{1,0:T(8,128)S(1)} %copy-done.15, f32[8,768]{1,0:T(8,128)S(1)} %copy-done.13, bf16[192,768]{1,0:T(8,128)(2,1)S(1)} %bitcast.28, ...), custom_call_target="tpu_custom_call" | custom-call | flops 2818572288 | bytes 8388608 | tf_op jit(solution)/shard_map/projector/pallas_call | solution.py:300
  134.3 2.4 %collective-permute-start.18 = (f32[8,768]{1,0:T(8,128)S(1)}, f32[8,768]{1,0:T(8,128)S(1)}, u32[]{:S(2)}, u32[]{:S(2)}) collective-permute-start(f32[8,768]{1,0:T(8,128)S(1)} %get-tuple-element.31.refs_0_), channel_id=1, source_target_pairs={{32,0},{64,32},{96,64},{128,96},{160,128},{192,160},{224,192},{256... | collective-permute-start | bytes 73736 | tf_op jit(solution)/shard_map/ppermute | solution.py:608
  136.7 11.4 %collective-permute-done.18.refs_2_ = f32[8,768]{1,0:T(8,128)S(1)} collective-permute-done((f32[8,768]{1,0:T(8,128)S(1)}, f32[8,768]{1,0:T(8,128)S(1)}, u32[]{:S(2)}, u32[]{:S(2)}) %collective-permute-start.18) | collective-permute-done | bytes 24608 | tf_op jit(solution)/shard_map/ppermute | solution.py:608
  150.2 13.5 %all_to_all.20.got_ref = bf16[32,32,128]{2,1,0:T(8,128)(2,1)S(1)} all-to-all(bf16[32,32,128]{2,1,0:T(8,128)(2,1)S(1)} %get-tuple-element.35), channel_id=1, replica_groups={{0,32,1,33,2,34,3,35,128,160,129,161,130,162,131,163,256,288,257,289,25..., dimensions={0} | all-to-all | bytes 524288 | tf_op jit(solution)/shard_map/all_to_all | solution.py:553
  164.3 23.1 %all_to_all.21.got_ref = bf16[16,32,128]{2,1,0:T(8,128)(2,1)S(1)} all-to-all(bf16[16,32,128]{2,1,0:T(8,128)(2,1)S(1)} %plane.1), channel_id=1, replica_groups={{0,4,8,12,16,20,24,28,64,68,72,76,80,84,88,92},{32,36,40,44,48,52,56,60..., dimensions={0} | all-to-all | bytes 262144 | tf_op jit(solution)/shard_map/all_to_all | solution.py:553
  188.6 6.4 %all-to-all-start.3 = ((bf16[32,16,128]{2,1,0:T(8,128)(2,1)}), bf16[32,16,128]{2,1,0:T(8,128)(2,1)S(1)}, u32[]{:S(2)}, u32[]{:S(2)}) async-start(bf16[32,16,128]{2,1,0:T(8,128)(2,1)} %get-tuple-element.38), calls=%async_computation.3 | async-start | bytes 262144 | tf_op jit(solution)/shard_map/all_to_all | solution.py:553
  196.7 6.1 %all-to-all-done.3.got_ref = bf16[32,16,128]{2,1,0:T(8,128)(2,1)S(1)} async-done(((bf16[32,16,128]{2,1,0:T(8,128)(2,1)}), bf16[32,16,128]{2,1,0:T(8,128)(2,1)S(1)}, u32[]{:S(2)}, u32[]{:S(2)}) %all-to-all-start.3) | async-done | bytes 131104 | tf_op jit(solution)/shard_map/all_to_all | solution.py:553
  (98 shorter events, 35.5 us)
Async XLA Ops:
  1.7 44.8 %copy-start.9 = (f32[512]{0:T(512)S(1)}, f32[512]{0:T(512)}, u32[]{:S(2)}) copy-start(f32[512]{0:T(512)} %param.12) | copy-start | bytes 6148
  2.7 29.2 %collective-permute-start.6 = (bf16[16,3584]{1,0:T(8,128)(2,1)S(1)}, bf16[16,3584]{1,0:T(8,128)(2,1)S(1)}, u32[]{:S(2)}, u32[]{:S(2)}) collective-permute-start(bf16[16,3584]{1,0:T(8,128)(2,1)S(1)} %constant_dynamic-slice_fusion), channel_id=1, source_target_pairs={{0,92},{1,93},{2,94},{3,95},{4,88},{5,89},{6,90},{7,91},{8,84},{9,... | collective-permute-start | bytes 344072 | tf_op jit(solution)/shard_map/ppermute | solution.py:565
  14.7 50.9 %collective-permute-start = (bf16[64,3584]{1,0:T(8,128)(2,1)S(1)}, bf16[64,3584]{1,0:T(8,128)(2,1)S(1)}, u32[]{:S(2)}, u32[]{:S(2)}) collective-permute-start(bf16[64,3584]{1,0:T(8,128)(2,1)S(1)} %pad_maximum_fusion.2), channel_id=1, source_target_pairs={{0,384},{1,385},{2,386},{3,387},{4,388},{5,389},{6,390},{7,391},{8... | collective-permute-start | bytes 1376264 | tf_op jit(solution)/shard_map/ppermute | solution.py:565
  19.1 48.8 %collective-permute-start.1 = (bf16[64,3584]{1,0:T(8,128)(2,1)S(1)}, bf16[64,3584]{1,0:T(8,128)(2,1)S(1)}, u32[]{:S(2)}, u32[]{:S(2)}) collective-permute-start(bf16[64,3584]{1,0:T(8,128)(2,1)S(1)} %pad_maximum_fusion.2), channel_id=1, source_target_pairs={{0,128},{1,129},{2,130},{3,131},{4,132},{5,133},{6,134},{7,135},{8... | collective-permute-start | bytes 1376264 | tf_op jit(solution)/shard_map/ppermute | solution.py:565
  22.3 24.1 %all-to-all-start = ((f32[16,8,128]{2,1,0:T(8,128)}), f32[16,8,128]{2,1,0:T(8,128)S(1)}, u32[]{:S(2)}, u32[]{:S(2)}) async-start(f32[16,8,128]{2,1,0:T(8,128)} %stats.1), calls=%async_computation | async-start | bytes 131072 | tf_op jit(solution)/shard_map/all_to_all | solution.py:644
  32.0 6.6 %collective-permute-start.7 = (bf16[16,3584]{1,0:T(8,128)(2,1)S(1)}, bf16[16,3584]{1,0:T(8,128)(2,1)S(1)}, u32[]{:S(2)}, u32[]{:S(2)}) collective-permute-start(bf16[16,3584]{1,0:T(8,128)(2,1)S(1)} %collective-permute-done.6), channel_id=1, source_target_pairs={{0,1},{1,0},{2,3},{3,2},{4,5},{5,4},{6,7},{7,6},{8,9},{9,8},{10,11... | collective-permute-start | bytes 344072 | tf_op jit(solution)/shard_map/ppermute | solution.py:565
  38.6 24.1 %collective-permute-start.8 = (bf16[32,3584]{1,0:T(8,128)(2,1)S(1)}, bf16[32,3584]{1,0:T(8,128)(2,1)S(1)}, u32[]{:S(2)}, u32[]{:S(2)}) collective-permute-start(bf16[32,3584]{1,0:T(8,128)(2,1)S(1)} %pad_maximum_fusion.5), channel_id=1, source_target_pairs={{0,3},{1,2},{2,1},{3,0},{4,7},{5,6},{6,5},{7,4},{8,11},{9,10},{10,... | collective-permute-start | bytes 688136 | tf_op jit(solution)/shard_map/ppermute | solution.py:565
  48.3 34.5 %collective-permute-start.4 = (f32[8,768]{1,0:T(8,128)S(1)}, f32[8,768]{1,0:T(8,128)S(1)}, u32[]{:S(2)}, u32[]{:S(2)}) collective-permute-start(f32[8,768]{1,0:T(8,128)S(1)} %get-tuple-element.25), channel_id=1, source_target_pairs={{32,0},{64,32},{96,64},{128,96},{160,128},{192,160},{224,192},{256... | collective-permute-start | bytes 73736 | tf_op jit(solution)/shard_map/ppermute | solution.py:608
  50.7 32.0 %collective-permute-start.5 = (f32[8,768]{1,0:T(8,128)S(1)}, f32[8,768]{1,0:T(8,128)S(1)}, u32[]{:S(2)}, u32[]{:S(2)}) collective-permute-start(f32[8,768]{1,0:T(8,128)S(1)} %get-tuple-element.26), channel_id=1, source_target_pairs={{0,32},{32,64},{64,96},{96,128},{128,160},{160,192},{192,224},{224... | collective-permute-start | bytes 73736 | tf_op jit(solution)/shard_map/ppermute | solution.py:608
  62.8 21.9 %collective-permute-start.9 = (bf16[64,3584]{1,0:T(8,128)(2,1)S(1)}, bf16[64,3584]{1,0:T(8,128)(2,1)S(1)}, u32[]{:S(2)}, u32[]{:S(2)}) collective-permute-start(bf16[64,3584]{1,0:T(8,128)(2,1)S(1)} %pad_maximum_fusion.4), channel_id=1, source_target_pairs={{0,384},{1,385},{2,386},{3,387},{4,388},{5,389},{6,390},{7,391},{8... | collective-permute-start | bytes 1376264 | tf_op jit(solution)/shard_map/ppermute | solution.py:565
  65.7 14.0 %collective-permute-start.2 = (bf16[32,3584]{1,0:T(8,128)(2,1)S(1)}, bf16[32,3584]{1,0:T(8,128)(2,1)S(1)}, u32[]{:S(2)}, u32[]{:S(2)}) collective-permute-start(bf16[32,3584]{1,0:T(8,128)(2,1)S(1)} %slice.24), channel_id=1, source_target_pairs={{0,384},{1,385},{2,386},{3,387},{4,388},{5,389},{6,390},{7,391},{8... | collective-permute-start | bytes 688136 | tf_op jit(solution)/shard_map/ppermute | solution.py:565
  68.0 14.0 %collective-permute-start.3 = (bf16[32,3584]{1,0:T(8,128)(2,1)S(1)}, bf16[32,3584]{1,0:T(8,128)(2,1)S(1)}, u32[]{:S(2)}, u32[]{:S(2)}) collective-permute-start(bf16[32,3584]{1,0:T(8,128)(2,1)S(1)} %slice.25), channel_id=1, source_target_pairs={{0,128},{1,129},{2,130},{3,131},{4,132},{5,133},{6,134},{7,135},{8... | collective-permute-start | bytes 688136 | tf_op jit(solution)/shard_map/ppermute | solution.py:565
  79.6 15.4 %collective-permute-start.10 = (bf16[64,3584]{1,0:T(8,128)(2,1)S(1)}, bf16[64,3584]{1,0:T(8,128)(2,1)S(1)}, u32[]{:S(2)}, u32[]{:S(2)}) collective-permute-start(bf16[64,3584]{1,0:T(8,128)(2,1)S(1)} %pad_maximum_fusion.4), channel_id=1, source_target_pairs={{0,128},{1,129},{2,130},{3,131},{4,132},{5,133},{6,134},{7,135},{8... | collective-permute-start | bytes 1376264 | tf_op jit(solution)/shard_map/ppermute | solution.py:565
  82.8 33.0 %collective-permute-start.13 = (bf16[192,3584]{1,0:T(8,128)(2,1)S(1)}, bf16[192,3584]{1,0:T(8,128)(2,1)}, u32[]{:S(2)}, u32[]{:S(2)}) collective-permute-start(bf16[192,3584]{1,0:T(8,128)(2,1)S(1)} %pad_maximum_fusion.refs_9_), channel_id=1, source_target_pairs={{0,32},{1,33},{2,34},{3,35},{4,36},{5,37},{6,38},{7,39},{8,40},{9,... | collective-permute-start | bytes 4128776 | tf_op jit(solution)/shard_map/ppermute | solution.py:565
  84.7 16.7 %collective-permute-start.11 = (bf16[32,3584]{1,0:T(8,128)(2,1)S(1)}, bf16[32,3584]{1,0:T(8,128)(2,1)S(1)}, u32[]{:S(2)}, u32[]{:S(2)}) collective-permute-start(bf16[32,3584]{1,0:T(8,128)(2,1)S(1)} %slice.26), channel_id=1, source_target_pairs={{0,384},{1,385},{2,386},{3,387},{4,388},{5,389},{6,390},{7,391},{8... | collective-permute-start | bytes 688136 | tf_op jit(solution)/shard_map/ppermute | solution.py:565
  95.2 20.6 %collective-permute-start.15 = (bf16[192,3584]{1,0:T(8,128)(2,1)S(1)}, bf16[192,3584]{1,0:T(8,128)(2,1)}, u32[]{:S(2)}, u32[]{:S(2)}) collective-permute-start(bf16[192,3584]{1,0:T(8,128)(2,1)S(1)} %pad_maximum_fusion.1.refs_11_), channel_id=1, source_target_pairs={{0,32},{1,33},{2,34},{3,35},{4,36},{5,37},{6,38},{7,39},{8,40},{9,... | collective-permute-start | bytes 4128776 | tf_op jit(solution)/shard_map/ppermute | solution.py:565
  97.5 18.3 %collective-permute-start.14 = (bf16[64,3584]{1,0:T(8,128)(2,1)}, bf16[64,3584]{1,0:T(8,128)(2,1)}, u32[]{:S(2)}, u32[]{:S(2)}) collective-permute-start(bf16[64,3584]{1,0:T(8,128)(2,1)} %pad_maximum_fusion.3.refs_10_), channel_id=1, source_target_pairs={{0,32},{1,33},{2,34},{3,35},{4,36},{5,37},{6,38},{7,39},{8,40},{9,... | collective-permute-start | bytes 1376264 | tf_op jit(solution)/shard_map/ppermute | solution.py:565
  99.5 9.9 %collective-permute-start.12 = (bf16[32,3584]{1,0:T(8,128)(2,1)S(1)}, bf16[32,3584]{1,0:T(8,128)(2,1)S(1)}, u32[]{:S(2)}, u32[]{:S(2)}) collective-permute-start(bf16[32,3584]{1,0:T(8,128)(2,1)S(1)} %slice.27), channel_id=1, source_target_pairs={{0,128},{1,129},{2,130},{3,131},{4,132},{5,133},{6,134},{7,135},{8... | collective-permute-start | bytes 688136 | tf_op jit(solution)/shard_map/ppermute | solution.py:565
  110.1 5.6 %collective-permute-start.16 = (bf16[64,3584]{1,0:T(8,128)(2,1)}, bf16[64,3584]{1,0:T(8,128)(2,1)}, u32[]{:S(2)}, u32[]{:S(2)}) collective-permute-start(bf16[64,3584]{1,0:T(8,128)(2,1)} %constant_dynamic-update-slice_fusion.refs_12_), channel_id=1, source_target_pairs={{0,32},{1,33},{2,34},{3,35},{4,36},{5,37},{6,38},{7,39},{8,40},{9,... | collective-permute-start | bytes 1376264 | tf_op jit(solution)/shard_map/ppermute | solution.py:565
  132.2 62.8 %copy-start.5 = (f32[16,512]{1,0:T(8,128)S(1)}, f32[16,512]{1,0:T(8,128)}, u32[]{:S(2)}) copy-start(f32[16,512]{1,0:T(8,128)} %copy-done.3) | copy-start | bytes 98308
  132.2 62.8 %copy-start.8 = (f32[16,512]{1,0:T(8,128)S(1)}, f32[16,512]{1,0:T(8,128)}, u32[]{:S(2)}) copy-start(f32[16,512]{1,0:T(8,128)} %copy-done.6) | copy-start | bytes 98308
  132.2 4.5 %collective-permute-start.17 = (f32[8,768]{1,0:T(8,128)S(1)}, f32[8,768]{1,0:T(8,128)S(1)}, u32[]{:S(2)}, u32[]{:S(2)}) collective-permute-start(f32[8,768]{1,0:T(8,128)S(1)} %get-tuple-element.31.refs_0_), channel_id=1, source_target_pairs={{0,32},{32,64},{64,96},{96,128},{128,160},{160,192},{192,224},{224... | collective-permute-start | bytes 73736 | tf_op jit(solution)/shard_map/ppermute | solution.py:608
  134.3 13.9 %collective-permute-start.18 = (f32[8,768]{1,0:T(8,128)S(1)}, f32[8,768]{1,0:T(8,128)S(1)}, u32[]{:S(2)}, u32[]{:S(2)}) collective-permute-start(f32[8,768]{1,0:T(8,128)S(1)} %get-tuple-element.31.refs_0_), channel_id=1, source_target_pairs={{32,0},{64,32},{96,64},{128,96},{160,128},{192,160},{224,192},{256... | collective-permute-start | bytes 73736 | tf_op jit(solution)/shard_map/ppermute | solution.py:608
  188.6 14.1 %all-to-all-start.3 = ((bf16[32,16,128]{2,1,0:T(8,128)(2,1)}), bf16[32,16,128]{2,1,0:T(8,128)(2,1)S(1)}, u32[]{:S(2)}, u32[]{:S(2)}) async-start(bf16[32,16,128]{2,1,0:T(8,128)(2,1)} %get-tuple-element.38), calls=%async_computation.3 | async-start | bytes 262144 | tf_op jit(solution)/shard_map/all_to_all | solution.py:553
  (20 other events, 312.5 us)

commit v4 on v3

--- a/solution.py
+++ b/solution.py
@@ -25,7 +25,7 @@
 PART = 16
 
 
-def params(limit_mb=48):
+def params(limit_mb=12):
     return pltpu.CompilerParams(vmem_limit_bytes=limit_mb << 20)
 
 
@@ -185,7 +185,8 @@
     zhi, core, x = at_ref[0], at_ref[1], at_ref[4]
     depth = width // (XS * ZHI * CORES)
     slab = hidden // (XS * ZHI * CORES)
-    rows = ew_ref.shape[0]
+    taken = PATCH * PATCH
+    rows = taken * SUB
     copies = []
     own, own_other = (own_near, own_far), (own_near_other, own_far_other)
     cross, cross_other = (cross_near, cross_far), (cross_near_other, cross_far_other)
@@ -242,7 +243,11 @@
         lines.append(got[0:SUB] + got[SUB : 2 * SUB] + got[2 * SUB :])
     patches_t = jnp.concatenate(lines, axis=0)
     patches = patches_t.T
-    ew_top, ew_low = parts(ew_ref[...])
+    empty = jnp.zeros((SUB - LATENT, width), F32)
+    spread = []
+    for k in range(taken):
+        spread += [ew_ref[k * LATENT : (k + 1) * LATENT, :], empty]
+    ew_top, ew_low = parts(jnp.concatenate(spread, axis=0))
     p_top, p_low = parts(patches[:tokens])
     embedded = nn(p_top, ew_top) + nn(p_low, ew_top) + nn(p_top, ew_low)
     emb[...] = (embedded + eb_ref[...]).astype(BF16)
@@ -293,7 +298,7 @@
 
 
 def projector(at, lat, below, above, target, ew, eb, pib, pob, pieces, across):
-    rows, width = ew.shape
+    rows, width = PATCH * PATCH * SUB, ew.shape[1]
     hidden, align = pib.shape[1], pob.shape[1]
     tokens = target.shape[0]
     flops = 2 * tokens * (2 * width * hidden + 2 * hidden * align)
@@ -305,7 +310,7 @@
         ),
         in_specs=[pl.BlockSpec(memory_space=pltpu.SMEM)]
         + [vmem()] * 8
-        + [pl.BlockSpec(memory_space=pltpu.HBM)] * len(pieces),
+        + [pl.BlockSpec(memory_space=pl.ANY)] * len(pieces),
         out_specs=(vmem(), vmem()),
         scratch_shapes=[
             pltpu.VMEM((width, hidden), BF16),
@@ -316,7 +321,7 @@
             pltpu.VMEM((256, width), F32),
             pltpu.SemaphoreType.DMA((60,)),
         ],
-        compiler_params=params(),
+        compiler_params=params(32),
         cost_estimate=pl.CostEstimate(
             flops=flops, bytes_accessed=8 << 20, transcendentals=2 * tokens * hidden
         ),
@@ -636,13 +641,13 @@
     taps = conv_weight.reshape(LATENT, TAPS, channels).transpose(1, 0, 2)
     taps = jnp.pad(taps, ((0, 0), (0, SUB - LATENT), (0, 0))).reshape(TAPS * SUB, channels)
     taps_full = jnp.pad(taps, ((0, LANES - TAPS * SUB), (0, 0)))
-    spread = jnp.pad(
-        embed_weight.reshape(PATCH * PATCH, LATENT, width), ((0, 0), (0, SUB - LATENT), (0, 0))
-    ).reshape(PATCH * PATCH * SUB, width)
 
     sums = group_stats(flat, peers)
     stats = lax.all_to_all(sums, "rows", 0, 0, tiled=True)
+    far, sums_ = lax.optimization_barrier((far, sums))
     cross = along_y(far)
+    cross, own_near, own_far = lax.optimization_barrier((cross, own_near, own_far))
+    stats, own_far = lax.optimization_barrier((stats, own_far))
     cross_near, cross_far = along_x(cross)
     lat, up, down, mean, inv = conv_forward(stats, flat, gain, bias, taps, across, members)
     above, below = neighbours(up, down)
@@ -654,7 +659,7 @@
     at = at.astype(jnp.int32)
     target = targets.reshape(-1, align)
     embed_part, grad_lat = projector(
-        at, lat, below, above, target, spread, embed_bias.reshape(1, -1),
+        at, lat, below, above, target, embed_weight, embed_bias.reshape(1, -1),
         proj_in_bias.reshape(1, -1), proj_out_bias.reshape(1, -1), pieces, across,
     )
     after, before = neighbours(grad_lat, grad_lat)

time: 205 us -> 208 us (1.015)
  starting transfers between devices: 87.3 us -> 100 us
  waiting for transfers between devices: 45.4 us -> 33.4 us
  local copies, waits for them, and re-layouts: 10.3 us -> 13.8 us
  blocking collectives: 36.6 us -> 33.7 us
    ppermute x15, waiting for transfers between devices: 24.7 us -> 15.4 us  [moved(): return lax.ppermute(value, ('rows', 'batch'), pairs)]
    ppermute x15, starting transfers between devices: 52.4 us -> 60 us  [moved(): return lax.ppermute(value, ('rows', 'batch'), pairs)]
    ppermute x2, starting transfers between devices: 14 us -> 17.3 us  [neighbours(): lax.ppermute(down, 'rows', forward)]
    all_to_all x1, waiting for transfers between devices: 3.22 us -> 0.01 us  [shards(): stats = lax.all_to_all(sums, 'rows', 0, 0, tiled=True)]
    all_to_all x2, blocking collectives: 36.6 us -> 33.7 us  [exchanged(): lax.all_to_all(value, BOTH, 0, 0, axis_index_groups=groups, tiled=True)]
    unnamed x48 -> x36, local copies, waits for them, and re-layouts: 5.97 us -> 8.75 us
    reshape x2 -> x0, local copies, waits for them, and re-layouts: 2.34 us -> none  [the longest x1 1.49 us: shards(): embed_weight.reshape(PATCH * PATCH, LATENT, width)]
    ppermute x2, starting transfers between devices: 4.87 us -> 7.05 us  [neighbours(): lax.ppermute(up, 'rows', backward)]
  transfers between devices with their start and end apart: 21 -> 21, of which waited for: 7 -> 6; matrix products, arithmetic and copies ran while one was open for 3% -> 5% of each run, Pallas kernels for 2% -> 2%
where the time goes in v4:
time: 208 us; the launch traced here: 206 us
  starting transfers between devices  100 us (48%)
  blocking collectives  33.7 us (16%)
  waiting for transfers between devices  33.4 us (16%)
  Pallas kernels  20.6 us (10%)
  local copies, waits for them, and re-layouts  13.8 us (7%)
  other arithmetic  3.12 us (2%)
    ppermute x15, starting transfers between devices, moved(): return lax.ppermute(value, ('rows', 'batch'), pairs)  60 us
    all_to_all x2, blocking collectives, exchanged(): lax.all_to_all(value, BOTH, 0, 0, axis_index_groups=groups, tiled=True)  33.7 us
    ppermute x2, starting transfers between devices, neighbours(): lax.ppermute(down, 'rows', forward)  17.3 us
    ppermute x15, waiting for transfers between devices, moved(): return lax.ppermute(value, ('rows', 'batch'), pairs)  15.4 us
    pallas_call x1, Pallas kernels, projector(): pl.pallas_call(lambda *refs: mlp_kernel(across, width, hidden, align, *re...  11.9 us
    ppermute x2, waiting for transfers between devices, neighbours(): lax.ppermute(up, 'rows', backward)  11.9 us
    all_to_all x1, starting transfers between devices, shards(): stats = lax.all_to_all(sums, 'rows', 0, 0, tiled=True)  9.61 us
    unnamed x36, local copies, waits for them, and re-layouts  8.75 us
  transfers between devices with their start and end apart: 21, of which 6 were waited for; matrix products, arithmetic and copies ran while one was open for 5% of the time, Pallas kernels for 2%

profile of v4, /device:TPU:1, one launch (start us, length us, event | category | flops | bytes accessed | tf_op | source)
XLA Modules:
  0.0 206.2 jit_solution(13114370595113226463)
XLA Ops:
  2.8 12.0 %collective-permute-start = (bf16[16,3584]{1,0:T(8,128)(2,1)S(1)}, bf16[16,3584]{1,0:T(8,128)(2,1)S(1)}, u32[]{:S(2)}, u32[]{:S(2)}) collective-permute-start(bf16[16,3584]{1,0:T(8,128)(2,1)S(1)} %constant_dynamic-slice_fusion), channel_id=1, source_target_pairs={{0,92},{1,93},{2,94},{3,95},{4,88},{5,89},{6,90},{7,91},{8,84},{9,... | collective-permute-start | bytes 344072 | tf_op jit(solution)/shard_map/ppermute | solution.py:570
  14.7 4.4 %collective-permute-start.3 = (bf16[64,3584]{1,0:T(8,128)(2,1)S(1)}, bf16[64,3584]{1,0:T(8,128)(2,1)S(1)}, u32[]{:S(2)}, u32[]{:S(2)}) collective-permute-start(bf16[64,3584]{1,0:T(8,128)(2,1)S(1)} %pad_maximum_fusion.1), channel_id=1, source_target_pairs={{0,384},{1,385},{2,386},{3,387},{4,388},{5,389},{6,390},{7,391},{8... | collective-permute-start | bytes 1376264 | tf_op jit(solution)/shard_map/ppermute | solution.py:570
  22.4 9.6 %all-to-all-start = ((f32[16,8,128]{2,1,0:T(8,128)}), f32[16,8,128]{2,1,0:T(8,128)S(1)}, u32[]{:S(2)}, u32[]{:S(2)}) async-start(f32[16,8,128]{2,1,0:T(8,128)} %stats.1), calls=%async_computation | async-start | bytes 131072 | tf_op jit(solution)/shard_map/all_to_all | solution.py:646
  32.0 3.2 %collective-permute-start.1 = (bf16[16,3584]{1,0:T(8,128)(2,1)S(1)}, bf16[16,3584]{1,0:T(8,128)(2,1)S(1)}, u32[]{:S(2)}, u32[]{:S(2)}) collective-permute-start(bf16[16,3584]{1,0:T(8,128)(2,1)S(1)} %collective-permute-done), channel_id=1, source_target_pairs={{0,1},{1,0},{2,3},{3,2},{4,5},{5,4},{6,7},{7,6},{8,9},{9,8},{10,11... | collective-permute-start | bytes 344072 | tf_op jit(solution)/shard_map/ppermute | solution.py:570
  35.4 3.2 %collective-permute-done.1 = bf16[16,3584]{1,0:T(8,128)(2,1)S(1)} collective-permute-done((bf16[16,3584]{1,0:T(8,128)(2,1)S(1)}, bf16[16,3584]{1,0:T(8,128)(2,1)S(1)}, u32[]{:S(2)}, u32[]{:S(2)}) %collective-permute-start.1) | collective-permute-done | bytes 114720 | tf_op jit(solution)/shard_map/ppermute | solution.py:570
  38.7 4.6 %collective-permute-start.2 = (bf16[32,3584]{1,0:T(8,128)(2,1)S(1)}, bf16[32,3584]{1,0:T(8,128)(2,1)S(1)}, u32[]{:S(2)}, u32[]{:S(2)}) collective-permute-start(bf16[32,3584]{1,0:T(8,128)(2,1)S(1)} %pad_maximum_fusion.4), channel_id=1, source_target_pairs={{0,3},{1,2},{2,1},{3,0},{4,7},{5,6},{6,5},{7,4},{8,11},{9,10},{10,... | collective-permute-start | bytes 688136 | tf_op jit(solution)/shard_map/ppermute | solution.py:570
  43.4 4.2 %collective-permute-start.5 = (bf16[32,3584]{1,0:T(8,128)(2,1)S(1)}, bf16[32,3584]{1,0:T(8,128)(2,1)S(1)}, u32[]{:S(2)}, u32[]{:S(2)}) collective-permute-start(bf16[32,3584]{1,0:T(8,128)(2,1)S(1)} %slice.24), channel_id=1, source_target_pairs={{0,384},{1,385},{2,386},{3,387},{4,388},{5,389},{6,390},{7,391},{8... | collective-permute-start | bytes 688136 | tf_op jit(solution)/shard_map/ppermute | solution.py:570
  52.3 4.4 %collective-permute-done.6 = bf16[32,3584]{1,0:T(8,128)(2,1)S(1)} collective-permute-done((bf16[32,3584]{1,0:T(8,128)(2,1)S(1)}, bf16[32,3584]{1,0:T(8,128)(2,1)S(1)}, u32[]{:S(2)}, u32[]{:S(2)}) %collective-permute-start.6) | collective-permute-done | bytes 229408 | tf_op jit(solution)/shard_map/ppermute | solution.py:570
  58.7 3.4 %collective-permute-start.10 = (bf16[64,3584]{1,0:T(8,128)(2,1)}, bf16[64,3584]{1,0:T(8,128)(2,1)}, u32[]{:S(2)}, u32[]{:S(2)}) collective-permute-start(bf16[64,3584]{1,0:T(8,128)(2,1)} %pad_maximum_fusion.2), channel_id=1, source_target_pairs={{0,128},{1,129},{2,130},{3,131},{4,132},{5,133},{6,134},{7,135},{8... | collective-permute-start | bytes 1376264 | tf_op jit(solution)/shard_map/ppermute | solution.py:570
  63.9 5.1 %collective-permute-start.7 = (f32[8,768]{1,0:T(8,128)S(1)}, f32[8,768]{1,0:T(8,128)S(1)}, u32[]{:S(2)}, u32[]{:S(2)}) collective-permute-start(f32[8,768]{1,0:T(8,128)S(1)} %get-tuple-element.36), channel_id=1, source_target_pairs={{32,0},{64,32},{96,64},{128,96},{160,128},{192,160},{224,192},{256... | collective-permute-start | bytes 73736 | tf_op jit(solution)/shard_map/ppermute | solution.py:613
  69.0 11.7 %collective-permute-start.8 = (f32[8,768]{1,0:T(8,128)S(1)}, f32[8,768]{1,0:T(8,128)S(1)}, u32[]{:S(2)}, u32[]{:S(2)}) collective-permute-start(f32[8,768]{1,0:T(8,128)S(1)} %get-tuple-element.37), channel_id=1, source_target_pairs={{0,32},{32,64},{64,96},{96,128},{128,160},{160,192},{192,224},{224... | collective-permute-start | bytes 73736 | tf_op jit(solution)/shard_map/ppermute | solution.py:613
  85.4 9.6 %collective-permute-start.11 = (bf16[32,3584]{1,0:T(8,128)(2,1)S(1)}, bf16[32,3584]{1,0:T(8,128)(2,1)S(1)}, u32[]{:S(2)}, u32[]{:S(2)}) collective-permute-start(bf16[32,3584]{1,0:T(8,128)(2,1)S(1)} %slice.26), channel_id=1, source_target_pairs={{0,384},{1,385},{2,386},{3,387},{4,388},{5,389},{6,390},{7,391},{8... | collective-permute-start | bytes 688136 | tf_op jit(solution)/shard_map/ppermute | solution.py:570
  98.7 2.2 %collective-permute-start.15 = (bf16[192,3584]{1,0:T(8,128)(2,1)}, bf16[192,3584]{1,0:T(8,128)(2,1)}, u32[]{:S(2)}, u32[]{:S(2)}) collective-permute-start(bf16[192,3584]{1,0:T(8,128)(2,1)} %constant_dynamic-update-slice_fusion.refs_11_), channel_id=1, source_target_pairs={{0,32},{1,33},{2,34},{3,35},{4,36},{5,37},{6,38},{7,39},{8,40},{9,... | collective-permute-start | bytes 4128776 | tf_op jit(solution)/shard_map/ppermute | solution.py:570
  100.9 2.1 %collective-permute-start.14 = (bf16[64,3584]{1,0:T(8,128)(2,1)S(1)}, bf16[64,3584]{1,0:T(8,128)(2,1)}, u32[]{:S(2)}, u32[]{:S(2)}) collective-permute-start(bf16[64,3584]{1,0:T(8,128)(2,1)S(1)} %pad_maximum_fusion.3.refs_10_), channel_id=1, source_target_pairs={{0,32},{1,33},{2,34},{3,35},{4,36},{5,37},{6,38},{7,39},{8,40},{9,... | collective-permute-start | bytes 1376264 | tf_op jit(solution)/shard_map/ppermute | solution.py:570
  104.0 3.7 %collective-permute-start.12 = (bf16[32,3584]{1,0:T(8,128)(2,1)S(1)}, bf16[32,3584]{1,0:T(8,128)(2,1)S(1)}, u32[]{:S(2)}, u32[]{:S(2)}) collective-permute-start(bf16[32,3584]{1,0:T(8,128)(2,1)S(1)} %slice.27), channel_id=1, source_target_pairs={{0,128},{1,129},{2,130},{3,131},{4,132},{5,133},{6,134},{7,135},{8... | collective-permute-start | bytes 688136 | tf_op jit(solution)/shard_map/ppermute | solution.py:570
  107.8 6.3 %collective-permute-done.12 = bf16[32,3584]{1,0:T(8,128)(2,1)S(1)} collective-permute-done((bf16[32,3584]{1,0:T(8,128)(2,1)S(1)}, bf16[32,3584]{1,0:T(8,128)(2,1)S(1)}, u32[]{:S(2)}, u32[]{:S(2)}) %collective-permute-start.12) | collective-permute-done | bytes 229408 | tf_op jit(solution)/shard_map/ppermute | solution.py:570
  114.1 3.0 %collective-permute-start.16 = (bf16[64,3584]{1,0:T(8,128)(2,1)S(1)}, bf16[64,3584]{1,0:T(8,128)(2,1)}, u32[]{:S(2)}, u32[]{:S(2)}) collective-permute-start(bf16[64,3584]{1,0:T(8,128)(2,1)S(1)} %constant_dynamic-update-slice_fusion.3.refs_12_), channel_id=1, source_target_pairs={{0,32},{1,33},{2,34},{3,35},{4,36},{5,37},{6,38},{7,39},{8,40},{9,... | collective-permute-start | bytes 1376264 | tf_op jit(solution)/shard_map/ppermute | solution.py:570
  122.4 11.9 %projector.1 = (f32[32,1024]{1,0:T(8,128)S(1)}, f32[8,768]{1,0:T(8,128)S(1)}) custom-call(s32[5]{0:T(128)S(1)} %stack.23.refs_0_.at_ref, f32[8,768]{1,0:T(8,128)S(1)} %copy-done.10, f32[8,768]{1,0:T(8,128)S(1)} %copy-done.6, f32[8,768]{1,0:T(8,128)S(1)} %collective-permute-done.7.refs_3_, bf16[192,768]{1,0:T(8,128)(2,1)S(1)} %bitcast.26, ...), custom_call_target="tpu_custom_call" | custom-call | flops 2818572288 | bytes 8388608 | tf_op jit(solution)/shard_map/projector/pallas_call | solution.py:305
  134.3 5.6 %collective-permute-start.17 = (f32[8,768]{1,0:T(8,128)S(1)}, f32[8,768]{1,0:T(8,128)S(1)}, u32[]{:S(2)}, u32[]{:S(2)}) collective-permute-start(f32[8,768]{1,0:T(8,128)S(1)} %get-tuple-element.43.refs_0_), channel_id=1, source_target_pairs={{0,32},{32,64},{64,96},{96,128},{128,160},{160,192},{192,224},{224... | collective-permute-start | bytes 73736 | tf_op jit(solution)/shard_map/ppermute | solution.py:613
  141.9 11.9 %collective-permute-done.18.refs_2_ = f32[8,768]{1,0:T(8,128)S(1)} collective-permute-done((f32[8,768]{1,0:T(8,128)S(1)}, f32[8,768]{1,0:T(8,128)S(1)}, u32[]{:S(2)}, u32[]{:S(2)}) %collective-permute-start.18) | collective-permute-done | bytes 24608 | tf_op jit(solution)/shard_map/ppermute | solution.py:613
  155.8 11.0 %all_to_all.20.got_ref = bf16[32,32,128]{2,1,0:T(8,128)(2,1)S(1)} all-to-all(bf16[32,32,128]{2,1,0:T(8,128)(2,1)S(1)} %get-tuple-element.47), channel_id=1, replica_groups={{0,32,1,33,2,34,3,35,128,160,129,161,130,162,131,163,256,288,257,289,25..., dimensions={0} | all-to-all | bytes 524288 | tf_op jit(solution)/shard_map/all_to_all | solution.py:558
  167.4 22.7 %all_to_all.21.got_ref = bf16[16,32,128]{2,1,0:T(8,128)(2,1)S(1)} all-to-all(bf16[16,32,128]{2,1,0:T(8,128)(2,1)S(1)} %plane.1), channel_id=1, replica_groups={{0,4,8,12,16,20,24,28,64,68,72,76,80,84,88,92},{32,36,40,44,48,52,56,60..., dimensions={0} | all-to-all | bytes 262144 | tf_op jit(solution)/shard_map/all_to_all | solution.py:558
  191.3 6.4 %all-to-all-start.3 = ((bf16[32,16,128]{2,1,0:T(8,128)(2,1)}), bf16[32,16,128]{2,1,0:T(8,128)(2,1)S(1)}, u32[]{:S(2)}, u32[]{:S(2)}) async-start(bf16[32,16,128]{2,1,0:T(8,128)(2,1)} %get-tuple-element.50), calls=%async_computation.3 | async-start | bytes 262144 | tf_op jit(solution)/shard_map/all_to_all | solution.py:558
  199.3 6.1 %all-to-all-done.3.got_ref = bf16[32,16,128]{2,1,0:T(8,128)(2,1)S(1)} async-done(((bf16[32,16,128]{2,1,0:T(8,128)(2,1)}), bf16[32,16,128]{2,1,0:T(8,128)(2,1)S(1)}, u32[]{:S(2)}, u32[]{:S(2)}) %all-to-all-start.3) | async-done | bytes 131104 | tf_op jit(solution)/shard_map/all_to_all | solution.py:558
  (84 shorter events, 36.5 us)
Async XLA Ops:
  0.6 34.6 %copy-start.14 = (bf16[4,4608]{1,0:T(4,128)(2,1)S(1)}, bf16[4,4608]{1,0:T(4,128)(2,1)}, u32[]{:S(2)}) copy-start(bf16[4,4608]{1,0:T(4,128)(2,1)} %param.14) | copy-start | bytes 110596
  2.8 29.2 %collective-permute-start = (bf16[16,3584]{1,0:T(8,128)(2,1)S(1)}, bf16[16,3584]{1,0:T(8,128)(2,1)S(1)}, u32[]{:S(2)}, u32[]{:S(2)}) collective-permute-start(bf16[16,3584]{1,0:T(8,128)(2,1)S(1)} %constant_dynamic-slice_fusion), channel_id=1, source_target_pairs={{0,92},{1,93},{2,94},{3,95},{4,88},{5,89},{6,90},{7,91},{8,84},{9,... | collective-permute-start | bytes 344072 | tf_op jit(solution)/shard_map/ppermute | solution.py:570
  14.7 28.6 %collective-permute-start.3 = (bf16[64,3584]{1,0:T(8,128)(2,1)S(1)}, bf16[64,3584]{1,0:T(8,128)(2,1)S(1)}, u32[]{:S(2)}, u32[]{:S(2)}) collective-permute-start(bf16[64,3584]{1,0:T(8,128)(2,1)S(1)} %pad_maximum_fusion.1), channel_id=1, source_target_pairs={{0,384},{1,385},{2,386},{3,387},{4,388},{5,389},{6,390},{7,391},{8... | collective-permute-start | bytes 1376264 | tf_op jit(solution)/shard_map/ppermute | solution.py:570
  19.1 28.4 %collective-permute-start.4 = (bf16[64,3584]{1,0:T(8,128)(2,1)S(1)}, bf16[64,3584]{1,0:T(8,128)(2,1)S(1)}, u32[]{:S(2)}, u32[]{:S(2)}) collective-permute-start(bf16[64,3584]{1,0:T(8,128)(2,1)S(1)} %pad_maximum_fusion.1), channel_id=1, source_target_pairs={{0,128},{1,129},{2,130},{3,131},{4,132},{5,133},{6,134},{7,135},{8... | collective-permute-start | bytes 1376264 | tf_op jit(solution)/shard_map/ppermute | solution.py:570
  21.1 29.2 %copy-start.11 = (bf16[64,2048]{1,0:T(8,128)(2,1)S(1)}, bf16[64,2048]{1,0:T(8,128)(2,1)}, u32[]{:S(2)}) copy-start(bf16[64,2048]{1,0:T(8,128)(2,1)} %param.17) | copy-start | bytes 786436
  22.4 39.7 %all-to-all-start = ((f32[16,8,128]{2,1,0:T(8,128)}), f32[16,8,128]{2,1,0:T(8,128)S(1)}, u32[]{:S(2)}, u32[]{:S(2)}) async-start(f32[16,8,128]{2,1,0:T(8,128)} %stats.1), calls=%async_computation | async-start | bytes 131072 | tf_op jit(solution)/shard_map/all_to_all | solution.py:646
  32.0 6.6 %collective-permute-start.1 = (bf16[16,3584]{1,0:T(8,128)(2,1)S(1)}, bf16[16,3584]{1,0:T(8,128)(2,1)S(1)}, u32[]{:S(2)}, u32[]{:S(2)}) collective-permute-start(bf16[16,3584]{1,0:T(8,128)(2,1)S(1)} %collective-permute-done), channel_id=1, source_target_pairs={{0,1},{1,0},{2,3},{3,2},{4,5},{5,4},{6,7},{7,6},{8,9},{9,8},{10,11... | collective-permute-start | bytes 344072 | tf_op jit(solution)/shard_map/ppermute | solution.py:570
  38.7 12.7 %collective-permute-start.2 = (bf16[32,3584]{1,0:T(8,128)(2,1)S(1)}, bf16[32,3584]{1,0:T(8,128)(2,1)S(1)}, u32[]{:S(2)}, u32[]{:S(2)}) collective-permute-start(bf16[32,3584]{1,0:T(8,128)(2,1)S(1)} %pad_maximum_fusion.4), channel_id=1, source_target_pairs={{0,3},{1,2},{2,1},{3,0},{4,7},{5,6},{6,5},{7,4},{8,11},{9,10},{10,... | collective-permute-start | bytes 688136 | tf_op jit(solution)/shard_map/ppermute | solution.py:570
  43.4 8.9 %collective-permute-start.5 = (bf16[32,3584]{1,0:T(8,128)(2,1)S(1)}, bf16[32,3584]{1,0:T(8,128)(2,1)S(1)}, u32[]{:S(2)}, u32[]{:S(2)}) collective-permute-start(bf16[32,3584]{1,0:T(8,128)(2,1)S(1)} %slice.24), channel_id=1, source_target_pairs={{0,384},{1,385},{2,386},{3,387},{4,388},{5,389},{6,390},{7,391},{8... | collective-permute-start | bytes 688136 | tf_op jit(solution)/shard_map/ppermute | solution.py:570
  48.3 8.4 %collective-permute-start.6 = (bf16[32,3584]{1,0:T(8,128)(2,1)S(1)}, bf16[32,3584]{1,0:T(8,128)(2,1)S(1)}, u32[]{:S(2)}, u32[]{:S(2)}) collective-permute-start(bf16[32,3584]{1,0:T(8,128)(2,1)S(1)} %slice.25), channel_id=1, source_target_pairs={{0,128},{1,129},{2,130},{3,131},{4,132},{5,133},{6,134},{7,135},{8... | collective-permute-start | bytes 688136 | tf_op jit(solution)/shard_map/ppermute | solution.py:570
  56.8 27.7 %collective-permute-start.9 = (bf16[64,3584]{1,0:T(8,128)(2,1)}, bf16[64,3584]{1,0:T(8,128)(2,1)}, u32[]{:S(2)}, u32[]{:S(2)}) collective-permute-start(bf16[64,3584]{1,0:T(8,128)(2,1)} %pad_maximum_fusion.2), channel_id=1, source_target_pairs={{0,384},{1,385},{2,386},{3,387},{4,388},{5,389},{6,390},{7,391},{8... | collective-permute-start | bytes 1376264 | tf_op jit(solution)/shard_map/ppermute | solution.py:570
  58.7 38.2 %collective-permute-start.10 = (bf16[64,3584]{1,0:T(8,128)(2,1)}, bf16[64,3584]{1,0:T(8,128)(2,1)}, u32[]{:S(2)}, u32[]{:S(2)}) collective-permute-start(bf16[64,3584]{1,0:T(8,128)(2,1)} %pad_maximum_fusion.2), channel_id=1, source_target_pairs={{0,128},{1,129},{2,130},{3,131},{4,132},{5,133},{6,134},{7,135},{8... | collective-permute-start | bytes 1376264 | tf_op jit(solution)/shard_map/ppermute | solution.py:570
  63.9 18.7 %collective-permute-start.7 = (f32[8,768]{1,0:T(8,128)S(1)}, f32[8,768]{1,0:T(8,128)S(1)}, u32[]{:S(2)}, u32[]{:S(2)}) collective-permute-start(f32[8,768]{1,0:T(8,128)S(1)} %get-tuple-element.36), channel_id=1, source_target_pairs={{32,0},{64,32},{96,64},{128,96},{160,128},{192,160},{224,192},{256... | collective-permute-start | bytes 73736 | tf_op jit(solution)/shard_map/ppermute | solution.py:613
  69.0 13.5 %collective-permute-start.8 = (f32[8,768]{1,0:T(8,128)S(1)}, f32[8,768]{1,0:T(8,128)S(1)}, u32[]{:S(2)}, u32[]{:S(2)}) collective-permute-start(f32[8,768]{1,0:T(8,128)S(1)} %get-tuple-element.37), channel_id=1, source_target_pairs={{0,32},{32,64},{64,96},{96,128},{128,160},{160,192},{192,224},{224... | collective-permute-start | bytes 73736 | tf_op jit(solution)/shard_map/ppermute | solution.py:613
  82.5 36.1 %collective-permute-start.13 = (bf16[192,3584]{1,0:T(8,128)(2,1)S(1)}, bf16[192,3584]{1,0:T(8,128)(2,1)}, u32[]{:S(2)}, u32[]{:S(2)}) collective-permute-start(bf16[192,3584]{1,0:T(8,128)(2,1)S(1)} %pad_maximum_fusion.refs_9_), channel_id=1, source_target_pairs={{0,32},{1,33},{2,34},{3,35},{4,36},{5,37},{6,38},{7,39},{8,40},{9,... | collective-permute-start | bytes 4128776 | tf_op jit(solution)/shard_map/ppermute | solution.py:570
  85.4 22.3 %collective-permute-start.11 = (bf16[32,3584]{1,0:T(8,128)(2,1)S(1)}, bf16[32,3584]{1,0:T(8,128)(2,1)S(1)}, u32[]{:S(2)}, u32[]{:S(2)}) collective-permute-start(bf16[32,3584]{1,0:T(8,128)(2,1)S(1)} %slice.26), channel_id=1, source_target_pairs={{0,384},{1,385},{2,386},{3,387},{4,388},{5,389},{6,390},{7,391},{8... | collective-permute-start | bytes 688136 | tf_op jit(solution)/shard_map/ppermute | solution.py:570
  96.9 21.8 %copy-start.3 = (bf16[12,1,16,768]{3,2,1,0:T(8,128)(2,1)S(1)}, bf16[12,1,16,768]{3,2,1,0:T(8,128)(2,1)}, u32[]{:S(2)}) copy-start(bf16[12,1,16,768]{3,2,1,0:T(8,128)(2,1)} %param.21) | copy-start | bytes 884740
  98.7 19.9 %collective-permute-start.15 = (bf16[192,3584]{1,0:T(8,128)(2,1)}, bf16[192,3584]{1,0:T(8,128)(2,1)}, u32[]{:S(2)}, u32[]{:S(2)}) collective-permute-start(bf16[192,3584]{1,0:T(8,128)(2,1)} %constant_dynamic-update-slice_fusion.refs_11_), channel_id=1, source_target_pairs={{0,32},{1,33},{2,34},{3,35},{4,36},{5,37},{6,38},{7,39},{8,40},{9,... | collective-permute-start | bytes 4128776 | tf_op jit(solution)/shard_map/ppermute | solution.py:570
  100.9 16.3 %collective-permute-start.14 = (bf16[64,3584]{1,0:T(8,128)(2,1)S(1)}, bf16[64,3584]{1,0:T(8,128)(2,1)}, u32[]{:S(2)}, u32[]{:S(2)}) collective-permute-start(bf16[64,3584]{1,0:T(8,128)(2,1)S(1)} %pad_maximum_fusion.3.refs_10_), channel_id=1, source_target_pairs={{0,32},{1,33},{2,34},{3,35},{4,36},{5,37},{6,38},{7,39},{8,40},{9,... | collective-permute-start | bytes 1376264 | tf_op jit(solution)/shard_map/ppermute | solution.py:570
  104.0 10.0 %collective-permute-start.12 = (bf16[32,3584]{1,0:T(8,128)(2,1)S(1)}, bf16[32,3584]{1,0:T(8,128)(2,1)S(1)}, u32[]{:S(2)}, u32[]{:S(2)}) collective-permute-start(bf16[32,3584]{1,0:T(8,128)(2,1)S(1)} %slice.27), channel_id=1, source_target_pairs={{0,128},{1,129},{2,130},{3,131},{4,132},{5,133},{6,134},{7,135},{8... | collective-permute-start | bytes 688136 | tf_op jit(solution)/shard_map/ppermute | solution.py:570
  114.1 4.6 %collective-permute-start.16 = (bf16[64,3584]{1,0:T(8,128)(2,1)S(1)}, bf16[64,3584]{1,0:T(8,128)(2,1)}, u32[]{:S(2)}, u32[]{:S(2)}) collective-permute-start(bf16[64,3584]{1,0:T(8,128)(2,1)S(1)} %constant_dynamic-update-slice_fusion.3.refs_12_), channel_id=1, source_target_pairs={{0,32},{1,33},{2,34},{3,35},{4,36},{5,37},{6,38},{7,39},{8,40},{9,... | collective-permute-start | bytes 1376264 | tf_op jit(solution)/shard_map/ppermute | solution.py:570
  134.3 7.6 %collective-permute-start.17 = (f32[8,768]{1,0:T(8,128)S(1)}, f32[8,768]{1,0:T(8,128)S(1)}, u32[]{:S(2)}, u32[]{:S(2)}) collective-permute-start(f32[8,768]{1,0:T(8,128)S(1)} %get-tuple-element.43.refs_0_), channel_id=1, source_target_pairs={{0,32},{32,64},{64,96},{96,128},{128,160},{160,192},{192,224},{224... | collective-permute-start | bytes 73736 | tf_op jit(solution)/shard_map/ppermute | solution.py:613
  139.9 13.9 %collective-permute-start.18 = (f32[8,768]{1,0:T(8,128)S(1)}, f32[8,768]{1,0:T(8,128)S(1)}, u32[]{:S(2)}, u32[]{:S(2)}) collective-permute-start(f32[8,768]{1,0:T(8,128)S(1)} %get-tuple-element.43.refs_0_), channel_id=1, source_target_pairs={{32,0},{64,32},{96,64},{128,96},{160,128},{192,160},{224,192},{256... | collective-permute-start | bytes 73736 | tf_op jit(solution)/shard_map/ppermute | solution.py:613
  191.3 14.1 %all-to-all-start.3 = ((bf16[32,16,128]{2,1,0:T(8,128)(2,1)}), bf16[32,16,128]{2,1,0:T(8,128)(2,1)S(1)}, u32[]{:S(2)}, u32[]{:S(2)}) async-start(bf16[32,16,128]{2,1,0:T(8,128)(2,1)} %get-tuple-element.50), calls=%async_computation.3 | async-start | bytes 262144 | tf_op jit(solution)/shard_map/all_to_all | solution.py:558
  (13 other events, 92.8 us)

commit v5 on v2

--- a/solution.py
+++ b/solution.py
@@ -21,9 +21,11 @@
 LANES = 128
 STAT_ROWS = 16
 CHUNKS, CHUNK_ROWS, ALL_ROWS = 32, 16, 32
-
-
-def params(limit_mb=48):
+CONV_COST = 20_000_000_000
+PART = 16
+
+
+def params(limit_mb=12):
     return pltpu.CompilerParams(vmem_limit_bytes=limit_mb << 20)
 
 
@@ -68,6 +70,11 @@
 
 def unpack_stats(packed):
     return jnp.concatenate([packed, pltpu.roll(packed, LANES // 2, 1)], axis=0)
+
+
+def parts(v):
+    top = v.astype(BF16)
+    return top, (v - top.astype(F32)).astype(BF16)
 
 
 def halves(packed):
@@ -161,6 +168,9 @@
         out_specs=(vmem(),) * 5,
         scratch_shapes=[pltpu.VMEM((images * cells, channels), BF16)],
         compiler_params=params(),
+        cost_estimate=pl.CostEstimate(
+            flops=CONV_COST, bytes_accessed=features.size * 2, transcendentals=features.size
+        ),
         name="conv",
     )(stats, features, gain, bias, kernel_rows)
 
@@ -174,6 +184,8 @@
     zhi, core = at_ref[0], at_ref[1]
     depth = width // (XS * ZHI * CORES)
     slab = hidden // (XS * ZHI * CORES)
+    taken = PATCH * PATCH
+    rows = taken * SUB
     copies = []
 
     for piece, of_zhi, of_core in (
@@ -222,7 +234,14 @@
         lines.append(got[0:SUB] + got[SUB : 2 * SUB] + got[2 * SUB :])
     patches_t = jnp.concatenate(lines, axis=0)
     patches = patches_t.T
-    emb[...] = (nn(patches, ew_ref[...], HIGH) + eb_ref[...])[:tokens].astype(BF16)
+    empty = jnp.zeros((SUB - LATENT, width), F32)
+    spread = []
+    for k in range(taken):
+        spread += [ew_ref[k * LATENT : (k + 1) * LATENT, :], empty]
+    ew_top, ew_low = parts(jnp.concatenate(spread, axis=0))
+    p_top, p_low = parts(patches[:tokens])
+    embedded = nn(p_top, ew_top) + nn(p_low, ew_top) + nn(p_top, ew_low)
+    emb[...] = (embedded + eb_ref[...]).astype(BF16)
 
     for copy in copies:
         copy.wait()
@@ -256,8 +275,12 @@
         grad_emb[0:tokens, :] += nt(grad_hidden, w_in[:, at])
 
     grad = grad_emb[...]
-    embed_ref[...] = nn(patches_t, grad, HIGH)
-    grad_patch = nt(ew_ref[...], grad, HIGH)
+    g_top, g_low = parts(grad)
+    t_top, t_low = parts(patches_t)
+    both = nn(jnp.concatenate([t_top, t_low], axis=0), g_top)
+    embed_ref[...] = both[:rows] + both[rows:] + nn(t_top, g_low)
+    both = nt(jnp.concatenate([ew_top, ew_low], axis=0), g_top)
+    grad_patch = both[:rows] + both[rows:] + nt(ew_top, g_low)
     total = jnp.zeros((SUB, cells), F32)
     for position, pick in enumerate(picks):
         part = grad_patch[position * SUB : (position + 1) * SUB].astype(BF16)
@@ -266,7 +289,7 @@
 
 
 def projector(at, lat, below, above, target, ew, eb, pib, pob, pieces, across):
-    rows, width = ew.shape
+    rows, width = PATCH * PATCH * SUB, ew.shape[1]
     hidden, align = pib.shape[1], pob.shape[1]
     tokens = target.shape[0]
     flops = 2 * tokens * (2 * width * hidden + 2 * hidden * align)
@@ -278,7 +301,7 @@
         ),
         in_specs=[pl.BlockSpec(memory_space=pltpu.SMEM)]
         + [vmem()] * 8
-        + [pl.BlockSpec(memory_space=pl.ANY)] * len(pieces),
+        + [pl.BlockSpec(memory_space=pltpu.HBM)] * len(pieces),
         out_specs=(vmem(), vmem()),
         scratch_shapes=[
             pltpu.VMEM((width, hidden), BF16),
@@ -289,7 +312,7 @@
             pltpu.VMEM((256, width), F32),
             pltpu.SemaphoreType.DMA((48,)),
         ],
-        compiler_params=params(),
+        compiler_params=params(32),
         cost_estimate=pl.CostEstimate(
             flops=flops, bytes_accessed=8 << 20, transcendentals=2 * tokens * hidden
         ),
@@ -514,11 +537,19 @@
     for h in range(ZHI)
     for d in range(ZLO)
 ]
-SHEET = [
-    [device(x, h, c, d, y) for x in range(XS) for y in range(YS)]
+ALONG_X = [
+    [device(x, h, c, d, y) for x in range(XS)]
     for h in range(ZHI)
+    for c in range(CORES)
     for d in range(ZLO)
+    for y in range(YS)
+]
+ALONG_Y = [
+    [device(x, h, c, d, y) for y in range(YS)]
+    for x in range(XS)
+    for h in range(ZHI)
     for c in range(CORES)
+    for d in range(ZLO)
 ]
 COLUMN = [
     [device(x, h, c, d, y) for h in range(ZHI) for d in range(ZLO)]
@@ -546,13 +577,12 @@
 
 def crossed(shard):
     y = lax.axis_index("batch") % YS
-    part = shard.shape[0] // YS
-    mine = lax.dynamic_slice_in_dim(shard, y * part, part, axis=0)
-    return mine, moved(mine, lambda x, h, c, d, y: (x, 1 - h, c, ZLO - 1 - d, y))
-
-
-def sheet(part):
-    return lax.all_gather(part, BOTH, axis_index_groups=SHEET, tiled=True)
+    mine = lax.dynamic_slice_in_dim(shard, y * PART, PART, axis=0)
+    return moved(mine, lambda x, h, c, d, y: (x, 1 - h, c, ZLO - 1 - d, y))
+
+
+def gathered(part, groups):
+    return lax.all_gather(part, BOTH, axis_index_groups=groups, tiled=True)
 
 
 def swapped(value):
@@ -589,29 +619,26 @@
     shard = jnp.concatenate(
         [proj_in] + [proj_out[at : at + depth] for at in range(0, proj_out.shape[0], depth)], axis=1
     )
-    mine, far = crossed(shard)
-    own = sheet(mine)
+    far = crossed(shard)
+    own = gathered(shard, ALONG_X)
     taps = conv_weight.reshape(LATENT, TAPS, channels).transpose(1, 0, 2)
     taps = jnp.pad(taps, ((0, 0), (0, SUB - LATENT), (0, 0))).reshape(TAPS * SUB, channels)
     taps_full = jnp.pad(taps, ((0, LANES - TAPS * SUB), (0, 0)))
-    spread = jnp.pad(
-        embed_weight.reshape(PATCH * PATCH, LATENT, width), ((0, 0), (0, SUB - LATENT), (0, 0))
-    ).reshape(PATCH * PATCH * SUB, width)
 
     sums = group_stats(flat, peers)
-    far, _ = lax.optimization_barrier((far, sums))
-    cross = sheet(far)
     stats = lax.all_to_all(sums, "rows", 0, 0, tiled=True)
+    far, sums_ = lax.optimization_barrier((far, sums))
+    cross = gathered(gathered(far, ALONG_Y), ALONG_X)
     lat, up, down, mean, inv = conv_forward(stats, flat, gain, bias, taps, across, members)
     above, below = neighbours(up, down)
-    own, cross, lat = lax.optimization_barrier((own, cross, lat))
+    own, above, below = lax.optimization_barrier((own, above, below))
     pieces = [own, cross, swapped(own), swapped(cross)]
     rows, batch = lax.axis_index("rows"), lax.axis_index("batch")
     at = jnp.stack([(rows // CORES) % ZHI, rows % CORES, batch % YS, batch // YS])
     at = at.astype(jnp.int32)
     target = targets.reshape(-1, align)
     embed_part, grad_lat = projector(
-        at, lat, below, above, target, spread, embed_bias.reshape(1, -1),
+        at, lat, below, above, target, embed_weight, embed_bias.reshape(1, -1),
         proj_in_bias.reshape(1, -1), proj_out_bias.reshape(1, -1), pieces, across,
     )
     after, before = neighbours(grad_lat, grad_lat)

time: 259 us -> 197 us (0.76)
  waiting for transfers between devices: 128 us -> 46.8 us
  blocking collectives: 30.2 us -> 42.8 us
  starting transfers between devices: 55.1 us -> 65.5 us
    all_gather x2, waiting for transfers between devices: 76.8 us -> 0.02 us  [gathered(): return lax.all_gather(part, BOTH, axis_index_groups=groups, tiled=True)]
    all_gather x0 -> x1, blocking collectives: none -> 12.3 us  [gathered(): return lax.all_gather(part, BOTH, axis_index_groups=groups, tiled=True)]
    ppermute x2, waiting for transfers between devices: 23.3 us -> 11.9 us  [neighbours(): lax.ppermute(up, 'rows', backward)]
    ppermute x2, starting transfers between devices: 14.9 us -> 24.9 us  [neighbours(): lax.ppermute(down, 'rows', forward)]
    ppermute x3, waiting for transfers between devices: 8.31 us -> 13.3 us  [moved(): return lax.ppermute(value, ('rows', 'batch'), pairs)]
  transfers between devices with their start and end apart: 11 -> 11, of which waited for: 7 -> 7; matrix products, arithmetic and copies ran while one was open for 0% -> 1% of each run, Pallas kernels for 2% -> 2%
where the time goes in v5:
time: 197 us
  starting transfers between devices  65.5 us (33%)
  waiting for transfers between devices  46.8 us (24%)
  blocking collectives  42.8 us (22%)
  Pallas kernels  20.2 us (10%)
  between operations  14.4 us (7%)
  local copies, waits for them, and re-layouts  5.06 us (3%)
    all_to_all x2, blocking collectives, exchanged(): lax.all_to_all(value, BOTH, 0, 0, axis_index_groups=groups, tiled=True)  30.5 us
    ppermute x2, starting transfers between devices, neighbours(): lax.ppermute(down, 'rows', forward)  24.9 us
    ppermute x3, starting transfers between devices, moved(): return lax.ppermute(value, ('rows', 'batch'), pairs)  16.3 us
    all_to_all x1, waiting for transfers between devices, shards(): stats = lax.all_to_all(sums, 'rows', 0, 0, tiled=True)  14.4 us
    all_to_all x1, starting transfers between devices, shards(): stats = lax.all_to_all(sums, 'rows', 0, 0, tiled=True)  13.7 us
    ppermute x3, waiting for transfers between devices, moved(): return lax.ppermute(value, ('rows', 'batch'), pairs)  13.3 us
    all_gather x1, blocking collectives, gathered(): return lax.all_gather(part, BOTH, axis_index_groups=groups, tiled=True)  12.3 us
    ppermute x2, waiting for transfers between devices, neighbours(): lax.ppermute(up, 'rows', backward)  11.9 us
  transfers between devices with their start and end apart: 11, of which 7 were waited for; matrix products, arithmetic and copies ran while one was open for 1% of the time, Pallas kernels for 2%

profile of v5, /device:TPU:1, one launch (start us, length us, event | category | flops | bytes accessed | tf_op | source)
XLA Modules:
  0.0 196.6 jit_solution(3854747615530202377)
XLA Ops:
  8.3 1.8 pad_maximum_fusion
  11.0 11.9 %collective-permute-start.2 = (bf16[16,3584]{1,0:T(8,128)(2,1)S(1)}, bf16[16,3584]{1,0:T(8,128)(2,1)S(1)}, u32[]{:S(2)}, u32[]{:S(2)}) collective-permute-start(bf16[16,3584]{1,0:T(8,128)(2,1)S(1)} %constant_dynamic-slice_fusion), channel_id=1, source_target_pairs={{0,92},{1,93},{2,94},{3,95},{4,88},{5,89},{6,90},{7,91},{8,84},{9,... | collective-permute-start | bytes 344072 | tf_op jit(solution)/shard_map/ppermute | solution.py:575
  24.3 9.2 %collective-permute-done.2 = bf16[16,3584]{1,0:T(8,128)(2,1)S(1)} collective-permute-done((bf16[16,3584]{1,0:T(8,128)(2,1)S(1)}, bf16[16,3584]{1,0:T(8,128)(2,1)S(1)}, u32[]{:S(2)}, u32[]{:S(2)}) %collective-permute-start.2) | collective-permute-done | bytes 114720 | tf_op jit(solution)/shard_map/ppermute | solution.py:575
  33.5 12.3 %all_gather.10 = bf16[64,3584]{1,0:T(8,128)(2,1)} all-gather(bf16[16,3584]{1,0:T(8,128)(2,1)S(1)} %collective-permute-done.2), channel_id=1, replica_groups={{0,1,2,3},{4,5,6,7},{8,9,10,11},{12,13,14,15},{16,17,18,19},{20,21,22,2..., dimensions={0}, use_global_device_ids=true | all-gather | bytes 573440 | tf_op jit(solution)/shard_map/all_gather | solution.py:585
  45.8 13.7 %all-to-all-start = ((f32[16,8,128]{2,1,0:T(8,128)}), f32[16,8,128]{2,1,0:T(8,128)S(1)}, u32[]{:S(2)}, u32[]{:S(2)}) async-start(f32[16,8,128]{2,1,0:T(8,128)} %stats.1), calls=%async_computation | async-start | bytes 131072 | tf_op jit(solution)/shard_map/all_to_all | solution.py:629
  59.6 14.4 %all-to-all-done.refs_0_ = f32[16,8,128]{2,1,0:T(8,128)S(1)} async-done(((f32[16,8,128]{2,1,0:T(8,128)}), f32[16,8,128]{2,1,0:T(8,128)S(1)}, u32[]{:S(2)}, u32[]{:S(2)}) %all-to-all-start) | async-done | bytes 65568 | tf_op jit(solution)/shard_map/all_to_all | solution.py:629
  75.2 2.3 %collective-permute-start = (f32[8,768]{1,0:T(8,128)S(1)}, f32[8,768]{1,0:T(8,128)S(1)}, u32[]{:S(2)}, u32[]{:S(2)}) collective-permute-start(f32[8,768]{1,0:T(8,128)S(1)} %get-tuple-element.25), channel_id=1, source_target_pairs={{32,0},{64,32},{96,64},{128,96},{160,128},{192,160},{224,192},{256... | collective-permute-start | bytes 73736 | tf_op jit(solution)/shard_map/ppermute | solution.py:596
  77.6 11.9 %collective-permute-start.1 = (f32[8,768]{1,0:T(8,128)S(1)}, f32[8,768]{1,0:T(8,128)S(1)}, u32[]{:S(2)}, u32[]{:S(2)}) collective-permute-start(f32[8,768]{1,0:T(8,128)S(1)} %get-tuple-element.26), channel_id=1, source_target_pairs={{0,32},{32,64},{64,96},{96,128},{128,160},{160,192},{192,224},{224... | collective-permute-start | bytes 73736 | tf_op jit(solution)/shard_map/ppermute | solution.py:596
  90.5 1.9 collective-permute-start.3
  92.4 2.4 %collective-permute-start.4 = (bf16[256,3584]{1,0:T(8,128)(2,1)}, bf16[256,3584]{1,0:T(8,128)(2,1)}, u32[]{:S(2)}, u32[]{:S(2)}) collective-permute-start(bf16[256,3584]{1,0:T(8,128)(2,1)} %all-gather.5.cloned.1.call-done.refs_10_), channel_id=1, source_target_pairs={{0,32},{1,33},{2,34},{3,35},{4,36},{5,37},{6,38},{7,39},{8,40},{9,... | collective-permute-start | bytes 5505032 | tf_op jit(solution)/shard_map/ppermute | solution.py:575
  95.0 1.4 collective-permute-done.3.refs_11_
  96.3 2.8 %collective-permute-done.4.refs_12_ = bf16[256,3584]{1,0:T(8,128)(2,1)} collective-permute-done((bf16[256,3584]{1,0:T(8,128)(2,1)}, bf16[256,3584]{1,0:T(8,128)(2,1)}, u32[]{:S(2)}, u32[]{:S(2)}) %collective-permute-start.4) | collective-permute-done | bytes 1835040 | tf_op jit(solution)/shard_map/ppermute | solution.py:575
  99.1 1.5 copy-done.3
  100.6 1.5 copy-done.4
  102.1 11.6 %projector.1 = (f32[32,1024]{1,0:T(8,128)S(1)}, f32[8,768]{1,0:T(8,128)S(1)}) custom-call(s32[4]{0:T(128)S(1)} %pad_add_fusion.refs_0_.at_ref, f32[8,768]{1,0:T(8,128)S(1)} %get-tuple-element.24.refs_1_, f32[8,768]{1,0:T(8,128)S(1)} %collective-permute-done.1.refs_2_, f32[8,768]{1,0:T(8,128)S(1)} %collective-permute-done.refs_3_, ...), custom_call_target="tpu_custom_call" | custom-call | flops 2818572288 | bytes 8388608 | tf_op jit(solution)/shard_map/projector/pallas_call | solution.py:296
  113.7 12.9 %collective-permute-start.5 = (f32[8,768]{1,0:T(8,128)S(1)}, f32[8,768]{1,0:T(8,128)S(1)}, u32[]{:S(2)}, u32[]{:S(2)}) collective-permute-start(f32[8,768]{1,0:T(8,128)S(1)} %get-tuple-element.31.refs_0_), channel_id=1, source_target_pairs={{0,32},{32,64},{64,96},{96,128},{128,160},{160,192},{192,224},{224... | collective-permute-start | bytes 73736 | tf_op jit(solution)/shard_map/ppermute | solution.py:596
  126.7 1.9 collective-permute-start.6
  128.6 11.9 %collective-permute-done.6.refs_2_ = f32[8,768]{1,0:T(8,128)S(1)} collective-permute-done((f32[8,768]{1,0:T(8,128)S(1)}, f32[8,768]{1,0:T(8,128)S(1)}, u32[]{:S(2)}, u32[]{:S(2)}) %collective-permute-start.6) | collective-permute-done | bytes 24608 | tf_op jit(solution)/shard_map/ppermute | solution.py:596
  140.5 2.0 %back.1 = (bf16[32,32,128]{2,1,0:T(8,128)(2,1)S(1)}, f32[12,64,512]{2,1,0:T(8,128)S(1)}) custom-call(f32[8,768]{1,0:T(8,128)S(1)} %get-tuple-element.31.refs_0_, f32[8,768]{1,0:T(8,128)S(1)} %collective-permute-done.5.refs_1_, f32[8,768]{1,0:T(8,128)S(1)} %collective-permute-done.6.refs_2_, bf16[12,64,512]{2,1,0:T(8,128)(2,1)S(1)} %bitcast.18, ...), custom_call_target="tpu_custom_call" | custom-call | tf_op jit(solution)/shard_map/back/pallas_call | solution.py:393
  142.6 13.6 %all_to_all.20.got_ref = bf16[32,32,128]{2,1,0:T(8,128)(2,1)S(1)} all-to-all(bf16[32,32,128]{2,1,0:T(8,128)(2,1)S(1)} %get-tuple-element.35), channel_id=1, replica_groups={{0,32,1,33,2,34,3,35,128,160,129,161,130,162,131,163,256,288,257,289,25..., dimensions={0} | all-to-all | bytes 524288 | tf_op jit(solution)/shard_map/all_to_all | solution.py:563
  156.8 16.9 %all_to_all.21.got_ref = bf16[16,32,128]{2,1,0:T(8,128)(2,1)S(1)} all-to-all(bf16[16,32,128]{2,1,0:T(8,128)(2,1)S(1)} %plane.1), channel_id=1, replica_groups={{0,4,8,12,16,20,24,28,64,68,72,76,80,84,88,92},{32,36,40,44,48,52,56,60..., dimensions={0} | all-to-all | bytes 262144 | tf_op jit(solution)/shard_map/all_to_all | solution.py:563
  174.9 6.4 %all-to-all-start.3 = ((bf16[32,16,128]{2,1,0:T(8,128)(2,1)}), bf16[32,16,128]{2,1,0:T(8,128)(2,1)S(1)}, u32[]{:S(2)}, u32[]{:S(2)}) async-start(bf16[32,16,128]{2,1,0:T(8,128)(2,1)} %get-tuple-element.38), calls=%async_computation.3 | async-start | bytes 262144 | tf_op jit(solution)/shard_map/all_to_all | solution.py:563
  181.3 1.6 last.1
  182.9 6.1 %all-to-all-done.3.got_ref = bf16[32,16,128]{2,1,0:T(8,128)(2,1)S(1)} async-done(((bf16[32,16,128]{2,1,0:T(8,128)(2,1)}), bf16[32,16,128]{2,1,0:T(8,128)(2,1)S(1)}, u32[]{:S(2)}, u32[]{:S(2)}) %all-to-all-start.3) | async-done | bytes 131104 | tf_op jit(solution)/shard_map/all_to_all | solution.py:563
  (42 shorter events, 8.2 us)
Async XLA Ops:
  7.2 15.8 %copy-start = (bf16[12,2,32,512]{3,2,1,0:T(8,128)(2,1)S(1)}, bf16[12,2,32,512]{3,2,1,0:T(8,128)(2,1)}, u32[]{:S(2)}) copy-start(bf16[12,2,32,512]{3,2,1,0:T(8,128)(2,1)} %param.11) | copy-start | bytes 2359300
  7.2 83.3 %all-gather.3.cloned.1.call-start = ((), (), s32[]{:S(2)}) async-start(), calls=%async_computation.4 | async-start | bytes 2293760 | tf_op jit(solution)/shard_map/all_gather | solution.py:585
  8.2 51.3 %copy-start.9 = (bf16[4,4608]{1,0:T(4,128)(2,1)S(1)}, bf16[4,4608]{1,0:T(4,128)(2,1)}, u32[]{:S(2)}) copy-start(bf16[4,4608]{1,0:T(4,128)(2,1)} %param.14) | copy-start | bytes 110596
  8.3 65.8 %copy-start.1 = (f32[512]{0:T(512)S(1)}, f32[512]{0:T(512)}, u32[]{:S(2)}) copy-start(f32[512]{0:T(512)} %param.12) | copy-start | bytes 6148
  8.3 65.8 %copy-start.2 = (f32[512]{0:T(512)S(1)}, f32[512]{0:T(512)}, u32[]{:S(2)}) copy-start(f32[512]{0:T(512)} %param.13) | copy-start | bytes 6148
  10.1 82.3 %all-gather.5.cloned.1.call-start = ((), (), s32[]{:S(2)}) async-start(), calls=%async_computation.5 | async-start | bytes 2293760 | tf_op jit(solution)/shard_map/all_gather | solution.py:585
  11.0 22.5 %collective-permute-start.2 = (bf16[16,3584]{1,0:T(8,128)(2,1)S(1)}, bf16[16,3584]{1,0:T(8,128)(2,1)S(1)}, u32[]{:S(2)}, u32[]{:S(2)}) collective-permute-start(bf16[16,3584]{1,0:T(8,128)(2,1)S(1)} %constant_dynamic-slice_fusion), channel_id=1, source_target_pairs={{0,92},{1,93},{2,94},{3,95},{4,88},{5,89},{6,90},{7,91},{8,84},{9,... | collective-permute-start | bytes 344072 | tf_op jit(solution)/shard_map/ppermute | solution.py:575
  45.8 28.2 %all-to-all-start = ((f32[16,8,128]{2,1,0:T(8,128)}), f32[16,8,128]{2,1,0:T(8,128)S(1)}, u32[]{:S(2)}, u32[]{:S(2)}) async-start(f32[16,8,128]{2,1,0:T(8,128)} %stats.1), calls=%async_computation | async-start | bytes 131072 | tf_op jit(solution)/shard_map/all_to_all | solution.py:629
  74.0 20.8 %copy-start.10 = (f32[768]{0:T(1024)S(1)}, f32[768]{0:T(1024)}, u32[]{:S(2)}) copy-start(f32[768]{0:T(1024)} %param.20) | copy-start | bytes 9220
  74.0 25.0 %copy-start.5 = (bf16[12,1,16,768]{3,2,1,0:T(8,128)(2,1)S(1)}, bf16[12,1,16,768]{3,2,1,0:T(8,128)(2,1)}, u32[]{:S(2)}) copy-start(bf16[12,1,16,768]{3,2,1,0:T(8,128)(2,1)} %param.21) | copy-start | bytes 884740
  74.1 25.0 %copy-start.6 = (f32[16,1024]{1,0:T(8,128)S(1)}, f32[16,1024]{1,0:T(8,128)}, u32[]{:S(2)}) copy-start(f32[16,1024]{1,0:T(8,128)} %refs_5_.1) | copy-start | bytes 196612
  74.1 25.0 %copy-start.7 = (f32[2048]{0:T(1024)S(1)}, f32[2048]{0:T(1024)}, u32[]{:S(2)}) copy-start(f32[2048]{0:T(1024)} %param.18) | copy-start | bytes 24580
  74.1 25.0 %copy-start.8 = (f32[1024]{0:T(1024)S(1)}, f32[1024]{0:T(1024)}, u32[]{:S(2)}) copy-start(f32[1024]{0:T(1024)} %param.16) | copy-start | bytes 12292
  75.2 14.3 %collective-permute-start = (f32[8,768]{1,0:T(8,128)S(1)}, f32[8,768]{1,0:T(8,128)S(1)}, u32[]{:S(2)}, u32[]{:S(2)}) collective-permute-start(f32[8,768]{1,0:T(8,128)S(1)} %get-tuple-element.25), channel_id=1, source_target_pairs={{32,0},{64,32},{96,64},{128,96},{160,128},{192,160},{224,192},{256... | collective-permute-start | bytes 73736 | tf_op jit(solution)/shard_map/ppermute | solution.py:596
  77.6 12.9 %collective-permute-start.1 = (f32[8,768]{1,0:T(8,128)S(1)}, f32[8,768]{1,0:T(8,128)S(1)}, u32[]{:S(2)}, u32[]{:S(2)}) collective-permute-start(f32[8,768]{1,0:T(8,128)S(1)} %get-tuple-element.26), channel_id=1, source_target_pairs={{0,32},{32,64},{64,96},{96,128},{128,160},{160,192},{192,224},{224... | collective-permute-start | bytes 73736 | tf_op jit(solution)/shard_map/ppermute | solution.py:596
  90.5 5.9 %collective-permute-start.3 = (bf16[256,3584]{1,0:T(8,128)(2,1)}, bf16[256,3584]{1,0:T(8,128)(2,1)S(1)}, u32[]{:S(2)}, u32[]{:S(2)}) collective-permute-start(bf16[256,3584]{1,0:T(8,128)(2,1)} %all-gather.3.cloned.1.call-done.refs_9_), channel_id=1, source_target_pairs={{0,32},{1,33},{2,34},{3,35},{4,36},{5,37},{6,38},{7,39},{8,40},{9,... | collective-permute-start | bytes 5505032 | tf_op jit(solution)/shard_map/ppermute | solution.py:575
  92.4 6.7 %collective-permute-start.4 = (bf16[256,3584]{1,0:T(8,128)(2,1)}, bf16[256,3584]{1,0:T(8,128)(2,1)}, u32[]{:S(2)}, u32[]{:S(2)}) collective-permute-start(bf16[256,3584]{1,0:T(8,128)(2,1)} %all-gather.5.cloned.1.call-done.refs_10_), channel_id=1, source_target_pairs={{0,32},{1,33},{2,34},{3,35},{4,36},{5,37},{6,38},{7,39},{8,40},{9,... | collective-permute-start | bytes 5505032 | tf_op jit(solution)/shard_map/ppermute | solution.py:575
  99.1 1.5 copy-start.3
  100.6 1.5 copy-start.4
  113.7 14.9 %collective-permute-start.5 = (f32[8,768]{1,0:T(8,128)S(1)}, f32[8,768]{1,0:T(8,128)S(1)}, u32[]{:S(2)}, u32[]{:S(2)}) collective-permute-start(f32[8,768]{1,0:T(8,128)S(1)} %get-tuple-element.31.refs_0_), channel_id=1, source_target_pairs={{0,32},{32,64},{64,96},{96,128},{128,160},{160,192},{192,224},{224... | collective-permute-start | bytes 73736 | tf_op jit(solution)/shard_map/ppermute | solution.py:596
  126.7 13.9 %collective-permute-start.6 = (f32[8,768]{1,0:T(8,128)S(1)}, f32[8,768]{1,0:T(8,128)S(1)}, u32[]{:S(2)}, u32[]{:S(2)}) collective-permute-start(f32[8,768]{1,0:T(8,128)S(1)} %get-tuple-element.31.refs_0_), channel_id=1, source_target_pairs={{32,0},{64,32},{96,64},{128,96},{160,128},{192,160},{224,192},{256... | collective-permute-start | bytes 73736 | tf_op jit(solution)/shard_map/ppermute | solution.py:596
  174.9 14.1 %all-to-all-start.3 = ((bf16[32,16,128]{2,1,0:T(8,128)(2,1)}), bf16[32,16,128]{2,1,0:T(8,128)(2,1)S(1)}, u32[]{:S(2)}, u32[]{:S(2)}) async-start(bf16[32,16,128]{2,1,0:T(8,128)(2,1)} %get-tuple-element.38), calls=%async_computation.3 | async-start | bytes 262144 | tf_op jit(solution)/shard_map/all_to_all | solution.py:563
Sparse Core Ops, SparseCore 0:
  10.7 41.6 all-gather.2
  54.4 36.3 all-gather.4

commit v6 on v5

--- a/solution.py
+++ b/solution.py
@@ -188,25 +188,25 @@
     rows = taken * SUB
     copies = []
 
-    for piece, of_zhi, of_core in (
-        (own, zhi, core),
-        (own_other, zhi, 1 - core),
-        (cross, 1 - zhi, core),
-        (cross_other, 1 - zhi, 1 - core),
-    ):
+    def place(piece, at, shard, size):
+        lines = pl.ds(at, size)
+
+        def put(columns, into):
+            copy = pltpu.make_async_copy(piece.at[lines, columns], into, sems.at[len(copies)])
+            copy.start()
+            copies.append(copy)
+
+        line = pl.multiple_of(shard * depth, size)
+        put(pl.ds(0, hidden), w_in.at[pl.ds(line, size), :])
+        for part in range(slab // depth):
+            line = pl.multiple_of(shard * slab + part * depth, size)
+            put(pl.ds(hidden + part * align, align), w_out.at[pl.ds(line, size), :])
+
+    for near, far, of_core in ((own, cross, core), (own_other, cross_other, 1 - core)):
         for x in range(XS):
-            shard = x * (ZHI * CORES) + of_zhi * CORES + of_core
-            lines = pl.ds(x * depth, depth)
-
-            def put(columns, into):
-                copy = pltpu.make_async_copy(piece.at[lines, columns], into, sems.at[len(copies)])
-                copy.start()
-                copies.append(copy)
-
-            put(pl.ds(0, hidden), w_in.at[pl.ds(pl.multiple_of(shard * depth, depth), depth), :])
-            for part in range(slab // depth):
-                begin = pl.multiple_of(shard * slab + part * depth, depth)
-                put(pl.ds(hidden + part * align, align), w_out.at[pl.ds(begin, depth), :])
+            shard = x * (ZHI * CORES) + of_core
+            for piece, of_zhi in ((near, zhi), (far, 1 - zhi)):
+                place(piece, x * depth, shard + of_zhi * CORES, depth)
 
     lat = lat_ref[...] + below_ref[...] + above_ref[...]
     top = lat.astype(BF16)
@@ -544,12 +544,12 @@
     for d in range(ZLO)
     for y in range(YS)
 ]
-ALONG_Y = [
-    [device(x, h, c, d, y) for y in range(YS)]
-    for x in range(XS)
+ALONG_PAIR = [
+    [device(x, h, c, d, 2 * p + k) for x in range(XS) for k in range(2)]
     for h in range(ZHI)
     for c in range(CORES)
     for d in range(ZLO)
+    for p in range(YS // 2)
 ]
 COLUMN = [
     [device(x, h, c, d, y) for h in range(ZHI) for d in range(ZLO)]
@@ -575,10 +575,37 @@
     return lax.ppermute(value, ("rows", "batch"), pairs)
 
 
-def crossed(shard):
-    y = lax.axis_index("batch") % YS
-    mine = lax.dynamic_slice_in_dim(shard, y * PART, PART, axis=0)
-    return moved(mine, lambda x, h, c, d, y: (x, 1 - h, c, ZLO - 1 - d, y))
+def shard_kernel(at_ref, in_ref, out_ref, shard_ref, half_ref):
+    depth, hidden = in_ref.shape
+    align = out_ref.shape[1]
+    shard_ref[:, 0:hidden] = in_ref[...]
+    for part in range(out_ref.shape[0] // depth):
+        shard_ref[:, hidden + part * align : hidden + (part + 1) * align] = out_ref[
+            part * depth : (part + 1) * depth, :
+        ]
+    size = half_ref.shape[0]
+    begin = pl.multiple_of(lax.rem(at_ref[2], 2) * size, size)
+    half_ref[...] = shard_ref[pl.ds(begin, size), :]
+
+
+def shard_of(at, proj_in, proj_out):
+    depth, hidden = proj_in.shape
+    columns = hidden + proj_out.size // depth
+    return pl.pallas_call(
+        shard_kernel,
+        out_shape=(
+            jax.ShapeDtypeStruct((depth, columns), BF16),
+            jax.ShapeDtypeStruct((depth // 2, columns), BF16),
+        ),
+        in_specs=[pl.BlockSpec(memory_space=pltpu.SMEM), vmem(), vmem()],
+        out_specs=(vmem(), vmem()),
+        compiler_params=params(),
+        name="shard",
+    )(at, proj_in, proj_out)
+
+
+def crossed(half):
+    return moved(half, lambda x, h, c, d, y: (x, 1 - h, c, ZLO - 1 - d, y))
 
 
 def gathered(part, groups):
@@ -615,11 +642,10 @@
     members = peers * height * across * (channels // GROUPS)
     flat = features.reshape(images, height * across, channels)
     gain, bias = norm_gain.reshape(1, channels), norm_bias.reshape(1, channels)
-    depth = proj_in.shape[0]
-    shard = jnp.concatenate(
-        [proj_in] + [proj_out[at : at + depth] for at in range(0, proj_out.shape[0], depth)], axis=1
-    )
-    far = crossed(shard)
+    rows, batch = lax.axis_index("rows"), lax.axis_index("batch")
+    at = jnp.stack([(rows // CORES) % ZHI, rows % CORES, batch % YS, batch // YS])
+    at = at.astype(jnp.int32)
+    shard, half = shard_of(at, proj_in, proj_out)
     own = gathered(shard, ALONG_X)
     taps = conv_weight.reshape(LATENT, TAPS, channels).transpose(1, 0, 2)
     taps = jnp.pad(taps, ((0, 0), (0, SUB - LATENT), (0, 0))).reshape(TAPS * SUB, channels)
@@ -627,15 +653,13 @@
 
     sums = group_stats(flat, peers)
     stats = lax.all_to_all(sums, "rows", 0, 0, tiled=True)
-    far, sums_ = lax.optimization_barrier((far, sums))
-    cross = gathered(gathered(far, ALONG_Y), ALONG_X)
+    cross, stats = lax.optimization_barrier((crossed(half), stats))
+    cross = jnp.broadcast_to(cross[None], (2 * XS, *cross.shape))
+    cross = exchanged(cross, ALONG_PAIR).reshape(own.shape)
     lat, up, down, mean, inv = conv_forward(stats, flat, gain, bias, taps, across, members)
     above, below = neighbours(up, down)
-    own, above, below = lax.optimization_barrier((own, above, below))
+    cross, own, above, below = lax.optimization_barrier((cross, own, above, below))
     pieces = [own, cross, swapped(own), swapped(cross)]
-    rows, batch = lax.axis_index("rows"), lax.axis_index("batch")
-    at = jnp.stack([(rows // CORES) % ZHI, rows % CORES, batch % YS, batch // YS])
-    at = at.astype(jnp.int32)
     target = targets.reshape(-1, align)
     embed_part, grad_lat = projector(
         at, lat, below, above, target, embed_weight, embed_bias.reshape(1, -1),

time: 197 us -> 197 us (level)
  blocking collectives: 42.8 us -> 33.3 us
  waiting for transfers between devices: 46.8 us -> 55.8 us
    all_to_all x1, waiting for transfers between devices: 14.4 us -> 0.01 us  [shards(): stats = lax.all_to_all(sums, 'rows', 0, 0, tiled=True)]
    ppermute x3, waiting for transfers between devices: 13.3 us -> 26.3 us  [moved(): return lax.ppermute(value, ('rows', 'batch'), pairs)]
    all_gather x1 -> x0, blocking collectives: 12.3 us -> none  [gathered(): return lax.all_gather(part, BOTH, axis_index_groups=groups, tiled=True)]
    all_to_all x1 -> x2, waiting for transfers between devices: 6.15 us -> 16.6 us  [exchanged(): lax.all_to_all(value, BOTH, 0, 0, axis_index_groups=groups, tiled=True)]
    ppermute x2, starting transfers between devices: 24.9 us -> 17.8 us  [neighbours(): lax.ppermute(down, 'rows', forward)]
    all_to_all x1, starting transfers between devices: 13.7 us -> 19.1 us  [shards(): stats = lax.all_to_all(sums, 'rows', 0, 0, tiled=True)]
    all_to_all x1 -> x2, starting transfers between devices: 6.36 us -> 11.5 us  [exchanged(): lax.all_to_all(value, BOTH, 0, 0, axis_index_groups=groups, tiled=True)]
    ppermute x3, starting transfers between devices: 16.3 us -> 13.1 us  [moved(): return lax.ppermute(value, ('rows', 'batch'), pairs)]
where the time goes in v6:
time: 197 us
  starting transfers between devices  66.3 us (34%)
  waiting for transfers between devices  55.8 us (28%)
  blocking collectives  33.3 us (17%)
  Pallas kernels  21 us (11%)
  between operations  14.3 us (7%)
  local copies, waits for them, and re-layouts  6.01 us (3%)
    all_to_all x2, blocking collectives, exchanged(): lax.all_to_all(value, BOTH, 0, 0, axis_index_groups=groups, tiled=True)  33.3 us
    ppermute x3, waiting for transfers between devices, moved(): return lax.ppermute(value, ('rows', 'batch'), pairs)  26.3 us
    all_to_all x1, starting transfers between devices, shards(): stats = lax.all_to_all(sums, 'rows', 0, 0, tiled=True)  19.1 us
    ppermute x2, starting transfers between devices, neighbours(): lax.ppermute(down, 'rows', forward)  17.8 us
    all_to_all x2, waiting for transfers between devices, exchanged(): lax.all_to_all(value, BOTH, 0, 0, axis_index_groups=groups, tiled=True)  16.6 us
    ppermute x3, starting transfers between devices, moved(): return lax.ppermute(value, ('rows', 'batch'), pairs)  13.1 us
    ppermute x2, waiting for transfers between devices, neighbours(): lax.ppermute(up, 'rows', backward)  11.9 us
    all_to_all x2, starting transfers between devices, exchanged(): lax.all_to_all(value, BOTH, 0, 0, axis_index_groups=groups, tiled=True)  11.5 us
  transfers between devices with their start and end apart: 11, of which 7 were waited for; matrix products, arithmetic and copies ran while one was open for 1% of the time, Pallas kernels for 2%

profile of v6, /device:TPU:1, one launch (start us, length us, event | category | flops | bytes accessed | tf_op | source)
XLA Modules:
  0.0 196.8 jit_solution(14807855946346855855)
XLA Ops:
  9.2 1.3 shard.1
  13.0 19.1 %all-to-all-start = ((f32[16,8,128]{2,1,0:T(8,128)}), f32[16,8,128]{2,1,0:T(8,128)S(1)}, u32[]{:S(2)}, u32[]{:S(2)}) async-start(f32[16,8,128]{2,1,0:T(8,128)} %stats.1), calls=%async_computation | async-start | bytes 131072 | tf_op jit(solution)/shard_map/all_to_all | solution.py:655
  32.1 7.7 %collective-permute-start = (bf16[32,3584]{1,0:T(8,128)(2,1)S(1)}, bf16[32,3584]{1,0:T(8,128)(2,1)S(1)}, u32[]{:S(2)}, u32[]{:S(2)}) collective-permute-start(bf16[32,3584]{1,0:T(8,128)(2,1)S(1)} %get-tuple-element.28), channel_id=1, source_target_pairs={{0,92},{1,93},{2,94},{3,95},{4,88},{5,89},{6,90},{7,91},{8,84},{9,... | collective-permute-start | bytes 688136 | tf_op jit(solution)/shard_map/ppermute | solution.py:575
  39.9 22.3 %collective-permute-done = bf16[32,3584]{1,0:T(8,128)(2,1)S(1)} collective-permute-done((bf16[32,3584]{1,0:T(8,128)(2,1)S(1)}, bf16[32,3584]{1,0:T(8,128)(2,1)S(1)}, u32[]{:S(2)}, u32[]{:S(2)}) %collective-permute-start) | collective-permute-done | bytes 229408 | tf_op jit(solution)/shard_map/ppermute | solution.py:575
  62.2 1.4 broadcast_in_dim.2
  63.5 5.1 %all-to-all-start.1 = ((bf16[8,32,3584]{2,1,0:T(8,128)(2,1)}), bf16[8,32,3584]{2,1,0:T(8,128)(2,1)S(1)}, u32[]{:S(2)}, u32[]{:S(2)}) async-start(bf16[8,32,3584]{2,1,0:T(8,128)(2,1)} %broadcast_in_dim.2), calls=%async_computation.1 | async-start | bytes 3670016 | tf_op jit(solution)/shard_map/all_to_all | solution.py:563
  69.9 2.9 %collective-permute-start.1 = (f32[8,768]{1,0:T(8,128)S(1)}, f32[8,768]{1,0:T(8,128)S(1)}, u32[]{:S(2)}, u32[]{:S(2)}) collective-permute-start(f32[8,768]{1,0:T(8,128)S(1)} %get-tuple-element.33), channel_id=1, source_target_pairs={{32,0},{64,32},{96,64},{128,96},{160,128},{192,160},{224,192},{256... | collective-permute-start | bytes 73736 | tf_op jit(solution)/shard_map/ppermute | solution.py:623
  72.8 11.4 %collective-permute-start.2 = (f32[8,768]{1,0:T(8,128)S(1)}, f32[8,768]{1,0:T(8,128)S(1)}, u32[]{:S(2)}, u32[]{:S(2)}) collective-permute-start(f32[8,768]{1,0:T(8,128)S(1)} %get-tuple-element.34), channel_id=1, source_target_pairs={{0,32},{32,64},{64,96},{96,128},{128,160},{160,192},{192,224},{224... | collective-permute-start | bytes 73736 | tf_op jit(solution)/shard_map/ppermute | solution.py:623
  85.1 10.5 %all-to-all-done.1 = bf16[8,32,3584]{2,1,0:T(8,128)(2,1)S(1)} async-done(((bf16[8,32,3584]{2,1,0:T(8,128)(2,1)}), bf16[8,32,3584]{2,1,0:T(8,128)(2,1)S(1)}, u32[]{:S(2)}, u32[]{:S(2)}) %all-to-all-start.1) | async-done | bytes 1835040 | tf_op jit(solution)/shard_map/all_to_all | solution.py:563
  95.6 3.5 %collective-permute-start.3 = (bf16[256,3584]{1,0:T(8,128)(2,1)}, bf16[256,3584]{1,0:T(8,128)(2,1)S(1)}, u32[]{:S(2)}, u32[]{:S(2)}) collective-permute-start(bf16[256,3584]{1,0:T(8,128)(2,1)} %all-gather.2.cloned.1.call-done.refs_9_), channel_id=1, source_target_pairs={{0,32},{1,33},{2,34},{3,35},{4,36},{5,37},{6,38},{7,39},{8,40},{9,... | collective-permute-start | bytes 5505032 | tf_op jit(solution)/shard_map/ppermute | solution.py:575
  99.1 1.9 collective-permute-start.4
  101.1 1.6 collective-permute-done.3.refs_11_
  102.7 2.4 %collective-permute-done.4.refs_12_ = bf16[256,3584]{1,0:T(8,128)(2,1)S(1)} collective-permute-done((bf16[256,3584]{1,0:T(8,128)(2,1)S(1)}, bf16[256,3584]{1,0:T(8,128)(2,1)S(1)}, u32[]{:S(2)}, u32[]{:S(2)}) %collective-permute-start.4) | collective-permute-done | bytes 1835040 | tf_op jit(solution)/shard_map/ppermute | solution.py:575
  105.2 1.5 copy-done.6
  106.6 11.0 %projector.1 = (f32[32,1024]{1,0:T(8,128)S(1)}, f32[8,768]{1,0:T(8,128)S(1)}) custom-call(s32[4]{0:T(128)S(1)} %pad_add_fusion.at_ref.refs_0_, f32[8,768]{1,0:T(8,128)S(1)} %get-tuple-element.30.refs_1_, f32[8,768]{1,0:T(8,128)S(1)} %collective-permute-done.2.refs_2_, f32[8,768]{1,0:T(8,128)S(1)} %collective-permute-done.1.refs_3_, ...), custom_call_target="tpu_custom_call" | custom-call | flops 2818572288 | bytes 8388608 | tf_op jit(solution)/shard_map/projector/pallas_call | solution.py:296
  117.7 6.4 %collective-permute-start.5 = (f32[8,768]{1,0:T(8,128)S(1)}, f32[8,768]{1,0:T(8,128)S(1)}, u32[]{:S(2)}, u32[]{:S(2)}) collective-permute-start(f32[8,768]{1,0:T(8,128)S(1)} %get-tuple-element.39.refs_0_), channel_id=1, source_target_pairs={{0,32},{32,64},{64,96},{96,128},{128,160},{160,192},{192,224},{224... | collective-permute-start | bytes 73736 | tf_op jit(solution)/shard_map/ppermute | solution.py:623
  124.0 1.9 collective-permute-start.6
  126.0 11.9 %collective-permute-done.6.refs_2_ = f32[8,768]{1,0:T(8,128)S(1)} collective-permute-done((f32[8,768]{1,0:T(8,128)S(1)}, f32[8,768]{1,0:T(8,128)S(1)}, u32[]{:S(2)}, u32[]{:S(2)}) %collective-permute-start.6) | collective-permute-done | bytes 24608 | tf_op jit(solution)/shard_map/ppermute | solution.py:623
  137.9 2.0 %back.1 = (bf16[32,32,128]{2,1,0:T(8,128)(2,1)S(1)}, f32[12,64,512]{2,1,0:T(8,128)S(1)}) custom-call(f32[8,768]{1,0:T(8,128)S(1)} %get-tuple-element.39.refs_0_, f32[8,768]{1,0:T(8,128)S(1)} %collective-permute-done.5.refs_1_, f32[8,768]{1,0:T(8,128)S(1)} %collective-permute-done.6.refs_2_, bf16[12,64,512]{2,1,0:T(8,128)(2,1)S(1)} %bitcast.19, ...), custom_call_target="tpu_custom_call" | custom-call | tf_op jit(solution)/shard_map/back/pallas_call | solution.py:393
  139.9 13.2 %all_to_all.25.got_ref = bf16[32,32,128]{2,1,0:T(8,128)(2,1)S(1)} all-to-all(bf16[32,32,128]{2,1,0:T(8,128)(2,1)S(1)} %get-tuple-element.43), channel_id=1, replica_groups={{0,32,1,33,2,34,3,35,128,160,129,161,130,162,131,163,256,288,257,289,25..., dimensions={0} | all-to-all | bytes 524288 | tf_op jit(solution)/shard_map/all_to_all | solution.py:563
  153.8 20.1 %all_to_all.26.got_ref = bf16[16,32,128]{2,1,0:T(8,128)(2,1)S(1)} all-to-all(bf16[16,32,128]{2,1,0:T(8,128)(2,1)S(1)} %plane.1), channel_id=1, replica_groups={{0,4,8,12,16,20,24,28,64,68,72,76,80,84,88,92},{32,36,40,44,48,52,56,60..., dimensions={0} | all-to-all | bytes 262144 | tf_op jit(solution)/shard_map/all_to_all | solution.py:563
  175.0 6.4 %all-to-all-start.4 = ((bf16[32,16,128]{2,1,0:T(8,128)(2,1)}), bf16[32,16,128]{2,1,0:T(8,128)(2,1)S(1)}, u32[]{:S(2)}, u32[]{:S(2)}) async-start(bf16[32,16,128]{2,1,0:T(8,128)(2,1)} %get-tuple-element.46), calls=%async_computation.4 | async-start | bytes 262144 | tf_op jit(solution)/shard_map/all_to_all | solution.py:563
  181.4 1.6 last.1
  183.1 6.1 %all-to-all-done.4.got_ref = bf16[32,16,128]{2,1,0:T(8,128)(2,1)S(1)} async-done(((bf16[32,16,128]{2,1,0:T(8,128)(2,1)}), bf16[32,16,128]{2,1,0:T(8,128)(2,1)S(1)}, u32[]{:S(2)}, u32[]{:S(2)}) %all-to-all-start.4) | async-done | bytes 131104 | tf_op jit(solution)/shard_map/all_to_all | solution.py:563
  (43 shorter events, 9.2 us)
Async XLA Ops:
  7.2 32.6 %copy-start.11 = (bf16[4,4608]{1,0:T(4,128)(2,1)S(1)}, bf16[4,4608]{1,0:T(4,128)(2,1)}, u32[]{:S(2)}) copy-start(bf16[4,4608]{1,0:T(4,128)(2,1)} %param.14) | copy-start | bytes 110596
  7.2 88.4 %all-gather.2.cloned.1.call-start = ((), (), s32[]{:S(2)}) async-start(), calls=%async_computation.5 | async-start | bytes 2293760 | tf_op jit(solution)/shard_map/all_gather | solution.py:612
  7.3 1.0 copy-start.2
  8.3 0.9 copy-start.3
  10.6 1.1 copy-start
  13.0 49.1 %all-to-all-start = ((f32[16,8,128]{2,1,0:T(8,128)}), f32[16,8,128]{2,1,0:T(8,128)S(1)}, u32[]{:S(2)}, u32[]{:S(2)}) async-start(f32[16,8,128]{2,1,0:T(8,128)} %stats.1), calls=%async_computation | async-start | bytes 131072 | tf_op jit(solution)/shard_map/all_to_all | solution.py:655
  32.1 30.0 %collective-permute-start = (bf16[32,3584]{1,0:T(8,128)(2,1)S(1)}, bf16[32,3584]{1,0:T(8,128)(2,1)S(1)}, u32[]{:S(2)}, u32[]{:S(2)}) collective-permute-start(bf16[32,3584]{1,0:T(8,128)(2,1)S(1)} %get-tuple-element.28), channel_id=1, source_target_pairs={{0,92},{1,93},{2,94},{3,95},{4,88},{5,89},{6,90},{7,91},{8,84},{9,... | collective-permute-start | bytes 688136 | tf_op jit(solution)/shard_map/ppermute | solution.py:575
  63.5 5.1 %copy-start.1 = (bf16[12,2,32,512]{3,2,1,0:T(8,128)(2,1)S(1)}, bf16[12,2,32,512]{3,2,1,0:T(8,128)(2,1)}, u32[]{:S(2)}) copy-start(bf16[12,2,32,512]{3,2,1,0:T(8,128)(2,1)} %param.11) | copy-start | bytes 2359300
  63.5 5.1 %copy-start.4 = (f32[512]{0:T(512)S(1)}, f32[512]{0:T(512)}, u32[]{:S(2)}) copy-start(f32[512]{0:T(512)} %param.12) | copy-start | bytes 6148
  63.5 5.1 %copy-start.5 = (f32[512]{0:T(512)S(1)}, f32[512]{0:T(512)}, u32[]{:S(2)}) copy-start(f32[512]{0:T(512)} %param.13) | copy-start | bytes 6148
  63.5 32.0 %all-to-all-start.1 = ((bf16[8,32,3584]{2,1,0:T(8,128)(2,1)}), bf16[8,32,3584]{2,1,0:T(8,128)(2,1)S(1)}, u32[]{:S(2)}, u32[]{:S(2)}) async-start(bf16[8,32,3584]{2,1,0:T(8,128)(2,1)} %broadcast_in_dim.2), calls=%async_computation.1 | async-start | bytes 3670016 | tf_op jit(solution)/shard_map/all_to_all | solution.py:563
  68.7 32.4 %copy-start.12 = (f32[768]{0:T(1024)S(1)}, f32[768]{0:T(1024)}, u32[]{:S(2)}) copy-start(f32[768]{0:T(1024)} %param.20) | copy-start | bytes 9220
  68.7 36.4 %copy-start.7 = (bf16[12,1,16,768]{3,2,1,0:T(8,128)(2,1)S(1)}, bf16[12,1,16,768]{3,2,1,0:T(8,128)(2,1)}, u32[]{:S(2)}) copy-start(bf16[12,1,16,768]{3,2,1,0:T(8,128)(2,1)} %param.21) | copy-start | bytes 884740
  68.7 36.4 %copy-start.8 = (f32[16,1024]{1,0:T(8,128)S(1)}, f32[16,1024]{1,0:T(8,128)}, u32[]{:S(2)}) copy-start(f32[16,1024]{1,0:T(8,128)} %refs_5_.1) | copy-start | bytes 196612
  68.7 36.4 %copy-start.9 = (f32[2048]{0:T(1024)S(1)}, f32[2048]{0:T(1024)}, u32[]{:S(2)}) copy-start(f32[2048]{0:T(1024)} %param.18) | copy-start | bytes 24580
  68.7 36.4 %copy-start.10 = (f32[1024]{0:T(1024)S(1)}, f32[1024]{0:T(1024)}, u32[]{:S(2)}) copy-start(f32[1024]{0:T(1024)} %param.16) | copy-start | bytes 12292
  69.9 14.3 %collective-permute-start.1 = (f32[8,768]{1,0:T(8,128)S(1)}, f32[8,768]{1,0:T(8,128)S(1)}, u32[]{:S(2)}, u32[]{:S(2)}) collective-permute-start(f32[8,768]{1,0:T(8,128)S(1)} %get-tuple-element.33), channel_id=1, source_target_pairs={{32,0},{64,32},{96,64},{128,96},{160,128},{192,160},{224,192},{256... | collective-permute-start | bytes 73736 | tf_op jit(solution)/shard_map/ppermute | solution.py:623
  72.8 12.3 %collective-permute-start.2 = (f32[8,768]{1,0:T(8,128)S(1)}, f32[8,768]{1,0:T(8,128)S(1)}, u32[]{:S(2)}, u32[]{:S(2)}) collective-permute-start(f32[8,768]{1,0:T(8,128)S(1)} %get-tuple-element.34), channel_id=1, source_target_pairs={{0,32},{32,64},{64,96},{96,128},{128,160},{160,192},{192,224},{224... | collective-permute-start | bytes 73736 | tf_op jit(solution)/shard_map/ppermute | solution.py:623
  95.6 7.1 %collective-permute-start.3 = (bf16[256,3584]{1,0:T(8,128)(2,1)}, bf16[256,3584]{1,0:T(8,128)(2,1)S(1)}, u32[]{:S(2)}, u32[]{:S(2)}) collective-permute-start(bf16[256,3584]{1,0:T(8,128)(2,1)} %all-gather.2.cloned.1.call-done.refs_9_), channel_id=1, source_target_pairs={{0,32},{1,33},{2,34},{3,35},{4,36},{5,37},{6,38},{7,39},{8,40},{9,... | collective-permute-start | bytes 5505032 | tf_op jit(solution)/shard_map/ppermute | solution.py:575
  99.1 6.0 %collective-permute-start.4 = (bf16[256,3584]{1,0:T(8,128)(2,1)S(1)}, bf16[256,3584]{1,0:T(8,128)(2,1)S(1)}, u32[]{:S(2)}, u32[]{:S(2)}) collective-permute-start(bf16[256,3584]{1,0:T(8,128)(2,1)S(1)} %bitcast.21), channel_id=1, source_target_pairs={{0,32},{1,33},{2,34},{3,35},{4,36},{5,37},{6,38},{7,39},{8,40},{9,... | collective-permute-start | bytes 5505032 | tf_op jit(solution)/shard_map/ppermute | solution.py:575
  105.1 1.5 copy-start.6
  117.7 8.3 %collective-permute-start.5 = (f32[8,768]{1,0:T(8,128)S(1)}, f32[8,768]{1,0:T(8,128)S(1)}, u32[]{:S(2)}, u32[]{:S(2)}) collective-permute-start(f32[8,768]{1,0:T(8,128)S(1)} %get-tuple-element.39.refs_0_), channel_id=1, source_target_pairs={{0,32},{32,64},{64,96},{96,128},{128,160},{160,192},{192,224},{224... | collective-permute-start | bytes 73736 | tf_op jit(solution)/shard_map/ppermute | solution.py:623
  124.0 13.9 %collective-permute-start.6 = (f32[8,768]{1,0:T(8,128)S(1)}, f32[8,768]{1,0:T(8,128)S(1)}, u32[]{:S(2)}, u32[]{:S(2)}) collective-permute-start(f32[8,768]{1,0:T(8,128)S(1)} %get-tuple-element.39.refs_0_), channel_id=1, source_target_pairs={{32,0},{64,32},{96,64},{128,96},{160,128},{192,160},{224,192},{256... | collective-permute-start | bytes 73736 | tf_op jit(solution)/shard_map/ppermute | solution.py:623
  175.0 14.1 %all-to-all-start.4 = ((bf16[32,16,128]{2,1,0:T(8,128)(2,1)}), bf16[32,16,128]{2,1,0:T(8,128)(2,1)S(1)}, u32[]{:S(2)}, u32[]{:S(2)}) async-start(bf16[32,16,128]{2,1,0:T(8,128)(2,1)} %get-tuple-element.46), calls=%async_computation.4 | async-start | bytes 262144 | tf_op jit(solution)/shard_map/all_to_all | solution.py:563
Sparse Core Ops, SparseCore 0:
  10.7 41.9 all-gather.1

commit v7 on v6

--- a/solution.py
+++ b/solution.py
@@ -178,17 +178,18 @@
 def mlp_kernel(
     across, width, hidden, align, at_ref, lat_ref, below_ref, above_ref, target_ref,
     ew_ref, eb_ref, pib_ref, pob_ref,
-    own, cross, own_other, cross_other,
+    own_near, own_far, cross, own_near_other, own_far_other, cross_other,
     embed_ref, gl_ref, w_in, w_out, pre, emb, acc, grad_emb, sems,
 ):
-    zhi, core = at_ref[0], at_ref[1]
+    zhi, core, x = at_ref[0], at_ref[1], at_ref[4]
     depth = width // (XS * ZHI * CORES)
     slab = hidden // (XS * ZHI * CORES)
     taken = PATCH * PATCH
     rows = taken * SUB
     copies = []
 
-    def place(piece, at, shard, size):
+    def place(piece, at, source_x, of_zhi, of_core, begin=0, size=depth):
+        shard = lax.rem(source_x, XS) * (ZHI * CORES) + of_zhi * CORES + of_core
         lines = pl.ds(at, size)
 
         def put(columns, into):
@@ -196,17 +197,23 @@
             copy.start()
             copies.append(copy)
 
-        line = pl.multiple_of(shard * depth, size)
+        line = pl.multiple_of(shard * depth + begin, size)
         put(pl.ds(0, hidden), w_in.at[pl.ds(line, size), :])
         for part in range(slab // depth):
-            line = pl.multiple_of(shard * slab + part * depth, size)
+            line = pl.multiple_of(shard * slab + part * depth + begin, size)
             put(pl.ds(hidden + part * align, align), w_out.at[pl.ds(line, size), :])
 
-    for near, far, of_core in ((own, cross, core), (own_other, cross_other, 1 - core)):
-        for x in range(XS):
-            shard = x * (ZHI * CORES) + of_core
-            for piece, of_zhi in ((near, zhi), (far, 1 - zhi)):
-                place(piece, x * depth, shard + of_zhi * CORES, depth)
+    half = depth // 2
+    for near, opposite, far, of_core in (
+        (own_near, own_far, cross, core),
+        (own_near_other, own_far_other, cross_other, 1 - core),
+    ):
+        for k, step in enumerate((0, 1, XS - 1)):
+            place(near, k * depth, x + step, zhi, of_core)
+        for begin in (0, half):
+            place(opposite, begin, x + 2, zhi, of_core, begin, half)
+        for k in range(XS):
+            place(far, k * depth, k, 1 - zhi, of_core)
 
     lat = lat_ref[...] + below_ref[...] + above_ref[...]
     top = lat.astype(BF16)
@@ -310,7 +317,7 @@
             pltpu.VMEM((tokens, width), BF16),
             pltpu.VMEM((tokens, align), F32),
             pltpu.VMEM((256, width), F32),
-            pltpu.SemaphoreType.DMA((48,)),
+            pltpu.SemaphoreType.DMA((54,)),
         ],
         compiler_params=params(32),
         cost_estimate=pl.CostEstimate(
@@ -537,19 +544,11 @@
     for h in range(ZHI)
     for d in range(ZLO)
 ]
-ALONG_X = [
-    [device(x, h, c, d, y) for x in range(XS)]
+SHEET = [
+    [device(x, h, c, d, y) for x in range(XS) for y in range(YS)]
     for h in range(ZHI)
+    for d in range(ZLO)
     for c in range(CORES)
-    for d in range(ZLO)
-    for y in range(YS)
-]
-ALONG_PAIR = [
-    [device(x, h, c, d, 2 * p + k) for x in range(XS) for k in range(2)]
-    for h in range(ZHI)
-    for c in range(CORES)
-    for d in range(ZLO)
-    for p in range(YS // 2)
 ]
 COLUMN = [
     [device(x, h, c, d, y) for h in range(ZHI) for d in range(ZLO)]
@@ -575,7 +574,7 @@
     return lax.ppermute(value, ("rows", "batch"), pairs)
 
 
-def shard_kernel(at_ref, in_ref, out_ref, shard_ref, half_ref):
+def shard_kernel(at_ref, in_ref, out_ref, shard_ref, part_ref):
     depth, hidden = in_ref.shape
     align = out_ref.shape[1]
     shard_ref[:, 0:hidden] = in_ref[...]
@@ -583,9 +582,9 @@
         shard_ref[:, hidden + part * align : hidden + (part + 1) * align] = out_ref[
             part * depth : (part + 1) * depth, :
         ]
-    size = half_ref.shape[0]
-    begin = pl.multiple_of(lax.rem(at_ref[2], 2) * size, size)
-    half_ref[...] = shard_ref[pl.ds(begin, size), :]
+    size = part_ref.shape[0]
+    begin = pl.multiple_of(at_ref[2] * size, size)
+    part_ref[...] = shard_ref[pl.ds(begin, size), :]
 
 
 def shard_of(at, proj_in, proj_out):
@@ -595,7 +594,7 @@
         shard_kernel,
         out_shape=(
             jax.ShapeDtypeStruct((depth, columns), BF16),
-            jax.ShapeDtypeStruct((depth // 2, columns), BF16),
+            jax.ShapeDtypeStruct((depth // YS, columns), BF16),
         ),
         in_specs=[pl.BlockSpec(memory_space=pltpu.SMEM), vmem(), vmem()],
         out_specs=(vmem(), vmem()),
@@ -604,12 +603,24 @@
     )(at, proj_in, proj_out)
 
 
-def crossed(half):
-    return moved(half, lambda x, h, c, d, y: (x, 1 - h, c, ZLO - 1 - d, y))
-
-
-def gathered(part, groups):
-    return lax.all_gather(part, BOTH, axis_index_groups=groups, tiled=True)
+def crossed(part):
+    return moved(part, lambda x, h, c, d, y: (x, 1 - h, c, ZLO - 1 - d, y))
+
+
+def from_next(value):
+    return moved(value, lambda x, h, c, d, y: ((x + XS - 1) % XS, h, c, d, y))
+
+
+def from_last(value):
+    return moved(value, lambda x, h, c, d, y: ((x + 1) % XS, h, c, d, y))
+
+
+def along_x(shard):
+    half = shard.shape[0] // 2
+    plus, minus = from_next(shard), from_last(shard)
+    near = jnp.concatenate([shard, plus, minus], axis=0)
+    opposite = jnp.concatenate([from_next(plus[:half]), from_last(minus[half:])], axis=0)
+    return near, opposite
 
 
 def swapped(value):
@@ -643,23 +654,24 @@
     flat = features.reshape(images, height * across, channels)
     gain, bias = norm_gain.reshape(1, channels), norm_bias.reshape(1, channels)
     rows, batch = lax.axis_index("rows"), lax.axis_index("batch")
-    at = jnp.stack([(rows // CORES) % ZHI, rows % CORES, batch % YS, batch // YS])
+    at = jnp.stack([(rows // CORES) % ZHI, rows % CORES, batch % YS, batch // YS, rows // (ZHI * CORES)])
     at = at.astype(jnp.int32)
-    shard, half = shard_of(at, proj_in, proj_out)
-    own = gathered(shard, ALONG_X)
+    shard, part = shard_of(at, proj_in, proj_out)
+    own_near, own_far = along_x(shard)
     taps = conv_weight.reshape(LATENT, TAPS, channels).transpose(1, 0, 2)
     taps = jnp.pad(taps, ((0, 0), (0, SUB - LATENT), (0, 0))).reshape(TAPS * SUB, channels)
     taps_full = jnp.pad(taps, ((0, LANES - TAPS * SUB), (0, 0)))
 
     sums = group_stats(flat, peers)
     stats = lax.all_to_all(sums, "rows", 0, 0, tiled=True)
-    cross, stats = lax.optimization_barrier((crossed(half), stats))
-    cross = jnp.broadcast_to(cross[None], (2 * XS, *cross.shape))
-    cross = exchanged(cross, ALONG_PAIR).reshape(own.shape)
+    cross, stats = lax.optimization_barrier((crossed(part), stats))
+    cross = jnp.broadcast_to(cross[None], (XS * YS, *cross.shape))
+    cross = exchanged(cross, SHEET).reshape(-1, shard.shape[1])
     lat, up, down, mean, inv = conv_forward(stats, flat, gain, bias, taps, across, members)
     above, below = neighbours(up, down)
-    cross, own, above, below = lax.optimization_barrier((cross, own, above, below))
-    pieces = [own, cross, swapped(own), swapped(cross)]
+    cross, own_near, own_far, above, below = lax.optimization_barrier((cross, own_near, own_far, above, below))
+    pieces = [own_near, own_far, cross]
+    pieces = pieces + [swapped(v) for v in pieces]
     target = targets.reshape(-1, align)
     embed_part, grad_lat = projector(
         at, lat, below, above, target, embed_weight, embed_bias.reshape(1, -1),

time: 197 us -> 179 us (0.909)
  waiting for transfers between devices: 55.8 us -> 28.6 us
  starting transfers between devices: 66.3 us -> 81.3 us
  between operations: 14.3 us -> 0.98 us
  local copies, waits for them, and re-layouts: 6.01 us -> 9.62 us
  other arithmetic: 0.08 us -> 2.37 us
    ppermute x3 -> x8, waiting for transfers between devices: 26.3 us -> 10.5 us  [moved(): return lax.ppermute(value, ('rows', 'batch'), pairs)]
    ppermute x3 -> x8, starting transfers between devices: 13.1 us -> 26.7 us  [moved(): return lax.ppermute(value, ('rows', 'batch'), pairs)]
    all_to_all x2, waiting for transfers between devices: 16.6 us -> 6.14 us  [exchanged(): lax.all_to_all(value, BOTH, 0, 0, axis_index_groups=groups, tiled=True)]
    concatenate x0 -> x2, other arithmetic: none -> 2.37 us  [the longest x1 2.34 us: along_x(): near = jnp.concatenate([shard, plus, minus], axis=0)]
    unnamed x27 -> x25, local copies, waits for them, and re-layouts: 4.58 us -> 5.37 us
  transfers between devices with their start and end apart: 11 -> 15, of which waited for: 7 -> 5; matrix products, arithmetic and copies ran while one was open for 1% -> 4% of each run, Pallas kernels for 2% -> 2%
where the time goes in v7:
time: 179 us; the launch traced here: 178 us
  starting transfers between devices  81.3 us (45%)
  blocking collectives  34.2 us (19%)
  waiting for transfers between devices  28.6 us (16%)
  Pallas kernels  20.5 us (11%)
  local copies, waits for them, and re-layouts  9.62 us (5%)
  other arithmetic  2.37 us (1%)
    all_to_all x2, blocking collectives, exchanged(): lax.all_to_all(value, BOTH, 0, 0, axis_index_groups=groups, tiled=True)  34.2 us
    ppermute x8, starting transfers between devices, moved(): return lax.ppermute(value, ('rows', 'batch'), pairs)  26.7 us
    all_to_all x1, starting transfers between devices, shards(): stats = lax.all_to_all(sums, 'rows', 0, 0, tiled=True)  19.1 us
    ppermute x2, starting transfers between devices, neighbours(): lax.ppermute(down, 'rows', forward)  17.9 us
    all_to_all x2, starting transfers between devices, exchanged(): lax.all_to_all(value, BOTH, 0, 0, axis_index_groups=groups, tiled=True)  13.1 us
    ppermute x2, waiting for transfers between devices, neighbours(): lax.ppermute(up, 'rows', backward)  11.9 us
    pallas_call x1, Pallas kernels, projector(): pl.pallas_call(lambda *refs: mlp_kernel(across, width, hidden, align, *re...  11.3 us
    ppermute x8, waiting for transfers between devices, moved(): return lax.ppermute(value, ('rows', 'batch'), pairs)  10.5 us
  transfers between devices with their start and end apart: 15, of which 5 were waited for; matrix products, arithmetic and copies ran while one was open for 4% of the time, Pallas kernels for 2%

profile of v7, /device:TPU:1, one launch (start us, length us, event | category | flops | bytes accessed | tf_op | source)
XLA Modules:
  0.0 177.5 jit_solution(8848884541284549000)
XLA Ops:
  3.1 19.1 %all-to-all-start = ((f32[16,8,128]{2,1,0:T(8,128)}), f32[16,8,128]{2,1,0:T(8,128)S(1)}, u32[]{:S(2)}, u32[]{:S(2)}) async-start(f32[16,8,128]{2,1,0:T(8,128)} %stats.1), calls=%async_computation | async-start | bytes 131072 | tf_op jit(solution)/shard_map/all_to_all | solution.py:666
  24.7 7.7 %collective-permute-start = (bf16[16,3584]{1,0:T(8,128)(2,1)S(1)}, bf16[16,3584]{1,0:T(8,128)(2,1)S(1)}, u32[]{:S(2)}, u32[]{:S(2)}) collective-permute-start(bf16[16,3584]{1,0:T(8,128)(2,1)S(1)} %get-tuple-element.29), channel_id=1, source_target_pairs={{0,92},{1,93},{2,94},{3,95},{4,88},{5,89},{6,90},{7,91},{8,84},{9,... | collective-permute-start | bytes 344072 | tf_op jit(solution)/shard_map/ppermute | solution.py:574
  32.4 4.3 %collective-permute-start.1 = (bf16[64,3584]{1,0:T(8,128)(2,1)S(1)}, bf16[64,3584]{1,0:T(8,128)(2,1)}, u32[]{:S(2)}, u32[]{:S(2)}) collective-permute-start(bf16[64,3584]{1,0:T(8,128)(2,1)S(1)} %get-tuple-element.33), channel_id=1, source_target_pairs={{0,384},{1,385},{2,386},{3,387},{4,388},{5,389},{6,390},{7,391},{8... | collective-permute-start | bytes 1376264 | tf_op jit(solution)/shard_map/ppermute | solution.py:574
  36.7 1.9 %collective-permute-start.2 = (bf16[64,3584]{1,0:T(8,128)(2,1)S(1)}, bf16[64,3584]{1,0:T(8,128)(2,1)}, u32[]{:S(2)}, u32[]{:S(2)}) collective-permute-start(bf16[64,3584]{1,0:T(8,128)(2,1)S(1)} %get-tuple-element.33), channel_id=1, source_target_pairs={{0,128},{1,129},{2,130},{3,131},{4,132},{5,133},{6,134},{7,135},{8... | collective-permute-start | bytes 1376264 | tf_op jit(solution)/shard_map/ppermute | solution.py:574
  39.5 4.8 %collective-permute-done = bf16[16,3584]{1,0:T(8,128)(2,1)S(1)} collective-permute-done((bf16[16,3584]{1,0:T(8,128)(2,1)S(1)}, bf16[16,3584]{1,0:T(8,128)(2,1)S(1)}, u32[]{:S(2)}, u32[]{:S(2)}) %collective-permute-start) | collective-permute-done | bytes 114720 | tf_op jit(solution)/shard_map/ppermute | solution.py:574
  45.7 6.7 %all-to-all-start.1 = ((bf16[16,16,3584]{2,1,0:T(8,128)(2,1)}), bf16[16,16,3584]{2,1,0:T(8,128)(2,1)S(1)}, u32[]{:S(2)}, u32[]{:S(2)}) async-start(bf16[16,16,3584]{2,1,0:T(8,128)(2,1)} %broadcast_in_dim.2), calls=%async_computation.1 | async-start | bytes 3670016 | tf_op jit(solution)/shard_map/all_to_all | solution.py:562
  53.6 2.6 %collective-permute-start.5 = (f32[8,768]{1,0:T(8,128)S(1)}, f32[8,768]{1,0:T(8,128)S(1)}, u32[]{:S(2)}, u32[]{:S(2)}) collective-permute-start(f32[8,768]{1,0:T(8,128)S(1)} %get-tuple-element.34), channel_id=1, source_target_pairs={{32,0},{64,32},{96,64},{128,96},{160,128},{192,160},{224,192},{256... | collective-permute-start | bytes 73736 | tf_op jit(solution)/shard_map/ppermute | solution.py:634
  56.3 11.6 %collective-permute-start.6 = (f32[8,768]{1,0:T(8,128)S(1)}, f32[8,768]{1,0:T(8,128)S(1)}, u32[]{:S(2)}, u32[]{:S(2)}) collective-permute-start(f32[8,768]{1,0:T(8,128)S(1)} %get-tuple-element.35), channel_id=1, source_target_pairs={{0,32},{32,64},{64,96},{96,128},{128,160},{160,192},{192,224},{224... | collective-permute-start | bytes 73736 | tf_op jit(solution)/shard_map/ppermute | solution.py:634
  68.9 4.5 %collective-permute-start.3 = (bf16[32,3584]{1,0:T(8,128)(2,1)S(1)}, bf16[32,3584]{1,0:T(8,128)(2,1)S(1)}, u32[]{:S(2)}, u32[]{:S(2)}) collective-permute-start(bf16[32,3584]{1,0:T(8,128)(2,1)S(1)} %slice.8), channel_id=1, source_target_pairs={{0,384},{1,385},{2,386},{3,387},{4,388},{5,389},{6,390},{7,391},{8... | collective-permute-start | bytes 688136 | tf_op jit(solution)/shard_map/ppermute | solution.py:574
  74.4 2.1 %collective-permute-start.4 = (bf16[32,3584]{1,0:T(8,128)(2,1)S(1)}, bf16[32,3584]{1,0:T(8,128)(2,1)S(1)}, u32[]{:S(2)}, u32[]{:S(2)}) collective-permute-start(bf16[32,3584]{1,0:T(8,128)(2,1)S(1)} %slice.9), channel_id=1, source_target_pairs={{0,128},{1,129},{2,130},{3,131},{4,132},{5,133},{6,134},{7,135},{8... | collective-permute-start | bytes 688136 | tf_op jit(solution)/shard_map/ppermute | solution.py:574
  76.5 2.3 %pad_maximum_fusion.refs_9_ = bf16[192,3584]{1,0:T(8,128)(2,1)} fusion(bf16[64,3584]{1,0:T(8,128)(2,1)} %collective-permute-done.2, bf16[64,3584]{1,0:T(8,128)(2,1)} %collective-permute-done.1, bf16[64,3584]{1,0:T(8,128)(2,1)S(1)} %get-tuple-element.33), kind=kLoop, calls=%fused_computation | loop fusion | flops 4128768 | bytes 2752512 | tf_op jit(solution)/shard_map/concatenate | solution.py:621
  78.8 3.7 %collective-permute-done.4 = bf16[32,3584]{1,0:T(8,128)(2,1)S(1)} collective-permute-done((bf16[32,3584]{1,0:T(8,128)(2,1)S(1)}, bf16[32,3584]{1,0:T(8,128)(2,1)S(1)}, u32[]{:S(2)}, u32[]{:S(2)}) %collective-permute-start.4) | collective-permute-done | bytes 229408 | tf_op jit(solution)/shard_map/ppermute | solution.py:574
  82.6 1.9 %collective-permute-start.9 = (bf16[256,3584]{1,0:T(8,128)(2,1)S(1)}, bf16[256,3584]{1,0:T(8,128)(2,1)S(1)}, u32[]{:S(2)}, u32[]{:S(2)}) collective-permute-start(bf16[256,3584]{1,0:T(8,128)(2,1)S(1)} %bitcast.22), channel_id=1, source_target_pairs={{0,32},{1,33},{2,34},{3,35},{4,36},{5,37},{6,38},{7,39},{8,40},{9,... | collective-permute-start | bytes 5505032 | tf_op jit(solution)/shard_map/ppermute | solution.py:574
  84.5 2.4 %collective-permute-start.7 = (bf16[192,3584]{1,0:T(8,128)(2,1)}, bf16[192,3584]{1,0:T(8,128)(2,1)S(1)}, u32[]{:S(2)}, u32[]{:S(2)}) collective-permute-start(bf16[192,3584]{1,0:T(8,128)(2,1)} %pad_maximum_fusion.refs_9_), channel_id=1, source_target_pairs={{0,32},{1,33},{2,34},{3,35},{4,36},{5,37},{6,38},{7,39},{8,40},{9,... | collective-permute-start | bytes 4128776 | tf_op jit(solution)/shard_map/ppermute | solution.py:574
  86.9 1.9 %collective-permute-start.8 = (bf16[64,3584]{1,0:T(8,128)(2,1)S(1)}, bf16[64,3584]{1,0:T(8,128)(2,1)S(1)}, u32[]{:S(2)}, u32[]{:S(2)}) collective-permute-start(bf16[64,3584]{1,0:T(8,128)(2,1)S(1)} %pad_maximum_fusion.1.refs_10_), channel_id=1, source_target_pairs={{0,32},{1,33},{2,34},{3,35},{4,36},{5,37},{6,38},{7,39},{8,40},{9,... | collective-permute-start | bytes 1376264 | tf_op jit(solution)/shard_map/ppermute | solution.py:574
  88.9 2.0 %collective-permute-done.8.refs_13_ = bf16[64,3584]{1,0:T(8,128)(2,1)S(1)} collective-permute-done((bf16[64,3584]{1,0:T(8,128)(2,1)S(1)}, bf16[64,3584]{1,0:T(8,128)(2,1)S(1)}, u32[]{:S(2)}, u32[]{:S(2)}) %collective-permute-start.8) | collective-permute-done | bytes 458784 | tf_op jit(solution)/shard_map/ppermute | solution.py:574
  93.2 11.3 %projector.1 = (f32[32,1024]{1,0:T(8,128)S(1)}, f32[8,768]{1,0:T(8,128)S(1)}) custom-call(s32[5]{0:T(128)S(1)} %stack.23.at_ref.refs_0_, f32[8,768]{1,0:T(8,128)S(1)} %get-tuple-element.31.refs_1_, f32[8,768]{1,0:T(8,128)S(1)} %collective-permute-done.6.refs_2_, f32[8,768]{1,0:T(8,128)S(1)} %collective-permute-done.5.refs_3_, bf16[192,768]{1,0:T(8,128)(2,1)S(1)} %bitcast.29, ...), custom_call_target="tpu_custom_call" | custom-call | flops 2818572288 | bytes 8388608 | tf_op jit(solution)/shard_map/projector/pallas_call | solution.py:303
  104.5 6.2 %collective-permute-start.10 = (f32[8,768]{1,0:T(8,128)S(1)}, f32[8,768]{1,0:T(8,128)S(1)}, u32[]{:S(2)}, u32[]{:S(2)}) collective-permute-start(f32[8,768]{1,0:T(8,128)S(1)} %get-tuple-element.41.refs_0_), channel_id=1, source_target_pairs={{0,32},{32,64},{64,96},{96,128},{128,160},{160,192},{192,224},{224... | collective-permute-start | bytes 73736 | tf_op jit(solution)/shard_map/ppermute | solution.py:634
  112.7 11.9 %collective-permute-done.11.refs_2_ = f32[8,768]{1,0:T(8,128)S(1)} collective-permute-done((f32[8,768]{1,0:T(8,128)S(1)}, f32[8,768]{1,0:T(8,128)S(1)}, u32[]{:S(2)}, u32[]{:S(2)}) %collective-permute-start.11) | collective-permute-done | bytes 24608 | tf_op jit(solution)/shard_map/ppermute | solution.py:634
  124.6 2.0 %back.1 = (bf16[32,32,128]{2,1,0:T(8,128)(2,1)S(1)}, f32[12,64,512]{2,1,0:T(8,128)S(1)}) custom-call(f32[8,768]{1,0:T(8,128)S(1)} %get-tuple-element.41.refs_0_, f32[8,768]{1,0:T(8,128)S(1)} %collective-permute-done.10.refs_1_, f32[8,768]{1,0:T(8,128)S(1)} %collective-permute-done.11.refs_2_, bf16[12,64,512]{2,1,0:T(8,128)(2,1)S(1)} %bitcast.20, ...), custom_call_target="tpu_custom_call" | custom-call | tf_op jit(solution)/shard_map/back/pallas_call | solution.py:400
  126.7 15.3 %all_to_all.25.got_ref = bf16[32,32,128]{2,1,0:T(8,128)(2,1)S(1)} all-to-all(bf16[32,32,128]{2,1,0:T(8,128)(2,1)S(1)} %get-tuple-element.45), channel_id=1, replica_groups={{0,32,1,33,2,34,3,35,128,160,129,161,130,162,131,163,256,288,257,289,25..., dimensions={0} | all-to-all | bytes 524288 | tf_op jit(solution)/shard_map/all_to_all | solution.py:562
  142.6 18.9 %all_to_all.26.got_ref = bf16[16,32,128]{2,1,0:T(8,128)(2,1)S(1)} all-to-all(bf16[16,32,128]{2,1,0:T(8,128)(2,1)S(1)} %plane.1), channel_id=1, replica_groups={{0,4,8,12,16,20,24,28,64,68,72,76,80,84,88,92},{32,36,40,44,48,52,56,60..., dimensions={0} | all-to-all | bytes 262144 | tf_op jit(solution)/shard_map/all_to_all | solution.py:562
  162.7 6.4 %all-to-all-start.4 = ((bf16[32,16,128]{2,1,0:T(8,128)(2,1)}), bf16[32,16,128]{2,1,0:T(8,128)(2,1)S(1)}, u32[]{:S(2)}, u32[]{:S(2)}) async-start(bf16[32,16,128]{2,1,0:T(8,128)(2,1)} %get-tuple-element.48), calls=%async_computation.4 | async-start | bytes 262144 | tf_op jit(solution)/shard_map/all_to_all | solution.py:562
  170.7 6.1 %all-to-all-done.4.got_ref = bf16[32,16,128]{2,1,0:T(8,128)(2,1)S(1)} async-done(((bf16[32,16,128]{2,1,0:T(8,128)(2,1)}), bf16[32,16,128]{2,1,0:T(8,128)(2,1)S(1)}, u32[]{:S(2)}, u32[]{:S(2)}) %all-to-all-start.4) | async-done | bytes 131104 | tf_op jit(solution)/shard_map/all_to_all | solution.py:562
  (52 shorter events, 18.8 us)
Async XLA Ops:
  0.6 1.1 copy-start
  3.1 41.2 %all-to-all-start = ((f32[16,8,128]{2,1,0:T(8,128)}), f32[16,8,128]{2,1,0:T(8,128)S(1)}, u32[]{:S(2)}, u32[]{:S(2)}) async-start(f32[16,8,128]{2,1,0:T(8,128)} %stats.1), calls=%async_computation | async-start | bytes 131072 | tf_op jit(solution)/shard_map/all_to_all | solution.py:666
  24.7 19.6 %collective-permute-start = (bf16[16,3584]{1,0:T(8,128)(2,1)S(1)}, bf16[16,3584]{1,0:T(8,128)(2,1)S(1)}, u32[]{:S(2)}, u32[]{:S(2)}) collective-permute-start(bf16[16,3584]{1,0:T(8,128)(2,1)S(1)} %get-tuple-element.29), channel_id=1, source_target_pairs={{0,92},{1,93},{2,94},{3,95},{4,88},{5,89},{6,90},{7,91},{8,84},{9,... | collective-permute-start | bytes 344072 | tf_op jit(solution)/shard_map/ppermute | solution.py:574
  32.4 35.6 %collective-permute-start.1 = (bf16[64,3584]{1,0:T(8,128)(2,1)S(1)}, bf16[64,3584]{1,0:T(8,128)(2,1)}, u32[]{:S(2)}, u32[]{:S(2)}) collective-permute-start(bf16[64,3584]{1,0:T(8,128)(2,1)S(1)} %get-tuple-element.33), channel_id=1, source_target_pairs={{0,384},{1,385},{2,386},{3,387},{4,388},{5,389},{6,390},{7,391},{8... | collective-permute-start | bytes 1376264 | tf_op jit(solution)/shard_map/ppermute | solution.py:574
  36.7 36.7 %collective-permute-start.2 = (bf16[64,3584]{1,0:T(8,128)(2,1)S(1)}, bf16[64,3584]{1,0:T(8,128)(2,1)}, u32[]{:S(2)}, u32[]{:S(2)}) collective-permute-start(bf16[64,3584]{1,0:T(8,128)(2,1)S(1)} %get-tuple-element.33), channel_id=1, source_target_pairs={{0,128},{1,129},{2,130},{3,131},{4,132},{5,133},{6,134},{7,135},{8... | collective-permute-start | bytes 1376264 | tf_op jit(solution)/shard_map/ppermute | solution.py:574
  45.7 6.7 %copy-start.1 = (bf16[12,2,32,512]{3,2,1,0:T(8,128)(2,1)S(1)}, bf16[12,2,32,512]{3,2,1,0:T(8,128)(2,1)}, u32[]{:S(2)}) copy-start(bf16[12,2,32,512]{3,2,1,0:T(8,128)(2,1)} %param.11) | copy-start | bytes 2359300
  45.7 6.8 %copy-start.5 = (f32[512]{0:T(512)S(1)}, f32[512]{0:T(512)}, u32[]{:S(2)}) copy-start(f32[512]{0:T(512)} %param.12) | copy-start | bytes 6148
  45.7 6.8 %copy-start.6 = (f32[512]{0:T(512)S(1)}, f32[512]{0:T(512)}, u32[]{:S(2)}) copy-start(f32[512]{0:T(512)} %param.13) | copy-start | bytes 6148
  45.7 36.9 %all-to-all-start.1 = ((bf16[16,16,3584]{2,1,0:T(8,128)(2,1)}), bf16[16,16,3584]{2,1,0:T(8,128)(2,1)S(1)}, u32[]{:S(2)}, u32[]{:S(2)}) async-start(bf16[16,16,3584]{2,1,0:T(8,128)(2,1)} %broadcast_in_dim.2), calls=%async_computation.1 | async-start | bytes 3670016 | tf_op jit(solution)/shard_map/all_to_all | solution.py:562
  53.6 28.9 %collective-permute-start.5 = (f32[8,768]{1,0:T(8,128)S(1)}, f32[8,768]{1,0:T(8,128)S(1)}, u32[]{:S(2)}, u32[]{:S(2)}) collective-permute-start(f32[8,768]{1,0:T(8,128)S(1)} %get-tuple-element.34), channel_id=1, source_target_pairs={{32,0},{64,32},{96,64},{128,96},{160,128},{192,160},{224,192},{256... | collective-permute-start | bytes 73736 | tf_op jit(solution)/shard_map/ppermute | solution.py:634
  56.3 26.3 %collective-permute-start.6 = (f32[8,768]{1,0:T(8,128)S(1)}, f32[8,768]{1,0:T(8,128)S(1)}, u32[]{:S(2)}, u32[]{:S(2)}) collective-permute-start(f32[8,768]{1,0:T(8,128)S(1)} %get-tuple-element.35), channel_id=1, source_target_pairs={{0,32},{32,64},{64,96},{96,128},{128,160},{160,192},{192,224},{224... | collective-permute-start | bytes 73736 | tf_op jit(solution)/shard_map/ppermute | solution.py:634
  68.9 9.9 %collective-permute-start.3 = (bf16[32,3584]{1,0:T(8,128)(2,1)S(1)}, bf16[32,3584]{1,0:T(8,128)(2,1)S(1)}, u32[]{:S(2)}, u32[]{:S(2)}) collective-permute-start(bf16[32,3584]{1,0:T(8,128)(2,1)S(1)} %slice.8), channel_id=1, source_target_pairs={{0,384},{1,385},{2,386},{3,387},{4,388},{5,389},{6,390},{7,391},{8... | collective-permute-start | bytes 688136 | tf_op jit(solution)/shard_map/ppermute | solution.py:574
  74.4 14.5 %copy-start.11 = (f32[768]{0:T(1024)S(1)}, f32[768]{0:T(1024)}, u32[]{:S(2)}) copy-start(f32[768]{0:T(1024)} %param.20) | copy-start | bytes 9220
  74.4 16.5 %copy-start.8 = (f32[16,1024]{1,0:T(8,128)S(1)}, f32[16,1024]{1,0:T(8,128)}, u32[]{:S(2)}) copy-start(f32[16,1024]{1,0:T(8,128)} %refs_5_.1) | copy-start | bytes 196612
  74.4 16.5 %copy-start.9 = (f32[2048]{0:T(1024)S(1)}, f32[2048]{0:T(1024)}, u32[]{:S(2)}) copy-start(f32[2048]{0:T(1024)} %param.18) | copy-start | bytes 24580
  74.4 16.5 %copy-start.10 = (f32[1024]{0:T(1024)S(1)}, f32[1024]{0:T(1024)}, u32[]{:S(2)}) copy-start(f32[1024]{0:T(1024)} %param.16) | copy-start | bytes 12292
  74.4 8.1 %collective-permute-start.4 = (bf16[32,3584]{1,0:T(8,128)(2,1)S(1)}, bf16[32,3584]{1,0:T(8,128)(2,1)S(1)}, u32[]{:S(2)}, u32[]{:S(2)}) collective-permute-start(bf16[32,3584]{1,0:T(8,128)(2,1)S(1)} %slice.9), channel_id=1, source_target_pairs={{0,128},{1,129},{2,130},{3,131},{4,132},{5,133},{6,134},{7,135},{8... | collective-permute-start | bytes 688136 | tf_op jit(solution)/shard_map/ppermute | solution.py:574
  82.6 8.3 %collective-permute-start.9 = (bf16[256,3584]{1,0:T(8,128)(2,1)S(1)}, bf16[256,3584]{1,0:T(8,128)(2,1)S(1)}, u32[]{:S(2)}, u32[]{:S(2)}) collective-permute-start(bf16[256,3584]{1,0:T(8,128)(2,1)S(1)} %bitcast.22), channel_id=1, source_target_pairs={{0,32},{1,33},{2,34},{3,35},{4,36},{5,37},{6,38},{7,39},{8,40},{9,... | collective-permute-start | bytes 5505032 | tf_op jit(solution)/shard_map/ppermute | solution.py:574
  84.5 6.4 %collective-permute-start.7 = (bf16[192,3584]{1,0:T(8,128)(2,1)}, bf16[192,3584]{1,0:T(8,128)(2,1)S(1)}, u32[]{:S(2)}, u32[]{:S(2)}) collective-permute-start(bf16[192,3584]{1,0:T(8,128)(2,1)} %pad_maximum_fusion.refs_9_), channel_id=1, source_target_pairs={{0,32},{1,33},{2,34},{3,35},{4,36},{5,37},{6,38},{7,39},{8,40},{9,... | collective-permute-start | bytes 4128776 | tf_op jit(solution)/shard_map/ppermute | solution.py:574
  86.9 4.0 %collective-permute-start.8 = (bf16[64,3584]{1,0:T(8,128)(2,1)S(1)}, bf16[64,3584]{1,0:T(8,128)(2,1)S(1)}, u32[]{:S(2)}, u32[]{:S(2)}) collective-permute-start(bf16[64,3584]{1,0:T(8,128)(2,1)S(1)} %pad_maximum_fusion.1.refs_10_), channel_id=1, source_target_pairs={{0,32},{1,33},{2,34},{3,35},{4,36},{5,37},{6,38},{7,39},{8,40},{9,... | collective-permute-start | bytes 1376264 | tf_op jit(solution)/shard_map/ppermute | solution.py:574
  90.9 1.3 copy-start.2
  104.5 8.2 %collective-permute-start.10 = (f32[8,768]{1,0:T(8,128)S(1)}, f32[8,768]{1,0:T(8,128)S(1)}, u32[]{:S(2)}, u32[]{:S(2)}) collective-permute-start(f32[8,768]{1,0:T(8,128)S(1)} %get-tuple-element.41.refs_0_), channel_id=1, source_target_pairs={{0,32},{32,64},{64,96},{96,128},{128,160},{160,192},{192,224},{224... | collective-permute-start | bytes 73736 | tf_op jit(solution)/shard_map/ppermute | solution.py:634
  110.8 13.9 %collective-permute-start.11 = (f32[8,768]{1,0:T(8,128)S(1)}, f32[8,768]{1,0:T(8,128)S(1)}, u32[]{:S(2)}, u32[]{:S(2)}) collective-permute-start(f32[8,768]{1,0:T(8,128)S(1)} %get-tuple-element.41.refs_0_), channel_id=1, source_target_pairs={{32,0},{64,32},{96,64},{128,96},{160,128},{192,160},{224,192},{256... | collective-permute-start | bytes 73736 | tf_op jit(solution)/shard_map/ppermute | solution.py:634
  162.7 14.1 %all-to-all-start.4 = ((bf16[32,16,128]{2,1,0:T(8,128)(2,1)}), bf16[32,16,128]{2,1,0:T(8,128)(2,1)S(1)}, u32[]{:S(2)}, u32[]{:S(2)}) async-start(bf16[32,16,128]{2,1,0:T(8,128)(2,1)} %get-tuple-element.48), calls=%async_computation.4 | async-start | bytes 262144 | tf_op jit(solution)/shard_map/all_to_all | solution.py:562
  (3 other events, 2.8 us)

commit v8 on v7

--- a/solution.py
+++ b/solution.py
@@ -253,11 +253,10 @@
     for copy in copies:
         copy.wait()
 
-    step = 512
+    step = 1024
     acc[...] = jnp.zeros_like(acc)
 
-    @pl.loop(0, hidden // step)
-    def _(tile):
+    for tile in range(hidden // step):
         at = pl.ds(pl.multiple_of(tile * step, step), step)
         h = nn(emb[...], w_in[:, at]) + pib_ref[:, at]
         pre[:, at] = h
@@ -272,8 +271,7 @@
     grad_out = (-inv_len * (unit_target - cosine * unit_proj)).astype(BF16)
     grad_emb[...] = jnp.zeros_like(grad_emb)
 
-    @pl.loop(0, hidden // step)
-    def _(tile):
+    for tile in range(hidden // step):
         at = pl.ds(pl.multiple_of(tile * step, step), step)
         back = nt(grad_out, w_out[at, :])
         h = pre[:, at]
@@ -664,14 +662,16 @@
 
     sums = group_stats(flat, peers)
     stats = lax.all_to_all(sums, "rows", 0, 0, tiled=True)
-    cross, stats = lax.optimization_barrier((crossed(part), stats))
+    cross, stats, own_near, own_far = lax.optimization_barrier((crossed(part), stats, own_near, own_far))
     cross = jnp.broadcast_to(cross[None], (XS * YS, *cross.shape))
     cross = exchanged(cross, SHEET).reshape(-1, shard.shape[1])
     lat, up, down, mean, inv = conv_forward(stats, flat, gain, bias, taps, across, members)
     above, below = neighbours(up, down)
-    cross, own_near, own_far, above, below = lax.optimization_barrier((cross, own_near, own_far, above, below))
+    own_near, own_far, above, below = lax.optimization_barrier((own_near, own_far, above, below))
     pieces = [own_near, own_far, cross]
-    pieces = pieces + [swapped(v) for v in pieces]
+    others = [swapped(own_near), swapped(own_far)]
+    cross, others = lax.optimization_barrier((cross, others))
+    pieces = [own_near, own_far, cross] + others + [swapped(cross)]
     target = targets.reshape(-1, align)
     embed_part, grad_lat = projector(
         at, lat, below, above, target, embed_weight, embed_bias.reshape(1, -1),

time: 179 us -> 187 us (1.045)
  blocking collectives: 34.2 us -> 39.4 us
  local copies, waits for them, and re-layouts: 9.62 us -> 12 us
  Pallas kernels: 20.5 us -> 18.5 us
  waiting for transfers between devices: 28.6 us -> 30.6 us
    all_to_all x1, starting transfers between devices: 19.1 us -> 9.61 us  [shards(): stats = lax.all_to_all(sums, 'rows', 0, 0, tiled=True)]
    ppermute x8, starting transfers between devices: 26.7 us -> 33.8 us  [moved(): return lax.ppermute(value, ('rows', 'batch'), pairs)]
    all_to_all x2, blocking collectives: 34.2 us -> 39.4 us  [exchanged(): lax.all_to_all(value, BOTH, 0, 0, axis_index_groups=groups, tiled=True)]
    ppermute x2, starting transfers between devices: 17.9 us -> 23.1 us  [neighbours(): lax.ppermute(down, 'rows', forward)]
    unnamed x25 -> x35, local copies, waits for them, and re-layouts: 5.37 us -> 9.6 us
    all_to_all x2, starting transfers between devices: 13.1 us -> 10.8 us  [exchanged(): lax.all_to_all(value, BOTH, 0, 0, axis_index_groups=groups, tiled=True)]
    pallas_call x1, Pallas kernels: 11.3 us -> 9.29 us  [projector(): pl.pallas_call(lambda *refs: mlp_kernel(across, width, hidden, align, *re...]
  transfers between devices with their start and end apart: 15 -> 15, of which waited for: 5 -> 7; matrix products, arithmetic and copies ran while one was open for 4% -> 1% of each run, Pallas kernels for 2% -> 2%
where the time goes in v8:
time: 187 us; the launch traced here: 186 us
  starting transfers between devices  82.8 us (44%)
  blocking collectives  39.4 us (21%)
  waiting for transfers between devices  30.6 us (16%)
  Pallas kernels  18.5 us (10%)
  local copies, waits for them, and re-layouts  12 us (6%)
    all_to_all x2, blocking collectives, exchanged(): lax.all_to_all(value, BOTH, 0, 0, axis_index_groups=groups, tiled=True)  39.4 us
    ppermute x8, starting transfers between devices, moved(): return lax.ppermute(value, ('rows', 'batch'), pairs)  33.8 us
    ppermute x2, starting transfers between devices, neighbours(): lax.ppermute(down, 'rows', forward)  23.1 us
    ppermute x2, waiting for transfers between devices, neighbours(): lax.ppermute(up, 'rows', backward)  11.9 us
    ppermute x8, waiting for transfers between devices, moved(): return lax.ppermute(value, ('rows', 'batch'), pairs)  11.6 us
    all_to_all x2, starting transfers between devices, exchanged(): lax.all_to_all(value, BOTH, 0, 0, axis_index_groups=groups, tiled=True)  10.8 us
    all_to_all x1, starting transfers between devices, shards(): stats = lax.all_to_all(sums, 'rows', 0, 0, tiled=True)  9.61 us
    unnamed x35, local copies, waits for them, and re-layouts  9.6 us
  transfers between devices with their start and end apart: 15, of which 7 were waited for; matrix products, arithmetic and copies ran while one was open for 1% of the time, Pallas kernels for 2%

profile of v8, /device:TPU:1, one launch (start us, length us, event | category | flops | bytes accessed | tf_op | source)
XLA Modules:
  0.0 185.6 jit_solution(4614113664360175426)
XLA Ops:
  3.2 5.2 %collective-permute-start.1 = (bf16[64,3584]{1,0:T(8,128)(2,1)S(1)}, bf16[64,3584]{1,0:T(8,128)(2,1)S(1)}, u32[]{:S(2)}, u32[]{:S(2)}) collective-permute-start(bf16[64,3584]{1,0:T(8,128)(2,1)S(1)} %get-tuple-element.34), channel_id=1, source_target_pairs={{0,384},{1,385},{2,386},{3,387},{4,388},{5,389},{6,390},{7,391},{8... | collective-permute-start | bytes 1376264 | tf_op jit(solution)/shard_map/ppermute | solution.py:572
  8.5 1.9 %collective-permute-start.2 = (bf16[64,3584]{1,0:T(8,128)(2,1)S(1)}, bf16[64,3584]{1,0:T(8,128)(2,1)S(1)}, u32[]{:S(2)}, u32[]{:S(2)}) collective-permute-start(bf16[64,3584]{1,0:T(8,128)(2,1)S(1)} %get-tuple-element.34), channel_id=1, source_target_pairs={{0,128},{1,129},{2,130},{3,131},{4,132},{5,133},{6,134},{7,135},{8... | collective-permute-start | bytes 1376264 | tf_op jit(solution)/shard_map/ppermute | solution.py:572
  10.4 11.1 %collective-permute-start = (bf16[16,3584]{1,0:T(8,128)(2,1)S(1)}, bf16[16,3584]{1,0:T(8,128)(2,1)S(1)}, u32[]{:S(2)}, u32[]{:S(2)}) collective-permute-start(bf16[16,3584]{1,0:T(8,128)(2,1)S(1)} %get-tuple-element.33), channel_id=1, source_target_pairs={{0,92},{1,93},{2,94},{3,95},{4,88},{5,89},{6,90},{7,91},{8,84},{9,... | collective-permute-start | bytes 344072 | tf_op jit(solution)/shard_map/ppermute | solution.py:572
  24.0 9.6 %all-to-all-start = ((f32[16,8,128]{2,1,0:T(8,128)}), f32[16,8,128]{2,1,0:T(8,128)S(1)}, u32[]{:S(2)}, u32[]{:S(2)}) async-start(f32[16,8,128]{2,1,0:T(8,128)} %stats.1), calls=%async_computation | async-start | bytes 131072 | tf_op jit(solution)/shard_map/all_to_all | solution.py:664
  34.5 4.5 %collective-permute-start.3 = (bf16[32,3584]{1,0:T(8,128)(2,1)S(1)}, bf16[32,3584]{1,0:T(8,128)(2,1)S(1)}, u32[]{:S(2)}, u32[]{:S(2)}) collective-permute-start(bf16[32,3584]{1,0:T(8,128)(2,1)S(1)} %slice.8), channel_id=1, source_target_pairs={{0,384},{1,385},{2,386},{3,387},{4,388},{5,389},{6,390},{7,391},{8... | collective-permute-start | bytes 688136 | tf_op jit(solution)/shard_map/ppermute | solution.py:572
  39.0 1.9 %collective-permute-start.4 = (bf16[32,3584]{1,0:T(8,128)(2,1)S(1)}, bf16[32,3584]{1,0:T(8,128)(2,1)S(1)}, u32[]{:S(2)}, u32[]{:S(2)}) collective-permute-start(bf16[32,3584]{1,0:T(8,128)(2,1)S(1)} %slice.9), channel_id=1, source_target_pairs={{0,128},{1,129},{2,130},{3,131},{4,132},{5,133},{6,134},{7,135},{8... | collective-permute-start | bytes 688136 | tf_op jit(solution)/shard_map/ppermute | solution.py:572
  43.6 5.4 %collective-permute-done.4 = bf16[32,3584]{1,0:T(8,128)(2,1)S(1)} collective-permute-done((bf16[32,3584]{1,0:T(8,128)(2,1)S(1)}, bf16[32,3584]{1,0:T(8,128)(2,1)S(1)}, u32[]{:S(2)}, u32[]{:S(2)}) %collective-permute-start.4) | collective-permute-done | bytes 229408 | tf_op jit(solution)/shard_map/ppermute | solution.py:572
  50.5 4.4 %all-to-all-start.1 = ((bf16[16,16,3584]{2,1,0:T(8,128)(2,1)}), bf16[16,16,3584]{2,1,0:T(8,128)(2,1)S(1)}, u32[]{:S(2)}, u32[]{:S(2)}) async-start(bf16[16,16,3584]{2,1,0:T(8,128)(2,1)} %broadcast_in_dim.2), calls=%async_computation.1 | async-start | bytes 3670016 | tf_op jit(solution)/shard_map/all_to_all | solution.py:560
  56.2 3.7 %collective-permute-start.5 = (f32[8,768]{1,0:T(8,128)S(1)}, f32[8,768]{1,0:T(8,128)S(1)}, u32[]{:S(2)}, u32[]{:S(2)}) collective-permute-start(f32[8,768]{1,0:T(8,128)S(1)} %get-tuple-element.39), channel_id=1, source_target_pairs={{32,0},{64,32},{96,64},{128,96},{160,128},{192,160},{224,192},{256... | collective-permute-start | bytes 73736 | tf_op jit(solution)/shard_map/ppermute | solution.py:632
  59.9 11.4 %collective-permute-start.6 = (f32[8,768]{1,0:T(8,128)S(1)}, f32[8,768]{1,0:T(8,128)S(1)}, u32[]{:S(2)}, u32[]{:S(2)}) collective-permute-start(f32[8,768]{1,0:T(8,128)S(1)} %get-tuple-element.40), channel_id=1, source_target_pairs={{0,32},{32,64},{64,96},{96,128},{128,160},{160,192},{192,224},{224... | collective-permute-start | bytes 73736 | tf_op jit(solution)/shard_map/ppermute | solution.py:632
  72.2 1.9 %collective-permute-start.7 = (bf16[192,3584]{1,0:T(8,128)(2,1)S(1)}, bf16[192,3584]{1,0:T(8,128)(2,1)S(1)}, u32[]{:S(2)}, u32[]{:S(2)}) collective-permute-start(bf16[192,3584]{1,0:T(8,128)(2,1)S(1)} %copy-done.2), channel_id=1, source_target_pairs={{0,32},{1,33},{2,34},{3,35},{4,36},{5,37},{6,38},{7,39},{8,40},{9,... | collective-permute-start | bytes 4128776 | tf_op jit(solution)/shard_map/ppermute | solution.py:572
  74.1 2.4 %collective-permute-start.8 = (bf16[64,3584]{1,0:T(8,128)(2,1)S(1)}, bf16[64,3584]{1,0:T(8,128)(2,1)S(1)}, u32[]{:S(2)}, u32[]{:S(2)}) collective-permute-start(bf16[64,3584]{1,0:T(8,128)(2,1)S(1)} %pad_maximum_fusion.1.refs_10_), channel_id=1, source_target_pairs={{0,32},{1,33},{2,34},{3,35},{4,36},{5,37},{6,38},{7,39},{8,40},{9,... | collective-permute-start | bytes 1376264 | tf_op jit(solution)/shard_map/ppermute | solution.py:572
  79.8 4.8 %collective-permute-start.9 = (bf16[256,3584]{1,0:T(8,128)(2,1)S(1)}, bf16[256,3584]{1,0:T(8,128)(2,1)S(1)}, u32[]{:S(2)}, u32[]{:S(2)}) collective-permute-start(bf16[256,3584]{1,0:T(8,128)(2,1)S(1)} %bitcast.22), channel_id=1, source_target_pairs={{0,32},{1,33},{2,34},{3,35},{4,36},{5,37},{6,38},{7,39},{8,40},{9,... | collective-permute-start | bytes 5505032 | tf_op jit(solution)/shard_map/ppermute | solution.py:572
  84.6 3.4 %collective-permute-done.9.refs_14_ = bf16[256,3584]{1,0:T(8,128)(2,1)S(1)} collective-permute-done((bf16[256,3584]{1,0:T(8,128)(2,1)S(1)}, bf16[256,3584]{1,0:T(8,128)(2,1)S(1)}, u32[]{:S(2)}, u32[]{:S(2)}) %collective-permute-start.9) | collective-permute-done | bytes 1835040 | tf_op jit(solution)/shard_map/ppermute | solution.py:572
  92.6 9.3 %projector.1 = (f32[32,1024]{1,0:T(8,128)S(1)}, f32[8,768]{1,0:T(8,128)S(1)}) custom-call(s32[5]{0:T(128)S(1)} %stack.23.at_ref.refs_0_, f32[8,768]{1,0:T(8,128)S(1)} %get-tuple-element.36.refs_1_, f32[8,768]{1,0:T(8,128)S(1)} %collective-permute-done.6.refs_2_, f32[8,768]{1,0:T(8,128)S(1)} %collective-permute-done.5.refs_3_, bf16[192,768]{1,0:T(8,128)(2,1)S(1)} %bitcast.29, ...), custom_call_target="tpu_custom_call" | custom-call | flops 2818572288 | bytes 8388608 | tf_op jit(solution)/shard_map/projector/pallas_call | solution.py:301
  101.9 11.7 %collective-permute-start.10 = (f32[8,768]{1,0:T(8,128)S(1)}, f32[8,768]{1,0:T(8,128)S(1)}, u32[]{:S(2)}, u32[]{:S(2)}) collective-permute-start(f32[8,768]{1,0:T(8,128)S(1)} %get-tuple-element.49.refs_0_), channel_id=1, source_target_pairs={{0,32},{32,64},{64,96},{96,128},{128,160},{160,192},{192,224},{224... | collective-permute-start | bytes 73736 | tf_op jit(solution)/shard_map/ppermute | solution.py:632
  113.6 1.9 %collective-permute-start.11 = (f32[8,768]{1,0:T(8,128)S(1)}, f32[8,768]{1,0:T(8,128)S(1)}, u32[]{:S(2)}, u32[]{:S(2)}) collective-permute-start(f32[8,768]{1,0:T(8,128)S(1)} %get-tuple-element.49.refs_0_), channel_id=1, source_target_pairs={{32,0},{64,32},{96,64},{128,96},{160,128},{192,160},{224,192},{256... | collective-permute-start | bytes 73736 | tf_op jit(solution)/shard_map/ppermute | solution.py:632
  115.6 11.9 %collective-permute-done.11.refs_2_ = f32[8,768]{1,0:T(8,128)S(1)} collective-permute-done((f32[8,768]{1,0:T(8,128)S(1)}, f32[8,768]{1,0:T(8,128)S(1)}, u32[]{:S(2)}, u32[]{:S(2)}) %collective-permute-start.11) | collective-permute-done | bytes 24608 | tf_op jit(solution)/shard_map/ppermute | solution.py:632
  127.5 2.0 %back.1 = (bf16[32,32,128]{2,1,0:T(8,128)(2,1)S(1)}, f32[12,64,512]{2,1,0:T(8,128)S(1)}) custom-call(f32[8,768]{1,0:T(8,128)S(1)} %get-tuple-element.49.refs_0_, f32[8,768]{1,0:T(8,128)S(1)} %collective-permute-done.10.refs_1_, f32[8,768]{1,0:T(8,128)S(1)} %collective-permute-done.11.refs_2_, bf16[12,64,512]{2,1,0:T(8,128)(2,1)S(1)} %bitcast.20, ...), custom_call_target="tpu_custom_call" | custom-call | tf_op jit(solution)/shard_map/back/pallas_call | solution.py:398
  129.5 15.0 %all_to_all.25.got_ref = bf16[32,32,128]{2,1,0:T(8,128)(2,1)S(1)} all-to-all(bf16[32,32,128]{2,1,0:T(8,128)(2,1)S(1)} %get-tuple-element.53), channel_id=1, replica_groups={{0,32,1,33,2,34,3,35,128,160,129,161,130,162,131,163,256,288,257,289,25..., dimensions={0} | all-to-all | bytes 524288 | tf_op jit(solution)/shard_map/all_to_all | solution.py:560
  145.2 24.4 %all_to_all.26.got_ref = bf16[16,32,128]{2,1,0:T(8,128)(2,1)S(1)} all-to-all(bf16[16,32,128]{2,1,0:T(8,128)(2,1)S(1)} %plane.1), channel_id=1, replica_groups={{0,4,8,12,16,20,24,28,64,68,72,76,80,84,88,92},{32,36,40,44,48,52,56,60..., dimensions={0} | all-to-all | bytes 262144 | tf_op jit(solution)/shard_map/all_to_all | solution.py:560
  170.8 6.4 %all-to-all-start.4 = ((bf16[32,16,128]{2,1,0:T(8,128)(2,1)}), bf16[32,16,128]{2,1,0:T(8,128)(2,1)S(1)}, u32[]{:S(2)}, u32[]{:S(2)}) async-start(bf16[32,16,128]{2,1,0:T(8,128)(2,1)} %get-tuple-element.56), calls=%async_computation.4 | async-start | bytes 262144 | tf_op jit(solution)/shard_map/all_to_all | solution.py:560
  177.1 1.6 last.1
  178.8 6.1 %all-to-all-done.4.got_ref = bf16[32,16,128]{2,1,0:T(8,128)(2,1)S(1)} async-done(((bf16[32,16,128]{2,1,0:T(8,128)(2,1)}), bf16[32,16,128]{2,1,0:T(8,128)(2,1)S(1)}, u32[]{:S(2)}, u32[]{:S(2)}) %all-to-all-start.4) | async-done | bytes 131104 | tf_op jit(solution)/shard_map/all_to_all | solution.py:560
  (62 shorter events, 22.6 us)
Async XLA Ops:
  3.2 31.2 %collective-permute-start.1 = (bf16[64,3584]{1,0:T(8,128)(2,1)S(1)}, bf16[64,3584]{1,0:T(8,128)(2,1)S(1)}, u32[]{:S(2)}, u32[]{:S(2)}) collective-permute-start(bf16[64,3584]{1,0:T(8,128)(2,1)S(1)} %get-tuple-element.34), channel_id=1, source_target_pairs={{0,384},{1,385},{2,386},{3,387},{4,388},{5,389},{6,390},{7,391},{8... | collective-permute-start | bytes 1376264 | tf_op jit(solution)/shard_map/ppermute | solution.py:572
  8.5 30.5 %collective-permute-start.2 = (bf16[64,3584]{1,0:T(8,128)(2,1)S(1)}, bf16[64,3584]{1,0:T(8,128)(2,1)S(1)}, u32[]{:S(2)}, u32[]{:S(2)}) collective-permute-start(bf16[64,3584]{1,0:T(8,128)(2,1)S(1)} %get-tuple-element.34), channel_id=1, source_target_pairs={{0,128},{1,129},{2,130},{3,131},{4,132},{5,133},{6,134},{7,135},{8... | collective-permute-start | bytes 1376264 | tf_op jit(solution)/shard_map/ppermute | solution.py:572
  10.4 38.6 %collective-permute-start = (bf16[16,3584]{1,0:T(8,128)(2,1)S(1)}, bf16[16,3584]{1,0:T(8,128)(2,1)S(1)}, u32[]{:S(2)}, u32[]{:S(2)}) collective-permute-start(bf16[16,3584]{1,0:T(8,128)(2,1)S(1)} %get-tuple-element.33), channel_id=1, source_target_pairs={{0,92},{1,93},{2,94},{3,95},{4,88},{5,89},{6,90},{7,91},{8,84},{9,... | collective-permute-start | bytes 344072 | tf_op jit(solution)/shard_map/ppermute | solution.py:572
  24.0 25.1 %all-to-all-start = ((f32[16,8,128]{2,1,0:T(8,128)}), f32[16,8,128]{2,1,0:T(8,128)S(1)}, u32[]{:S(2)}, u32[]{:S(2)}) async-start(f32[16,8,128]{2,1,0:T(8,128)} %stats.1), calls=%async_computation | async-start | bytes 131072 | tf_op jit(solution)/shard_map/all_to_all | solution.py:664
  34.5 9.1 %collective-permute-start.3 = (bf16[32,3584]{1,0:T(8,128)(2,1)S(1)}, bf16[32,3584]{1,0:T(8,128)(2,1)S(1)}, u32[]{:S(2)}, u32[]{:S(2)}) collective-permute-start(bf16[32,3584]{1,0:T(8,128)(2,1)S(1)} %slice.8), channel_id=1, source_target_pairs={{0,384},{1,385},{2,386},{3,387},{4,388},{5,389},{6,390},{7,391},{8... | collective-permute-start | bytes 688136 | tf_op jit(solution)/shard_map/ppermute | solution.py:572
  39.0 10.0 %collective-permute-start.4 = (bf16[32,3584]{1,0:T(8,128)(2,1)S(1)}, bf16[32,3584]{1,0:T(8,128)(2,1)S(1)}, u32[]{:S(2)}, u32[]{:S(2)}) collective-permute-start(bf16[32,3584]{1,0:T(8,128)(2,1)S(1)} %slice.9), channel_id=1, source_target_pairs={{0,128},{1,129},{2,130},{3,131},{4,132},{5,133},{6,134},{7,135},{8... | collective-permute-start | bytes 688136 | tf_op jit(solution)/shard_map/ppermute | solution.py:572
  50.5 4.4 %copy-start.1 = (bf16[12,2,32,512]{3,2,1,0:T(8,128)(2,1)S(1)}, bf16[12,2,32,512]{3,2,1,0:T(8,128)(2,1)}, u32[]{:S(2)}) copy-start(bf16[12,2,32,512]{3,2,1,0:T(8,128)(2,1)} %param.11) | copy-start | bytes 2359300
  50.5 4.5 %copy-start.6 = (f32[512]{0:T(512)S(1)}, f32[512]{0:T(512)}, u32[]{:S(2)}) copy-start(f32[512]{0:T(512)} %param.12) | copy-start | bytes 6148
  50.5 4.5 %copy-start.7 = (f32[512]{0:T(512)S(1)}, f32[512]{0:T(512)}, u32[]{:S(2)}) copy-start(f32[512]{0:T(512)} %param.13) | copy-start | bytes 6148
  50.5 29.3 %all-to-all-start.1 = ((bf16[16,16,3584]{2,1,0:T(8,128)(2,1)}), bf16[16,16,3584]{2,1,0:T(8,128)(2,1)S(1)}, u32[]{:S(2)}, u32[]{:S(2)}) async-start(bf16[16,16,3584]{2,1,0:T(8,128)(2,1)} %broadcast_in_dim.2), calls=%async_computation.1 | async-start | bytes 3670016 | tf_op jit(solution)/shard_map/all_to_all | solution.py:560
  55.0 17.2 %copy-start.2 = (bf16[192,3584]{1,0:T(8,128)(2,1)S(1)}, bf16[192,3584]{1,0:T(8,128)(2,1)}, u32[]{:S(2)}) copy-start(bf16[192,3584]{1,0:T(8,128)(2,1)} %pad_maximum_fusion.refs_9_) | copy-start | bytes 4128772
  55.0 29.6 %copy-start.16 = (f32[768]{0:T(1024)S(1)}, f32[768]{0:T(1024)}, u32[]{:S(2)}) copy-start(f32[768]{0:T(1024)} %param.20) | copy-start | bytes 9220
  55.0 33.0 %copy-start.13 = (f32[16,1024]{1,0:T(8,128)S(1)}, f32[16,1024]{1,0:T(8,128)}, u32[]{:S(2)}) copy-start(f32[16,1024]{1,0:T(8,128)} %refs_5_.1) | copy-start | bytes 196612
  55.0 33.0 %copy-start.14 = (f32[2048]{0:T(1024)S(1)}, f32[2048]{0:T(1024)}, u32[]{:S(2)}) copy-start(f32[2048]{0:T(1024)} %param.18) | copy-start | bytes 24580
  55.0 32.9 %copy-start.15 = (f32[1024]{0:T(1024)S(1)}, f32[1024]{0:T(1024)}, u32[]{:S(2)}) copy-start(f32[1024]{0:T(1024)} %param.16) | copy-start | bytes 12292
  56.2 15.1 %collective-permute-start.5 = (f32[8,768]{1,0:T(8,128)S(1)}, f32[8,768]{1,0:T(8,128)S(1)}, u32[]{:S(2)}, u32[]{:S(2)}) collective-permute-start(f32[8,768]{1,0:T(8,128)S(1)} %get-tuple-element.39), channel_id=1, source_target_pairs={{32,0},{64,32},{96,64},{128,96},{160,128},{192,160},{224,192},{256... | collective-permute-start | bytes 73736 | tf_op jit(solution)/shard_map/ppermute | solution.py:632
  59.9 12.3 %collective-permute-start.6 = (f32[8,768]{1,0:T(8,128)S(1)}, f32[8,768]{1,0:T(8,128)S(1)}, u32[]{:S(2)}, u32[]{:S(2)}) collective-permute-start(f32[8,768]{1,0:T(8,128)S(1)} %get-tuple-element.40), channel_id=1, source_target_pairs={{0,32},{32,64},{64,96},{96,128},{128,160},{160,192},{192,224},{224... | collective-permute-start | bytes 73736 | tf_op jit(solution)/shard_map/ppermute | solution.py:632
  72.2 6.5 %collective-permute-start.7 = (bf16[192,3584]{1,0:T(8,128)(2,1)S(1)}, bf16[192,3584]{1,0:T(8,128)(2,1)S(1)}, u32[]{:S(2)}, u32[]{:S(2)}) collective-permute-start(bf16[192,3584]{1,0:T(8,128)(2,1)S(1)} %copy-done.2), channel_id=1, source_target_pairs={{0,32},{1,33},{2,34},{3,35},{4,36},{5,37},{6,38},{7,39},{8,40},{9,... | collective-permute-start | bytes 4128776 | tf_op jit(solution)/shard_map/ppermute | solution.py:572
  74.1 3.8 %collective-permute-start.8 = (bf16[64,3584]{1,0:T(8,128)(2,1)S(1)}, bf16[64,3584]{1,0:T(8,128)(2,1)S(1)}, u32[]{:S(2)}, u32[]{:S(2)}) collective-permute-start(bf16[64,3584]{1,0:T(8,128)(2,1)S(1)} %pad_maximum_fusion.1.refs_10_), channel_id=1, source_target_pairs={{0,32},{1,33},{2,34},{3,35},{4,36},{5,37},{6,38},{7,39},{8,40},{9,... | collective-permute-start | bytes 1376264 | tf_op jit(solution)/shard_map/ppermute | solution.py:572
  79.8 8.2 %collective-permute-start.9 = (bf16[256,3584]{1,0:T(8,128)(2,1)S(1)}, bf16[256,3584]{1,0:T(8,128)(2,1)S(1)}, u32[]{:S(2)}, u32[]{:S(2)}) collective-permute-start(bf16[256,3584]{1,0:T(8,128)(2,1)S(1)} %bitcast.22), channel_id=1, source_target_pairs={{0,32},{1,33},{2,34},{3,35},{4,36},{5,37},{6,38},{7,39},{8,40},{9,... | collective-permute-start | bytes 5505032 | tf_op jit(solution)/shard_map/ppermute | solution.py:572
  87.9 1.3 copy-start.3
  101.9 13.7 %collective-permute-start.10 = (f32[8,768]{1,0:T(8,128)S(1)}, f32[8,768]{1,0:T(8,128)S(1)}, u32[]{:S(2)}, u32[]{:S(2)}) collective-permute-start(f32[8,768]{1,0:T(8,128)S(1)} %get-tuple-element.49.refs_0_), channel_id=1, source_target_pairs={{0,32},{32,64},{64,96},{96,128},{128,160},{160,192},{192,224},{224... | collective-permute-start | bytes 73736 | tf_op jit(solution)/shard_map/ppermute | solution.py:632
  113.6 13.9 %collective-permute-start.11 = (f32[8,768]{1,0:T(8,128)S(1)}, f32[8,768]{1,0:T(8,128)S(1)}, u32[]{:S(2)}, u32[]{:S(2)}) collective-permute-start(f32[8,768]{1,0:T(8,128)S(1)} %get-tuple-element.49.refs_0_), channel_id=1, source_target_pairs={{32,0},{64,32},{96,64},{128,96},{160,128},{192,160},{224,192},{256... | collective-permute-start | bytes 73736 | tf_op jit(solution)/shard_map/ppermute | solution.py:632
  170.8 14.1 %all-to-all-start.4 = ((bf16[32,16,128]{2,1,0:T(8,128)(2,1)}), bf16[32,16,128]{2,1,0:T(8,128)(2,1)S(1)}, u32[]{:S(2)}, u32[]{:S(2)}) async-start(bf16[32,16,128]{2,1,0:T(8,128)(2,1)} %get-tuple-element.56), calls=%async_computation.4 | async-start | bytes 262144 | tf_op jit(solution)/shard_map/all_to_all | solution.py:560
  (8 other events, 8.2 us)

commit v9 on v8

--- a/solution.py
+++ b/solution.py
@@ -31,6 +31,10 @@
 
 def vmem():
     return pl.BlockSpec(memory_space=pltpu.VMEM)
+
+
+def in_hbm(v):
+    return pltpu.with_memory_space_constraint(v, pltpu.HBM)
 
 
 def sigmoid(v):
@@ -179,14 +183,15 @@
     across, width, hidden, align, at_ref, lat_ref, below_ref, above_ref, target_ref,
     ew_ref, eb_ref, pib_ref, pob_ref,
     own_near, own_far, cross, own_near_other, own_far_other, cross_other,
-    embed_ref, gl_ref, w_in, w_out, pre, emb, acc, grad_emb, sems,
+    embed_ref, gl_ref, w_in, w_out, pre, emb, acc, grad_emb, wanted, sems,
 ):
     zhi, core, x = at_ref[0], at_ref[1], at_ref[4]
     depth = width // (XS * ZHI * CORES)
     slab = hidden // (XS * ZHI * CORES)
     taken = PATCH * PATCH
     rows = taken * SUB
-    copies = []
+    copies = [pltpu.make_async_copy(target_ref, wanted, sems.at[0])]
+    copies[0].start()
 
     def place(piece, at, source_x, of_zhi, of_core, begin=0, size=depth):
         shard = lax.rem(source_x, XS) * (ZHI * CORES) + of_zhi * CORES + of_core
@@ -263,7 +268,7 @@
         acc[...] += nn((h * sigmoid(h)).astype(BF16), w_out[at, :])
 
     projected = acc[...] + pob_ref[...]
-    target = target_ref[...].astype(F32)
+    target = wanted[...].astype(F32)
     unit_target = target * lax.rsqrt(jnp.sum(target * target, axis=1, keepdims=True) + EPS_UNIT)
     inv_len = lax.rsqrt(jnp.sum(projected * projected, axis=1, keepdims=True) + EPS_UNIT)
     unit_proj = projected * inv_len
@@ -305,7 +310,9 @@
             jax.ShapeDtypeStruct(lat.shape, F32),
         ),
         in_specs=[pl.BlockSpec(memory_space=pltpu.SMEM)]
-        + [vmem()] * 8
+        + [vmem()] * 3
+        + [pl.BlockSpec(memory_space=pltpu.HBM)]
+        + [vmem()] * 4
         + [pl.BlockSpec(memory_space=pltpu.HBM)] * len(pieces),
         out_specs=(vmem(), vmem()),
         scratch_shapes=[
@@ -315,14 +322,15 @@
             pltpu.VMEM((tokens, width), BF16),
             pltpu.VMEM((tokens, align), F32),
             pltpu.VMEM((256, width), F32),
-            pltpu.SemaphoreType.DMA((54,)),
+            pltpu.VMEM((tokens, align), BF16),
+            pltpu.SemaphoreType.DMA((55,)),
         ],
         compiler_params=params(32),
         cost_estimate=pl.CostEstimate(
             flops=flops, bytes_accessed=8 << 20, transcendentals=2 * tokens * hidden
         ),
         name="projector",
-    )(at, lat, below, above, target, ew, eb, pib, pob, *pieces)
+    )(at, lat, below, above, in_hbm(target), ew, eb, pib, pob, in_hbm(pieces[0]), *pieces[1:])
 
 
 def back_kernel(
@@ -572,17 +580,27 @@
     return lax.ppermute(value, ("rows", "batch"), pairs)
 
 
-def shard_kernel(at_ref, in_ref, out_ref, shard_ref, part_ref):
+def shard_kernel(at_ref, in_ref, out_ref, shard_ref, part_ref, sems):
     depth, hidden = in_ref.shape
     align = out_ref.shape[1]
-    shard_ref[:, 0:hidden] = in_ref[...]
-    for part in range(out_ref.shape[0] // depth):
-        shard_ref[:, hidden + part * align : hidden + (part + 1) * align] = out_ref[
-            part * depth : (part + 1) * depth, :
-        ]
     size = part_ref.shape[0]
     begin = pl.multiple_of(at_ref[2] * size, size)
-    part_ref[...] = shard_ref[pl.ds(begin, size), :]
+    copies = []
+
+    def put(source, lines, into, columns):
+        copy = pltpu.make_async_copy(
+            source.at[lines], into.at[:, columns], sems.at[len(copies)]
+        )
+        copy.start()
+        copies.append(copy)
+
+    for into, first, count in ((part_ref, begin, size), (shard_ref, 0, depth)):
+        put(in_ref, pl.ds(first, count), into, pl.ds(0, hidden))
+        for part in range(out_ref.shape[0] // depth):
+            lines = pl.ds(part * depth + first, count)
+            put(out_ref, lines, into, pl.ds(hidden + part * align, align))
+    for copy in copies:
+        copy.wait()
 
 
 def shard_of(at, proj_in, proj_out):
@@ -594,11 +612,13 @@
             jax.ShapeDtypeStruct((depth, columns), BF16),
             jax.ShapeDtypeStruct((depth // YS, columns), BF16),
         ),
-        in_specs=[pl.BlockSpec(memory_space=pltpu.SMEM), vmem(), vmem()],
+        in_specs=[pl.BlockSpec(memory_space=pltpu.SMEM)]
+        + [pl.BlockSpec(memory_space=pltpu.HBM)] * 2,
         out_specs=(vmem(), vmem()),
+        scratch_shapes=[pltpu.SemaphoreType.DMA((6,))],
         compiler_params=params(),
         name="shard",
-    )(at, proj_in, proj_out)
+    )(at, in_hbm(proj_in), in_hbm(proj_out))
 
 
 def crossed(part):
@@ -662,16 +682,14 @@
 
     sums = group_stats(flat, peers)
     stats = lax.all_to_all(sums, "rows", 0, 0, tiled=True)
-    cross, stats, own_near, own_far = lax.optimization_barrier((crossed(part), stats, own_near, own_far))
+    cross, stats = lax.optimization_barrier((crossed(part), stats))
     cross = jnp.broadcast_to(cross[None], (XS * YS, *cross.shape))
     cross = exchanged(cross, SHEET).reshape(-1, shard.shape[1])
     lat, up, down, mean, inv = conv_forward(stats, flat, gain, bias, taps, across, members)
     above, below = neighbours(up, down)
-    own_near, own_far, above, below = lax.optimization_barrier((own_near, own_far, above, below))
+    cross, own_near, own_far, above, below = lax.optimization_barrier((cross, own_near, own_far, above, below))
     pieces = [own_near, own_far, cross]
-    others = [swapped(own_near), swapped(own_far)]
-    cross, others = lax.optimization_barrier((cross, others))
-    pieces = [own_near, own_far, cross] + others + [swapped(cross)]
+    pieces = pieces + [swapped(v) for v in pieces]
     target = targets.reshape(-1, align)
     embed_part, grad_lat = projector(
         at, lat, below, above, target, embed_weight, embed_bias.reshape(1, -1),

time: 187 us -> 174 us (0.930)
  local copies, waits for them, and re-layouts: 12 us -> 5.45 us
  blocking collectives: 39.4 us -> 34.4 us
  starting transfers between devices: 82.8 us -> 80.8 us
    all_to_all x1, starting transfers between devices: 9.61 us -> 19.1 us  [shards(): stats = lax.all_to_all(sums, 'rows', 0, 0, tiled=True)]
    unnamed x35 -> x17, local copies, waits for them, and re-layouts: 9.6 us -> 1.2 us
    ppermute x8, starting transfers between devices: 33.8 us -> 26.7 us  [moved(): return lax.ppermute(value, ('rows', 'batch'), pairs)]
    ppermute x2, starting transfers between devices: 23.1 us -> 17.3 us  [neighbours(): lax.ppermute(down, 'rows', forward)]
    all_to_all x2, blocking collectives: 39.4 us -> 34.4 us  [exchanged(): lax.all_to_all(value, BOTH, 0, 0, axis_index_groups=groups, tiled=True)]
    all_to_all x2, starting transfers between devices: 10.8 us -> 13.1 us  [exchanged(): lax.all_to_all(value, BOTH, 0, 0, axis_index_groups=groups, tiled=True)]
  transfers between devices with their start and end apart: 15 -> 15, of which waited for: 7 -> 5; matrix products, arithmetic and copies ran while one was open for 1% -> 4% of each run, Pallas kernels for 2% -> 3%
where the time goes in v9:
time: 174 us; the launch traced here: 173 us
  starting transfers between devices  80.8 us (46%)
  blocking collectives  34.4 us (20%)
  waiting for transfers between devices  29 us (17%)
  Pallas kernels  19.6 us (11%)
  local copies, waits for them, and re-layouts  5.45 us (3%)
  other arithmetic  2.37 us (1%)
    all_to_all x2, blocking collectives, exchanged(): lax.all_to_all(value, BOTH, 0, 0, axis_index_groups=groups, tiled=True)  34.4 us
    ppermute x8, starting transfers between devices, moved(): return lax.ppermute(value, ('rows', 'batch'), pairs)  26.7 us
    all_to_all x1, starting transfers between devices, shards(): stats = lax.all_to_all(sums, 'rows', 0, 0, tiled=True)  19.1 us
    ppermute x2, starting transfers between devices, neighbours(): lax.ppermute(down, 'rows', forward)  17.3 us
    all_to_all x2, starting transfers between devices, exchanged(): lax.all_to_all(value, BOTH, 0, 0, axis_index_groups=groups, tiled=True)  13.1 us
    ppermute x2, waiting for transfers between devices, neighbours(): lax.ppermute(up, 'rows', backward)  11.9 us
    ppermute x8, waiting for transfers between devices, moved(): return lax.ppermute(value, ('rows', 'batch'), pairs)  11 us
    pallas_call x1, Pallas kernels, projector(): pl.pallas_call(lambda *refs: mlp_kernel(across, width, hidden, align, *re...  9.27 us
  transfers between devices with their start and end apart: 15, of which 5 were waited for; matrix products, arithmetic and copies ran while one was open for 4% of the time, Pallas kernels for 3%

profile of v9, /device:TPU:1, one launch (start us, length us, event | category | flops | bytes accessed | tf_op | source)
XLA Modules:
  0.0 172.6 jit_solution(3370545209757194484)
XLA Ops:
  3.1 19.1 %all-to-all-start = ((f32[16,8,128]{2,1,0:T(8,128)}), f32[16,8,128]{2,1,0:T(8,128)S(1)}, u32[]{:S(2)}, u32[]{:S(2)}) async-start(f32[16,8,128]{2,1,0:T(8,128)} %stats.1), calls=%async_computation | async-start | bytes 131072 | tf_op jit(solution)/shard_map/all_to_all | solution.py:684
  23.9 7.7 %collective-permute-start = (bf16[16,3584]{1,0:T(8,128)(2,1)S(1)}, bf16[16,3584]{1,0:T(8,128)(2,1)S(1)}, u32[]{:S(2)}, u32[]{:S(2)}) collective-permute-start(bf16[16,3584]{1,0:T(8,128)(2,1)S(1)} %get-tuple-element.29), channel_id=1, source_target_pairs={{0,92},{1,93},{2,94},{3,95},{4,88},{5,89},{6,90},{7,91},{8,84},{9,... | collective-permute-start | bytes 344072 | tf_op jit(solution)/shard_map/ppermute | solution.py:580
  31.6 4.3 %collective-permute-start.1 = (bf16[64,3584]{1,0:T(8,128)(2,1)S(1)}, bf16[64,3584]{1,0:T(8,128)(2,1)}, u32[]{:S(2)}, u32[]{:S(2)}) collective-permute-start(bf16[64,3584]{1,0:T(8,128)(2,1)S(1)} %get-tuple-element.33), channel_id=1, source_target_pairs={{0,384},{1,385},{2,386},{3,387},{4,388},{5,389},{6,390},{7,391},{8... | collective-permute-start | bytes 1376264 | tf_op jit(solution)/shard_map/ppermute | solution.py:580
  35.9 1.9 %collective-permute-start.2 = (bf16[64,3584]{1,0:T(8,128)(2,1)S(1)}, bf16[64,3584]{1,0:T(8,128)(2,1)}, u32[]{:S(2)}, u32[]{:S(2)}) collective-permute-start(bf16[64,3584]{1,0:T(8,128)(2,1)S(1)} %get-tuple-element.33), channel_id=1, source_target_pairs={{0,128},{1,129},{2,130},{3,131},{4,132},{5,133},{6,134},{7,135},{8... | collective-permute-start | bytes 1376264 | tf_op jit(solution)/shard_map/ppermute | solution.py:580
  38.7 5.3 %collective-permute-done = bf16[16,3584]{1,0:T(8,128)(2,1)S(1)} collective-permute-done((bf16[16,3584]{1,0:T(8,128)(2,1)S(1)}, bf16[16,3584]{1,0:T(8,128)(2,1)S(1)}, u32[]{:S(2)}, u32[]{:S(2)}) %collective-permute-start) | collective-permute-done | bytes 114720 | tf_op jit(solution)/shard_map/ppermute | solution.py:580
  45.4 6.7 %all-to-all-start.1 = ((bf16[16,16,3584]{2,1,0:T(8,128)(2,1)}), bf16[16,16,3584]{2,1,0:T(8,128)(2,1)S(1)}, u32[]{:S(2)}, u32[]{:S(2)}) async-start(bf16[16,16,3584]{2,1,0:T(8,128)(2,1)} %broadcast_in_dim.2), calls=%async_computation.1 | async-start | bytes 3670016 | tf_op jit(solution)/shard_map/all_to_all | solution.py:568
  53.3 2.7 %collective-permute-start.5 = (f32[8,768]{1,0:T(8,128)S(1)}, f32[8,768]{1,0:T(8,128)S(1)}, u32[]{:S(2)}, u32[]{:S(2)}) collective-permute-start(f32[8,768]{1,0:T(8,128)S(1)} %get-tuple-element.34), channel_id=1, source_target_pairs={{32,0},{64,32},{96,64},{128,96},{160,128},{192,160},{224,192},{256... | collective-permute-start | bytes 73736 | tf_op jit(solution)/shard_map/ppermute | solution.py:652
  56.1 11.5 %collective-permute-start.6 = (f32[8,768]{1,0:T(8,128)S(1)}, f32[8,768]{1,0:T(8,128)S(1)}, u32[]{:S(2)}, u32[]{:S(2)}) collective-permute-start(f32[8,768]{1,0:T(8,128)S(1)} %get-tuple-element.35), channel_id=1, source_target_pairs={{0,32},{32,64},{64,96},{96,128},{128,160},{160,192},{192,224},{224... | collective-permute-start | bytes 73736 | tf_op jit(solution)/shard_map/ppermute | solution.py:652
  68.6 4.5 %collective-permute-start.3 = (bf16[32,3584]{1,0:T(8,128)(2,1)S(1)}, bf16[32,3584]{1,0:T(8,128)(2,1)S(1)}, u32[]{:S(2)}, u32[]{:S(2)}) collective-permute-start(bf16[32,3584]{1,0:T(8,128)(2,1)S(1)} %slice.8), channel_id=1, source_target_pairs={{0,384},{1,385},{2,386},{3,387},{4,388},{5,389},{6,390},{7,391},{8... | collective-permute-start | bytes 688136 | tf_op jit(solution)/shard_map/ppermute | solution.py:580
  74.1 2.1 %collective-permute-start.4 = (bf16[32,3584]{1,0:T(8,128)(2,1)S(1)}, bf16[32,3584]{1,0:T(8,128)(2,1)S(1)}, u32[]{:S(2)}, u32[]{:S(2)}) collective-permute-start(bf16[32,3584]{1,0:T(8,128)(2,1)S(1)} %slice.9), channel_id=1, source_target_pairs={{0,128},{1,129},{2,130},{3,131},{4,132},{5,133},{6,134},{7,135},{8... | collective-permute-start | bytes 688136 | tf_op jit(solution)/shard_map/ppermute | solution.py:580
  76.2 2.3 %pad_maximum_fusion.refs_9_ = bf16[192,3584]{1,0:T(8,128)(2,1)} fusion(bf16[64,3584]{1,0:T(8,128)(2,1)} %collective-permute-done.2, bf16[64,3584]{1,0:T(8,128)(2,1)} %collective-permute-done.1, bf16[64,3584]{1,0:T(8,128)(2,1)S(1)} %get-tuple-element.33), kind=kLoop, calls=%fused_computation | loop fusion | flops 4128768 | bytes 2752512 | tf_op jit(solution)/shard_map/concatenate | solution.py:639
  78.5 3.7 %collective-permute-done.4 = bf16[32,3584]{1,0:T(8,128)(2,1)S(1)} collective-permute-done((bf16[32,3584]{1,0:T(8,128)(2,1)S(1)}, bf16[32,3584]{1,0:T(8,128)(2,1)S(1)}, u32[]{:S(2)}, u32[]{:S(2)}) %collective-permute-start.4) | collective-permute-done | bytes 229408 | tf_op jit(solution)/shard_map/ppermute | solution.py:580
  82.3 1.9 %collective-permute-start.9 = (bf16[256,3584]{1,0:T(8,128)(2,1)S(1)}, bf16[256,3584]{1,0:T(8,128)(2,1)S(1)}, u32[]{:S(2)}, u32[]{:S(2)}) collective-permute-start(bf16[256,3584]{1,0:T(8,128)(2,1)S(1)} %bitcast.22), channel_id=1, source_target_pairs={{0,32},{1,33},{2,34},{3,35},{4,36},{5,37},{6,38},{7,39},{8,40},{9,... | collective-permute-start | bytes 5505032 | tf_op jit(solution)/shard_map/ppermute | solution.py:580
  84.2 2.4 %collective-permute-start.7 = (bf16[192,3584]{1,0:T(8,128)(2,1)}, bf16[192,3584]{1,0:T(8,128)(2,1)S(1)}, u32[]{:S(2)}, u32[]{:S(2)}) collective-permute-start(bf16[192,3584]{1,0:T(8,128)(2,1)} %pad_maximum_fusion.refs_9_), channel_id=1, source_target_pairs={{0,32},{1,33},{2,34},{3,35},{4,36},{5,37},{6,38},{7,39},{8,40},{9,... | collective-permute-start | bytes 4128776 | tf_op jit(solution)/shard_map/ppermute | solution.py:580
  86.6 1.9 %collective-permute-start.8 = (bf16[64,3584]{1,0:T(8,128)(2,1)S(1)}, bf16[64,3584]{1,0:T(8,128)(2,1)S(1)}, u32[]{:S(2)}, u32[]{:S(2)}) collective-permute-start(bf16[64,3584]{1,0:T(8,128)(2,1)S(1)} %pad_maximum_fusion.1.refs_10_), channel_id=1, source_target_pairs={{0,32},{1,33},{2,34},{3,35},{4,36},{5,37},{6,38},{7,39},{8,40},{9,... | collective-permute-start | bytes 1376264 | tf_op jit(solution)/shard_map/ppermute | solution.py:580
  88.6 2.0 %collective-permute-done.8.refs_13_ = bf16[64,3584]{1,0:T(8,128)(2,1)S(1)} collective-permute-done((bf16[64,3584]{1,0:T(8,128)(2,1)S(1)}, bf16[64,3584]{1,0:T(8,128)(2,1)S(1)}, u32[]{:S(2)}, u32[]{:S(2)}) %collective-permute-start.8) | collective-permute-done | bytes 458784 | tf_op jit(solution)/shard_map/ppermute | solution.py:580
  90.6 9.3 %projector.1 = (f32[32,1024]{1,0:T(8,128)S(1)}, f32[8,768]{1,0:T(8,128)S(1)}) custom-call(s32[5]{0:T(128)S(1)} %stack.23.at_ref.refs_0_, f32[8,768]{1,0:T(8,128)S(1)} %get-tuple-element.31.refs_1_, f32[8,768]{1,0:T(8,128)S(1)} %collective-permute-done.6.refs_2_, f32[8,768]{1,0:T(8,128)S(1)} %collective-permute-done.5.refs_3_, bf16[192,768]{1,0:T(8,128)(2,1)} %bitcast.33, ...), custom_call_target="tpu_custom_call" | custom-call | flops 2818572288 | bytes 8388608 | tf_op jit(solution)/shard_map/projector/pallas_call | solution.py:306
  99.9 5.7 %collective-permute-start.10 = (f32[8,768]{1,0:T(8,128)S(1)}, f32[8,768]{1,0:T(8,128)S(1)}, u32[]{:S(2)}, u32[]{:S(2)}) collective-permute-start(f32[8,768]{1,0:T(8,128)S(1)} %get-tuple-element.41.refs_0_), channel_id=1, source_target_pairs={{0,32},{32,64},{64,96},{96,128},{128,160},{160,192},{192,224},{224... | collective-permute-start | bytes 73736 | tf_op jit(solution)/shard_map/ppermute | solution.py:652
  107.6 11.9 %collective-permute-done.11.refs_2_ = f32[8,768]{1,0:T(8,128)S(1)} collective-permute-done((f32[8,768]{1,0:T(8,128)S(1)}, f32[8,768]{1,0:T(8,128)S(1)}, u32[]{:S(2)}, u32[]{:S(2)}) %collective-permute-start.11) | collective-permute-done | bytes 24608 | tf_op jit(solution)/shard_map/ppermute | solution.py:652
  119.5 2.0 %back.1 = (bf16[32,32,128]{2,1,0:T(8,128)(2,1)S(1)}, f32[12,64,512]{2,1,0:T(8,128)S(1)}) custom-call(f32[8,768]{1,0:T(8,128)S(1)} %get-tuple-element.41.refs_0_, f32[8,768]{1,0:T(8,128)S(1)} %collective-permute-done.10.refs_1_, f32[8,768]{1,0:T(8,128)S(1)} %collective-permute-done.11.refs_2_, bf16[12,64,512]{2,1,0:T(8,128)(2,1)S(1)} %bitcast.20, ...), custom_call_target="tpu_custom_call" | custom-call | tf_op jit(solution)/shard_map/back/pallas_call | solution.py:406
  121.6 15.3 %all_to_all.25.got_ref = bf16[32,32,128]{2,1,0:T(8,128)(2,1)S(1)} all-to-all(bf16[32,32,128]{2,1,0:T(8,128)(2,1)S(1)} %get-tuple-element.45), channel_id=1, replica_groups={{0,32,1,33,2,34,3,35,128,160,129,161,130,162,131,163,256,288,257,289,25..., dimensions={0} | all-to-all | bytes 524288 | tf_op jit(solution)/shard_map/all_to_all | solution.py:568
  137.5 19.0 %all_to_all.26.got_ref = bf16[16,32,128]{2,1,0:T(8,128)(2,1)S(1)} all-to-all(bf16[16,32,128]{2,1,0:T(8,128)(2,1)S(1)} %plane.1), channel_id=1, replica_groups={{0,4,8,12,16,20,24,28,64,68,72,76,80,84,88,92},{32,36,40,44,48,52,56,60..., dimensions={0} | all-to-all | bytes 262144 | tf_op jit(solution)/shard_map/all_to_all | solution.py:568
  157.7 6.4 %all-to-all-start.4 = ((bf16[32,16,128]{2,1,0:T(8,128)(2,1)}), bf16[32,16,128]{2,1,0:T(8,128)(2,1)S(1)}, u32[]{:S(2)}, u32[]{:S(2)}) async-start(bf16[32,16,128]{2,1,0:T(8,128)(2,1)} %get-tuple-element.48), calls=%async_computation.4 | async-start | bytes 262144 | tf_op jit(solution)/shard_map/all_to_all | solution.py:568
  165.7 6.1 %all-to-all-done.4.got_ref = bf16[32,16,128]{2,1,0:T(8,128)(2,1)S(1)} async-done(((bf16[32,16,128]{2,1,0:T(8,128)(2,1)}), bf16[32,16,128]{2,1,0:T(8,128)(2,1)S(1)}, u32[]{:S(2)}, u32[]{:S(2)}) %all-to-all-start.4) | async-done | bytes 131104 | tf_op jit(solution)/shard_map/all_to_all | solution.py:568
  (44 shorter events, 15.7 us)
Async XLA Ops:
  0.6 1.1 copy-start
  3.1 40.9 %all-to-all-start = ((f32[16,8,128]{2,1,0:T(8,128)}), f32[16,8,128]{2,1,0:T(8,128)S(1)}, u32[]{:S(2)}, u32[]{:S(2)}) async-start(f32[16,8,128]{2,1,0:T(8,128)} %stats.1), calls=%async_computation | async-start | bytes 131072 | tf_op jit(solution)/shard_map/all_to_all | solution.py:684
  23.9 20.1 %collective-permute-start = (bf16[16,3584]{1,0:T(8,128)(2,1)S(1)}, bf16[16,3584]{1,0:T(8,128)(2,1)S(1)}, u32[]{:S(2)}, u32[]{:S(2)}) collective-permute-start(bf16[16,3584]{1,0:T(8,128)(2,1)S(1)} %get-tuple-element.29), channel_id=1, source_target_pairs={{0,92},{1,93},{2,94},{3,95},{4,88},{5,89},{6,90},{7,91},{8,84},{9,... | collective-permute-start | bytes 344072 | tf_op jit(solution)/shard_map/ppermute | solution.py:580
  31.6 36.0 %collective-permute-start.1 = (bf16[64,3584]{1,0:T(8,128)(2,1)S(1)}, bf16[64,3584]{1,0:T(8,128)(2,1)}, u32[]{:S(2)}, u32[]{:S(2)}) collective-permute-start(bf16[64,3584]{1,0:T(8,128)(2,1)S(1)} %get-tuple-element.33), channel_id=1, source_target_pairs={{0,384},{1,385},{2,386},{3,387},{4,388},{5,389},{6,390},{7,391},{8... | collective-permute-start | bytes 1376264 | tf_op jit(solution)/shard_map/ppermute | solution.py:580
  35.9 37.2 %collective-permute-start.2 = (bf16[64,3584]{1,0:T(8,128)(2,1)S(1)}, bf16[64,3584]{1,0:T(8,128)(2,1)}, u32[]{:S(2)}, u32[]{:S(2)}) collective-permute-start(bf16[64,3584]{1,0:T(8,128)(2,1)S(1)} %get-tuple-element.33), channel_id=1, source_target_pairs={{0,128},{1,129},{2,130},{3,131},{4,132},{5,133},{6,134},{7,135},{8... | collective-permute-start | bytes 1376264 | tf_op jit(solution)/shard_map/ppermute | solution.py:580
  45.4 6.7 %copy-start.1 = (bf16[12,2,32,512]{3,2,1,0:T(8,128)(2,1)S(1)}, bf16[12,2,32,512]{3,2,1,0:T(8,128)(2,1)}, u32[]{:S(2)}) copy-start(bf16[12,2,32,512]{3,2,1,0:T(8,128)(2,1)} %param.11) | copy-start | bytes 2359300
  45.4 6.8 %copy-start.2 = (f32[512]{0:T(512)S(1)}, f32[512]{0:T(512)}, u32[]{:S(2)}) copy-start(f32[512]{0:T(512)} %param.12) | copy-start | bytes 6148
  45.4 6.8 %copy-start.3 = (f32[512]{0:T(512)S(1)}, f32[512]{0:T(512)}, u32[]{:S(2)}) copy-start(f32[512]{0:T(512)} %param.13) | copy-start | bytes 6148
  45.4 36.9 %all-to-all-start.1 = ((bf16[16,16,3584]{2,1,0:T(8,128)(2,1)}), bf16[16,16,3584]{2,1,0:T(8,128)(2,1)S(1)}, u32[]{:S(2)}, u32[]{:S(2)}) async-start(bf16[16,16,3584]{2,1,0:T(8,128)(2,1)} %broadcast_in_dim.2), calls=%async_computation.1 | async-start | bytes 3670016 | tf_op jit(solution)/shard_map/all_to_all | solution.py:568
  53.3 28.9 %collective-permute-start.5 = (f32[8,768]{1,0:T(8,128)S(1)}, f32[8,768]{1,0:T(8,128)S(1)}, u32[]{:S(2)}, u32[]{:S(2)}) collective-permute-start(f32[8,768]{1,0:T(8,128)S(1)} %get-tuple-element.34), channel_id=1, source_target_pairs={{32,0},{64,32},{96,64},{128,96},{160,128},{192,160},{224,192},{256... | collective-permute-start | bytes 73736 | tf_op jit(solution)/shard_map/ppermute | solution.py:652
  56.1 26.2 %collective-permute-start.6 = (f32[8,768]{1,0:T(8,128)S(1)}, f32[8,768]{1,0:T(8,128)S(1)}, u32[]{:S(2)}, u32[]{:S(2)}) collective-permute-start(f32[8,768]{1,0:T(8,128)S(1)} %get-tuple-element.35), channel_id=1, source_target_pairs={{0,32},{32,64},{64,96},{96,128},{128,160},{160,192},{192,224},{224... | collective-permute-start | bytes 73736 | tf_op jit(solution)/shard_map/ppermute | solution.py:652
  68.6 9.9 %collective-permute-start.3 = (bf16[32,3584]{1,0:T(8,128)(2,1)S(1)}, bf16[32,3584]{1,0:T(8,128)(2,1)S(1)}, u32[]{:S(2)}, u32[]{:S(2)}) collective-permute-start(bf16[32,3584]{1,0:T(8,128)(2,1)S(1)} %slice.8), channel_id=1, source_target_pairs={{0,384},{1,385},{2,386},{3,387},{4,388},{5,389},{6,390},{7,391},{8... | collective-permute-start | bytes 688136 | tf_op jit(solution)/shard_map/ppermute | solution.py:580
  74.1 14.5 %copy-start.7 = (f32[768]{0:T(1024)S(1)}, f32[768]{0:T(1024)}, u32[]{:S(2)}) copy-start(f32[768]{0:T(1024)} %param.20) | copy-start | bytes 9220
  74.1 16.5 %copy-start.4 = (f32[16,1024]{1,0:T(8,128)S(1)}, f32[16,1024]{1,0:T(8,128)}, u32[]{:S(2)}) copy-start(f32[16,1024]{1,0:T(8,128)} %refs_5_.1) | copy-start | bytes 196612
  74.1 16.5 %copy-start.5 = (f32[2048]{0:T(1024)S(1)}, f32[2048]{0:T(1024)}, u32[]{:S(2)}) copy-start(f32[2048]{0:T(1024)} %param.18) | copy-start | bytes 24580
  74.1 16.5 %copy-start.6 = (f32[1024]{0:T(1024)S(1)}, f32[1024]{0:T(1024)}, u32[]{:S(2)}) copy-start(f32[1024]{0:T(1024)} %param.16) | copy-start | bytes 12292
  74.1 8.1 %collective-permute-start.4 = (bf16[32,3584]{1,0:T(8,128)(2,1)S(1)}, bf16[32,3584]{1,0:T(8,128)(2,1)S(1)}, u32[]{:S(2)}, u32[]{:S(2)}) collective-permute-start(bf16[32,3584]{1,0:T(8,128)(2,1)S(1)} %slice.9), channel_id=1, source_target_pairs={{0,128},{1,129},{2,130},{3,131},{4,132},{5,133},{6,134},{7,135},{8... | collective-permute-start | bytes 688136 | tf_op jit(solution)/shard_map/ppermute | solution.py:580
  82.3 8.3 %collective-permute-start.9 = (bf16[256,3584]{1,0:T(8,128)(2,1)S(1)}, bf16[256,3584]{1,0:T(8,128)(2,1)S(1)}, u32[]{:S(2)}, u32[]{:S(2)}) collective-permute-start(bf16[256,3584]{1,0:T(8,128)(2,1)S(1)} %bitcast.22), channel_id=1, source_target_pairs={{0,32},{1,33},{2,34},{3,35},{4,36},{5,37},{6,38},{7,39},{8,40},{9,... | collective-permute-start | bytes 5505032 | tf_op jit(solution)/shard_map/ppermute | solution.py:580
  84.2 6.4 %collective-permute-start.7 = (bf16[192,3584]{1,0:T(8,128)(2,1)}, bf16[192,3584]{1,0:T(8,128)(2,1)S(1)}, u32[]{:S(2)}, u32[]{:S(2)}) collective-permute-start(bf16[192,3584]{1,0:T(8,128)(2,1)} %pad_maximum_fusion.refs_9_), channel_id=1, source_target_pairs={{0,32},{1,33},{2,34},{3,35},{4,36},{5,37},{6,38},{7,39},{8,40},{9,... | collective-permute-start | bytes 4128776 | tf_op jit(solution)/shard_map/ppermute | solution.py:580
  86.6 4.0 %collective-permute-start.8 = (bf16[64,3584]{1,0:T(8,128)(2,1)S(1)}, bf16[64,3584]{1,0:T(8,128)(2,1)S(1)}, u32[]{:S(2)}, u32[]{:S(2)}) collective-permute-start(bf16[64,3584]{1,0:T(8,128)(2,1)S(1)} %pad_maximum_fusion.1.refs_10_), channel_id=1, source_target_pairs={{0,32},{1,33},{2,34},{3,35},{4,36},{5,37},{6,38},{7,39},{8,40},{9,... | collective-permute-start | bytes 1376264 | tf_op jit(solution)/shard_map/ppermute | solution.py:580
  99.9 7.7 %collective-permute-start.10 = (f32[8,768]{1,0:T(8,128)S(1)}, f32[8,768]{1,0:T(8,128)S(1)}, u32[]{:S(2)}, u32[]{:S(2)}) collective-permute-start(f32[8,768]{1,0:T(8,128)S(1)} %get-tuple-element.41.refs_0_), channel_id=1, source_target_pairs={{0,32},{32,64},{64,96},{96,128},{128,160},{160,192},{192,224},{224... | collective-permute-start | bytes 73736 | tf_op jit(solution)/shard_map/ppermute | solution.py:652
  105.6 13.9 %collective-permute-start.11 = (f32[8,768]{1,0:T(8,128)S(1)}, f32[8,768]{1,0:T(8,128)S(1)}, u32[]{:S(2)}, u32[]{:S(2)}) collective-permute-start(f32[8,768]{1,0:T(8,128)S(1)} %get-tuple-element.41.refs_0_), channel_id=1, source_target_pairs={{32,0},{64,32},{96,64},{128,96},{160,128},{192,160},{224,192},{256... | collective-permute-start | bytes 73736 | tf_op jit(solution)/shard_map/ppermute | solution.py:652
  157.7 14.1 %all-to-all-start.4 = ((bf16[32,16,128]{2,1,0:T(8,128)(2,1)}), bf16[32,16,128]{2,1,0:T(8,128)(2,1)S(1)}, u32[]{:S(2)}, u32[]{:S(2)}) async-start(bf16[32,16,128]{2,1,0:T(8,128)(2,1)} %get-tuple-element.48), calls=%async_computation.4 | async-start | bytes 262144 | tf_op jit(solution)/shard_map/all_to_all | solution.py:568

commit v10 on v9

--- a/solution.py
+++ b/solution.py
@@ -126,8 +126,8 @@
 
 
 def conv_kernel(
-    across, members, st_ref, f_ref, gain_ref, bias_ref, k_ref,
-    lat_ref, up_ref, down_ref, mean_ref, inv_ref, act,
+    across, members, at_ref, st_ref, f_ref, gain_ref, bias_ref, k_ref,
+    lat_ref, far_ref, near_ref, mean_ref, inv_ref, act,
 ):
     images, cells, channels = f_ref.shape
     per_group = channels // GROUPS
@@ -157,18 +157,21 @@
     first, middle, last = line(0), line(1), line(2)
     last_up, first_down = roll(last, -across), roll(first, across)
     lat_ref[...] = middle + jnp.where(row == 0, last_up, first_down)
-    up_ref[...] = jnp.where(row == 1, roll(last, across), 0.0)
-    down_ref[...] = jnp.where(row == 0, roll(first, -across), 0.0)
-
-
-def conv_forward(stats, features, gain, bias, kernel_rows, across, members):
+    up = jnp.where(row == 1, roll(last, across), 0.0)
+    down = jnp.where(row == 0, roll(first, -across), 0.0)
+    upper = at_ref[1] == 1
+    far_ref[...] = jnp.where(upper, down, up)
+    near_ref[...] = jnp.where(upper, up, down)
+
+
+def conv_forward(at, stats, features, gain, bias, kernel_rows, across, members):
     images, cells, channels = features.shape
     line = jax.ShapeDtypeStruct((SUB, images * cells), F32)
     stat = jax.ShapeDtypeStruct((STAT_ROWS, channels), F32)
     return pl.pallas_call(
         lambda *refs: conv_kernel(across, members, *refs),
         out_shape=(line, line, line, stat, stat),
-        in_specs=[vmem()] * 5,
+        in_specs=[pl.BlockSpec(memory_space=pltpu.SMEM)] + [vmem()] * 5,
         out_specs=(vmem(),) * 5,
         scratch_shapes=[pltpu.VMEM((images * cells, channels), BF16)],
         compiler_params=params(),
@@ -176,7 +179,7 @@
             flops=CONV_COST, bytes_accessed=features.size * 2, transcendentals=features.size
         ),
         name="conv",
-    )(stats, features, gain, bias, kernel_rows)
+    )(at, stats, features, gain, bias, kernel_rows)
 
 
 def mlp_kernel(
@@ -334,12 +337,14 @@
 
 
 def back_kernel(
-    across, gl_ref, before_ref, after_ref, f_ref, mean_ref, inv_ref, gain_ref, bias_ref,
+    across, at_ref, gl_ref, far_ref, near_ref, f_ref, mean_ref, inv_ref, gain_ref, bias_ref,
     k_ref, embed_ref, send_ref, gs_ref, act, grads_t, by_bias, by_gain, pack,
 ):
     images, cells, channels = f_ref.shape
     per_group = channels // GROUPS
-    gl, before, after = gl_ref[...], before_ref[...], after_ref[...]
+    gl, far, near = gl_ref[...], far_ref[...], near_ref[...]
+    upper = at_ref[1] == 1
+    before, after = jnp.where(upper, near, far), jnp.where(upper, far, near)
     col, row = lane_masks(gl.shape, across)
     lines = (
         jnp.where(row == 0, roll(gl, -across), roll(after, across)),
@@ -401,7 +406,7 @@
         send_ref[r, 0:CHUNK_ROWS, :] = pack[r].astype(BF16)
 
 
-def conv_backward(gl, before, after, features, mean, inv, gain, bias, kernel_rows, embed, across):
+def conv_backward(at, gl, far, near, features, mean, inv, gain, bias, kernel_rows, embed, across):
     images, cells, channels = features.shape
     return pl.pallas_call(
         lambda *refs: back_kernel(across, *refs),
@@ -409,7 +414,7 @@
             jax.ShapeDtypeStruct((CHUNKS, ALL_ROWS, LANES), BF16),
             jax.ShapeDtypeStruct((images, cells, channels), F32),
         ),
-        in_specs=[vmem()] * 10,
+        in_specs=[pl.BlockSpec(memory_space=pltpu.SMEM)] + [vmem()] * 10,
         out_specs=(vmem(),) * 2,
         scratch_shapes=[
             pltpu.VMEM((images * cells, channels), BF16),
@@ -420,7 +425,7 @@
         ],
         compiler_params=params(),
         name="back",
-    )(gl, before, after, features, mean, inv, gain, bias, kernel_rows, embed)
+    )(at, gl, far, near, features, mean, inv, gain, bias, kernel_rows, embed)
 
 
 def last_kernel(members, got_ref, f_ref, mean_ref, inv_ref, gain_ref, gs_ref, out_ref):
@@ -645,11 +650,12 @@
     return moved(value, lambda x, h, c, d, y: (x, h, 1 - c, d, y))
 
 
-def neighbours(up, down):
+def neighbours(far, near):
     count = lax.axis_size("rows")
-    forward = [(i, i + 1) for i in range(count - 1)]
-    backward = [(b, a) for a, b in forward]
-    return lax.ppermute(up, "rows", backward), lax.ppermute(down, "rows", forward)
+    pairs = [(r, r + 1) for r in range(1, count - 1, 2)]
+    pairs = pairs + [(b, a) for a, b in pairs]
+    inside = [(r, r ^ 1) for r in range(count)]
+    return lax.ppermute(far, "rows", pairs), lax.ppermute(near, "rows", inside)
 
 
 def shards(
@@ -680,13 +686,14 @@
     taps = jnp.pad(taps, ((0, 0), (0, SUB - LATENT), (0, 0))).reshape(TAPS * SUB, channels)
     taps_full = jnp.pad(taps, ((0, LANES - TAPS * SUB), (0, 0)))
 
+    flat, part = lax.optimization_barrier((flat, part))
     sums = group_stats(flat, peers)
     stats = lax.all_to_all(sums, "rows", 0, 0, tiled=True)
     cross, stats = lax.optimization_barrier((crossed(part), stats))
     cross = jnp.broadcast_to(cross[None], (XS * YS, *cross.shape))
     cross = exchanged(cross, SHEET).reshape(-1, shard.shape[1])
-    lat, up, down, mean, inv = conv_forward(stats, flat, gain, bias, taps, across, members)
-    above, below = neighbours(up, down)
+    lat, far, near, mean, inv = conv_forward(at, stats, flat, gain, bias, taps, across, members)
+    above, below = neighbours(far, near)
     cross, own_near, own_far, above, below = lax.optimization_barrier((cross, own_near, own_far, above, below))
     pieces = [own_near, own_far, cross]
     pieces = pieces + [swapped(v) for v in pieces]
@@ -695,9 +702,9 @@
         at, lat, below, above, target, embed_weight, embed_bias.reshape(1, -1),
         proj_in_bias.reshape(1, -1), proj_out_bias.reshape(1, -1), pieces, across,
     )
-    after, before = neighbours(grad_lat, grad_lat)
+    far, near = neighbours(grad_lat, grad_lat)
     send, grad_shift = conv_backward(
-        grad_lat, before, after, flat, mean, inv, gain, bias, taps_full, embed_part, across
+        at, grad_lat, far, near, flat, mean, inv, gain, bias, taps_full, embed_part, across
     )
     plane = exchanged(send, PLANE)
     column = exchanged(plane_total(at, plane), COLUMN)

time: 174 us -> 167 us (0.960)
  waiting for transfers between devices: 29 us -> 25.1 us
  starting transfers between devices: 80.8 us -> 78.3 us
    ppermute x4, waiting for transfers between devices: 11.9 us -> 5.78 us  [the longest x2 5.77 us: neighbours(): lax.ppermute(far, 'rows', pairs)]
    ppermute x4, starting transfers between devices: 21.9 us -> 18 us  [the longest x2 14.1 us: neighbours(): lax.ppermute(far, 'rows', pairs)]
    ppermute x8, waiting for transfers between devices: 11 us -> 13.2 us  [moved(): return lax.ppermute(value, ('rows', 'batch'), pairs)]
  transfers between devices with their start and end apart: 15 -> 15, of which waited for: 5 -> 6; matrix products, arithmetic and copies ran while one was open for 4% -> 4% of each run, Pallas kernels for 3% -> 2%
where the time goes in v10:
time: 167 us; the launch traced here: 166 us
  starting transfers between devices  78.3 us (47%)
  blocking collectives  33.2 us (20%)
  waiting for transfers between devices  25.1 us (15%)
  Pallas kernels  20.7 us (12%)
  local copies, waits for them, and re-layouts  5.45 us (3%)
  other arithmetic  2.37 us (1%)
    all_to_all x2, blocking collectives, exchanged(): lax.all_to_all(value, BOTH, 0, 0, axis_index_groups=groups, tiled=True)  33.2 us
    ppermute x8, starting transfers between devices, moved(): return lax.ppermute(value, ('rows', 'batch'), pairs)  28.2 us
    all_to_all x1, starting transfers between devices, shards(): stats = lax.all_to_all(sums, 'rows', 0, 0, tiled=True)  19.1 us
    ppermute x2, starting transfers between devices, neighbours(): lax.ppermute(far, 'rows', pairs)  14.1 us
    ppermute x8, waiting for transfers between devices, moved(): return lax.ppermute(value, ('rows', 'batch'), pairs)  13.2 us
    all_to_all x2, starting transfers between devices, exchanged(): lax.all_to_all(value, BOTH, 0, 0, axis_index_groups=groups, tiled=True)  13.1 us
    pallas_call x1, Pallas kernels, projector(): pl.pallas_call(lambda *refs: mlp_kernel(across, width, hidden, align, *re...  9.27 us
    all_to_all x2, waiting for transfers between devices, exchanged(): lax.all_to_all(value, BOTH, 0, 0, axis_index_groups=groups, tiled=True)  6.14 us
  transfers between devices with their start and end apart: 15, of which 6 were waited for; matrix products, arithmetic and copies ran while one was open for 4% of the time, Pallas kernels for 2%

profile of v10, /device:TPU:1, one launch (start us, length us, event | category | flops | bytes accessed | tf_op | source)
XLA Modules:
  0.0 166.2 jit_solution(280138470958047277)
XLA Ops:
  4.9 19.1 %all-to-all-start = ((f32[16,8,128]{2,1,0:T(8,128)}), f32[16,8,128]{2,1,0:T(8,128)S(1)}, u32[]{:S(2)}, u32[]{:S(2)}) async-start(f32[16,8,128]{2,1,0:T(8,128)} %stats.1), calls=%async_computation | async-start | bytes 131072 | tf_op jit(solution)/shard_map/all_to_all | solution.py:691
  24.0 7.7 %collective-permute-start = (bf16[16,3584]{1,0:T(8,128)(2,1)S(1)}, bf16[16,3584]{1,0:T(8,128)(2,1)S(1)}, u32[]{:S(2)}, u32[]{:S(2)}) collective-permute-start(bf16[16,3584]{1,0:T(8,128)(2,1)S(1)} %get-tuple-element.32), channel_id=1, source_target_pairs={{0,92},{1,93},{2,94},{3,95},{4,88},{5,89},{6,90},{7,91},{8,84},{9,... | collective-permute-start | bytes 344072 | tf_op jit(solution)/shard_map/ppermute | solution.py:585
  31.7 4.3 %collective-permute-start.1 = (bf16[64,3584]{1,0:T(8,128)(2,1)S(1)}, bf16[64,3584]{1,0:T(8,128)(2,1)}, u32[]{:S(2)}, u32[]{:S(2)}) collective-permute-start(bf16[64,3584]{1,0:T(8,128)(2,1)S(1)} %get-tuple-element.37), channel_id=1, source_target_pairs={{0,384},{1,385},{2,386},{3,387},{4,388},{5,389},{6,390},{7,391},{8... | collective-permute-start | bytes 1376264 | tf_op jit(solution)/shard_map/ppermute | solution.py:585
  36.0 1.9 %collective-permute-start.2 = (bf16[64,3584]{1,0:T(8,128)(2,1)S(1)}, bf16[64,3584]{1,0:T(8,128)(2,1)}, u32[]{:S(2)}, u32[]{:S(2)}) collective-permute-start(bf16[64,3584]{1,0:T(8,128)(2,1)S(1)} %get-tuple-element.37), channel_id=1, source_target_pairs={{0,128},{1,129},{2,130},{3,131},{4,132},{5,133},{6,134},{7,135},{8... | collective-permute-start | bytes 1376264 | tf_op jit(solution)/shard_map/ppermute | solution.py:585
  38.8 5.5 %collective-permute-done = bf16[16,3584]{1,0:T(8,128)(2,1)S(1)} collective-permute-done((bf16[16,3584]{1,0:T(8,128)(2,1)S(1)}, bf16[16,3584]{1,0:T(8,128)(2,1)S(1)}, u32[]{:S(2)}, u32[]{:S(2)}) %collective-permute-start) | collective-permute-done | bytes 114720 | tf_op jit(solution)/shard_map/ppermute | solution.py:585
  45.8 6.7 %all-to-all-start.1 = ((bf16[16,16,3584]{2,1,0:T(8,128)(2,1)}), bf16[16,16,3584]{2,1,0:T(8,128)(2,1)S(1)}, u32[]{:S(2)}, u32[]{:S(2)}) async-start(bf16[16,16,3584]{2,1,0:T(8,128)(2,1)} %broadcast_in_dim.2), calls=%async_computation.1 | async-start | bytes 3670016 | tf_op jit(solution)/shard_map/all_to_all | solution.py:573
  54.2 8.0 %collective-permute-start.5 = (f32[8,768]{1,0:T(8,128)S(1)}, f32[8,768]{1,0:T(8,128)S(1)}, u32[]{:S(2)}, u32[]{:S(2)}) collective-permute-start(f32[8,768]{1,0:T(8,128)S(1)} %get-tuple-element.38), channel_id=1, source_target_pairs={{32,64},{96,128},{160,192},{224,256},{288,320},{352,384},{416,448}... | collective-permute-start | bytes 73736 | tf_op jit(solution)/shard_map/ppermute | solution.py:658
  62.2 1.9 %collective-permute-start.6 = (f32[8,768]{1,0:T(8,128)S(1)}, f32[8,768]{1,0:T(8,128)S(1)}, u32[]{:S(2)}, u32[]{:S(2)}) collective-permute-start(f32[8,768]{1,0:T(8,128)S(1)} %get-tuple-element.39), channel_id=1, source_target_pairs={{0,32},{32,0},{64,96},{96,64},{128,160},{160,128},{192,224},{224,1... | collective-permute-start | bytes 73736 | tf_op jit(solution)/shard_map/ppermute | solution.py:658
  65.1 4.8 %collective-permute-start.3 = (bf16[32,3584]{1,0:T(8,128)(2,1)S(1)}, bf16[32,3584]{1,0:T(8,128)(2,1)S(1)}, u32[]{:S(2)}, u32[]{:S(2)}) collective-permute-start(bf16[32,3584]{1,0:T(8,128)(2,1)S(1)} %slice.8), channel_id=1, source_target_pairs={{0,384},{1,385},{2,386},{3,387},{4,388},{5,389},{6,390},{7,391},{8... | collective-permute-start | bytes 688136 | tf_op jit(solution)/shard_map/ppermute | solution.py:585
  70.9 2.1 %collective-permute-start.4 = (bf16[32,3584]{1,0:T(8,128)(2,1)S(1)}, bf16[32,3584]{1,0:T(8,128)(2,1)S(1)}, u32[]{:S(2)}, u32[]{:S(2)}) collective-permute-start(bf16[32,3584]{1,0:T(8,128)(2,1)S(1)} %slice.9), channel_id=1, source_target_pairs={{0,128},{1,129},{2,130},{3,131},{4,132},{5,133},{6,134},{7,135},{8... | collective-permute-start | bytes 688136 | tf_op jit(solution)/shard_map/ppermute | solution.py:585
  72.9 2.3 %pad_maximum_fusion.refs_9_ = bf16[192,3584]{1,0:T(8,128)(2,1)} fusion(bf16[64,3584]{1,0:T(8,128)(2,1)} %collective-permute-done.2, bf16[64,3584]{1,0:T(8,128)(2,1)} %collective-permute-done.1, bf16[64,3584]{1,0:T(8,128)(2,1)S(1)} %get-tuple-element.37), kind=kLoop, calls=%fused_computation | loop fusion | flops 4128768 | bytes 2752512 | tf_op jit(solution)/shard_map/concatenate | solution.py:644
  75.3 3.2 %collective-permute-done.3 = bf16[32,3584]{1,0:T(8,128)(2,1)S(1)} collective-permute-done((bf16[32,3584]{1,0:T(8,128)(2,1)S(1)}, bf16[32,3584]{1,0:T(8,128)(2,1)S(1)}, u32[]{:S(2)}, u32[]{:S(2)}) %collective-permute-start.3) | collective-permute-done | bytes 229408 | tf_op jit(solution)/shard_map/ppermute | solution.py:585
  78.5 2.8 %collective-permute-done.4 = bf16[32,3584]{1,0:T(8,128)(2,1)S(1)} collective-permute-done((bf16[32,3584]{1,0:T(8,128)(2,1)S(1)}, bf16[32,3584]{1,0:T(8,128)(2,1)S(1)}, u32[]{:S(2)}, u32[]{:S(2)}) %collective-permute-start.4) | collective-permute-done | bytes 229408 | tf_op jit(solution)/shard_map/ppermute | solution.py:585
  81.3 3.2 %collective-permute-start.9 = (bf16[256,3584]{1,0:T(8,128)(2,1)S(1)}, bf16[256,3584]{1,0:T(8,128)(2,1)S(1)}, u32[]{:S(2)}, u32[]{:S(2)}) collective-permute-start(bf16[256,3584]{1,0:T(8,128)(2,1)S(1)} %bitcast.22), channel_id=1, source_target_pairs={{0,32},{1,33},{2,34},{3,35},{4,36},{5,37},{6,38},{7,39},{8,40},{9,... | collective-permute-start | bytes 5505032 | tf_op jit(solution)/shard_map/ppermute | solution.py:585
  86.5 2.4 %collective-permute-start.8 = (bf16[64,3584]{1,0:T(8,128)(2,1)S(1)}, bf16[64,3584]{1,0:T(8,128)(2,1)S(1)}, u32[]{:S(2)}, u32[]{:S(2)}) collective-permute-start(bf16[64,3584]{1,0:T(8,128)(2,1)S(1)} %pad_maximum_fusion.1.refs_10_), channel_id=1, source_target_pairs={{0,32},{1,33},{2,34},{3,35},{4,36},{5,37},{6,38},{7,39},{8,40},{9,... | collective-permute-start | bytes 1376264 | tf_op jit(solution)/shard_map/ppermute | solution.py:585
  90.6 9.3 %projector.1 = (f32[32,1024]{1,0:T(8,128)S(1)}, f32[8,768]{1,0:T(8,128)S(1)}) custom-call(s32[5]{0:T(128)S(1)} %stack.23.at_ref.refs_0_, f32[8,768]{1,0:T(8,128)S(1)} %get-tuple-element.35.refs_1_, f32[8,768]{1,0:T(8,128)S(1)} %collective-permute-done.6.refs_2_, f32[8,768]{1,0:T(8,128)S(1)} %collective-permute-done.5.refs_3_, bf16[192,768]{1,0:T(8,128)(2,1)} %bitcast.33, ...), custom_call_target="tpu_custom_call" | custom-call | flops 2818572288 | bytes 8388608 | tf_op jit(solution)/shard_map/projector/pallas_call | solution.py:309
  99.8 6.1 %collective-permute-start.10 = (f32[8,768]{1,0:T(8,128)S(1)}, f32[8,768]{1,0:T(8,128)S(1)}, u32[]{:S(2)}, u32[]{:S(2)}) collective-permute-start(f32[8,768]{1,0:T(8,128)S(1)} %get-tuple-element.45.refs_1_), channel_id=1, source_target_pairs={{32,64},{96,128},{160,192},{224,256},{288,320},{352,384},{416,448}... | collective-permute-start | bytes 73736 | tf_op jit(solution)/shard_map/ppermute | solution.py:658
  106.0 1.9 %collective-permute-start.11 = (f32[8,768]{1,0:T(8,128)S(1)}, f32[8,768]{1,0:T(8,128)S(1)}, u32[]{:S(2)}, u32[]{:S(2)}) collective-permute-start(f32[8,768]{1,0:T(8,128)S(1)} %get-tuple-element.45.refs_1_), channel_id=1, source_target_pairs={{0,32},{32,0},{64,96},{96,64},{128,160},{160,128},{192,224},{224,1... | collective-permute-start | bytes 73736 | tf_op jit(solution)/shard_map/ppermute | solution.py:658
  107.9 5.8 %collective-permute-done.10.refs_2_ = f32[8,768]{1,0:T(8,128)S(1)} collective-permute-done((f32[8,768]{1,0:T(8,128)S(1)}, f32[8,768]{1,0:T(8,128)S(1)}, u32[]{:S(2)}, u32[]{:S(2)}) %collective-permute-start.10) | collective-permute-done | bytes 24608 | tf_op jit(solution)/shard_map/ppermute | solution.py:658
  113.7 2.6 %back.1 = (bf16[32,32,128]{2,1,0:T(8,128)(2,1)S(1)}, f32[12,64,512]{2,1,0:T(8,128)S(1)}) custom-call(s32[5]{0:T(128)S(1)} %stack.23.at_ref.refs_0_, f32[8,768]{1,0:T(8,128)S(1)} %get-tuple-element.45.refs_1_, f32[8,768]{1,0:T(8,128)S(1)} %collective-permute-done.10.refs_2_, f32[8,768]{1,0:T(8,128)S(1)} %collective-permute-done.11.refs_3_, ...), custom_call_target="tpu_custom_call" | custom-call | tf_op jit(solution)/shard_map/back/pallas_call | solution.py:411
  116.3 14.7 %all_to_all.25.got_ref = bf16[32,32,128]{2,1,0:T(8,128)(2,1)S(1)} all-to-all(bf16[32,32,128]{2,1,0:T(8,128)(2,1)S(1)} %get-tuple-element.49), channel_id=1, replica_groups={{0,32,1,33,2,34,3,35,128,160,129,161,130,162,131,163,256,288,257,289,25..., dimensions={0} | all-to-all | bytes 524288 | tf_op jit(solution)/shard_map/all_to_all | solution.py:573
  131.6 18.5 %all_to_all.26.got_ref = bf16[16,32,128]{2,1,0:T(8,128)(2,1)S(1)} all-to-all(bf16[16,32,128]{2,1,0:T(8,128)(2,1)S(1)} %plane.1), channel_id=1, replica_groups={{0,4,8,12,16,20,24,28,64,68,72,76,80,84,88,92},{32,36,40,44,48,52,56,60..., dimensions={0} | all-to-all | bytes 262144 | tf_op jit(solution)/shard_map/all_to_all | solution.py:573
  151.3 6.4 %all-to-all-start.4 = ((bf16[32,16,128]{2,1,0:T(8,128)(2,1)}), bf16[32,16,128]{2,1,0:T(8,128)(2,1)S(1)}, u32[]{:S(2)}, u32[]{:S(2)}) async-start(bf16[32,16,128]{2,1,0:T(8,128)(2,1)} %get-tuple-element.52), calls=%async_computation.4 | async-start | bytes 262144 | tf_op jit(solution)/shard_map/all_to_all | solution.py:573
  159.3 6.1 %all-to-all-done.4.got_ref = bf16[32,16,128]{2,1,0:T(8,128)(2,1)S(1)} async-done(((bf16[32,16,128]{2,1,0:T(8,128)(2,1)}), bf16[32,16,128]{2,1,0:T(8,128)(2,1)S(1)}, u32[]{:S(2)}, u32[]{:S(2)}) %all-to-all-start.4) | async-done | bytes 131104 | tf_op jit(solution)/shard_map/all_to_all | solution.py:573
  (44 shorter events, 17.9 us)
Async XLA Ops:
  2.5 1.1 copy-start
  4.9 39.4 %all-to-all-start = ((f32[16,8,128]{2,1,0:T(8,128)}), f32[16,8,128]{2,1,0:T(8,128)S(1)}, u32[]{:S(2)}, u32[]{:S(2)}) async-start(f32[16,8,128]{2,1,0:T(8,128)} %stats.1), calls=%async_computation | async-start | bytes 131072 | tf_op jit(solution)/shard_map/all_to_all | solution.py:691
  24.0 20.3 %collective-permute-start = (bf16[16,3584]{1,0:T(8,128)(2,1)S(1)}, bf16[16,3584]{1,0:T(8,128)(2,1)S(1)}, u32[]{:S(2)}, u32[]{:S(2)}) collective-permute-start(bf16[16,3584]{1,0:T(8,128)(2,1)S(1)} %get-tuple-element.32), channel_id=1, source_target_pairs={{0,92},{1,93},{2,94},{3,95},{4,88},{5,89},{6,90},{7,91},{8,84},{9,... | collective-permute-start | bytes 344072 | tf_op jit(solution)/shard_map/ppermute | solution.py:585
  31.7 32.5 %collective-permute-start.1 = (bf16[64,3584]{1,0:T(8,128)(2,1)S(1)}, bf16[64,3584]{1,0:T(8,128)(2,1)}, u32[]{:S(2)}, u32[]{:S(2)}) collective-permute-start(bf16[64,3584]{1,0:T(8,128)(2,1)S(1)} %get-tuple-element.37), channel_id=1, source_target_pairs={{0,384},{1,385},{2,386},{3,387},{4,388},{5,389},{6,390},{7,391},{8... | collective-permute-start | bytes 1376264 | tf_op jit(solution)/shard_map/ppermute | solution.py:585
  36.0 33.9 %collective-permute-start.2 = (bf16[64,3584]{1,0:T(8,128)(2,1)S(1)}, bf16[64,3584]{1,0:T(8,128)(2,1)}, u32[]{:S(2)}, u32[]{:S(2)}) collective-permute-start(bf16[64,3584]{1,0:T(8,128)(2,1)S(1)} %get-tuple-element.37), channel_id=1, source_target_pairs={{0,128},{1,129},{2,130},{3,131},{4,132},{5,133},{6,134},{7,135},{8... | collective-permute-start | bytes 1376264 | tf_op jit(solution)/shard_map/ppermute | solution.py:585
  45.7 6.7 %copy-start.1 = (bf16[12,2,32,512]{3,2,1,0:T(8,128)(2,1)S(1)}, bf16[12,2,32,512]{3,2,1,0:T(8,128)(2,1)}, u32[]{:S(2)}) copy-start(bf16[12,2,32,512]{3,2,1,0:T(8,128)(2,1)} %param.11) | copy-start | bytes 2359300
  45.7 6.8 %copy-start.2 = (f32[512]{0:T(512)S(1)}, f32[512]{0:T(512)}, u32[]{:S(2)}) copy-start(f32[512]{0:T(512)} %param.12) | copy-start | bytes 6148
  45.7 6.8 %copy-start.3 = (f32[512]{0:T(512)S(1)}, f32[512]{0:T(512)}, u32[]{:S(2)}) copy-start(f32[512]{0:T(512)} %param.13) | copy-start | bytes 6148
  45.8 35.6 %all-to-all-start.1 = ((bf16[16,16,3584]{2,1,0:T(8,128)(2,1)}), bf16[16,16,3584]{2,1,0:T(8,128)(2,1)S(1)}, u32[]{:S(2)}, u32[]{:S(2)}) async-start(bf16[16,16,3584]{2,1,0:T(8,128)(2,1)} %broadcast_in_dim.2), calls=%async_computation.1 | async-start | bytes 3670016 | tf_op jit(solution)/shard_map/all_to_all | solution.py:573
  54.2 27.1 %collective-permute-start.5 = (f32[8,768]{1,0:T(8,128)S(1)}, f32[8,768]{1,0:T(8,128)S(1)}, u32[]{:S(2)}, u32[]{:S(2)}) collective-permute-start(f32[8,768]{1,0:T(8,128)S(1)} %get-tuple-element.38), channel_id=1, source_target_pairs={{32,64},{96,128},{160,192},{224,256},{288,320},{352,384},{416,448}... | collective-permute-start | bytes 73736 | tf_op jit(solution)/shard_map/ppermute | solution.py:658
  62.2 19.1 %collective-permute-start.6 = (f32[8,768]{1,0:T(8,128)S(1)}, f32[8,768]{1,0:T(8,128)S(1)}, u32[]{:S(2)}, u32[]{:S(2)}) collective-permute-start(f32[8,768]{1,0:T(8,128)S(1)} %get-tuple-element.39), channel_id=1, source_target_pairs={{0,32},{32,0},{64,96},{96,64},{128,160},{160,128},{192,224},{224,1... | collective-permute-start | bytes 73736 | tf_op jit(solution)/shard_map/ppermute | solution.py:658
  65.1 13.4 %collective-permute-start.3 = (bf16[32,3584]{1,0:T(8,128)(2,1)S(1)}, bf16[32,3584]{1,0:T(8,128)(2,1)S(1)}, u32[]{:S(2)}, u32[]{:S(2)}) collective-permute-start(bf16[32,3584]{1,0:T(8,128)(2,1)S(1)} %slice.8), channel_id=1, source_target_pairs={{0,384},{1,385},{2,386},{3,387},{4,388},{5,389},{6,390},{7,391},{8... | collective-permute-start | bytes 688136 | tf_op jit(solution)/shard_map/ppermute | solution.py:585
  70.8 18.0 %copy-start.7 = (f32[768]{0:T(1024)S(1)}, f32[768]{0:T(1024)}, u32[]{:S(2)}) copy-start(f32[768]{0:T(1024)} %param.20) | copy-start | bytes 9220
  70.9 19.7 %copy-start.4 = (f32[16,1024]{1,0:T(8,128)S(1)}, f32[16,1024]{1,0:T(8,128)}, u32[]{:S(2)}) copy-start(f32[16,1024]{1,0:T(8,128)} %refs_5_.1) | copy-start | bytes 196612
  70.9 19.7 %copy-start.5 = (f32[2048]{0:T(1024)S(1)}, f32[2048]{0:T(1024)}, u32[]{:S(2)}) copy-start(f32[2048]{0:T(1024)} %param.18) | copy-start | bytes 24580
  70.9 19.7 %copy-start.6 = (f32[1024]{0:T(1024)S(1)}, f32[1024]{0:T(1024)}, u32[]{:S(2)}) copy-start(f32[1024]{0:T(1024)} %param.16) | copy-start | bytes 12292
  70.9 10.4 %collective-permute-start.4 = (bf16[32,3584]{1,0:T(8,128)(2,1)S(1)}, bf16[32,3584]{1,0:T(8,128)(2,1)S(1)}, u32[]{:S(2)}, u32[]{:S(2)}) collective-permute-start(bf16[32,3584]{1,0:T(8,128)(2,1)S(1)} %slice.9), channel_id=1, source_target_pairs={{0,128},{1,129},{2,130},{3,131},{4,132},{5,133},{6,134},{7,135},{8... | collective-permute-start | bytes 688136 | tf_op jit(solution)/shard_map/ppermute | solution.py:585
  81.3 9.2 %collective-permute-start.9 = (bf16[256,3584]{1,0:T(8,128)(2,1)S(1)}, bf16[256,3584]{1,0:T(8,128)(2,1)S(1)}, u32[]{:S(2)}, u32[]{:S(2)}) collective-permute-start(bf16[256,3584]{1,0:T(8,128)(2,1)S(1)} %bitcast.22), channel_id=1, source_target_pairs={{0,32},{1,33},{2,34},{3,35},{4,36},{5,37},{6,38},{7,39},{8,40},{9,... | collective-permute-start | bytes 5505032 | tf_op jit(solution)/shard_map/ppermute | solution.py:585
  84.5 6.0 %collective-permute-start.7 = (bf16[192,3584]{1,0:T(8,128)(2,1)}, bf16[192,3584]{1,0:T(8,128)(2,1)S(1)}, u32[]{:S(2)}, u32[]{:S(2)}) collective-permute-start(bf16[192,3584]{1,0:T(8,128)(2,1)} %pad_maximum_fusion.refs_9_), channel_id=1, source_target_pairs={{0,32},{1,33},{2,34},{3,35},{4,36},{5,37},{6,38},{7,39},{8,40},{9,... | collective-permute-start | bytes 4128776 | tf_op jit(solution)/shard_map/ppermute | solution.py:585
  86.5 4.1 %collective-permute-start.8 = (bf16[64,3584]{1,0:T(8,128)(2,1)S(1)}, bf16[64,3584]{1,0:T(8,128)(2,1)S(1)}, u32[]{:S(2)}, u32[]{:S(2)}) collective-permute-start(bf16[64,3584]{1,0:T(8,128)(2,1)S(1)} %pad_maximum_fusion.1.refs_10_), channel_id=1, source_target_pairs={{0,32},{1,33},{2,34},{3,35},{4,36},{5,37},{6,38},{7,39},{8,40},{9,... | collective-permute-start | bytes 1376264 | tf_op jit(solution)/shard_map/ppermute | solution.py:585
  99.8 13.9 %collective-permute-start.10 = (f32[8,768]{1,0:T(8,128)S(1)}, f32[8,768]{1,0:T(8,128)S(1)}, u32[]{:S(2)}, u32[]{:S(2)}) collective-permute-start(f32[8,768]{1,0:T(8,128)S(1)} %get-tuple-element.45.refs_1_), channel_id=1, source_target_pairs={{32,64},{96,128},{160,192},{224,256},{288,320},{352,384},{416,448}... | collective-permute-start | bytes 73736 | tf_op jit(solution)/shard_map/ppermute | solution.py:658
  106.0 7.7 %collective-permute-start.11 = (f32[8,768]{1,0:T(8,128)S(1)}, f32[8,768]{1,0:T(8,128)S(1)}, u32[]{:S(2)}, u32[]{:S(2)}) collective-permute-start(f32[8,768]{1,0:T(8,128)S(1)} %get-tuple-element.45.refs_1_), channel_id=1, source_target_pairs={{0,32},{32,0},{64,96},{96,64},{128,160},{160,128},{192,224},{224,1... | collective-permute-start | bytes 73736 | tf_op jit(solution)/shard_map/ppermute | solution.py:658
  151.3 14.1 %all-to-all-start.4 = ((bf16[32,16,128]{2,1,0:T(8,128)(2,1)}), bf16[32,16,128]{2,1,0:T(8,128)(2,1)S(1)}, u32[]{:S(2)}, u32[]{:S(2)}) async-start(bf16[32,16,128]{2,1,0:T(8,128)(2,1)} %get-tuple-element.52), calls=%async_computation.4 | async-start | bytes 262144 | tf_op jit(solution)/shard_map/all_to_all | solution.py:573

commit v11 on v10

--- a/solution.py
+++ b/solution.py
@@ -196,30 +196,28 @@
     copies = [pltpu.make_async_copy(target_ref, wanted, sems.at[0])]
     copies[0].start()
 
-    def place(piece, at, source_x, of_zhi, of_core, begin=0, size=depth):
+    def place(piece, at, source_x, of_zhi, of_core):
         shard = lax.rem(source_x, XS) * (ZHI * CORES) + of_zhi * CORES + of_core
-        lines = pl.ds(at, size)
+        lines = pl.ds(at, depth)
 
         def put(columns, into):
             copy = pltpu.make_async_copy(piece.at[lines, columns], into, sems.at[len(copies)])
             copy.start()
             copies.append(copy)
 
-        line = pl.multiple_of(shard * depth + begin, size)
-        put(pl.ds(0, hidden), w_in.at[pl.ds(line, size), :])
+        line = pl.multiple_of(shard * depth, depth)
+        put(pl.ds(0, hidden), w_in.at[pl.ds(line, depth), :])
         for part in range(slab // depth):
-            line = pl.multiple_of(shard * slab + part * depth + begin, size)
-            put(pl.ds(hidden + part * align, align), w_out.at[pl.ds(line, size), :])
-
-    half = depth // 2
+            line = pl.multiple_of(shard * slab + part * depth, depth)
+            put(pl.ds(hidden + part * align, align), w_out.at[pl.ds(line, depth), :])
+
     for near, opposite, far, of_core in (
         (own_near, own_far, cross, core),
         (own_near_other, own_far_other, cross_other, 1 - core),
     ):
         for k, step in enumerate((0, 1, XS - 1)):
             place(near, k * depth, x + step, zhi, of_core)
-        for begin in (0, half):
-            place(opposite, begin, x + 2, zhi, of_core, begin, half)
+        place(opposite, 0, x + 2, zhi, of_core)
         for k in range(XS):
             place(far, k * depth, k, 1 - zhi, of_core)
 
@@ -326,7 +324,7 @@
             pltpu.VMEM((tokens, align), F32),
             pltpu.VMEM((256, width), F32),
             pltpu.VMEM((tokens, align), BF16),
-            pltpu.SemaphoreType.DMA((55,)),
+            pltpu.SemaphoreType.DMA((49,)),
         ],
         compiler_params=params(32),
         cost_estimate=pl.CostEstimate(
@@ -639,11 +637,8 @@
 
 
 def along_x(shard):
-    half = shard.shape[0] // 2
     plus, minus = from_next(shard), from_last(shard)
-    near = jnp.concatenate([shard, plus, minus], axis=0)
-    opposite = jnp.concatenate([from_next(plus[:half]), from_last(minus[half:])], axis=0)
-    return near, opposite
+    return jnp.concatenate([shard, plus, minus], axis=0), from_next(plus)
 
 
 def swapped(value):

time: 167 us -> 174 us (1.042)
  waiting for transfers between devices: 25.1 us -> 32.5 us
  local copies, waits for them, and re-layouts: 5.45 us -> 3.55 us
  blocking collectives: 33.2 us -> 35.1 us
    ppermute x8 -> x7, waiting for transfers between devices: 13.2 us -> 19.5 us  [moved(): return lax.ppermute(value, ('rows', 'batch'), pairs)]
    slice x2 -> x0, local copies, waits for them, and re-layouts: 1.91 us -> none  [the longest x1 0.96 us: along_x(): minus[half:]]
    all_to_all x2, blocking collectives: 33.2 us -> 35.1 us  [exchanged(): lax.all_to_all(value, BOTH, 0, 0, axis_index_groups=groups, tiled=True)]
    ppermute x8 -> x7, starting transfers between devices: 28.2 us -> 26.7 us  [moved(): return lax.ppermute(value, ('rows', 'batch'), pairs)]
  transfers between devices with their start and end apart: 15 -> 14, of which waited for: 6 -> 5; matrix products, arithmetic and copies ran while one was open for 4% -> 3% of each run, Pallas kernels for 2% -> 2%
where the time goes in v11:
time: 174 us; the launch traced here: 173 us
  starting transfers between devices  78.1 us (45%)
  blocking collectives  35.1 us (20%)
  waiting for transfers between devices  32.5 us (19%)
  Pallas kernels  20.4 us (12%)
  local copies, waits for them, and re-layouts  3.55 us (2%)
  other arithmetic  2.34 us (1%)
    all_to_all x2, blocking collectives, exchanged(): lax.all_to_all(value, BOTH, 0, 0, axis_index_groups=groups, tiled=True)  35.1 us
    ppermute x7, starting transfers between devices, moved(): return lax.ppermute(value, ('rows', 'batch'), pairs)  26.7 us
    ppermute x7, waiting for transfers between devices, moved(): return lax.ppermute(value, ('rows', 'batch'), pairs)  19.5 us
    all_to_all x1, starting transfers between devices, shards(): stats = lax.all_to_all(sums, 'rows', 0, 0, tiled=True)  19.1 us
    ppermute x2, starting transfers between devices, neighbours(): lax.ppermute(far, 'rows', pairs)  15 us
    all_to_all x2, starting transfers between devices, exchanged(): lax.all_to_all(value, BOTH, 0, 0, axis_index_groups=groups, tiled=True)  13.1 us
    pallas_call x1, Pallas kernels, projector(): pl.pallas_call(lambda *refs: mlp_kernel(across, width, hidden, align, *re...  8.91 us
    ppermute x2, waiting for transfers between devices, neighbours(): lax.ppermute(far, 'rows', pairs)  6.91 us
  transfers between devices with their start and end apart: 14, of which 5 were waited for; matrix products, arithmetic and copies ran while one was open for 3% of the time, Pallas kernels for 2%

profile of v11, /device:TPU:1, one launch (start us, length us, event | category | flops | bytes accessed | tf_op | source)
XLA Modules:
  0.0 172.9 jit_solution(11605472160898728990)
XLA Ops:
  4.9 19.1 %all-to-all-start = ((f32[16,8,128]{2,1,0:T(8,128)}), f32[16,8,128]{2,1,0:T(8,128)S(1)}, u32[]{:S(2)}, u32[]{:S(2)}) async-start(f32[16,8,128]{2,1,0:T(8,128)} %stats.1), calls=%async_computation | async-start | bytes 131072 | tf_op jit(solution)/shard_map/all_to_all | solution.py:686
  24.0 7.7 %collective-permute-start = (bf16[16,3584]{1,0:T(8,128)(2,1)S(1)}, bf16[16,3584]{1,0:T(8,128)(2,1)S(1)}, u32[]{:S(2)}, u32[]{:S(2)}) collective-permute-start(bf16[16,3584]{1,0:T(8,128)(2,1)S(1)} %get-tuple-element.32), channel_id=1, source_target_pairs={{0,92},{1,93},{2,94},{3,95},{4,88},{5,89},{6,90},{7,91},{8,84},{9,... | collective-permute-start | bytes 344072 | tf_op jit(solution)/shard_map/ppermute | solution.py:583
  31.7 4.3 %collective-permute-start.1 = (bf16[64,3584]{1,0:T(8,128)(2,1)S(1)}, bf16[64,3584]{1,0:T(8,128)(2,1)}, u32[]{:S(2)}, u32[]{:S(2)}) collective-permute-start(bf16[64,3584]{1,0:T(8,128)(2,1)S(1)} %get-tuple-element.37), channel_id=1, source_target_pairs={{0,384},{1,385},{2,386},{3,387},{4,388},{5,389},{6,390},{7,391},{8... | collective-permute-start | bytes 1376264 | tf_op jit(solution)/shard_map/ppermute | solution.py:583
  36.0 1.9 %collective-permute-start.2 = (bf16[64,3584]{1,0:T(8,128)(2,1)S(1)}, bf16[64,3584]{1,0:T(8,128)(2,1)}, u32[]{:S(2)}, u32[]{:S(2)}) collective-permute-start(bf16[64,3584]{1,0:T(8,128)(2,1)S(1)} %get-tuple-element.37), channel_id=1, source_target_pairs={{0,128},{1,129},{2,130},{3,131},{4,132},{5,133},{6,134},{7,135},{8... | collective-permute-start | bytes 1376264 | tf_op jit(solution)/shard_map/ppermute | solution.py:583
  38.8 5.5 %collective-permute-done = bf16[16,3584]{1,0:T(8,128)(2,1)S(1)} collective-permute-done((bf16[16,3584]{1,0:T(8,128)(2,1)S(1)}, bf16[16,3584]{1,0:T(8,128)(2,1)S(1)}, u32[]{:S(2)}, u32[]{:S(2)}) %collective-permute-start) | collective-permute-done | bytes 114720 | tf_op jit(solution)/shard_map/ppermute | solution.py:583
  45.8 6.7 %all-to-all-start.1 = ((bf16[16,16,3584]{2,1,0:T(8,128)(2,1)}), bf16[16,16,3584]{2,1,0:T(8,128)(2,1)S(1)}, u32[]{:S(2)}, u32[]{:S(2)}) async-start(bf16[16,16,3584]{2,1,0:T(8,128)(2,1)} %broadcast_in_dim.2), calls=%async_computation.1 | async-start | bytes 3670016 | tf_op jit(solution)/shard_map/all_to_all | solution.py:571
  54.3 8.1 %collective-permute-start.4 = (f32[8,768]{1,0:T(8,128)S(1)}, f32[8,768]{1,0:T(8,128)S(1)}, u32[]{:S(2)}, u32[]{:S(2)}) collective-permute-start(f32[8,768]{1,0:T(8,128)S(1)} %get-tuple-element.38), channel_id=1, source_target_pairs={{32,64},{96,128},{160,192},{224,256},{288,320},{352,384},{416,448}... | collective-permute-start | bytes 73736 | tf_op jit(solution)/shard_map/ppermute | solution.py:653
  62.4 1.9 %collective-permute-start.5 = (f32[8,768]{1,0:T(8,128)S(1)}, f32[8,768]{1,0:T(8,128)S(1)}, u32[]{:S(2)}, u32[]{:S(2)}) collective-permute-start(f32[8,768]{1,0:T(8,128)S(1)} %get-tuple-element.39), channel_id=1, source_target_pairs={{0,32},{32,0},{64,96},{96,64},{128,160},{160,128},{192,224},{224,1... | collective-permute-start | bytes 73736 | tf_op jit(solution)/shard_map/ppermute | solution.py:653
  64.3 4.8 %collective-permute-start.3 = (bf16[64,3584]{1,0:T(8,128)(2,1)}, bf16[64,3584]{1,0:T(8,128)(2,1)}, u32[]{:S(2)}, u32[]{:S(2)}) collective-permute-start(bf16[64,3584]{1,0:T(8,128)(2,1)} %collective-permute-done.1), channel_id=1, source_target_pairs={{0,384},{1,385},{2,386},{3,387},{4,388},{5,389},{6,390},{7,391},{8... | collective-permute-start | bytes 1376264 | tf_op jit(solution)/shard_map/ppermute | solution.py:583
  69.1 2.3 %pad_maximum_fusion.refs_9_ = bf16[192,3584]{1,0:T(8,128)(2,1)} fusion(bf16[64,3584]{1,0:T(8,128)(2,1)} %collective-permute-done.2, bf16[64,3584]{1,0:T(8,128)(2,1)} %collective-permute-done.1, bf16[64,3584]{1,0:T(8,128)(2,1)S(1)} %get-tuple-element.37), kind=kLoop, calls=%fused_computation | loop fusion | flops 4128768 | bytes 2752512 | tf_op jit(solution)/shard_map/concatenate | solution.py:641
  71.5 12.1 %collective-permute-done.3.refs_10_ = bf16[64,3584]{1,0:T(8,128)(2,1)} collective-permute-done((bf16[64,3584]{1,0:T(8,128)(2,1)}, bf16[64,3584]{1,0:T(8,128)(2,1)}, u32[]{:S(2)}, u32[]{:S(2)}) %collective-permute-start.3) | collective-permute-done | bytes 458784 | tf_op jit(solution)/shard_map/ppermute | solution.py:583
  83.5 3.7 %collective-permute-start.8 = (bf16[256,3584]{1,0:T(8,128)(2,1)S(1)}, bf16[256,3584]{1,0:T(8,128)(2,1)S(1)}, u32[]{:S(2)}, u32[]{:S(2)}) collective-permute-start(bf16[256,3584]{1,0:T(8,128)(2,1)S(1)} %bitcast.22), channel_id=1, source_target_pairs={{0,32},{1,33},{2,34},{3,35},{4,36},{5,37},{6,38},{7,39},{8,40},{9,... | collective-permute-start | bytes 5505032 | tf_op jit(solution)/shard_map/ppermute | solution.py:583
  87.3 1.9 %collective-permute-start.6 = (bf16[192,3584]{1,0:T(8,128)(2,1)}, bf16[192,3584]{1,0:T(8,128)(2,1)S(1)}, u32[]{:S(2)}, u32[]{:S(2)}) collective-permute-start(bf16[192,3584]{1,0:T(8,128)(2,1)} %pad_maximum_fusion.refs_9_), channel_id=1, source_target_pairs={{0,32},{1,33},{2,34},{3,35},{4,36},{5,37},{6,38},{7,39},{8,40},{9,... | collective-permute-start | bytes 4128776 | tf_op jit(solution)/shard_map/ppermute | solution.py:583
  89.2 2.4 %collective-permute-start.7 = (bf16[64,3584]{1,0:T(8,128)(2,1)}, bf16[64,3584]{1,0:T(8,128)(2,1)S(1)}, u32[]{:S(2)}, u32[]{:S(2)}) collective-permute-start(bf16[64,3584]{1,0:T(8,128)(2,1)} %collective-permute-done.3.refs_10_), channel_id=1, source_target_pairs={{0,32},{1,33},{2,34},{3,35},{4,36},{5,37},{6,38},{7,39},{8,40},{9,... | collective-permute-start | bytes 1376264 | tf_op jit(solution)/shard_map/ppermute | solution.py:583
  91.6 1.9 %collective-permute-done.7.refs_13_ = bf16[64,3584]{1,0:T(8,128)(2,1)S(1)} collective-permute-done((bf16[64,3584]{1,0:T(8,128)(2,1)}, bf16[64,3584]{1,0:T(8,128)(2,1)S(1)}, u32[]{:S(2)}, u32[]{:S(2)}) %collective-permute-start.7) | collective-permute-done | bytes 458784 | tf_op jit(solution)/shard_map/ppermute | solution.py:583
  93.5 8.9 %projector.1 = (f32[32,1024]{1,0:T(8,128)S(1)}, f32[8,768]{1,0:T(8,128)S(1)}) custom-call(s32[5]{0:T(128)S(1)} %stack.23.at_ref.refs_0_, f32[8,768]{1,0:T(8,128)S(1)} %get-tuple-element.35.refs_1_, f32[8,768]{1,0:T(8,128)S(1)} %collective-permute-done.5.refs_2_, f32[8,768]{1,0:T(8,128)S(1)} %collective-permute-done.4.refs_3_, bf16[192,768]{1,0:T(8,128)(2,1)} %bitcast.33, ...), custom_call_target="tpu_custom_call" | custom-call | flops 2818572288 | bytes 8388608 | tf_op jit(solution)/shard_map/projector/pallas_call | solution.py:307
  102.4 2.3 %collective-permute-start.10 = (f32[8,768]{1,0:T(8,128)S(1)}, f32[8,768]{1,0:T(8,128)S(1)}, u32[]{:S(2)}, u32[]{:S(2)}) collective-permute-start(f32[8,768]{1,0:T(8,128)S(1)} %get-tuple-element.45.refs_1_), channel_id=1, source_target_pairs={{0,32},{32,0},{64,96},{96,64},{128,160},{160,128},{192,224},{224,1... | collective-permute-start | bytes 73736 | tf_op jit(solution)/shard_map/ppermute | solution.py:653
  104.7 6.9 %collective-permute-start.9 = (f32[8,768]{1,0:T(8,128)S(1)}, f32[8,768]{1,0:T(8,128)S(1)}, u32[]{:S(2)}, u32[]{:S(2)}) collective-permute-start(f32[8,768]{1,0:T(8,128)S(1)} %get-tuple-element.45.refs_1_), channel_id=1, source_target_pairs={{32,64},{96,128},{160,192},{224,256},{288,320},{352,384},{416,448}... | collective-permute-start | bytes 73736 | tf_op jit(solution)/shard_map/ppermute | solution.py:653
  111.7 6.9 %collective-permute-done.9.refs_2_ = f32[8,768]{1,0:T(8,128)S(1)} collective-permute-done((f32[8,768]{1,0:T(8,128)S(1)}, f32[8,768]{1,0:T(8,128)S(1)}, u32[]{:S(2)}, u32[]{:S(2)}) %collective-permute-start.9) | collective-permute-done | bytes 24608 | tf_op jit(solution)/shard_map/ppermute | solution.py:653
  118.6 2.6 %back.1 = (bf16[32,32,128]{2,1,0:T(8,128)(2,1)S(1)}, f32[12,64,512]{2,1,0:T(8,128)S(1)}) custom-call(s32[5]{0:T(128)S(1)} %stack.23.at_ref.refs_0_, f32[8,768]{1,0:T(8,128)S(1)} %get-tuple-element.45.refs_1_, f32[8,768]{1,0:T(8,128)S(1)} %collective-permute-done.9.refs_2_, f32[8,768]{1,0:T(8,128)S(1)} %collective-permute-done.10.refs_3_, ...), custom_call_target="tpu_custom_call" | custom-call | tf_op jit(solution)/shard_map/back/pallas_call | solution.py:409
  121.2 16.7 %all_to_all.25.got_ref = bf16[32,32,128]{2,1,0:T(8,128)(2,1)S(1)} all-to-all(bf16[32,32,128]{2,1,0:T(8,128)(2,1)S(1)} %get-tuple-element.49), channel_id=1, replica_groups={{0,32,1,33,2,34,3,35,128,160,129,161,130,162,131,163,256,288,257,289,25..., dimensions={0} | all-to-all | bytes 524288 | tf_op jit(solution)/shard_map/all_to_all | solution.py:571
  138.4 18.4 %all_to_all.26.got_ref = bf16[16,32,128]{2,1,0:T(8,128)(2,1)S(1)} all-to-all(bf16[16,32,128]{2,1,0:T(8,128)(2,1)S(1)} %plane.1), channel_id=1, replica_groups={{0,4,8,12,16,20,24,28,64,68,72,76,80,84,88,92},{32,36,40,44,48,52,56,60..., dimensions={0} | all-to-all | bytes 262144 | tf_op jit(solution)/shard_map/all_to_all | solution.py:571
  158.1 6.4 %all-to-all-start.4 = ((bf16[32,16,128]{2,1,0:T(8,128)(2,1)}), bf16[32,16,128]{2,1,0:T(8,128)(2,1)S(1)}, u32[]{:S(2)}, u32[]{:S(2)}) async-start(bf16[32,16,128]{2,1,0:T(8,128)(2,1)} %get-tuple-element.52), calls=%async_computation.4 | async-start | bytes 262144 | tf_op jit(solution)/shard_map/all_to_all | solution.py:571
  166.1 6.1 %all-to-all-done.4.got_ref = bf16[32,16,128]{2,1,0:T(8,128)(2,1)S(1)} async-done(((bf16[32,16,128]{2,1,0:T(8,128)(2,1)}), bf16[32,16,128]{2,1,0:T(8,128)(2,1)S(1)}, u32[]{:S(2)}, u32[]{:S(2)}) %all-to-all-start.4) | async-done | bytes 131104 | tf_op jit(solution)/shard_map/all_to_all | solution.py:571
  (39 shorter events, 12.4 us)
Async XLA Ops:
  2.5 1.1 copy-start
  4.9 39.4 %all-to-all-start = ((f32[16,8,128]{2,1,0:T(8,128)}), f32[16,8,128]{2,1,0:T(8,128)S(1)}, u32[]{:S(2)}, u32[]{:S(2)}) async-start(f32[16,8,128]{2,1,0:T(8,128)} %stats.1), calls=%async_computation | async-start | bytes 131072 | tf_op jit(solution)/shard_map/all_to_all | solution.py:686
  24.0 20.3 %collective-permute-start = (bf16[16,3584]{1,0:T(8,128)(2,1)S(1)}, bf16[16,3584]{1,0:T(8,128)(2,1)S(1)}, u32[]{:S(2)}, u32[]{:S(2)}) collective-permute-start(bf16[16,3584]{1,0:T(8,128)(2,1)S(1)} %get-tuple-element.32), channel_id=1, source_target_pairs={{0,92},{1,93},{2,94},{3,95},{4,88},{5,89},{6,90},{7,91},{8,84},{9,... | collective-permute-start | bytes 344072 | tf_op jit(solution)/shard_map/ppermute | solution.py:583
  31.7 32.6 %collective-permute-start.1 = (bf16[64,3584]{1,0:T(8,128)(2,1)S(1)}, bf16[64,3584]{1,0:T(8,128)(2,1)}, u32[]{:S(2)}, u32[]{:S(2)}) collective-permute-start(bf16[64,3584]{1,0:T(8,128)(2,1)S(1)} %get-tuple-element.37), channel_id=1, source_target_pairs={{0,384},{1,385},{2,386},{3,387},{4,388},{5,389},{6,390},{7,391},{8... | collective-permute-start | bytes 1376264 | tf_op jit(solution)/shard_map/ppermute | solution.py:583
  36.0 33.1 %collective-permute-start.2 = (bf16[64,3584]{1,0:T(8,128)(2,1)S(1)}, bf16[64,3584]{1,0:T(8,128)(2,1)}, u32[]{:S(2)}, u32[]{:S(2)}) collective-permute-start(bf16[64,3584]{1,0:T(8,128)(2,1)S(1)} %get-tuple-element.37), channel_id=1, source_target_pairs={{0,128},{1,129},{2,130},{3,131},{4,132},{5,133},{6,134},{7,135},{8... | collective-permute-start | bytes 1376264 | tf_op jit(solution)/shard_map/ppermute | solution.py:583
  45.7 6.7 %copy-start.1 = (bf16[12,2,32,512]{3,2,1,0:T(8,128)(2,1)S(1)}, bf16[12,2,32,512]{3,2,1,0:T(8,128)(2,1)}, u32[]{:S(2)}) copy-start(bf16[12,2,32,512]{3,2,1,0:T(8,128)(2,1)} %param.11) | copy-start | bytes 2359300
  45.8 6.8 %copy-start.2 = (f32[512]{0:T(512)S(1)}, f32[512]{0:T(512)}, u32[]{:S(2)}) copy-start(f32[512]{0:T(512)} %param.12) | copy-start | bytes 6148
  45.8 6.8 %copy-start.3 = (f32[512]{0:T(512)S(1)}, f32[512]{0:T(512)}, u32[]{:S(2)}) copy-start(f32[512]{0:T(512)} %param.13) | copy-start | bytes 6148
  45.8 37.8 %all-to-all-start.1 = ((bf16[16,16,3584]{2,1,0:T(8,128)(2,1)}), bf16[16,16,3584]{2,1,0:T(8,128)(2,1)S(1)}, u32[]{:S(2)}, u32[]{:S(2)}) async-start(bf16[16,16,3584]{2,1,0:T(8,128)(2,1)} %broadcast_in_dim.2), calls=%async_computation.1 | async-start | bytes 3670016 | tf_op jit(solution)/shard_map/all_to_all | solution.py:571
  54.2 37.4 %copy-start.7 = (f32[768]{0:T(1024)S(1)}, f32[768]{0:T(1024)}, u32[]{:S(2)}) copy-start(f32[768]{0:T(1024)} %param.20) | copy-start | bytes 9220
  54.2 39.3 %copy-start.4 = (f32[16,1024]{1,0:T(8,128)S(1)}, f32[16,1024]{1,0:T(8,128)}, u32[]{:S(2)}) copy-start(f32[16,1024]{1,0:T(8,128)} %refs_5_.1) | copy-start | bytes 196612
  54.2 39.3 %copy-start.5 = (f32[2048]{0:T(1024)S(1)}, f32[2048]{0:T(1024)}, u32[]{:S(2)}) copy-start(f32[2048]{0:T(1024)} %param.18) | copy-start | bytes 24580
  54.3 39.3 %copy-start.6 = (f32[1024]{0:T(1024)S(1)}, f32[1024]{0:T(1024)}, u32[]{:S(2)}) copy-start(f32[1024]{0:T(1024)} %param.16) | copy-start | bytes 12292
  54.3 17.2 %collective-permute-start.4 = (f32[8,768]{1,0:T(8,128)S(1)}, f32[8,768]{1,0:T(8,128)S(1)}, u32[]{:S(2)}, u32[]{:S(2)}) collective-permute-start(f32[8,768]{1,0:T(8,128)S(1)} %get-tuple-element.38), channel_id=1, source_target_pairs={{32,64},{96,128},{160,192},{224,256},{288,320},{352,384},{416,448}... | collective-permute-start | bytes 73736 | tf_op jit(solution)/shard_map/ppermute | solution.py:653
  62.4 9.1 %collective-permute-start.5 = (f32[8,768]{1,0:T(8,128)S(1)}, f32[8,768]{1,0:T(8,128)S(1)}, u32[]{:S(2)}, u32[]{:S(2)}) collective-permute-start(f32[8,768]{1,0:T(8,128)S(1)} %get-tuple-element.39), channel_id=1, source_target_pairs={{0,32},{32,0},{64,96},{96,64},{128,160},{160,128},{192,224},{224,1... | collective-permute-start | bytes 73736 | tf_op jit(solution)/shard_map/ppermute | solution.py:653
  64.3 19.2 %collective-permute-start.3 = (bf16[64,3584]{1,0:T(8,128)(2,1)}, bf16[64,3584]{1,0:T(8,128)(2,1)}, u32[]{:S(2)}, u32[]{:S(2)}) collective-permute-start(bf16[64,3584]{1,0:T(8,128)(2,1)} %collective-permute-done.1), channel_id=1, source_target_pairs={{0,384},{1,385},{2,386},{3,387},{4,388},{5,389},{6,390},{7,391},{8... | collective-permute-start | bytes 1376264 | tf_op jit(solution)/shard_map/ppermute | solution.py:583
  83.5 10.0 %collective-permute-start.8 = (bf16[256,3584]{1,0:T(8,128)(2,1)S(1)}, bf16[256,3584]{1,0:T(8,128)(2,1)S(1)}, u32[]{:S(2)}, u32[]{:S(2)}) collective-permute-start(bf16[256,3584]{1,0:T(8,128)(2,1)S(1)} %bitcast.22), channel_id=1, source_target_pairs={{0,32},{1,33},{2,34},{3,35},{4,36},{5,37},{6,38},{7,39},{8,40},{9,... | collective-permute-start | bytes 5505032 | tf_op jit(solution)/shard_map/ppermute | solution.py:583
  87.3 6.2 %collective-permute-start.6 = (bf16[192,3584]{1,0:T(8,128)(2,1)}, bf16[192,3584]{1,0:T(8,128)(2,1)S(1)}, u32[]{:S(2)}, u32[]{:S(2)}) collective-permute-start(bf16[192,3584]{1,0:T(8,128)(2,1)} %pad_maximum_fusion.refs_9_), channel_id=1, source_target_pairs={{0,32},{1,33},{2,34},{3,35},{4,36},{5,37},{6,38},{7,39},{8,40},{9,... | collective-permute-start | bytes 4128776 | tf_op jit(solution)/shard_map/ppermute | solution.py:583
  89.2 4.3 %collective-permute-start.7 = (bf16[64,3584]{1,0:T(8,128)(2,1)}, bf16[64,3584]{1,0:T(8,128)(2,1)S(1)}, u32[]{:S(2)}, u32[]{:S(2)}) collective-permute-start(bf16[64,3584]{1,0:T(8,128)(2,1)} %collective-permute-done.3.refs_10_), channel_id=1, source_target_pairs={{0,32},{1,33},{2,34},{3,35},{4,36},{5,37},{6,38},{7,39},{8,40},{9,... | collective-permute-start | bytes 1376264 | tf_op jit(solution)/shard_map/ppermute | solution.py:583
  102.4 9.2 %collective-permute-start.10 = (f32[8,768]{1,0:T(8,128)S(1)}, f32[8,768]{1,0:T(8,128)S(1)}, u32[]{:S(2)}, u32[]{:S(2)}) collective-permute-start(f32[8,768]{1,0:T(8,128)S(1)} %get-tuple-element.45.refs_1_), channel_id=1, source_target_pairs={{0,32},{32,0},{64,96},{96,64},{128,160},{160,128},{192,224},{224,1... | collective-permute-start | bytes 73736 | tf_op jit(solution)/shard_map/ppermute | solution.py:653
  104.7 13.9 %collective-permute-start.9 = (f32[8,768]{1,0:T(8,128)S(1)}, f32[8,768]{1,0:T(8,128)S(1)}, u32[]{:S(2)}, u32[]{:S(2)}) collective-permute-start(f32[8,768]{1,0:T(8,128)S(1)} %get-tuple-element.45.refs_1_), channel_id=1, source_target_pairs={{32,64},{96,128},{160,192},{224,256},{288,320},{352,384},{416,448}... | collective-permute-start | bytes 73736 | tf_op jit(solution)/shard_map/ppermute | solution.py:653
  158.1 14.1 %all-to-all-start.4 = ((bf16[32,16,128]{2,1,0:T(8,128)(2,1)}), bf16[32,16,128]{2,1,0:T(8,128)(2,1)S(1)}, u32[]{:S(2)}, u32[]{:S(2)}) async-start(bf16[32,16,128]{2,1,0:T(8,128)(2,1)} %get-tuple-element.52), calls=%async_computation.4 | async-start | bytes 262144 | tf_op jit(solution)/shard_map/all_to_all | solution.py:571
